TPU v7x, 32 devices: a whole 2x2x4 slice. The times are simulated.
32 devices in a mesh: dp: 8 (over y, x, core), mp: 4 (over z).
Axes of the slice: x: 2, y: 2, z: 4, core: 2. Of those that a mesh axis runs over, the one named last changes fastest.
Arguments:
- features: bfloat16 [16384, 2048], P('dp', 'mp'), may hold values from -6 to 6
- neighbour_lists: int32 [16384, 32], P('dp'), may hold values from -1 to 2047, as said below
- node_counts: int32 [8], P('dp'), may hold values from 1024 to 2048, as said below
- weight: bfloat16 [2048, 2048], P(None, 'mp'), may hold values from -0.375 to 0.375
- bias_terms: bfloat16 [2048], P('mp'), may hold values from -1.796875 to 1.796875
- cotangent: bfloat16 [16384, 2048], P('dp', 'mp'), may hold values from -6 to 6
Outputs:
- output: bfloat16 [16384, 2048], P('dp', 'mp')
- features_grad: bfloat16 [16384, 2048], P('dp', 'mp')
- weight_grad: float32 [2048, 2048], P(None, 'mp')
- bias_grad: float32 [2048], P('mp')
Inputs may be any that keep to these rules, and one draw needn't show every extreme that they name: `node_counts`: in every draw some group holds exactly 2048 true nodes and another exactly half of that. `neighbour_lists`: each row lists its neighbours first and fills the rest with -1. Neighbours are true nodes of the same group and the same cluster, never the row itself, and may repeat; clusters are runs of consecutive slots. Padding rows hold only -1. In every group the first row has 32 neighbours.
All inputs are finite; a program needn't handle non-finite values.
Results may differ from a plain program's by a relative error of at most 0.0064.
Values may be sent and summed in bfloat16 or wider, within the bound.
No kernel may reach another device: no remote copies, remote signals or barrier semaphores. Data moves between devices by JAX's collectives and lax.ppermute only.
A program may use at most 192 MiB of HBM per device.

v0:
```python
import jax
import jax.numpy as jnp
from jax import lax
from jax.sharding import PartitionSpec as P


def block_size():
    return 512


def neighbour_parts(neighbour_lists):
    present = neighbour_lists >= 0
    clamped = jnp.where(present, neighbour_lists, 0)
    degree = jnp.sum(present.astype(jnp.float32), axis=1)
    return (present, clamped, degree)


def silu_slope(linear):
    sigma = jax.nn.sigmoid(linear)
    return sigma * (1.0 + linear * (1.0 - sigma))


def aggregate(features, neighbour_lists):
    height, breadth = features.shape
    present, clamped, degree = neighbour_parts(neighbour_lists)
    stride = block_size()
    slots_wide = neighbour_lists.shape[1]

    def one_block(inputs):
        indices, chosen, itself, divisor = inputs
        picked = jnp.take(features, indices, axis=0)
        summed = jnp.sum(jnp.where(chosen[:, :, None], picked.astype(jnp.float32), 0.0), axis=1)
        return (summed + 2.0 * itself.astype(jnp.float32)) / (divisor + 1.0)[:, None]

    blocks = lax.map(
        one_block,
        (
            clamped.reshape(-1, stride, slots_wide),
            present.reshape(-1, stride, slots_wide),
            features.reshape(-1, stride, breadth),
            degree.reshape(-1, stride),
        ),
    )
    return blocks.reshape(height, breadth)


def spread_back(gradient, neighbour_lists):
    height, breadth = gradient.shape
    present, clamped, degree = neighbour_parts(neighbour_lists)
    stride = block_size()
    slots_wide = neighbour_lists.shape[1]
    scaled = gradient.astype(jnp.float32) / (degree + 1.0)[:, None]

    def add_block(summed, inputs):
        indices, chosen, portion = inputs
        values = jnp.where(chosen[:, :, None], portion[:, None, :], 0.0)
        return (summed.at[indices.reshape(-1)].add(values.reshape(-1, breadth)), None)

    summed, unused = lax.scan(
        add_block,
        2.0 * scaled,
        (
            clamped.reshape(-1, stride, slots_wide),
            present.reshape(-1, stride, slots_wide),
            scaled.reshape(-1, stride, breadth),
        ),
    )
    return summed


def local(features, neighbour_lists, node_counts, weight, bias_terms, cotangent):
    mp_count = lax.axis_size("mp")
    column_slot = lax.axis_index("mp")
    height = features.shape[0]
    row_share = height // mp_count
    gathered_rows = lax.all_to_all(
        aggregate(features, neighbour_lists).astype(jnp.bfloat16),
        "mp",
        split_axis=0,
        concat_axis=1,
        tiled=True,
    )
    weight_full, bias_full = (
        lax.all_gather(weight, "mp", axis=1, tiled=True),
        lax.all_gather(bias_terms, "mp", axis=0, tiled=True),
    )
    first_row = column_slot * row_share
    living = (first_row + jnp.arange(row_share) < node_counts[0]).astype(jnp.float32)[:, None]
    linear = jnp.dot(
        gathered_rows, weight_full, preferred_element_type=jnp.float32
    ) + bias_full.astype(jnp.float32)
    result_rows = (jax.nn.silu(linear) * living).astype(jnp.bfloat16)
    output = lax.all_to_all(result_rows, "mp", split_axis=1, concat_axis=0, tiled=True)
    upstream = lax.all_to_all(cotangent, "mp", split_axis=0, concat_axis=1, tiled=True)
    again_rows = lax.all_to_all(
        aggregate(features, neighbour_lists).astype(jnp.bfloat16),
        "mp",
        split_axis=0,
        concat_axis=1,
        tiled=True,
    )
    again_linear = jnp.dot(
        again_rows, weight_full, preferred_element_type=jnp.float32
    ) + bias_full.astype(jnp.float32)
    grad_linear = (upstream.astype(jnp.float32) * silu_slope(again_linear) * living).astype(
        jnp.bfloat16
    )
    weight_part = lax.dot_general(
        again_rows, grad_linear, (((0,), (0,)), ((), ())), preferred_element_type=jnp.float32
    )
    bias_part = jnp.sum(grad_linear.astype(jnp.float32), axis=0)
    grad_rows = lax.dot_general(
        grad_linear, weight_full, (((1,), (1,)), ((), ())), preferred_element_type=jnp.float32
    ).astype(jnp.bfloat16)
    grad_local = lax.all_to_all(grad_rows, "mp", split_axis=1, concat_axis=0, tiled=True)
    features_grad = spread_back(grad_local, neighbour_lists).astype(jnp.bfloat16)
    weight_all, bias_all = lax.psum((weight_part, bias_part), ("dp", "mp"))
    columns = weight.shape[1]
    weight_grad = lax.dynamic_slice_in_dim(weight_all, column_slot * columns, columns, 1)
    bias_grad = lax.dynamic_slice_in_dim(bias_all, column_slot * columns, columns, 0)
    return (output, features_grad, weight_grad, bias_grad)


def solution(mesh):
    in_specs = (P("dp", "mp"), P("dp", None), P("dp"), P(None, "mp"), P("mp"), P("dp", "mp"))
    out_specs = (P("dp", "mp"), P("dp", "mp"), P(None, "mp"), P("mp"))
    return jax.shard_map(local, mesh=mesh, in_specs=in_specs, out_specs=out_specs, check_vma=False)
```

profile of v0, /device:TPU:0, one launch (start us, length us, event | category | flops | bytes accessed | tf_op | source)
XLA Modules:
  0.0 1054.5 jit_solution(5844433434456474789)
XLA Ops:
  7.9 6.3 all-to-all-start.2
  16.7 316.8 %while.24 = (s32[]{:T(128)}, bf16[4,512,512]{1,2,0:T(8,128)(2,1)}, pred[4,512,32]{2,1,0:T(8,128)(4,1)}, s32[4,512,32]{2,1,0:T(8,128)}, bf16[2048,512]{1,0:T(8,12...) while((s32[]{:T(128)}, bf16[4,512,512]{1,2,0:T(8,128)(2,1)}, ...), condition=%wide.region_3.5_spmd, body=%wide.region_1.4_spmd.sunk | while | flops 34718208 | bytes 56121456 | solution.py:35
  18.8 66.3 %gather_fusion = bf16[16384,512]{1,0:T(8,128)(2,1)} fusion(bf16[2048,512]{1,0:T(8,128)(2,1)S(1)} %bitcast.70, s32[16384]{0:T(1024)S(1)} %broadcast_clamp_fusion.2), kind=kCustom, calls=%fused_computation.clone.clone.1 | custom fusion | bytes 33619968 | tf_op jit(solution)/shard_map/while/body/eval_jaxpr/jit(_take)/gather | solution.py:31
  85.0 9.7 select_reduce_fusion.2
  98.0 66.3 %gather_fusion = bf16[16384,512]{1,0:T(8,128)(2,1)} fusion(bf16[2048,512]{1,0:T(8,128)(2,1)S(1)} %bitcast.70, s32[16384]{0:T(1024)S(1)} %broadcast_clamp_fusion.2), kind=kCustom, calls=%fused_computation.clone.clone.1 | custom fusion | bytes 33619968 | tf_op jit(solution)/shard_map/while/body/eval_jaxpr/jit(_take)/gather | solution.py:31
  164.2 9.7 select_reduce_fusion.2
  177.2 66.3 %gather_fusion = bf16[16384,512]{1,0:T(8,128)(2,1)} fusion(bf16[2048,512]{1,0:T(8,128)(2,1)S(1)} %bitcast.70, s32[16384]{0:T(1024)S(1)} %broadcast_clamp_fusion.2), kind=kCustom, calls=%fused_computation.clone.clone.1 | custom fusion | bytes 33619968 | tf_op jit(solution)/shard_map/while/body/eval_jaxpr/jit(_take)/gather | solution.py:31
  243.4 9.7 select_reduce_fusion.2
  256.3 66.3 %gather_fusion = bf16[16384,512]{1,0:T(8,128)(2,1)} fusion(bf16[2048,512]{1,0:T(8,128)(2,1)S(1)} %bitcast.70, s32[16384]{0:T(1024)S(1)} %broadcast_clamp_fusion.2), kind=kCustom, calls=%fused_computation.clone.clone.1 | custom fusion | bytes 33619968 | tf_op jit(solution)/shard_map/while/body/eval_jaxpr/jit(_take)/gather | solution.py:31
  322.6 9.7 select_reduce_fusion.2
  333.5 5.2 all-to-all-start
  339.4 52.3 %all-gather = bf16[4,1,512]{2,1,0:T(2,128)(2,1)S(1)} all-gather(bf16[1,1,512]{2,1,0:T(2,128)(2,1)S(1)} %reshape.147), channel_id=1, replica_groups=mesh['dp'=8,'mp'=4] {'mp'}, dimensions={0}, use_global_device_ids=true | all-gather | bytes 5120 | tf_op jit(solution)/shard_map/all_gather | solution.py:85
  393.9 2.7 copy.33
  396.6 12.3 %convert_reduce_fusion = (f32[2048]{0:T(1024)S(1)}, bf16[512,2048]{1,0:T(8,128)(2,1)}, bf16[512,2048]{1,0:T(8,128)(2,1)S(1)}) fusion(f32[512]{0:T(512)S(1)} %fusion.2, f32[512,2048]{1,0:T(8,128)} %bitcast.76, f32[2048]{0:T(1024)S(1)} %bitcast.83, bf16[512,2048]{0,1:T(8,128)(2,1)S(1)} %bitcast.78, bf16[2048,2048]{1,0:T(8,128)(2,1)} %all-gather.3.cloned.1.call-done), kind=kOutput, calls=%fused_computation.20 | convolution fusion | flops 4311742464 | bytes 18892800 | tf_op jit(solution)/shard_map/dot_general | solution.py:89
  410.3 3.6 all-to-all-start.1
  413.9 8.5 convolution_convert_fusion
  424.0 34.9 %all-to-all-done.1 = bf16[512,4,512]{2,0,1:T(8,128)(2,1)S(1)} async-done(((bf16[512,4,512]{2,0,1:T(8,128)(2,1)}), bf16[512,4,512]{2,0,1:T(8,128)(2,1)S(1)}, u32[]{:S(2)}, u32[]{:S(2)}) %all-to-all-start.1) | async-done | bytes 2097184 | tf_op jit(solution)/shard_map/all_to_all | solution.py:93
  460.2 3.6 all-to-all-start.3
  464.0 12.5 %fusion.3 = f32[2048,2048]{1,0:T(8,128)} fusion(bf16[512,2048]{0,1:T(8,128)(2,1)} %bitcast.79, bf16[512,2048]{1,0:T(8,128)(2,1)} %get-tuple-element.112), kind=kOutput, calls=%fused_computation.35 | convolution fusion | flops 4294967296 | bytes 20971520 | tf_op jit(solution)/shard_map/dot_general | solution.py:108
  476.5 70.6 %psum.15 = f32[2048]{0:T(1024)S(1)} all-reduce(f32[2048]{0:T(1024)S(1)} %get-tuple-element.111), channel_id=1, replica_groups=mesh['dp'=8,'mp'=4] {'dp','mp'}, use_global_device_ids=true, to_apply=%region_9.11 | all-reduce | flops 2048 | bytes 16384 | tf_op jit(solution)/shard_map/psum | solution.py:117
  547.7 2.6 fusion.1
  552.8 485.1 %while.25 = (s32[]{:T(128)}, f32[2048,512]{1,0:T(8,128)}, s32[4,512,32]{2,1,0:T(8,128)}, pred[4,512,32]{2,1,0:T(8,128)(4,1)}, f32[4,512,512]{2,1,0:T(8,128)}, /*index=5*/s32[]{:T(128)}) while((s32[]{:T(128)}, f32[2048,512]{1,0:T(8,128)}, s32[4,512,32]{2,1,0:T(8,128)}, pred[4,512,32]{2,1,0:T(8,128)(4,1)}, f32[4,512,512]{2,1,0:T(8,128)}, ...), condition=%wide.region_6.8_spmd, body=%wide.region_4.7_spmd.sunk | while | flops 16826368 | bytes 137904224 | solution.py:59
  556.3 11.4 %bitcast_select_fusion.2 = f32[16384,512]{1,0:T(8,128)} fusion(f32[512,512]{1,0:T(8,128)S(1)} %dynamic-slice_bitcast_fusion.5, pred[16384]{0:T(1024)(128)(4,1)S(1)} %broadcast_in_dim.95), kind=kLoop, calls=%fused_computation.2.clone.1 | loop fusion | flops 8388608 | bytes 34619392 | tf_op jit(solution)/shard_map/while/body/eval_jaxpr/jit(_where)/select_n | solution.py:56
  567.7 105.1 %scatter_fusion = f32[2048,512]{1,0:T(8,128)} fusion(f32[2048,512]{1,0:T(8,128)} %get-tuple-element.225, s32[16384]{0:T(1024)S(1)} %bitcast.75, f32[16384,512]{1,0:T(8,128)} %bitcast_select_fusion.2), kind=kCustom, calls=%fused_computation.1.clone.1 | custom fusion | flops 8388608 | bytes 100728832 | tf_op jit(solution)/shard_map/while/body/eval_jaxpr/scatter-add | solution.py:57
  676.4 11.2 %bitcast_select_fusion.2 = f32[16384,512]{1,0:T(8,128)} fusion(f32[512,512]{1,0:T(8,128)S(1)} %dynamic-slice_bitcast_fusion.5, pred[16384]{0:T(1024)(128)(4,1)S(1)} %broadcast_in_dim.95), kind=kLoop, calls=%fused_computation.2.clone.1 | loop fusion | flops 8388608 | bytes 34619392 | tf_op jit(solution)/shard_map/while/body/eval_jaxpr/jit(_where)/select_n | solution.py:56
  687.5 105.2 %scatter_fusion = f32[2048,512]{1,0:T(8,128)} fusion(f32[2048,512]{1,0:T(8,128)} %get-tuple-element.225, s32[16384]{0:T(1024)S(1)} %bitcast.75, f32[16384,512]{1,0:T(8,128)} %bitcast_select_fusion.2), kind=kCustom, calls=%fused_computation.1.clone.1 | custom fusion | flops 8388608 | bytes 100728832 | tf_op jit(solution)/shard_map/while/body/eval_jaxpr/scatter-add | solution.py:57
  796.2 11.1 %bitcast_select_fusion.2 = f32[16384,512]{1,0:T(8,128)} fusion(f32[512,512]{1,0:T(8,128)S(1)} %dynamic-slice_bitcast_fusion.5, pred[16384]{0:T(1024)(128)(4,1)S(1)} %broadcast_in_dim.95), kind=kLoop, calls=%fused_computation.2.clone.1 | loop fusion | flops 8388608 | bytes 34619392 | tf_op jit(solution)/shard_map/while/body/eval_jaxpr/jit(_where)/select_n | solution.py:56
  807.4 105.2 %scatter_fusion = f32[2048,512]{1,0:T(8,128)} fusion(f32[2048,512]{1,0:T(8,128)} %get-tuple-element.225, s32[16384]{0:T(1024)S(1)} %bitcast.75, f32[16384,512]{1,0:T(8,128)} %bitcast_select_fusion.2), kind=kCustom, calls=%fused_computation.1.clone.1 | custom fusion | flops 8388608 | bytes 100728832 | tf_op jit(solution)/shard_map/while/body/eval_jaxpr/scatter-add | solution.py:57
  916.0 11.1 %bitcast_select_fusion.2 = f32[16384,512]{1,0:T(8,128)} fusion(f32[512,512]{1,0:T(8,128)S(1)} %dynamic-slice_bitcast_fusion.5, pred[16384]{0:T(1024)(128)(4,1)S(1)} %broadcast_in_dim.95), kind=kLoop, calls=%fused_computation.2.clone.1 | loop fusion | flops 8388608 | bytes 34619392 | tf_op jit(solution)/shard_map/while/body/eval_jaxpr/jit(_where)/select_n | solution.py:56
  927.2 110.6 %scatter_fusion = f32[2048,512]{1,0:T(8,128)} fusion(f32[2048,512]{1,0:T(8,128)} %get-tuple-element.225, s32[16384]{0:T(1024)S(1)} %bitcast.75, f32[16384,512]{1,0:T(8,128)} %bitcast_select_fusion.2), kind=kCustom, calls=%fused_computation.1.clone.1 | custom fusion | flops 8388608 | bytes 100728832 | tf_op jit(solution)/shard_map/while/body/eval_jaxpr/scatter-add | solution.py:57
  1037.8 3.8 convert_element_type.81
  1041.6 4.8 constant_dynamic-slice_fusion.2
  (98 shorter events, 41.3 us)
Async XLA Ops:
  7.2 7.1 copy-start.4
  7.2 9.6 copy-start
  7.2 389.4 %all-gather.3.cloned.1.call-start = ((), (), s32[]{:S(2)}) async-start(), calls=%async_computation.4 | async-start | bytes 10485760 | tf_op jit(solution)/shard_map/all_gather | solution.py:84
  7.9 325.6 %all-to-all-start.2 = ((bf16[4,512,512]{2,1,0:T(8,128)(2,1)}), bf16[4,512,512]{2,1,0:T(8,128)(2,1)}, u32[]{:S(2)}, u32[]{:S(2)}) async-start(bf16[4,512,512]{2,1,0:T(8,128)(2,1)} %bitcast.77), calls=%async_computation.2 | async-start | bytes 4194304 | tf_op jit(solution)/shard_map/all_to_all | solution.py:94
  14.3 2.4 copy-start.5
  333.5 5.9 copy-start.7
  333.5 63.0 %all-to-all-start = ((bf16[4,512,512]{1,2,0:T(8,128)(2,1)}), bf16[4,512,512]{1,2,0:T(8,128)(2,1)S(1)}, u32[]{:S(2)}, u32[]{:S(2)}) async-start(bf16[4,512,512]{1,2,0:T(8,128)(2,1)} %get-tuple-element.83), calls=%async_computation | async-start | bytes 4194304 | tf_op jit(solution)/shard_map/all_to_all | solution.py:76
  396.6 12.3 %copy-start.3 = (bf16[4,512,512]{1,2,0:T(8,128)(2,1)}, bf16[4,512,512]{1,2,0:T(8,128)(2,1)S(1)}, u32[]{:S(2)}) copy-start(bf16[4,512,512]{1,2,0:T(8,128)(2,1)S(1)} %all-to-all-done) | copy-start | bytes 6291460
  410.3 48.5 %all-to-all-start.1 = ((bf16[512,4,512]{2,0,1:T(8,128)(2,1)}), bf16[512,4,512]{2,0,1:T(8,128)(2,1)S(1)}, u32[]{:S(2)}, u32[]{:S(2)}) async-start(bf16[512,4,512]{2,0,1:T(8,128)(2,1)} %bitcast.74), calls=%async_computation.1 | async-start | bytes 4194304 | tf_op jit(solution)/shard_map/all_to_all | solution.py:93
  422.5 41.5 %copy-start.6 = (f32[2048]{0:T(1024)S(1)}, f32[2048]{0:T(1024)}, u32[]{:S(2)}) copy-start(f32[2048]{0:T(1024)} %copy-done.5) | copy-start | bytes 24580
  458.8 1.3 copy-start.1
  460.2 87.6 %all-to-all-start.3 = ((bf16[512,4,512]{2,0,1:T(8,128)(2,1)}), bf16[512,4,512]{2,0,1:T(8,128)(2,1)S(1)}, u32[]{:S(2)}, u32[]{:S(2)}) async-start(bf16[512,4,512]{2,0,1:T(8,128)(2,1)} %bitcast.73), calls=%async_computation.3 | async-start | bytes 4194304 | tf_op jit(solution)/shard_map/all_to_all | solution.py:115
  463.8 577.8 %all-reduce.2.cloned.1.call-start = ((), (), s32[]{:S(2)}) async-start(), calls=%async_computation.5 | async-start | bytes 33554432 | tf_op jit(solution)/shard_map/psum | solution.py:117
  1041.6 4.8 copy-start.2
Sparse Core Ops, SparseCore 0:
  9.6 188.2 all-gather.2
  476.6 304.8 all-reduce.1
where the time goes:
time: 1070 us; the launch traced here: 1050 us
  other arithmetic  526 us (49%)
  local copies, waits for them, and re-layouts  303 us (28%)
  blocking collectives  123 us (11%)
  waiting for transfers between devices  35.6 us (3%)
  matrix products  33.3 us (3%)
  starting transfers between devices  19.1 us (2%)
  between operations  14.8 us (1%)
    scatter-add x4, other arithmetic, add_block(): summed.at[indices.reshape(-1)].add(values.reshape(-1, breadth))  426 us
    gather x4, local copies, waits for them, and re-layouts, one_block(): picked = jnp.take(features, indices, axis=0)  265 us
    psum x1, blocking collectives, local(): weight_all, bias_all = lax.psum((weight_part, bias_part), ('dp', 'mp'))  70.6 us
    all_gather x1, blocking collectives, local(): lax.all_gather(bias_terms, 'mp', axis=0, tiled=True)  52.3 us
    select_n x4, other arithmetic, add_block(): values = jnp.where(chosen[:, :, None], portion[:, None, :], 0.0)  44.8 us
    reduce_sum x4, other arithmetic, one_block(): jnp.sum(jnp.where(chosen[:, :, None], picked.astype(jnp.float32), 0.0), a...  38.6 us
    all_to_all x1, waiting for transfers between devices, local(): lax.all_to_all(result_rows, 'mp', split_axis=1, concat_axis=0, tiled=True)  34.9 us
  transfers between devices with their start and end apart: 6, of which 1 were waited for; matrix products, arithmetic and copies ran while one was open for 80% of the time, Pallas kernels for 0%

commit v1 on v0

v1 whole, which is shorter than its diff:
```python
import functools

import jax
import jax.numpy as jnp
from jax import lax
from jax.experimental import pallas as pl
from jax.experimental.pallas import tpu as pltpu
from jax.sharding import PartitionSpec as P

BF16 = jnp.bfloat16
F32 = jnp.float32
SLABS = 4
LANES = 128
VMEM_LIMIT = 48 << 20


def count_kernel(base, where_ref, packed_ref, lists_ref, feat_ref, counts_ref, same_ref, other_ref):
    rows, slots = lists_ref.shape
    step = pl.program_id(0)
    side = where_ref[0] % 2
    steps = pl.num_programs(0)
    block = (step + side * (steps // 2)) % steps
    row = lax.broadcasted_iota(jnp.int32, (LANES, 8 * slots), 0)
    owner = lax.broadcasted_iota(jnp.int32, (1, 8 * slots), 1) // slots

    def group(index):
        entry = packed_ref[index : index + 1, :]
        high = (entry >> 7) * 8 + owner
        low = entry & (LANES - 1)
        left = jnp.where(high == row, 1.0, 0.0).astype(BF16)
        right = jnp.where(low == row, 1.0, 0.0).astype(BF16)
        return lax.dot_general(left, right, (((1,), (1,)), ((), ())), preferred_element_type=F32)

    for pair in range(rows // 16):
        first, second = group(2 * pair), group(2 * pair + 1)
        for tile in range(counts_ref.shape[1] // LANES):
            counts_ref[pair * 16 : (pair + 1) * 16, tile * LANES : (tile + 1) * LANES] = jnp.concatenate(
                [first[tile * 8 : (tile + 1) * 8], second[tile * 8 : (tile + 1) * 8]], 0
            ).astype(BF16)
    down = lax.broadcasted_iota(jnp.int32, (LANES, LANES), 0)
    across = lax.broadcasted_iota(jnp.int32, (LANES, LANES), 1)
    twice = jnp.where(down == across, 2.0, 0.0)
    column = pl.multiple_of(base + block * rows, LANES)
    tile_view = counts_ref[:, pl.ds(column, LANES)].astype(F32)
    counts_ref[:, pl.ds(column, LANES)] = (tile_view + twice).astype(BF16)
    degree = jnp.sum(jnp.where(lists_ref[...] >= 0, 1.0, 0.0), axis=1, keepdims=True)
    total = jnp.dot(counts_ref[...], feat_ref[...], preferred_element_type=F32)
    result = (total / (degree + 1.0)).astype(BF16)

    @pl.when(step < steps // 2)
    def _():
        same_ref[...] = result

    @pl.when(step >= steps // 2)
    def _():
        other_ref[...] = result


def count_call(where, packed, lists, features, base, size):
    nodes, slots = lists.shape
    width = features.shape[1]
    rows = LANES
    steps = size // rows
    half = steps // 2

    def natural(step, where_ref):
        return (step + (where_ref[0] % 2) * half) % steps

    return pl.pallas_call(
        functools.partial(count_kernel, base),
        grid_spec=pltpu.PrefetchScalarGridSpec(
            num_scalar_prefetch=1,
            grid=(steps,),
            in_specs=[
                pl.BlockSpec((rows // 8, 8 * slots), lambda i, w: (base // rows + natural(i, w), 0)),
                pl.BlockSpec((rows, slots), lambda i, w: (base // rows + natural(i, w), 0)),
                pl.BlockSpec((nodes, width), lambda i, w: (0, 0)),
            ],
            out_specs=[
                pl.BlockSpec((rows, nodes), lambda i, w: (natural(i, w), 0)),
                pl.BlockSpec((rows, width), lambda i, w: (jnp.minimum(i, half - 1), 0)),
                pl.BlockSpec((rows, width), lambda i, w: (jnp.maximum(i - half, 0), 0)),
            ],
        ),
        out_shape=[
            jax.ShapeDtypeStruct((size, nodes), BF16),
            jax.ShapeDtypeStruct((size // 2, width), BF16),
            jax.ShapeDtypeStruct((size // 2, width), BF16),
        ],
        compiler_params=pltpu.CompilerParams(vmem_limit_bytes=VMEM_LIMIT),
        cost_estimate=pl.CostEstimate(
            flops=2 * size * nodes * (width + 512), bytes_accessed=2 * nodes * (size + width), transcendentals=0
        ),
        name="count_and_aggregate",
    )(where, packed, lists, features)


def row_kernel(
    base, where_ref, live_ref, part0, part1, part2, part3, cot_own, cot_sib, weight_own, weight_sib, bias_own, bias_sib,
    out_own, out_sib, grad_own, grad_sib, back0, back1, back2, back3,
):
    rows, width = cot_sib.shape
    place = where_ref[0]
    first = base + (place % 2) * rows
    slot = first + lax.broadcasted_iota(jnp.int32, (rows, width), 0)
    living = slot < live_ref[0]
    parts = (part0, part1, part2, part3)
    starts = [pl.multiple_of((place ^ code) * width, LANES) for code in range(4)]
    grads = []
    for weight, bias, cot, out, grad in (
        (weight_own, bias_own, cot_own, out_own, grad_own),
        (weight_sib, bias_sib, cot_sib, out_sib, grad_sib),
    ):
        linear = bias[...].astype(F32)
        for part, start in zip(parts, starts):
            linear = linear + jnp.dot(part[...], weight[pl.ds(start, width), :], preferred_element_type=F32)
        sigma = 1.0 / (1.0 + jnp.exp(-linear))
        out[...] = jnp.where(living, linear * sigma, 0.0).astype(BF16)
        slope = sigma * (1.0 + linear * (1.0 - sigma))
        value = jnp.where(living, cot[...].astype(F32) * slope, 0.0).astype(BF16)
        grad[...] = value
        grads.append(value)
    for back, start in zip((back0, back1, back2, back3), starts):
        total = jnp.zeros((rows, width), F32)
        for weight, value in zip((weight_own, weight_sib), grads):
            total = total + lax.dot_general(
                value, weight[pl.ds(start, width), :], (((1,), (1,)), ((), ())), preferred_element_type=F32
            )
        back[...] = total.astype(BF16)


def row_call(where, live, parts, cotangent, cot_sib, weight_own, weight_sib, bias_own, bias_sib, base):
    rows, width = cot_sib.shape
    depth = weight_own.shape[0]
    whole = lambda shape: pl.BlockSpec(shape, lambda i, w, c: (0, 0))
    chunk = whole((rows, width))
    return pl.pallas_call(
        functools.partial(row_kernel, base),
        grid_spec=pltpu.PrefetchScalarGridSpec(
            num_scalar_prefetch=2,
            grid=(1,),
            in_specs=[chunk] * 4
            + [pl.BlockSpec((rows, width), lambda i, w, c: (base // rows + w[0] % 2, 0)), chunk]
            + [whole((depth, width))] * 2
            + [whole((1, width))] * 2,
            out_specs=[chunk] * 8,
        ),
        out_shape=[jax.ShapeDtypeStruct((rows, width), BF16)] * 8,
        compiler_params=pltpu.CompilerParams(vmem_limit_bytes=VMEM_LIMIT),
        cost_estimate=pl.CostEstimate(
            flops=2 * 2 * rows * depth * 2 * width, bytes_accessed=2 * (14 * rows + 2 * depth) * width, transcendentals=rows * width * 2
        ),
        name="linear_and_slope",
    )(where, live, *parts, cotangent, cot_sib, weight_own, weight_sib, bias_own, bias_sib)


def product_kernel(slabs, where_ref, *refs):
    parts, grads, (kept, given) = refs[: 4 * slabs], refs[4 * slabs : 6 * slabs], refs[6 * slabs :]
    width = parts[0].shape[1]
    for half in range(2):
        for code in range(4):
            total = jnp.zeros((width, width), F32)
            for slab in range(slabs):
                total = total + lax.dot_general(
                    parts[4 * slab + code][...],
                    grads[2 * slab + half][...],
                    (((0,), (0,)), ((), ())),
                    preferred_element_type=F32,
                )
            block = where_ref[0] ^ code
            rows = pl.ds(pl.multiple_of((block % 2) * width, LANES), width)
            result = total.astype(BF16)

            @pl.when(block // 2 == where_ref[1])
            def _(half=half, rows=rows, result=result):
                kept[half, rows, :] = result

            @pl.when(block // 2 != where_ref[1])
            def _(half=half, rows=rows, result=result):
                given[half, rows, :] = result


def product_call(where, parts, grads):
    slabs = len(parts)
    rows, width = parts[0][0].shape
    operands = [p for quad in parts for p in quad] + [g for pair in grads for g in pair]
    outs = (2, 2 * width, width)
    return pl.pallas_call(
        functools.partial(product_kernel, slabs),
        grid_spec=pltpu.PrefetchScalarGridSpec(
            num_scalar_prefetch=1,
            grid=(1,),
            in_specs=[pl.BlockSpec((rows, width), lambda i, w: (0, 0))] * len(operands),
            out_specs=[pl.BlockSpec(outs, lambda i, w: (0, 0, 0))] * 2,
        ),
        out_shape=[jax.ShapeDtypeStruct(outs, BF16)] * 2,
        compiler_params=pltpu.CompilerParams(vmem_limit_bytes=VMEM_LIMIT),
        name="weight_product",
    )(where, *operands)


def spread_kernel(slabs, final, where_ref, *refs):
    side = where_ref[0] % 2
    out, scaled = refs[-2], refs[-1]
    total = refs[-3][...] if final else None
    for slab in range(slabs):
        counts, lists, near, level, far, cross = refs[6 * slab : 6 * slab + 6]
        rows = near.shape[0]
        mine = pl.multiple_of(side * rows, LANES)
        theirs = pl.multiple_of((1 - side) * rows, LANES)
        scaled[pl.ds(mine, rows), :] = near[...].astype(F32) + far[...].astype(F32)
        scaled[pl.ds(theirs, rows), :] = level[...].astype(F32) + cross[...].astype(F32)
        degree = jnp.sum(jnp.where(lists[...] >= 0, 1.0, 0.0), axis=1, keepdims=True)
        value = (scaled[...] / (degree + 1.0)).astype(BF16)
        term = lax.dot_general(counts[...], value, (((0,), (0,)), ((), ())), preferred_element_type=F32)
        total = term if total is None else total + term
    out[...] = total.astype(out.dtype)


def spread_call(where, lists, entries, slab_at, partial):
    slabs = len(entries)
    size, nodes = entries[0][0].shape
    rows, width = entries[0][1].shape
    slots = lists.shape[1]
    tile = 512
    operands, specs = [], []
    for index, entry in enumerate(entries):
        counts, backs = entry[0], entry[1:]
        at = slab_at[index]
        operands += [counts, lists, *backs]
        specs += [
            pl.BlockSpec((size, tile), lambda i, w: (0, i)),
            pl.BlockSpec((size, slots), lambda i, w, at=at: (at, 0)),
        ] + [pl.BlockSpec((rows, width), lambda i, w: (0, 0))] * 4
    final = partial is not None
    if final:
        operands.append(partial)
        specs.append(pl.BlockSpec((tile, width), lambda i, w: (i, 0)))
    return pl.pallas_call(
        functools.partial(spread_kernel, slabs, final),
        grid_spec=pltpu.PrefetchScalarGridSpec(
            num_scalar_prefetch=1,
            grid=(nodes // tile,),
            in_specs=specs,
            out_specs=pl.BlockSpec((tile, width), lambda i, w: (i, 0)),
            scratch_shapes=[pltpu.VMEM((size, width), F32)],
        ),
        out_shape=jax.ShapeDtypeStruct((nodes, width), BF16 if final else F32),
        compiler_params=pltpu.CompilerParams(vmem_limit_bytes=VMEM_LIMIT),
        name="spread_back",
    )(where, *operands)


def local(features, neighbour_lists, node_counts, weight, bias_terms, cotangent):
    dp_count = lax.axis_size("dp")
    mp_count = lax.axis_size("mp")
    bits = dp_count.bit_length() - 1
    place = lax.axis_index("mp")
    line = lax.axis_index("dp")
    side = place % 2
    core = line % 2
    where = place.astype(jnp.int32).reshape(1)
    nodes, width = features.shape
    depth = weight.shape[0]
    slots = neighbour_lists.shape[1]
    size = nodes // SLABS
    rows = size // 2
    live = node_counts.astype(jnp.int32)

    def across(value, code):
        return lax.ppermute(value, "mp", [(i, i ^ code) for i in range(mp_count)])

    orders = (list(range(1, bits)), list(range(bits - 1, 0, -1)))

    def along(value, stage):
        return lax.ppermute(value, "dp", [(i, i ^ (1 << orders[i % 2][stage])) for i in range(dp_count)])

    def over_core(value):
        return lax.ppermute(value, "dp", [(i, i ^ 1) for i in range(dp_count)])

    def stage_bit(stage):
        return jnp.where(core == 0, (line >> orders[0][stage]) & 1, (line >> orders[1][stage]) & 1)

    def join(mine, theirs, bit, axis=0):
        return jnp.where(
            bit == 0, jnp.concatenate([mine, theirs], axis), jnp.concatenate([theirs, mine], axis)
        )

    def gather_pieces(piece):
        for stage in range(bits - 1):
            piece = join(piece, along(piece, stage), stage_bit(stage))
        return join(piece, over_core(piece), core)

    piece_rows = depth // dp_count
    offset = core * (depth // 2)
    for stage in range(bits - 1):
        offset = offset + stage_bit(stage) * (piece_rows << stage)

    bias_own = bias_terms.reshape(1, width)
    bias_sib = across(bias_own, 1)
    weight_sib = gather_pieces(across(lax.dynamic_slice_in_dim(weight, offset, piece_rows, 0), 1))

    packed = neighbour_lists.reshape(nodes // 8, 8 * slots)
    cot_send = lax.dynamic_index_in_dim(cotangent.reshape(SLABS, 2, rows, width), 1 - side, 1, False)
    cot_sibs = [across(cot_send[slab], 1) for slab in range(SLABS)]
    counts, parts = [], []
    for slab in range(SLABS):
        block, same, other = count_call(where, packed, neighbour_lists, features, slab * size, size)
        counts.append(block)
        parts.append((same, across(other, 1), across(same, 2), across(other, 3)))
    out_pairs, grads, entries = [], [], []
    for slab in range(SLABS):
        results = row_call(
            where, live, parts[slab], cotangent, cot_sibs[slab], weight, weight_sib, bias_own, bias_sib, slab * size
        )
        out_own, out_sib, grad_own, grad_sib = results[:4]
        backs = results[4:]
        out_pairs.append((out_own, across(out_sib, 1)))
        grads.append((grad_own, grad_sib))
        entries.append((counts[slab], backs[0], across(backs[1], 1), across(backs[2], 2), across(backs[3], 3)))

    kept, given = product_call(jnp.stack([place, core]).astype(jnp.int32), parts, grads)
    terms = (kept.astype(F32) + over_core(given).astype(F32)).astype(BF16)

    def halve(value, bit, send):
        length = value.shape[1] // 2
        kept = lax.dynamic_slice_in_dim(value, bit * length, length, 1)
        given = lax.dynamic_slice_in_dim(value, (1 - bit) * length, length, 1)
        return (kept.astype(F32) + send(given).astype(F32)).astype(BF16)

    for stage in range(bits - 2, -1, -1):
        terms = halve(terms, stage_bit(stage), lambda v, stage=stage: along(v, stage))
    share = terms[0].astype(F32) + across(terms[1], 1).astype(F32)
    weight_grad = gather_pieces(share.astype(BF16)).astype(F32)

    sums = jnp.stack(
        [sum(jnp.sum(g[half].astype(F32), axis=0) for g in grads) for half in range(2)]
    )
    sums = sums + over_core(sums)
    for stage in range(bits - 1):
        sums = sums + along(sums, stage)
    bias_grad = sums[0] + across(sums[1], 1)

    output = jnp.concatenate([join(mine, theirs, side) for mine, theirs in out_pairs], 0)
    partial = spread_call(where, neighbour_lists, entries[:-1], list(range(SLABS - 1)), None)
    features_grad = spread_call(where, neighbour_lists, entries[-1:], [SLABS - 1], partial)
    return (output, features_grad, weight_grad, bias_grad)


def solution(mesh):
    in_specs = (P("dp", "mp"), P("dp", None), P("dp"), P(None, "mp"), P("mp"), P("dp", "mp"))
    out_specs = (P("dp", "mp"), P("dp", "mp"), P(None, "mp"), P("mp"))
    return jax.shard_map(local, mesh=mesh, in_specs=in_specs, out_specs=out_specs, check_vma=False)
```

time: 1070 us -> 333 us (0.31); the launches traced: 1050 us -> 332 us
  other arithmetic: 526 us -> 24.9 us
  local copies, waits for them, and re-layouts: 303 us -> 39.8 us
  blocking collectives: 123 us -> 0 us
  starting transfers between devices: 19.1 us -> 92.4 us
  waiting for transfers between devices: 35.6 us -> 108 us
  Pallas kernels: 0 us -> 65 us
  matrix products: 33.3 us -> 0 us
  between operations: 14.8 us -> 1.99 us
    scatter-add x4 -> x0, other arithmetic: 426 us -> none  [add_block(): summed.at[indices.reshape(-1)].add(values.reshape(-1, breadth))]
    gather x4 -> x0, local copies, waits for them, and re-layouts: 265 us -> none  [one_block(): picked = jnp.take(features, indices, axis=0)]
    ppermute x0 -> x48, waiting for transfers between devices: none -> 108 us  [the longest x36 69.5 us: across(): return lax.ppermute(value, 'mp', [(i, i ^ code) for i in range(mp_count)])]
    ppermute x0 -> x48, starting transfers between devices: none -> 92.4 us  [the longest x36 81.4 us: across(): return lax.ppermute(value, 'mp', [(i, i ^ code) for i in range(mp_count)])]
    psum x1 -> x0, blocking collectives: 70.6 us -> none  [local(): weight_all, bias_all = lax.psum((weight_part, bias_part), ('dp', 'mp'))]
    pallas_call x0 -> x11, Pallas kernels: none -> 65 us  [the longest x4 22.6 us: row_call(): pl.pallas_call(functools.partial(row_kernel, base), grid_spec=pltpu.Prefe...]
    all_gather x1 -> x0, blocking collectives: 52.3 us -> none  [local(): lax.all_gather(bias_terms, 'mp', axis=0, tiled=True)]
    reduce_sum x5 -> x4, other arithmetic: 38.7 us -> 1.35 us  [local(): jnp.sum(g[half].astype(F32), axis=0)]
  transfers between devices with their start and end apart: 6 -> 48, of which waited for: 1 -> 19; matrix products, arithmetic and copies ran while one was open for 80% -> 5% of each run, Pallas kernels for 0% -> 15%
where the time goes in v1:
time: 333 us; the launch traced here: 332 us
  waiting for transfers between devices  108 us (32%)
  starting transfers between devices  92.4 us (28%)
  Pallas kernels  65 us (20%)
  local copies, waits for them, and re-layouts  39.8 us (12%)
  other arithmetic  24.9 us (7%)
    ppermute x36, starting transfers between devices, across(): return lax.ppermute(value, 'mp', [(i, i ^ code) for i in range(mp_count)])  81.4 us
    ppermute x36, waiting for transfers between devices, across(): return lax.ppermute(value, 'mp', [(i, i ^ code) for i in range(mp_count)])  69.5 us
    unnamed x171, local copies, waits for them, and re-layouts  36.6 us
    ppermute x8, waiting for transfers between devices, along(): lax.ppermute(value, 'dp', [(i, i ^ 1 << orders[i % 2][stage]) for i in ra...  34 us
    pallas_call x4, Pallas kernels, row_call(): pl.pallas_call(functools.partial(row_kernel, base), grid_spec=pltpu.Prefe...  22.6 us
    pallas_call x4, Pallas kernels, count_call(): pl.pallas_call(functools.partial(count_kernel, base), grid_spec=pltpu.Pre...  16.2 us
    pallas_call x2, Pallas kernels, spread_call(): pl.pallas_call(functools.partial(spread_kernel, slabs, final), grid_spec=...  16 us
    select_n x9, other arithmetic, join(): jnp.where(bit == 0, jnp.concatenate([mine, theirs], axis), jnp.concatenat...  11.6 us
  transfers between devices with their start and end apart: 48, of which 19 were waited for; matrix products, arithmetic and copies ran while one was open for 5% of the time, Pallas kernels for 15%

profile of v1, /device:TPU:0, one launch (start us, length us, event | category | flops | bytes accessed | tf_op | source)
XLA Modules:
  0.0 332.1 jit_solution(17883826192030737738)
XLA Ops:
  4.7 6.3 %collective-permute-done.4 = bf16[256,512]{1,0:T(8,128)(2,1)S(1)} collective-permute-done((bf16[256,512]{1,0:T(8,128)(2,1)S(1)}, bf16[256,512]{1,0:T(8,128)(2,1)S(1)}, u32[]{:S(2)}, u32[]{:S(2)}) %collective-permute-start.4) | collective-permute-done | bytes 262176 | tf_op jit(solution)/shard_map/ppermute | solution.py:271
  12.7 4.7 %collective-permute-done.5 = bf16[256,512]{1,0:T(8,128)(2,1)S(1)} collective-permute-done((bf16[256,512]{1,0:T(8,128)(2,1)S(1)}, bf16[256,512]{1,0:T(8,128)(2,1)S(1)}, u32[]{:S(2)}, u32[]{:S(2)}) %collective-permute-start.5) | collective-permute-done | bytes 262176 | tf_op jit(solution)/shard_map/ppermute | solution.py:276
  21.7 5.2 %collective-permute-done.6 = bf16[512,512]{1,0:T(8,128)(2,1)S(1)} collective-permute-done((bf16[512,512]{1,0:T(8,128)(2,1)S(1)}, bf16[512,512]{1,0:T(8,128)(2,1)S(1)}, u32[]{:S(2)}, u32[]{:S(2)}) %collective-permute-start.6) | collective-permute-done | bytes 524320 | tf_op jit(solution)/shard_map/ppermute | solution.py:276
  29.9 4.5 %count_and_aggregate.7 = (bf16[512,2048]{1,0:T(8,128)(2,1)S(1)}, bf16[256,512]{1,0:T(8,128)(2,1)S(1)}, bf16[256,512]{1,0:T(8,128)(2,1)}) custom-call(s32[1]{0:T(128)} %bitcast.where_ref, s32[256,256]{1,0:T(8,128)S(1)} %copy-done.41, s32[2048,32]{1,0:T(8,128)S(1)} %copy.19.lists_ref.refs_1_.refs_7_.refs_13_, bf16[2048,512]{1,0:T(8,128)(2,1)S(1)} %copy-done.56), custom_call_target="tpu_custom_call" | custom-call | flops 2147483648 | bytes 4194304 | tf_op jit(solution)/shard_map/count_and_aggregate/pallas_call | solution.py:69
  43.1 3.9 %count_and_aggregate.6 = (bf16[512,2048]{1,0:T(8,128)(2,1)S(1)}, bf16[256,512]{1,0:T(8,128)(2,1)S(1)}, bf16[256,512]{1,0:T(8,128)(2,1)S(1)}) custom-call(s32[1]{0:T(128)} %bitcast.where_ref, s32[256,256]{1,0:T(8,128)S(1)} %copy-done.42, s32[2048,32]{1,0:T(8,128)S(1)} %copy.19.lists_ref.refs_1_.refs_7_.refs_13_, bf16[2048,512]{1,0:T(8,128)(2,1)S(1)} %copy-done.57), custom_call_target="tpu_custom_call" | custom-call | flops 2147483648 | bytes 4194304 | tf_op jit(solution)/shard_map/count_and_aggregate/pallas_call | solution.py:69
  48.3 3.8 %count_and_aggregate.5 = (bf16[512,2048]{1,0:T(8,128)(2,1)S(1)}, bf16[256,512]{1,0:T(8,128)(2,1)S(1)}, bf16[256,512]{1,0:T(8,128)(2,1)S(1)}) custom-call(s32[1]{0:T(128)} %bitcast.where_ref, s32[256,256]{1,0:T(8,128)S(1)} %copy-done.42, s32[2048,32]{1,0:T(8,128)S(1)} %copy.19.lists_ref.refs_1_.refs_7_.refs_13_, bf16[2048,512]{1,0:T(8,128)(2,1)S(1)} %copy-done.58), custom_call_target="tpu_custom_call" | custom-call | flops 2147483648 | bytes 4194304 | tf_op jit(solution)/shard_map/count_and_aggregate/pallas_call | solution.py:69
  56.4 6.3 %collective-permute-done.21.part2.refs_14_ = bf16[256,512]{1,0:T(8,128)(2,1)} collective-permute-done((bf16[256,512]{1,0:T(8,128)(2,1)S(1)}, bf16[256,512]{1,0:T(8,128)(2,1)}, u32[]{:S(2)}, u32[]{:S(2)}) %collective-permute-start.21) | collective-permute-done | bytes 262176 | tf_op jit(solution)/shard_map/ppermute | solution.py:271
  62.8 4.0 %count_and_aggregate.4 = (bf16[512,2048]{1,0:T(8,128)(2,1)S(1)}, bf16[256,512]{1,0:T(8,128)(2,1)S(1)}, bf16[256,512]{1,0:T(8,128)(2,1)S(1)}) custom-call(s32[1]{0:T(128)} %bitcast.where_ref, s32[256,256]{1,0:T(8,128)S(1)} %copy-done.42, s32[2048,32]{1,0:T(8,128)S(1)} %copy.19.lists_ref.refs_1_.refs_7_.refs_13_, bf16[2048,512]{1,0:T(8,128)(2,1)S(1)} %copy-done.58), custom_call_target="tpu_custom_call" | custom-call | flops 2147483648 | bytes 4194304 | tf_op jit(solution)/shard_map/count_and_aggregate/pallas_call | solution.py:69
  69.5 3.2 collective-permute-done.23.cot_sib
  72.7 12.3 %collective-permute-done.15.part1.refs_9_ = bf16[256,512]{1,0:T(8,128)(2,1)S(1)} collective-permute-done((bf16[256,512]{1,0:T(8,128)(2,1)S(1)}, bf16[256,512]{1,0:T(8,128)(2,1)S(1)}, u32[]{:S(2)}, u32[]{:S(2)}) %collective-permute-start.15) | collective-permute-done | bytes 262176 | tf_op jit(solution)/shard_map/ppermute | solution.py:271
  89.5 4.2 %maximum_select_fusion.weight_sib = bf16[2048,512]{1,0:T(8,128)(2,1)} fusion(bf16[1024,512]{1,0:T(8,128)(2,1)} %collective-permute-done.7, bf16[1024,512]{1,0:T(8,128)(2,1)} %maximum_select_fusion.2, pred[]{:T(512)S(6)} %eq.12), kind=kLoop, calls=%fused_computation.1 | loop fusion | flops 9437184 | bytes 4194305 | tf_op jit(solution)/shard_map/jit(_where)/select_n | solution.py:285
  95.0 5.9 %linear_and_slope.7 = (bf16[256,512]{1,0:T(8,128)(2,1)S(1)}, bf16[256,512]{1,0:T(8,128)(2,1)S(1)}, bf16[256,512]{1,0:T(8,128)(2,1)S(1)}, bf16[256,512]{1,0:T(8,1...) custom-call(s32[1]{0:T(128)} %bitcast.where_ref, ...), custom_call_target="tpu_custom_call" | custom-call | flops 2147483648 | bytes 7864320 | tf_op jit(solution)/shard_map/linear_and_slope/pallas_call | solution.py:137
  108.5 3.7 %collective-permute-done.11.part2.refs_6_ = bf16[256,512]{1,0:T(8,128)(2,1)S(1)} collective-permute-done((bf16[256,512]{1,0:T(8,128)(2,1)S(1)}, bf16[256,512]{1,0:T(8,128)(2,1)S(1)}, u32[]{:S(2)}, u32[]{:S(2)}) %collective-permute-start.11) | collective-permute-done | bytes 262176 | tf_op jit(solution)/shard_map/ppermute | solution.py:271
  112.2 3.3 collective-permute-start.3
  115.4 5.8 %linear_and_slope.6 = (bf16[256,512]{1,0:T(8,128)(2,1)S(1)}, bf16[256,512]{1,0:T(8,128)(2,1)}, bf16[256,512]{1,0:T(8,128)(2,1)S(1)}, bf16[256,512]{1,0:T(8,128)(...) custom-call(s32[1]{0:T(128)} %bitcast.where_ref, ...), custom_call_target="tpu_custom_call" | custom-call | flops 2147483648 | bytes 7864320 | tf_op jit(solution)/shard_map/linear_and_slope/pallas_call | solution.py:137
  123.4 5.8 %linear_and_slope.5 = (bf16[256,512]{1,0:T(8,128)(2,1)S(1)}, bf16[256,512]{1,0:T(8,128)(2,1)}, bf16[256,512]{1,0:T(8,128)(2,1)S(1)}, bf16[256,512]{1,0:T(8,128)(...) custom-call(s32[1]{0:T(128)} %bitcast.where_ref, ...), custom_call_target="tpu_custom_call" | custom-call | flops 2147483648 | bytes 7864320 | tf_op jit(solution)/shard_map/linear_and_slope/pallas_call | solution.py:137
  135.4 5.1 %linear_and_slope.4 = (bf16[256,512]{1,0:T(8,128)(2,1)S(1)}, bf16[256,512]{1,0:T(8,128)(2,1)S(1)}, bf16[256,512]{1,0:T(8,128)(2,1)S(1)}, bf16[256,512]{1,0:T(8,1...) custom-call(s32[1]{0:T(128)} %bitcast.where_ref, ...), custom_call_target="tpu_custom_call" | custom-call | flops 2147483648 | bytes 7864320 | tf_op jit(solution)/shard_map/linear_and_slope/pallas_call | solution.py:137
  141.3 10.3 %weight_product.1 = (bf16[2,1024,512]{2,1,0:T(8,128)(2,1)}, bf16[2,1024,512]{2,1,0:T(8,128)(2,1)}) custom-call(s32[2]{0:T(128)S(1)} %pad_add_fusion.where_ref, bf16[256,512]{1,0:T(8,128)(2,1)S(1)} %get-tuple-element.50.part0.refs_0_, bf16[256,512]{1,0:T(8,128)(2,1)S(1)} %collective-permute-done.part1.refs_1_, ...), custom_call_target="tpu_custom_call" | custom-call | tf_op jit(solution)/shard_map/weight_product/pallas_call | solution.py:188
  151.7 4.5 %collective-permute-done.37 = bf16[2,1024,512]{2,1,0:T(8,128)(2,1)} collective-permute-done((bf16[2,1024,512]{2,1,0:T(8,128)(2,1)}, bf16[2,1024,512]{2,1,0:T(8,128)(2,1)}, u32[]{:S(2)}, u32[]{:S(2)}) %collective-permute-start.37) | collective-permute-done | bytes 2097184 | tf_op jit(solution)/shard_map/ppermute | solution.py:279
  164.0 12.5 %collective-permute-done.38 = bf16[2,512,512]{2,1,0:T(8,128)(2,1)} collective-permute-done((bf16[2,512,512]{2,1,0:T(8,128)(2,1)}, bf16[2,512,512]{2,1,0:T(8,128)(2,1)}, u32[]{:S(2)}, u32[]{:S(2)}) %collective-permute-start.38) | collective-permute-done | bytes 1048608 | tf_op jit(solution)/shard_map/ppermute | solution.py:276
  180.3 7.3 %collective-permute-done.39 = bf16[2,256,512]{2,1,0:T(8,128)(2,1)S(1)} collective-permute-done((bf16[2,256,512]{2,1,0:T(8,128)(2,1)S(1)}, bf16[2,256,512]{2,1,0:T(8,128)(2,1)S(1)}, u32[]{:S(2)}, u32[]{:S(2)}) %collective-permute-start.39) | collective-permute-done | bytes 524320 | tf_op jit(solution)/shard_map/ppermute | solution.py:276
  187.9 6.5 %collective-permute-done.40 = bf16[256,512]{1,0:T(8,128)(2,1)S(1)} collective-permute-done((bf16[256,512]{1,0:T(8,128)(2,1)S(1)}, bf16[256,512]{1,0:T(8,128)(2,1)S(1)}, u32[]{:S(2)}, u32[]{:S(2)}) %collective-permute-start.40) | collective-permute-done | bytes 262176 | tf_op jit(solution)/shard_map/ppermute | solution.py:271
  196.7 4.4 %collective-permute-done.45 = f32[2,512]{1,0:T(2,128)S(1)} collective-permute-done((f32[2,512]{1,0:T(2,128)S(1)}, f32[2,512]{1,0:T(2,128)S(1)}, u32[]{:S(2)}, u32[]{:S(2)}) %collective-permute-start.45) | collective-permute-done | bytes 4128 | tf_op jit(solution)/shard_map/ppermute | solution.py:276
  208.4 9.7 %collective-permute-done.47 = f32[512]{0:T(512)S(1)} collective-permute-done((f32[512]{0:T(512)S(1)}, f32[512]{0:T(512)S(1)}, u32[]{:S(2)}, u32[]{:S(2)}) %collective-permute-start.47) | collective-permute-done | bytes 2080 | tf_op jit(solution)/shard_map/ppermute | solution.py:271
  224.0 7.6 %collective-permute-done.28.refs_3_ = bf16[256,512]{1,0:T(8,128)(2,1)S(1)} collective-permute-done((bf16[256,512]{1,0:T(8,128)(2,1)S(1)}, bf16[256,512]{1,0:T(8,128)(2,1)S(1)}, u32[]{:S(2)}, u32[]{:S(2)}) %collective-permute-start.28) | collective-permute-done | bytes 262176 | tf_op jit(solution)/shard_map/ppermute | solution.py:271
  233.6 6.7 %collective-permute-done.29.refs_4_ = bf16[256,512]{1,0:T(8,128)(2,1)S(1)} collective-permute-done((bf16[256,512]{1,0:T(8,128)(2,1)S(1)}, bf16[256,512]{1,0:T(8,128)(2,1)S(1)}, u32[]{:S(2)}, u32[]{:S(2)}) %collective-permute-start.29) | collective-permute-done | bytes 262176 | tf_op jit(solution)/shard_map/ppermute | solution.py:271
  244.0 15.9 %collective-permute-start.34 = (bf16[256,512]{1,0:T(8,128)(2,1)S(1)}, bf16[256,512]{1,0:T(8,128)(2,1)S(1)}, u32[]{:S(2)}, u32[]{:S(2)}) collective-permute-start(bf16[256,512]{1,0:T(8,128)(2,1)S(1)} %copy-done.63), channel_id=1, source_target_pairs={{0,1},{1,0},{2,3},{3,2},{4,5},{5,4},{6,7},{7,6},{8,9},{9,8},{10,11... | collective-permute-start | bytes 786440 | tf_op jit(solution)/shard_map/ppermute | solution.py:271
  270.4 16.7 %collective-permute-start.19 = (bf16[256,512]{1,0:T(8,128)(2,1)}, bf16[256,512]{1,0:T(8,128)(2,1)}, u32[]{:S(2)}, u32[]{:S(2)}) collective-permute-start(bf16[256,512]{1,0:T(8,128)(2,1)} %get-tuple-element.61), channel_id=1, source_target_pairs={{0,1},{1,0},{2,3},{3,2},{4,5},{5,4},{6,7},{7,6},{8,9},{9,8},{10,11... | collective-permute-start | bytes 786440 | tf_op jit(solution)/shard_map/ppermute | solution.py:271
  291.0 4.9 %collective-permute-start.9 = (bf16[256,512]{1,0:T(8,128)(2,1)}, bf16[256,512]{1,0:T(8,128)(2,1)S(1)}, u32[]{:S(2)}, u32[]{:S(2)}) collective-permute-start(bf16[256,512]{1,0:T(8,128)(2,1)} %copy-done.59), channel_id=1, source_target_pairs={{0,1},{1,0},{2,3},{3,2},{4,5},{5,4},{6,7},{7,6},{8,9},{9,8},{10,11... | collective-permute-start | bytes 786440 | tf_op jit(solution)/shard_map/ppermute | solution.py:271
  306.9 10.4 %spread_back.2.refs_6_ = f32[2048,512]{1,0:T(8,128)} custom-call(s32[1]{0:T(128)} %bitcast.where_ref, bf16[512,2048]{1,0:T(8,128)(2,1)} %copy-done.2, s32[2048,32]{1,0:T(8,128)S(1)} %copy.19.lists_ref.refs_1_.refs_7_.refs_13_, bf16[256,512]{1,0:T(8,128)(2,1)S(1)} %copy-done.22, bf16[256,512]{1,0:T(8,128)(2,1)S(1)} %copy-done.24, ...), custom_call_target="tpu_custom_call" | custom-call | tf_op jit(solution)/shard_map/spread_back/pallas_call | solution.py:239
  317.4 5.6 %spread_back.3 = bf16[2048,512]{1,0:T(8,128)(2,1)} custom-call(s32[1]{0:T(128)} %bitcast.where_ref, bf16[512,2048]{1,0:T(8,128)(2,1)S(1)} %get-tuple-element.66.refs_0_, s32[2048,32]{1,0:T(8,128)S(1)} %copy.19.lists_ref.refs_1_.refs_7_.refs_13_, bf16[256,512]{1,0:T(8,128)(2,1)S(1)} %copy-done.51, bf16[256,512]{1,0:T(8,128)(2,1)S(1)} %copy-done.53, ...), custom_call_target="tpu_custom_call" | custom-call | tf_op jit(solution)/shard_map/spread_back/pallas_call | solution.py:239
  327.1 4.9 %fusion = f32[2048,512]{1,0:T(8,128)} fusion(bf16[1024,512]{1,0:T(8,128)(2,1)} %collective-permute-done.43, bf16[1024,512]{1,0:T(8,128)(2,1)} %maximum_select_fusion.3, pred[]{:T(512)S(6)} %eq.12), kind=kLoop, calls=%fused_computation.4 | loop fusion | flops 10485760 | bytes 6291457 | tf_op jit(solution)/shard_map/convert_element_type | solution.py:334
  (281 shorter events, 114.3 us)
Async XLA Ops:
  28.3 59.4 %collective-permute-start.7 = (bf16[1024,512]{1,0:T(8,128)(2,1)}, bf16[1024,512]{1,0:T(8,128)(2,1)}, u32[]{:S(2)}, u32[]{:S(2)}) collective-permute-start(bf16[1024,512]{1,0:T(8,128)(2,1)} %maximum_select_fusion.2), channel_id=1, source_target_pairs={{0,4},{4,0},{8,12},{12,8},{16,20},{20,16},{24,28},{28,24},{1,5},{5... | collective-permute-start | bytes 3145736 | tf_op jit(solution)/shard_map/ppermute | solution.py:279
  34.4 22.0 %collective-permute-start.20 = (bf16[256,512]{1,0:T(8,128)(2,1)}, bf16[256,512]{1,0:T(8,128)(2,1)}, u32[]{:S(2)}, u32[]{:S(2)}) collective-permute-start(bf16[256,512]{1,0:T(8,128)(2,1)} %get-tuple-element.63), channel_id=1, source_target_pairs={{0,1},{1,0},{2,3},{3,2},{4,5},{5,4},{6,7},{7,6},{8,9},{9,8},{10,11... | collective-permute-start | bytes 786440 | tf_op jit(solution)/shard_map/ppermute | solution.py:271
  36.1 30.7 %collective-permute-start.22 = (bf16[256,512]{1,0:T(8,128)(2,1)}, bf16[256,512]{1,0:T(8,128)(2,1)}, u32[]{:S(2)}, u32[]{:S(2)}) collective-permute-start(bf16[256,512]{1,0:T(8,128)(2,1)} %get-tuple-element.63), channel_id=1, source_target_pairs={{0,3},{1,2},{2,1},{3,0},{4,7},{5,6},{6,5},{7,4},{8,11},{9,10},{10,... | collective-permute-start | bytes 786440 | tf_op jit(solution)/shard_map/ppermute | solution.py:271
  38.6 24.1 %collective-permute-start.21 = (bf16[256,512]{1,0:T(8,128)(2,1)S(1)}, bf16[256,512]{1,0:T(8,128)(2,1)}, u32[]{:S(2)}, u32[]{:S(2)}) collective-permute-start(bf16[256,512]{1,0:T(8,128)(2,1)S(1)} %get-tuple-element.62.part0.refs_12_), channel_id=1, source_target_pairs={{0,2},{1,3},{2,0},{3,1},{4,6},{5,7},{6,4},{7,5},{8,10},{9,11},{10,... | collective-permute-start | bytes 786440 | tf_op jit(solution)/shard_map/ppermute | solution.py:271
  54.1 18.6 %collective-permute-start.23 = (bf16[256,512]{1,0:T(8,128)(2,1)S(1)}, bf16[256,512]{1,0:T(8,128)(2,1)S(1)}, u32[]{:S(2)}, u32[]{:S(2)}) collective-permute-start(bf16[256,512]{1,0:T(8,128)(2,1)S(1)} %get-tuple-element.99), channel_id=1, source_target_pairs={{0,1},{1,0},{2,3},{3,2},{4,5},{5,4},{6,7},{7,6},{8,9},{9,8},{10,11... | collective-permute-start | bytes 786440 | tf_op jit(solution)/shard_map/ppermute | solution.py:271
  56.4 28.7 %collective-permute-start.15 = (bf16[256,512]{1,0:T(8,128)(2,1)S(1)}, bf16[256,512]{1,0:T(8,128)(2,1)S(1)}, u32[]{:S(2)}, u32[]{:S(2)}) collective-permute-start(bf16[256,512]{1,0:T(8,128)(2,1)S(1)} %get-tuple-element.59), channel_id=1, source_target_pairs={{0,1},{1,0},{2,3},{3,2},{4,5},{5,4},{6,7},{7,6},{8,9},{9,8},{10,11... | collective-permute-start | bytes 786440 | tf_op jit(solution)/shard_map/ppermute | solution.py:271
  62.7 24.9 %collective-permute-start.16 = (bf16[256,512]{1,0:T(8,128)(2,1)S(1)}, bf16[256,512]{1,0:T(8,128)(2,1)S(1)}, u32[]{:S(2)}, u32[]{:S(2)}) collective-permute-start(bf16[256,512]{1,0:T(8,128)(2,1)S(1)} %get-tuple-element.58.part0.refs_8_), channel_id=1, source_target_pairs={{0,2},{1,3},{2,0},{3,1},{4,6},{5,7},{6,4},{7,5},{8,10},{9,11},{10,... | collective-permute-start | bytes 786440 | tf_op jit(solution)/shard_map/ppermute | solution.py:271
  66.8 26.8 %collective-permute-start.17 = (bf16[256,512]{1,0:T(8,128)(2,1)S(1)}, bf16[256,512]{1,0:T(8,128)(2,1)S(1)}, u32[]{:S(2)}, u32[]{:S(2)}) collective-permute-start(bf16[256,512]{1,0:T(8,128)(2,1)S(1)} %get-tuple-element.59), channel_id=1, source_target_pairs={{0,3},{1,2},{2,1},{3,0},{4,7},{5,6},{6,5},{7,4},{8,11},{9,10},{10,... | collective-permute-start | bytes 786440 | tf_op jit(solution)/shard_map/ppermute | solution.py:271
  72.7 33.1 %collective-permute-start.10 = (bf16[256,512]{1,0:T(8,128)(2,1)S(1)}, bf16[256,512]{1,0:T(8,128)(2,1)S(1)}, u32[]{:S(2)}, u32[]{:S(2)}) collective-permute-start(bf16[256,512]{1,0:T(8,128)(2,1)S(1)} %get-tuple-element.55), channel_id=1, source_target_pairs={{0,1},{1,0},{2,3},{3,2},{4,5},{5,4},{6,7},{7,6},{8,9},{9,8},{10,11... | collective-permute-start | bytes 786440 | tf_op jit(solution)/shard_map/ppermute | solution.py:271
  85.1 27.1 %collective-permute-start.12 = (bf16[256,512]{1,0:T(8,128)(2,1)S(1)}, bf16[256,512]{1,0:T(8,128)(2,1)S(1)}, u32[]{:S(2)}, u32[]{:S(2)}) collective-permute-start(bf16[256,512]{1,0:T(8,128)(2,1)S(1)} %get-tuple-element.55), channel_id=1, source_target_pairs={{0,3},{1,2},{2,1},{3,0},{4,7},{5,6},{6,5},{7,4},{8,11},{9,10},{10,... | collective-permute-start | bytes 786440 | tf_op jit(solution)/shard_map/ppermute | solution.py:271
  87.7 24.5 %collective-permute-start.11 = (bf16[256,512]{1,0:T(8,128)(2,1)S(1)}, bf16[256,512]{1,0:T(8,128)(2,1)S(1)}, u32[]{:S(2)}, u32[]{:S(2)}) collective-permute-start(bf16[256,512]{1,0:T(8,128)(2,1)S(1)} %get-tuple-element.54.part0.refs_4_), channel_id=1, source_target_pairs={{0,2},{1,3},{2,0},{3,1},{4,6},{5,7},{6,4},{7,5},{8,10},{9,11},{10,... | collective-permute-start | bytes 786440 | tf_op jit(solution)/shard_map/ppermute | solution.py:271
  93.6 29.7 %collective-permute-start.13 = (bf16[256,512]{1,0:T(8,128)(2,1)S(1)}, bf16[256,512]{1,0:T(8,128)(2,1)S(1)}, u32[]{:S(2)}, u32[]{:S(2)}) collective-permute-start(bf16[256,512]{1,0:T(8,128)(2,1)S(1)} %get-tuple-element.98), channel_id=1, source_target_pairs={{0,1},{1,0},{2,3},{3,2},{4,5},{5,4},{6,7},{7,6},{8,9},{9,8},{10,11... | collective-permute-start | bytes 786440 | tf_op jit(solution)/shard_map/ppermute | solution.py:271
  105.2 27.5 %collective-permute-start = (bf16[256,512]{1,0:T(8,128)(2,1)S(1)}, bf16[256,512]{1,0:T(8,128)(2,1)S(1)}, u32[]{:S(2)}, u32[]{:S(2)}) collective-permute-start(bf16[256,512]{1,0:T(8,128)(2,1)S(1)} %get-tuple-element.51), channel_id=1, source_target_pairs={{0,1},{1,0},{2,3},{3,2},{4,5},{5,4},{6,7},{7,6},{8,9},{9,8},{10,11... | collective-permute-start | bytes 786440 | tf_op jit(solution)/shard_map/ppermute | solution.py:271
  105.9 27.6 %collective-permute-start.2 = (bf16[256,512]{1,0:T(8,128)(2,1)S(1)}, bf16[256,512]{1,0:T(8,128)(2,1)S(1)}, u32[]{:S(2)}, u32[]{:S(2)}) collective-permute-start(bf16[256,512]{1,0:T(8,128)(2,1)S(1)} %get-tuple-element.51), channel_id=1, source_target_pairs={{0,3},{1,2},{2,1},{3,0},{4,7},{5,6},{6,5},{7,4},{8,11},{9,10},{10,... | collective-permute-start | bytes 786440 | tf_op jit(solution)/shard_map/ppermute | solution.py:271
  112.2 21.4 %collective-permute-start.1 = (bf16[256,512]{1,0:T(8,128)(2,1)S(1)}, bf16[256,512]{1,0:T(8,128)(2,1)S(1)}, u32[]{:S(2)}, u32[]{:S(2)}) collective-permute-start(bf16[256,512]{1,0:T(8,128)(2,1)S(1)} %get-tuple-element.50.part0.refs_0_), channel_id=1, source_target_pairs={{0,2},{1,3},{2,0},{3,1},{4,6},{5,7},{6,4},{7,5},{8,10},{9,11},{10,... | collective-permute-start | bytes 786440 | tf_op jit(solution)/shard_map/ppermute | solution.py:271
  112.2 23.3 %collective-permute-start.3 = (bf16[256,512]{1,0:T(8,128)(2,1)S(1)}, bf16[256,512]{1,0:T(8,128)(2,1)S(1)}, u32[]{:S(2)}, u32[]{:S(2)}) collective-permute-start(bf16[256,512]{1,0:T(8,128)(2,1)S(1)} %get-tuple-element.96), channel_id=1, source_target_pairs={{0,1},{1,0},{2,3},{3,2},{4,5},{5,4},{6,7},{7,6},{8,9},{9,8},{10,11... | collective-permute-start | bytes 786440 | tf_op jit(solution)/shard_map/ppermute | solution.py:271
  202.9 18.2 %collective-permute-start.25 = (bf16[256,512]{1,0:T(8,128)(2,1)S(1)}, bf16[256,512]{1,0:T(8,128)(2,1)S(1)}, u32[]{:S(2)}, u32[]{:S(2)}) collective-permute-start(bf16[256,512]{1,0:T(8,128)(2,1)S(1)} %copy-done.71), channel_id=1, source_target_pairs={{0,1},{1,0},{2,3},{3,2},{4,5},{5,4},{6,7},{7,6},{8,9},{9,8},{10,11... | collective-permute-start | bytes 786440 | tf_op jit(solution)/shard_map/ppermute | solution.py:271
  204.7 18.6 %collective-permute-start.26 = (bf16[256,512]{1,0:T(8,128)(2,1)S(1)}, bf16[256,512]{1,0:T(8,128)(2,1)S(1)}, u32[]{:S(2)}, u32[]{:S(2)}) collective-permute-start(bf16[256,512]{1,0:T(8,128)(2,1)S(1)} %copy-done.67), channel_id=1, source_target_pairs={{0,2},{1,3},{2,0},{3,1},{4,6},{5,7},{6,4},{7,5},{8,10},{9,11},{10,... | collective-permute-start | bytes 786440 | tf_op jit(solution)/shard_map/ppermute | solution.py:271
  206.1 53.9 %collective-permute-start.42 = (bf16[512,512]{1,0:T(8,128)(2,1)S(1)}, bf16[512,512]{1,0:T(8,128)(2,1)S(1)}, u32[]{:S(2)}, u32[]{:S(2)}) collective-permute-start(bf16[512,512]{1,0:T(8,128)(2,1)S(1)} %maximum_select_fusion.9), channel_id=1, source_target_pairs={{0,16},{4,12},{8,24},{12,4},{16,0},{20,28},{24,8},{28,20},{1,17},{... | collective-permute-start | bytes 1572872 | tf_op jit(solution)/shard_map/ppermute | solution.py:276
  218.7 21.5 %collective-permute-start.29 = (bf16[256,512]{1,0:T(8,128)(2,1)S(1)}, bf16[256,512]{1,0:T(8,128)(2,1)S(1)}, u32[]{:S(2)}, u32[]{:S(2)}) collective-permute-start(bf16[256,512]{1,0:T(8,128)(2,1)S(1)} %copy-done.79), channel_id=1, source_target_pairs={{0,2},{1,3},{2,0},{3,1},{4,6},{5,7},{6,4},{7,5},{8,10},{9,11},{10,... | collective-permute-start | bytes 786440 | tf_op jit(solution)/shard_map/ppermute | solution.py:271
  221.9 21.5 %collective-permute-start.30 = (bf16[256,512]{1,0:T(8,128)(2,1)S(1)}, bf16[256,512]{1,0:T(8,128)(2,1)S(1)}, u32[]{:S(2)}, u32[]{:S(2)}) collective-permute-start(bf16[256,512]{1,0:T(8,128)(2,1)S(1)} %copy-done.77), channel_id=1, source_target_pairs={{0,3},{1,2},{2,1},{3,0},{4,7},{5,6},{6,5},{7,4},{8,11},{9,10},{10,... | collective-permute-start | bytes 786440 | tf_op jit(solution)/shard_map/ppermute | solution.py:271
  224.0 37.9 %collective-permute-start.31 = (bf16[256,512]{1,0:T(8,128)(2,1)S(1)}, bf16[256,512]{1,0:T(8,128)(2,1)S(1)}, u32[]{:S(2)}, u32[]{:S(2)}) collective-permute-start(bf16[256,512]{1,0:T(8,128)(2,1)S(1)} %copy-done.73), channel_id=1, source_target_pairs={{0,1},{1,0},{2,3},{3,2},{4,5},{5,4},{6,7},{7,6},{8,9},{9,8},{10,11... | collective-permute-start | bytes 786440 | tf_op jit(solution)/shard_map/ppermute | solution.py:271
  232.3 32.1 %collective-permute-start.32 = (bf16[256,512]{1,0:T(8,128)(2,1)S(1)}, bf16[256,512]{1,0:T(8,128)(2,1)S(1)}, u32[]{:S(2)}, u32[]{:S(2)}) collective-permute-start(bf16[256,512]{1,0:T(8,128)(2,1)S(1)} %copy-done.69), channel_id=1, source_target_pairs={{0,2},{1,3},{2,0},{3,1},{4,6},{5,7},{6,4},{7,5},{8,10},{9,11},{10,... | collective-permute-start | bytes 786440 | tf_op jit(solution)/shard_map/ppermute | solution.py:271
  241.0 26.0 %collective-permute-start.33 = (bf16[256,512]{1,0:T(8,128)(2,1)S(1)}, bf16[256,512]{1,0:T(8,128)(2,1)S(1)}, u32[]{:S(2)}, u32[]{:S(2)}) collective-permute-start(bf16[256,512]{1,0:T(8,128)(2,1)S(1)} %copy-done.65), channel_id=1, source_target_pairs={{0,3},{1,2},{2,1},{3,0},{4,7},{5,6},{6,5},{7,4},{8,11},{9,10},{10,... | collective-permute-start | bytes 786440 | tf_op jit(solution)/shard_map/ppermute | solution.py:271
  244.0 25.6 %collective-permute-start.34 = (bf16[256,512]{1,0:T(8,128)(2,1)S(1)}, bf16[256,512]{1,0:T(8,128)(2,1)S(1)}, u32[]{:S(2)}, u32[]{:S(2)}) collective-permute-start(bf16[256,512]{1,0:T(8,128)(2,1)S(1)} %copy-done.63), channel_id=1, source_target_pairs={{0,1},{1,0},{2,3},{3,2},{4,5},{5,4},{6,7},{7,6},{8,9},{9,8},{10,11... | collective-permute-start | bytes 786440 | tf_op jit(solution)/shard_map/ppermute | solution.py:271
  260.0 29.7 %collective-permute-start.35 = (bf16[256,512]{1,0:T(8,128)(2,1)S(1)}, bf16[256,512]{1,0:T(8,128)(2,1)S(1)}, u32[]{:S(2)}, u32[]{:S(2)}) collective-permute-start(bf16[256,512]{1,0:T(8,128)(2,1)S(1)} %copy-done.61), channel_id=1, source_target_pairs={{0,2},{1,3},{2,0},{3,1},{4,6},{5,7},{6,4},{7,5},{8,10},{9,11},{10,... | collective-permute-start | bytes 786440 | tf_op jit(solution)/shard_map/ppermute | solution.py:271
  262.6 64.5 %collective-permute-start.43 = (bf16[1024,512]{1,0:T(8,128)(2,1)}, bf16[1024,512]{1,0:T(8,128)(2,1)}, u32[]{:S(2)}, u32[]{:S(2)}) collective-permute-start(bf16[1024,512]{1,0:T(8,128)(2,1)} %maximum_select_fusion.3), channel_id=1, source_target_pairs={{0,4},{4,0},{8,12},{12,8},{16,20},{20,16},{24,28},{28,24},{1,5},{5... | collective-permute-start | bytes 3145736 | tf_op jit(solution)/shard_map/ppermute | solution.py:279
  265.1 25.8 %collective-permute-start.36 = (bf16[256,512]{1,0:T(8,128)(2,1)}, bf16[256,512]{1,0:T(8,128)(2,1)}, u32[]{:S(2)}, u32[]{:S(2)}) collective-permute-start(bf16[256,512]{1,0:T(8,128)(2,1)} %get-tuple-element.85), channel_id=1, source_target_pairs={{0,3},{1,2},{2,1},{3,0},{4,7},{5,6},{6,5},{7,4},{8,11},{9,10},{10,... | collective-permute-start | bytes 786440 | tf_op jit(solution)/shard_map/ppermute | solution.py:271
  267.7 49.7 %collective-permute-start.27 = (bf16[256,512]{1,0:T(8,128)(2,1)}, bf16[256,512]{1,0:T(8,128)(2,1)}, u32[]{:S(2)}, u32[]{:S(2)}) collective-permute-start(bf16[256,512]{1,0:T(8,128)(2,1)} %get-tuple-element.70), channel_id=1, source_target_pairs={{0,3},{1,2},{2,1},{3,0},{4,7},{5,6},{6,5},{7,4},{8,11},{9,10},{10,... | collective-permute-start | bytes 786440 | tf_op jit(solution)/shard_map/ppermute | solution.py:271
  270.4 52.6 %collective-permute-start.19 = (bf16[256,512]{1,0:T(8,128)(2,1)}, bf16[256,512]{1,0:T(8,128)(2,1)}, u32[]{:S(2)}, u32[]{:S(2)}) collective-permute-start(bf16[256,512]{1,0:T(8,128)(2,1)} %get-tuple-element.61), channel_id=1, source_target_pairs={{0,1},{1,0},{2,3},{3,2},{4,5},{5,4},{6,7},{7,6},{8,9},{9,8},{10,11... | collective-permute-start | bytes 786440 | tf_op jit(solution)/shard_map/ppermute | solution.py:271
  290.4 33.9 %collective-permute-start.14 = (bf16[256,512]{1,0:T(8,128)(2,1)}, bf16[256,512]{1,0:T(8,128)(2,1)}, u32[]{:S(2)}, u32[]{:S(2)}) collective-permute-start(bf16[256,512]{1,0:T(8,128)(2,1)} %get-tuple-element.57), channel_id=1, source_target_pairs={{0,1},{1,0},{2,3},{3,2},{4,5},{5,4},{6,7},{7,6},{8,9},{9,8},{10,11... | collective-permute-start | bytes 786440 | tf_op jit(solution)/shard_map/ppermute | solution.py:271
  291.0 34.5 %collective-permute-start.9 = (bf16[256,512]{1,0:T(8,128)(2,1)}, bf16[256,512]{1,0:T(8,128)(2,1)S(1)}, u32[]{:S(2)}, u32[]{:S(2)}) collective-permute-start(bf16[256,512]{1,0:T(8,128)(2,1)} %copy-done.59), channel_id=1, source_target_pairs={{0,1},{1,0},{2,3},{3,2},{4,5},{5,4},{6,7},{7,6},{8,9},{9,8},{10,11... | collective-permute-start | bytes 786440 | tf_op jit(solution)/shard_map/ppermute | solution.py:271
  (101 other events, 1138.3 us)

commit v2 on v0

v2 whole, which is shorter than its diff:
```python
import functools

import jax
import jax.numpy as jnp
from jax import lax
from jax.experimental import pallas as pl
from jax.experimental.pallas import tpu as pltpu
from jax.sharding import PartitionSpec as P

BF16 = jnp.bfloat16
F32 = jnp.float32
GROUPS = ((4,), (4,))
LANES = 128
PAD = 16
VMEM_LIMIT = 48 << 20
SMALL = pl.CostEstimate(flops=1, bytes_accessed=1, transcendentals=0)
ANY = pl.BlockSpec(memory_space=pl.ANY)


def like(*shape, dtype=BF16):
    return jax.ShapeDtypeStruct(shape, dtype)


def fixed(*shape):
    return pl.BlockSpec(shape, lambda *_: (0,) * len(shape))


def call(kernel, name, scalars, operands, out_shape, in_specs=None, out_specs=None, grid=(1,), scratch=(), aliases=None):
    if in_specs is None:
        in_specs = [fixed(*o.shape) for o in operands]
    if out_specs is None:
        out_specs = [fixed(*o.shape) for o in out_shape]
    return pl.pallas_call(
        kernel,
        grid_spec=pltpu.PrefetchScalarGridSpec(
            num_scalar_prefetch=len(scalars), grid=grid, in_specs=in_specs, out_specs=out_specs, scratch_shapes=scratch
        ),
        out_shape=out_shape,
        compiler_params=pltpu.CompilerParams(vmem_limit_bytes=VMEM_LIMIT),
        input_output_aliases={len(scalars) + i: o for i, o in (aliases or {}).items()},
        cost_estimate=SMALL,
        name=name,
    )(*scalars, *operands)


def piece_kernel(at, weight, bias, out):
    rows = out.shape[0] - PAD
    out[:rows, :] = weight[...]
    out[rows:, :] = jnp.broadcast_to(bias[...].astype(F32), (PAD, out.shape[1])).astype(BF16)


def piece_call(at, weight, bias, rows):
    width = weight.shape[1]
    return call(
        piece_kernel,
        "weight_piece",
        (at,),
        (weight, bias),
        [like(rows + PAD, width)],
        in_specs=[pl.BlockSpec((rows, width), lambda i, s: (s[3], 0)), fixed(1, width)],
    )[0]


def count_kernel(base, slots, at, packed_ref, feat_ref, cot_ref, *refs):
    counts_ref, same_ref, other_ref, pack_ref, scale_ref = refs[-5:]
    rows = counts_ref.shape[0]
    step = pl.program_id(0)
    steps = pl.num_programs(0)
    block = (step + at[1] * (steps // 2)) % steps
    row = lax.broadcasted_iota(jnp.int32, (LANES, 8 * slots), 0)
    owner = lax.broadcasted_iota(jnp.int32, (1, 8 * slots), 1) // slots

    def group(index):
        entry = packed_ref[index : index + 1, :]
        high = (entry >> 7) * 8 + owner
        low = entry & (LANES - 1)
        left = jnp.where(high == row, 1.0, 0.0).astype(BF16)
        right = jnp.where(low == row, 1.0, 0.0).astype(BF16)
        return lax.dot_general(left, right, (((1,), (1,)), ((), ())), preferred_element_type=F32)

    for pair in range(rows // 16):
        first, second = group(2 * pair), group(2 * pair + 1)
        for tile in range(counts_ref.shape[1] // LANES):
            counts_ref[pair * 16 : (pair + 1) * 16, tile * LANES : (tile + 1) * LANES] = jnp.concatenate(
                [first[tile * 8 : (tile + 1) * 8], second[tile * 8 : (tile + 1) * 8]], 0
            ).astype(BF16)
    degree = jnp.sum(counts_ref[...].astype(F32), axis=1, keepdims=True)
    scale = 1.0 / (degree + 1.0)
    down = lax.broadcasted_iota(jnp.int32, (LANES, LANES), 0)
    across = lax.broadcasted_iota(jnp.int32, (LANES, LANES), 1)
    twice = jnp.where(down == across, 2.0, 0.0)
    column = pl.multiple_of(base + block * rows, LANES)
    tile_view = counts_ref[:, pl.ds(column, LANES)].astype(F32)
    counts_ref[:, pl.ds(column, LANES)] = (tile_view + twice).astype(BF16)
    total = jnp.dot(counts_ref[...], feat_ref[...], preferred_element_type=F32)
    result = (total * scale).astype(BF16)

    @pl.when(step < steps // 2)
    def _():
        same_ref[...] = result
        scale_ref[...] = scale

    @pl.when(step >= steps // 2)
    def _():
        other_ref[...] = result
        pack_ref[0] = result
        pack_ref[1] = cot_ref[...]


def count_call(at, packed, features, cotangent, base, size, counts):
    nodes, width = features.shape
    slots = packed.shape[1] // 8
    rows = LANES
    steps = size // rows
    half = steps // 2

    def natural(i, s):
        return base // rows + (i + s[1] * half) % steps

    def early(i, s):
        return jnp.minimum(i, half - 1), 0

    def late(i, s):
        return jnp.maximum(i - half, 0), 0

    operands = [packed, features, cotangent]
    specs = [
        pl.BlockSpec((rows // 8, 8 * slots), lambda i, s: (natural(i, s), 0)),
        fixed(nodes, width),
        pl.BlockSpec((rows, width), lambda i, s: (natural(i, s), 0)),
    ]
    aliases = {}
    if counts is not None:
        aliases = {len(operands): 0}
        operands.append(counts)
        specs.append(ANY)
    return call(
        functools.partial(count_kernel, base, slots),
        "count_and_aggregate",
        (at,),
        operands,
        [
            like(nodes, nodes),
            like(size // 2, width),
            like(size // 2, width),
            like(2, size // 2, width),
            like(size // 2, 1, dtype=F32),
        ],
        in_specs=specs,
        out_specs=[
            pl.BlockSpec((rows, nodes), lambda i, s: (natural(i, s), 0)),
            pl.BlockSpec((rows, width), early),
            pl.BlockSpec((rows, width), late),
            pl.BlockSpec((2, rows, width), lambda i, s: (0, *late(i, s))),
            pl.BlockSpec((rows, 1), early),
        ],
        grid=(steps,),
        aliases=aliases,
    )


def row_kernel(
    base, at, live, part0, near, part2, part3, scale, cot_own, weight_own, weight_sib, bias_own, bias_sib, *refs
):
    out_own, grads, back0, back_near, back2, back3 = refs[-6:]
    rows, width = part0.shape
    place = at[0]
    slot = base + at[1] * rows + lax.broadcasted_iota(jnp.int32, (rows, width), 0)
    living = slot < live[0]
    starts = [pl.multiple_of((place ^ code) * width, LANES) for code in range(4)]
    values = []
    for half, (weight, bias, cot) in enumerate(
        ((weight_own, bias_own, cot_own[...]), (weight_sib, bias_sib, near[1]))
    ):
        linear = bias[...].astype(F32)
        for part, start in zip((part0[...], near[0], part2[...], part3[...]), starts):
            linear = linear + jnp.dot(part, weight[pl.ds(start, width), :], preferred_element_type=F32)
        sigma = 1.0 / (1.0 + jnp.exp(-linear))
        result = jnp.where(living, linear * sigma, 0.0).astype(BF16)
        if half == 0:
            out_own[...] = result
        else:
            back_near[0] = result
        slope = sigma * (1.0 + linear * (1.0 - sigma))
        value = jnp.where(living, cot.astype(F32) * slope, 0.0).astype(BF16)
        grads[at[1] if half == 0 else 1 - at[1]] = value
        values.append(value)
    for code, start in enumerate(starts):
        total = jnp.zeros((rows, width), F32)
        for weight, value in zip((weight_own, weight_sib), values):
            total = total + lax.dot_general(
                value, weight[pl.ds(start, width), :], (((1,), (1,)), ((), ())), preferred_element_type=F32
            )
        total = (total * scale[...]).astype(BF16)
        if code == 1:
            back_near[1] = total
        else:
            (back0, None, back2, back3)[code][...] = total


def row_call(at, live, parts, scale, cotangent, weight_own, weight_sib, bias_own, bias_sib, base, start, all_rows, buffers):
    rows, width = parts[0].shape
    operands = [*parts, scale, cotangent, weight_own, weight_sib, bias_own, bias_sib]
    specs = [fixed(*o.shape) for o in operands]
    specs[5] = pl.BlockSpec((rows, width), lambda i, s, c: (base // rows + s[1], 0))
    flat, pair = like(all_rows, width), like(2, all_rows, width)
    here = (base - start) // 2 // rows
    flat_spec = pl.BlockSpec((rows, width), lambda i, s, c: (here, 0))
    pair_spec = pl.BlockSpec((2, rows, width), lambda i, s, c: (0, here, 0))
    aliases = {}
    if buffers is not None:
        aliases = {len(operands) + i: i for i in range(len(buffers))}
        operands += buffers
        specs += [ANY] * len(buffers)
    return call(
        functools.partial(row_kernel, base),
        "linear_and_slope",
        (at, live),
        operands,
        [flat, pair, flat, pair, flat, flat],
        in_specs=specs,
        out_specs=[flat_spec, pair_spec, flat_spec, pair_spec, flat_spec, flat_spec],
        aliases=aliases,
    )


def put_sums(ref, index, value):
    high = value.astype(BF16)
    low = (value - high.astype(F32)).astype(BF16)
    row = lax.broadcasted_iota(jnp.int32, (PAD, value.shape[1]), 0)
    both = jnp.where(row == 0, high.astype(F32), jnp.where(row == 1, low.astype(F32), 0.0))
    ref[(*index, slice(ref.shape[-2] - PAD, None), slice(None))] = both.astype(BF16)


def get_sums(ref, index):
    rows = ref[(*index, slice(ref.shape[-2] - PAD, None), slice(None))]
    return jnp.sum(rows.astype(F32), axis=0, keepdims=True)


def product_kernel(at, *refs):
    groups, refs, terms = len(GROUPS), refs[:-1], refs[-1]
    parts, grads = refs[:-groups], refs[-groups:]
    slabs = len(parts) // 4
    slices = []
    for group, units in enumerate(GROUPS):
        low = 0
        for _ in units:
            high = low + parts[4 * len(slices)].shape[-2]
            slices.append((group, slice(low, high)))
            low = high
    width = parts[0].shape[-1]
    for half in range(2):
        for code in range(4):
            total = jnp.zeros((width, width), F32)
            for slab in range(slabs):
                part = parts[4 * slab + code]
                part = part[0] if code == 1 else part[...]
                total = total + lax.dot_general(
                    part,
                    grads[slices[slab][0]][half, slices[slab][1], :],
                    (((0,), (0,)), ((), ())),
                    preferred_element_type=F32,
                )
            block = at[0] ^ code
            rows = pl.ds(pl.multiple_of((block % 2) * width, LANES), width)
            terms[block // 2, half, rows, :] = total.astype(BF16)
        sums = sum(jnp.sum(grad[half].astype(F32), axis=0, keepdims=True) for grad in grads)
        for side in range(2):
            put_sums(terms, (side, half), sums)


def product_call(at, parts, grads):
    width = grads[0].shape[-1]
    operands = [p for quad in parts for p in quad] + list(grads)
    return call(product_kernel, "weight_product", (at,), operands, [like(2, 2, 2 * width + PAD, width)])[0]


def fold_kernel(at, came, out):
    rows = out.shape[2] - PAD
    for half in range(2):
        sums = get_sums(came, (0, half)) + get_sums(came, (1, half))
        for part in range(2):
            low, high = part * rows, (part + 1) * rows
            total = came[0, half, low:high, :].astype(F32) + came[1, half, low:high, :].astype(F32)
            out[part, half, :rows, :] = total.astype(BF16)
            put_sums(out, (part, half), sums)


def fold_call(at, came):
    length, width = came.shape[2:]
    return call(fold_kernel, "fold_terms", (at,), (came,), [like(2, 2, (length - PAD) // 2 + PAD, width)])[0]


def part_kernel(at, came, out):
    rows = out.shape[1] - PAD
    for half in range(2):
        out[half, :rows, :] = (came[0, half, :rows, :].astype(F32) + came[1, half, :rows, :].astype(F32)).astype(BF16)
        put_sums(out, (half,), get_sums(came, (0, half)) + get_sums(came, (1, half)))


def part_call(at, came):
    return call(part_kernel, "part_terms", (at,), (came,), [like(*came.shape[1:])])[0]


def share_kernel(at, came, share, sums):
    rows = share.shape[1]
    total = (came[0, :rows, :].astype(F32) + came[1, :rows, :].astype(F32)).astype(BF16)
    share[0] = total
    share[1] = total
    sums[...] = get_sums(came, (0,)) + get_sums(came, (1,))


def share_call(at, came):
    two, length, width = came.shape
    return call(
        share_kernel, "share_terms", (at,), (came,), [like(2, length - PAD, width), like(1, width, dtype=F32)]
    )


def place_kernel(groups, at, *refs):
    out = refs[-1]
    for bases, mine, theirs in zip(groups, refs[0:-1:2], refs[1:-1:2]):
        for low, high in zip(bases, bases[1:]):
            rows = (high - low) // 2
            part = slice((low - bases[0]) // 2, (high - bases[0]) // 2)
            out[pl.ds(pl.multiple_of(low + at[1] * rows, 16), rows), :] = mine[part, :]
            out[pl.ds(pl.multiple_of(low + (1 - at[1]) * rows, 16), rows), :] = theirs[0, part, :]


def place_call(at, groups, pairs):
    width = pairs[0][0].shape[1]
    operands = [o for pair in pairs for o in pair]
    specs = [s for mine, _ in pairs for s in (fixed(*mine.shape), fixed(1, *mine.shape))]
    return call(
        functools.partial(place_kernel, groups), "place_rows", (at,), operands, [like(groups[-1][-1], width)], in_specs=specs
    )[0]


def spread_kernel(bases, final, at, counts, level, near, far, cross, *refs):
    out, scaled = refs[-2:]

    @pl.when(pl.program_id(0) == 0)
    def _():
        for low, high in zip(bases, bases[1:]):
            rows = (high - low) // 2
            low = low - bases[0]
            part = slice(low // 2, low // 2 + rows)
            mine = pl.ds(pl.multiple_of(low + at[1] * rows, LANES), rows)
            theirs = pl.ds(pl.multiple_of(low + (1 - at[1]) * rows, LANES), rows)
            scaled[mine, :] = (level[part, :].astype(F32) + far[part, :].astype(F32)).astype(BF16)
            scaled[theirs, :] = (near[0, part, :].astype(F32) + cross[part, :].astype(F32)).astype(BF16)

    total = lax.dot_general(counts[...], scaled[...], (((0,), (0,)), ((), ())), preferred_element_type=F32)
    if final:
        total = total + refs[0][...]
    out[...] = total.astype(out.dtype)


def spread_call(at, bases, counts, level, near, far, cross, partial, final):
    nodes = counts.shape[1]
    rows, width = level.shape
    tile = 512
    here = bases[0] // (2 * rows)
    operands = [counts, level, near, far, cross]
    specs = [
        pl.BlockSpec((2 * rows, tile), lambda i, s: (here, i)),
        fixed(rows, width),
        pl.BlockSpec((1, rows, width), lambda i, s: (1, 0, 0)),
        fixed(rows, width),
        fixed(rows, width),
    ]
    tiled = pl.BlockSpec((tile, width), lambda i, s: (i, 0))
    if partial is not None:
        operands.append(partial)
        specs.append(tiled)
    return call(
        functools.partial(spread_kernel, bases, partial is not None),
        "spread_back",
        (at,),
        operands,
        [like(nodes, width, dtype=BF16 if final else F32)],
        in_specs=specs,
        out_specs=[tiled],
        grid=(nodes // tile,),
        scratch=[pltpu.VMEM((2 * rows, width), BF16)],
    )[0]


def tie(value, *after):
    return lax.optimization_barrier((value, *after))[0]


def local(features, neighbour_lists, node_counts, weight, bias_terms, cotangent):
    dp_count = lax.axis_size("dp")
    mp_count = lax.axis_size("mp")
    bits = dp_count.bit_length() - 1
    place = lax.axis_index("mp")
    line = lax.axis_index("dp")
    core = line % 2
    nodes, width = features.shape
    depth = weight.shape[0]
    slots = neighbour_lists.shape[1]
    live = node_counts.astype(jnp.int32)
    orders = [(low, high) for low, high in zip(range(1, bits), range(bits - 1, 0, -1))] + [(0, 0)]
    piece_rows = depth // dp_count
    piece = jnp.int32(0)
    for stage, (low, high) in enumerate(orders):
        piece = piece + (jnp.where(core == 0, line >> low, line >> high) % 2 << stage)
    at = jnp.stack([place, place % 2, core, piece]).astype(jnp.int32)

    def across(value, code):
        return lax.ppermute(value, "mp", [(i, i ^ code) for i in range(mp_count)])

    def swap(value, stage):
        pairs = []
        for i in range(dp_count):
            bit = 1 << orders[stage][i % 2]
            if not i & bit:
                pairs.append([i, i | bit])
        return lax.all_to_all(value, "dp", 0, 0, axis_index_groups=pairs)

    def swap_sides(value):
        return lax.all_to_all(
            value, "mp", 0, 0, axis_index_groups=[[i, i + 1] for i in range(0, mp_count, 2)]
        )

    def gather_pieces(value):
        for stage in range(bits):
            value = swap(value, stage)
            value = value.reshape(-1, width)
            if stage < bits - 1:
                value = jnp.stack([value, value])
        return value

    unit = nodes // sum(map(sum, GROUPS))
    groups, low = [], 0
    for units in GROUPS:
        bases = [low]
        for length in units:
            low += length * unit
            bases.append(low)
        groups.append(bases)
    packed = neighbour_lists.reshape(nodes // 8, 8 * slots)
    counts, parts, scales = None, [], []
    bias_own = bias_terms.reshape(1, width)
    piece = across(piece_call(at, weight, bias_own, piece_rows), 1)
    slabs = [slab for bases in groups for slab in zip(bases, bases[1:])]

    def count_slab(slab, counts):
        low, high = slab
        return count_call(at, packed, features, cotangent, low, high - low, counts)

    def first_rows(piece, counts):
        rest = []
        for slab in slabs[1:]:
            rest.append(count_slab(slab, counts))
            counts = rest[-1][0]
        return gather_pieces(jnp.stack([piece[:piece_rows]] * 2)), [r[1:] for r in rest], counts

    def no_rows(piece, counts):
        return jax.tree.map(
            lambda shape: jnp.zeros(shape.shape, shape.dtype), jax.eval_shape(first_rows, piece, counts)
        )

    counts, *first = count_slab(slabs[0], None)
    first[:3] = [tie(value, piece) for value in first[:3]]
    weight_sib, rest, counts = lax.cond(live[0] > 0, first_rows, no_rows, piece, counts)
    bias_sib = piece[piece_rows : piece_rows + 1]
    for same, other, pack, scale in (first, *rest):
        parts.append((same, across(pack, 1), across(same, 2), across(other, 3)))
        scales.append(scale)

    sides, index = [], 0
    for bases in groups:
        buffers = None
        for low, high in zip(bases, bases[1:]):
            buffers = row_call(
                tie(at, scales[-1]), live, parts[index], scales[index], cotangent, weight, weight_sib, bias_own, bias_sib, low, bases[0],
                (bases[-1] - bases[0]) // 2, buffers,
            )
            index += 1
        sides.append(buffers)
    grads = [side[1] for side in sides]

    def fold_terms(parts, grads):
        came = swap(product_call(at, parts, grads), bits - 1)
        for stage in range(bits - 2, -1, -1):
            came = swap(fold_call(at, came), stage)
        return part_call(at, came)

    def no_terms(parts, grads):
        return jnp.zeros((2, piece_rows + PAD, width), BF16)

    def share_terms(came, counts, entry):
        share, bias_grad = share_call(at, came)
        partial = spread_call(at, groups[0], counts, *entry, None, False)
        return gather_pieces(share).astype(F32), bias_grad, partial

    def no_share(came, counts, entry):
        return jnp.zeros((depth, width), F32), jnp.zeros((1, width), F32), jnp.zeros((nodes, width), F32)

    terms = lax.cond(live[0] > 0, fold_terms, no_terms, parts, grads)
    pairs, entries = [], []
    for index, side in enumerate(sides):
        out_own, _, level, near, far, cross = side
        if index == 0:
            near, far, cross = (tie(value, parts[-1][2]) for value in (near, far, cross))
        if index == len(groups) - 1:
            came = swap_sides(tie(terms, *entries[0][1:]))
            near, far, cross = tie(near, came), tie(far, came), tie(cross, came)
        near, far, cross = across(near, 1), across(far, 2), across(cross, 3)
        pairs.append((out_own, near))
        entries.append((level, near, far, cross))
    weight_grad, bias_grad, partial = lax.cond(live[0] > 0, share_terms, no_share, came, counts, entries[0])
    features_grad = spread_call(at, groups[1], counts, *entries[1], partial, True)
    output = place_call(at, groups, pairs)
    return (output, features_grad, weight_grad, bias_grad.reshape(width))


def solution(mesh):
    in_specs = (P("dp", "mp"), P("dp", None), P("dp"), P(None, "mp"), P("mp"), P("dp", "mp"))
    out_specs = (P("dp", "mp"), P("dp", "mp"), P(None, "mp"), P("mp"))
    return jax.shard_map(local, mesh=mesh, in_specs=in_specs, out_specs=out_specs, check_vma=False)
```

time: 1070 us -> 265 us (0.25); the launches traced: 1050 us -> 263 us
  other arithmetic: 526 us -> 8.48 us
  local copies, waits for them, and re-layouts: 303 us -> 9.62 us
  Pallas kernels: 0 us -> 72.7 us
  blocking collectives: 123 us -> 76.9 us
  matrix products: 33.3 us -> 0 us
  waiting for transfers between devices: 35.6 us -> 64.9 us
  between operations: 14.8 us -> 1.46 us
    scatter-add x4 -> x0, other arithmetic: 426 us -> none  [add_block(): summed.at[indices.reshape(-1)].add(values.reshape(-1, breadth))]
    gather x4 -> x0, local copies, waits for them, and re-layouts: 265 us -> none  [one_block(): picked = jnp.take(features, indices, axis=0)]
    all_to_all x0 -> x8, blocking collectives: none -> 76.9 us  [the longest x7 67.4 us: swap(): return lax.all_to_all(value, 'dp', 0, 0, axis_index_groups=pairs)]
    pallas_call x0 -> x13, Pallas kernels: none -> 72.7 us  [call(): pl.pallas_call(kernel, grid_spec=pltpu.PrefetchScalarGridSpec(num_scalar_...]
    psum x1 -> x0, blocking collectives: 70.6 us -> none  [local(): weight_all, bias_all = lax.psum((weight_part, bias_part), ('dp', 'mp'))]
    ppermute x0 -> x13, waiting for transfers between devices: none -> 62.9 us  [across(): return lax.ppermute(value, 'mp', [(i, i ^ code) for i in range(mp_count)])]
    all_gather x1 -> x0, blocking collectives: 52.3 us -> none  [local(): lax.all_gather(bias_terms, 'mp', axis=0, tiled=True)]
    select_n x9 -> x0, other arithmetic: 45.1 us -> none  [the longest x4 44.8 us: add_block(): values = jnp.where(chosen[:, :, None], portion[:, None, :], 0.0)]
  transfers between devices with their start and end apart: 6 -> 15, of which waited for: 1 -> 5; matrix products, arithmetic and copies ran while one was open for 80% -> 5% of each run, Pallas kernels for 0% -> 25%
where the time goes in v2:
time: 265 us; the launch traced here: 263 us
  blocking collectives  76.9 us (29%)
  Pallas kernels  72.7 us (27%)
  waiting for transfers between devices  64.9 us (24%)
  starting transfers between devices  29 us (11%)
  local copies, waits for them, and re-layouts  9.62 us (4%)
  other arithmetic  8.48 us (3%)
    pallas_call x13, Pallas kernels, call(): pl.pallas_call(kernel, grid_spec=pltpu.PrefetchScalarGridSpec(num_scalar_...  72.7 us
    all_to_all x7, blocking collectives, swap(): return lax.all_to_all(value, 'dp', 0, 0, axis_index_groups=pairs)  67.4 us
    ppermute x13, waiting for transfers between devices, across(): return lax.ppermute(value, 'mp', [(i, i ^ code) for i in range(mp_count)])  62.9 us
    ppermute x13, starting transfers between devices, across(): return lax.ppermute(value, 'mp', [(i, i ^ code) for i in range(mp_count)])  20.1 us
    all_to_all x1, blocking collectives, swap_sides(): lax.all_to_all(value, 'mp', 0, 0, axis_index_groups=[[i, i + 1] for i in...  9.47 us
    all_to_all x2, starting transfers between devices, swap(): return lax.all_to_all(value, 'dp', 0, 0, axis_index_groups=pairs)  8.9 us
    another operation x4, other arithmetic, gather_pieces(): value = jnp.stack([value, value])  5.62 us
    unnamed x27, local copies, waits for them, and re-layouts  5.59 us
  transfers between devices with their start and end apart: 15, of which 5 were waited for; matrix products, arithmetic and copies ran while one was open for 5% of the time, Pallas kernels for 25%

profile of v2, /device:TPU:0, one launch (start us, length us, event | category | flops | bytes accessed | tf_op | source)
XLA Modules:
  0.0 263.3 jit_solution(6229509614785583448)
XLA Ops:
  3.6 3.1 %collective-permute-start = (bf16[272,512]{1,0:T(8,128)(2,1)S(1)}, bf16[272,512]{1,0:T(8,128)(2,1)}, u32[]{:S(2)}, u32[]{:S(2)}) collective-permute-start(bf16[272,512]{1,0:T(8,128)(2,1)S(1)} %weight_piece.1), channel_id=1, source_target_pairs={{0,1},{1,0},{2,3},{3,2},{4,5},{5,4},{6,7},{7,6},{8,9},{9,8},{10,11... | collective-permute-start | bytes 835592 | tf_op jit(solution)/shard_map/ppermute | solution.py:412
  9.6 11.5 %count_and_aggregate.3 = (bf16[2048,2048]{1,0:T(8,128)(2,1)}, bf16[512,512]{1,0:T(8,128)(2,1)}, bf16[512,512]{1,0:T(8,128)(2,1)}, bf16[2,512,512]{2,1,0:T(8,128)(2,1)}, f32[512,1]{1,0:T(8,128)S(1)}) custom-call(s32[4]{0:T(128)S(1)} %pad_add_fusion.at, s32[256,256]{1,0:T(8,128)S(1)} %reshape.48.packed_ref, bf16[2048,512]{1,0:T(8,128)(2,1)} %feat_ref.1, ...), custom_call_target="tpu_custom_call" | custom-call | flops 1 | bytes 1 | tf_op jit(solution)/shard_map/count_and_aggregate/pallas_call | solution.py:33
  22.1 2.8 %collective-permute-start.2 = (bf16[512,512]{1,0:T(8,128)(2,1)}, bf16[512,512]{1,0:T(8,128)(2,1)S(1)}, u32[]{:S(2)}, u32[]{:S(2)}) collective-permute-start(bf16[512,512]{1,0:T(8,128)(2,1)} %get-tuple-element.128.part0), channel_id=1, source_target_pairs={{0,2},{1,3},{2,0},{3,1},{4,6},{5,7},{6,4},{7,5},{8,10},{9,11},{10,... | collective-permute-start | bytes 1572872 | tf_op jit(solution)/shard_map/ppermute | solution.py:412
  26.2 34.7 %conditional.3 = (bf16[2048,512]{1,0:T(8,128)(2,1)S(1)}, bf16[512,512]{1,0:T(8,128)(2,1)}, bf16[512,512]{1,0:T(8,128)(2,1)}, bf16[2,512,512]{2,1,0:T(8,128)(2,1)...) conditional(s32[]{:T(128)} %bitcast.13, () %tuple.43, (bf16[272,512]{1,0:T(8,128)(2,1)}, s32[4]{0:T(128)S(1)}, ...), branch_computations={%region_0.1_spmd, %region_1.2_spmd} | conditional | flops 1835009 | bytes 14418001 | solution.py:467
  27.4 9.1 %all_to_all.41 = bf16[2,256,512]{2,1,0:T(8,128)(2,1)S(1)} all-to-all(bf16[2,256,512]{2,1,0:T(8,128)(2,1)S(1)} %pad_maximum_fusion.2), channel_id=1, replica_groups={{0,8},{4,20},{12,28},{16,24},{1,9},{5,21},{13,29},{17,25},{2,10},{6,22}..., dimensions={0} | all-to-all | bytes 1048576 | tf_op jit(solution)/shard_map/cond/branch_1_fun/all_to_all | solution.py:420
  37.6 4.5 %all-to-all-start.4 = ((bf16[2,512,512]{2,1,0:T(8,128)(2,1)}), bf16[2,512,512]{2,1,0:T(8,128)(2,1)}, u32[]{:S(2)}, u32[]{:S(2)}) async-start(bf16[2,512,512]{2,1,0:T(8,128)(2,1)} %pad_maximum_fusion.1), calls=%async_computation.4 | async-start | bytes 2097152 | tf_op jit(solution)/shard_map/cond/branch_1_fun/all_to_all | solution.py:420
  42.1 11.7 %count_and_aggregate.2 = (bf16[2048,2048]{1,0:T(8,128)(2,1)}, bf16[512,512]{1,0:T(8,128)(2,1)}, bf16[512,512]{1,0:T(8,128)(2,1)}, bf16[2,512,512]{2,1,0:T(8,128)(2,1)}, f32[512,1]{1,0:T(8,128)}) custom-call(s32[4]{0:T(128)S(1)} %get-tuple-element.53.at, s32[256,256]{1,0:T(8,128)S(1)} %get-tuple-element.54.packed_ref, ...), custom_call_target="tpu_custom_call", output_to_operand_aliasing={{0}: (4, {})} | custom-call | flops 1 | bytes 1 | tf_op jit(solution)/shard_map/cond/branch_1_fun/count_and_aggregate/pallas_call | solution.py:33
  55.5 5.4 %all_to_all.42 = bf16[2,1024,512]{2,1,0:T(8,128)(2,1)S(1)} all-to-all(bf16[2,1024,512]{2,1,0:T(8,128)(2,1)S(1)} %pad_maximum_fusion), channel_id=1, replica_groups={{0,4},{8,12},{16,20},{24,28},{1,5},{9,13},{17,21},{25,29},{2,6},{10,14}..., dimensions={0} | all-to-all | bytes 4194304 | tf_op jit(solution)/shard_map/cond/branch_1_fun/all_to_all | solution.py:420
  64.7 7.4 %collective-permute-done.3.part3 = bf16[512,512]{1,0:T(8,128)(2,1)} collective-permute-done((bf16[512,512]{1,0:T(8,128)(2,1)}, bf16[512,512]{1,0:T(8,128)(2,1)}, u32[]{:S(2)}, u32[]{:S(2)}) %collective-permute-start.3) | collective-permute-done | bytes 524320 | tf_op jit(solution)/shard_map/ppermute | solution.py:412
  72.2 9.7 %linear_and_slope.2 = (bf16[512,512]{1,0:T(8,128)(2,1)S(1)}, bf16[2,512,512]{2,1,0:T(8,128)(2,1)}, bf16[512,512]{1,0:T(8,128)(2,1)}, bf16[2,512,512]{2,1,0:T(8,1...) custom-call(s32[4]{0:T(128)S(1)} %pad_add_fusion.at, s32[1]{0:T(128)S(6)} %copy.34.live, ...), custom_call_target="tpu_custom_call" | custom-call | flops 1 | bytes 1 | tf_op jit(solution)/shard_map/linear_and_slope/pallas_call | solution.py:33
  81.9 11.2 %collective-permute-done.4.part2 = bf16[512,512]{1,0:T(8,128)(2,1)S(1)} collective-permute-done((bf16[512,512]{1,0:T(8,128)(2,1)}, bf16[512,512]{1,0:T(8,128)(2,1)S(1)}, u32[]{:S(2)}, u32[]{:S(2)}) %collective-permute-start.4) | collective-permute-done | bytes 524320 | tf_op jit(solution)/shard_map/ppermute | solution.py:412
  93.8 3.4 %collective-permute-start.7 = (bf16[512,512]{1,0:T(8,128)(2,1)S(1)}, bf16[512,512]{1,0:T(8,128)(2,1)S(1)}, u32[]{:S(2)}, u32[]{:S(2)}) collective-permute-start(bf16[512,512]{1,0:T(8,128)(2,1)S(1)} %copy-done.11), channel_id=1, source_target_pairs={{0,3},{1,2},{2,1},{3,0},{4,7},{5,6},{6,5},{7,4},{8,11},{9,10},{10,... | collective-permute-start | bytes 1572872 | tf_op jit(solution)/shard_map/ppermute | solution.py:412
  99.0 40.5 %collective-permute-done.7.part3 = bf16[512,512]{1,0:T(8,128)(2,1)S(1)} collective-permute-done((bf16[512,512]{1,0:T(8,128)(2,1)S(1)}, bf16[512,512]{1,0:T(8,128)(2,1)S(1)}, u32[]{:S(2)}, u32[]{:S(2)}) %collective-permute-start.7) | collective-permute-done | bytes 524320 | tf_op jit(solution)/shard_map/ppermute | solution.py:412
  139.6 7.8 %linear_and_slope.3 = (bf16[512,512]{1,0:T(8,128)(2,1)S(1)}, bf16[2,512,512]{2,1,0:T(8,128)(2,1)}, bf16[512,512]{1,0:T(8,128)(2,1)S(1)}, bf16[2,512,512]{2,1,0:T...) custom-call(s32[4]{0:T(128)S(1)} %pad_add_fusion.at, s32[1]{0:T(128)S(6)} %copy.34.live, ...), custom_call_target="tpu_custom_call" | custom-call | flops 1 | bytes 1 | tf_op jit(solution)/shard_map/linear_and_slope/pallas_call | solution.py:33
  149.0 51.1 %conditional.4 = (bf16[2,272,512]{2,1,0:T(8,128)(2,1)S(1)}) conditional(s32[]{:T(128)} %bitcast.13, () %tuple.50, (s32[4]{0:T(128)S(1)}, bf16[512,512]{1,0:T(8,128)(2,1)}, bf16[2,512,512]{2,1,0:T(8,128)(2,1)}, bf16[512,512]{1,0:T(8,128)(2,1)}, bf16[512,512]{1,0:T(8,128)(2,1)}, /*index=5*/bf16[512,512]{1,0:T(8,128)(2,1)}, ...), branch_computations={%region_2.3_spmd, %region_3.4_spmd} | conditional | flops 4 | bytes 15073292 | solution.py:502
  149.0 7.6 %weight_product.1 = bf16[2,2,1040,512]{3,2,1,0:T(8,128)(2,1)S(1)} custom-call(s32[4]{0:T(128)S(1)} %get-tuple-element.63.at, bf16[512,512]{1,0:T(8,128)(2,1)} %get-tuple-element.64.refs_0_, bf16[2,512,512]{2,1,0:T(8,128)(2,1)} %get-tuple-element.65.refs_1_, bf16[512,512]{1,0:T(8,128)(2,1)} %get-tuple-element.66.refs_2_, ...), custom_call_target="tpu_custom_call" | custom-call | flops 1 | bytes 1 | tf_op jit(solution)/shard_map/cond/branch_1_fun/weight_product/pallas_call | solution.py:33
  156.6 8.3 %all_to_all.43.came = bf16[2,2,1040,512]{3,2,1,0:T(8,128)(2,1)} all-to-all(bf16[2,2,1040,512]{3,2,1,0:T(8,128)(2,1)S(1)} %weight_product.1), channel_id=1, replica_groups={{0,4},{8,12},{16,20},{24,28},{1,5},{9,13},{17,21},{25,29},{2,6},{10,14}..., dimensions={0} | all-to-all | bytes 8519680 | tf_op jit(solution)/shard_map/cond/branch_1_fun/all_to_all | solution.py:420
  164.9 3.2 %fold_terms.2 = bf16[2,2,528,512]{3,2,1,0:T(8,128)(2,1)S(1)} custom-call(s32[4]{0:T(128)S(1)} %get-tuple-element.63.at, bf16[2,2,1040,512]{3,2,1,0:T(8,128)(2,1)} %all_to_all.43.came), custom_call_target="tpu_custom_call" | custom-call | flops 1 | bytes 1 | tf_op jit(solution)/shard_map/cond/branch_1_fun/fold_terms/pallas_call | solution.py:33
  168.1 17.9 %all_to_all.44.came = bf16[2,2,528,512]{3,2,1,0:T(8,128)(2,1)S(1)} all-to-all(bf16[2,2,528,512]{3,2,1,0:T(8,128)(2,1)S(1)} %fold_terms.2), channel_id=1, replica_groups={{0,16},{4,12},{8,24},{20,28},{1,17},{5,13},{9,25},{21,29},{2,18},{6,14}..., dimensions={0} | all-to-all | bytes 4325376 | tf_op jit(solution)/shard_map/cond/branch_1_fun/all_to_all | solution.py:420
  186.9 12.3 %all_to_all.45.came = bf16[2,2,272,512]{3,2,1,0:T(8,128)(2,1)S(1)} all-to-all(bf16[2,2,272,512]{3,2,1,0:T(8,128)(2,1)S(1)} %fold_terms.3), channel_id=1, replica_groups={{0,8},{4,20},{12,28},{16,24},{1,9},{5,21},{13,29},{17,25},{2,10},{6,22}..., dimensions={0} | all-to-all | bytes 2228224 | tf_op jit(solution)/shard_map/cond/branch_1_fun/all_to_all | solution.py:420
  200.1 9.5 %all_to_all.48 = bf16[2,272,512]{2,1,0:T(8,128)(2,1)S(1)} all-to-all(bf16[2,272,512]{2,1,0:T(8,128)(2,1)S(1)} %get-tuple-element.179), channel_id=1, replica_groups={{0,1},{2,3},{4,5},{6,7},{8,9},{10,11},{12,13},{14,15},{16,17},{18,19},{..., dimensions={0} | all-to-all | bytes 1114112 | tf_op jit(solution)/shard_map/all_to_all | solution.py:423
  210.6 2.5 collective-permute-start.11
  213.1 35.0 %conditional.5 = (f32[2048,512]{1,0:T(8,128)}, f32[2048,512]{1,0:T(8,128)}, f32[512]{0:T(512)}) conditional(s32[]{:T(128)} %bitcast.13, () %tuple.58, (s32[4]{0:T(128)S(1)}, bf16[2,272,512]{2,1,0:T(8,128)(2,1)S(1)}, bf16[2048,2048]{1,0:T(8,128)(2,1)}, bf16[512,512]{1,0:T(8,128)(2,1)}, bf16[2,512,512]{2,1,0:T(8,128)(2,1)}, ...), branch_computations={%region_4.5_spmd, %region_5.6_spmd} | conditional | flops 2621442 | bytes 19398712 | solution.py:514
  214.2 9.0 %all_to_all.46 = bf16[2,256,512]{2,1,0:T(8,128)(2,1)S(1)} all-to-all(bf16[2,256,512]{2,1,0:T(8,128)(2,1)S(1)} %get-tuple-element.76), channel_id=1, replica_groups={{0,8},{4,20},{12,28},{16,24},{1,9},{5,21},{13,29},{17,25},{2,10},{6,22}..., dimensions={0} | all-to-all | bytes 1048576 | tf_op jit(solution)/shard_map/cond/branch_1_fun/all_to_all | solution.py:420
  224.3 4.4 %all-to-all-start.7 = ((bf16[2,512,512]{2,1,0:T(8,128)(2,1)}), bf16[2,512,512]{2,1,0:T(8,128)(2,1)}, u32[]{:S(2)}, u32[]{:S(2)}) async-start(bf16[2,512,512]{2,1,0:T(8,128)(2,1)} %pad_maximum_fusion.4), calls=%async_computation.7 | async-start | bytes 2097152 | tf_op jit(solution)/shard_map/cond/branch_1_fun/all_to_all | solution.py:420
  228.7 7.6 %spread_back.2 = f32[2048,512]{1,0:T(8,128)} custom-call(s32[4]{0:T(128)S(1)} %get-tuple-element.74.at, bf16[2048,2048]{1,0:T(8,128)(2,1)} %get-tuple-element.77.counts, bf16[512,512]{1,0:T(8,128)(2,1)} %get-tuple-element.78.level, bf16[2,512,512]{2,1,0:T(8,128)(2,1)} %get-tuple-element.79.near, bf16[512,512]{1,0:T(8,128)(2,1)} %get-tuple-element.80.far, ...), custom_call_target="tpu_custom_call" | custom-call | flops 1 | bytes 1 | tf_op jit(solution)/shard_map/cond/branch_1_fun/spread_back/pallas_call | solution.py:33
  236.3 1.9 all-to-all-done.7
  240.0 5.4 %all_to_all.47 = bf16[2,1024,512]{2,1,0:T(8,128)(2,1)S(1)} all-to-all(bf16[2,1024,512]{2,1,0:T(8,128)(2,1)S(1)} %pad_maximum_fusion.3), channel_id=1, replica_groups={{0,4},{8,12},{16,20},{24,28},{1,5},{9,13},{17,21},{25,29},{2,6},{10,14}..., dimensions={0} | all-to-all | bytes 4194304 | tf_op jit(solution)/shard_map/cond/branch_1_fun/all_to_all | solution.py:420
  245.4 2.7 %bitcast_convert_fusion = f32[2048,512]{1,0:T(8,128)} fusion(bf16[2,1024,512]{2,1,0:T(8,128)(2,1)S(1)} %all_to_all.47), kind=kLoop, calls=%fused_computation.5 | loop fusion | flops 1048576 | bytes 6291456 | tf_op jit(solution)/shard_map/cond/branch_1_fun/convert_element_type | solution.py:497
  248.1 3.8 %collective-permute-done.10.refs_3_.near = bf16[2,512,512]{2,1,0:T(8,128)(2,1)S(1)} collective-permute-done((bf16[2,512,512]{2,1,0:T(8,128)(2,1)}, bf16[2,512,512]{2,1,0:T(8,128)(2,1)S(1)}, u32[]{:S(2)}, u32[]{:S(2)}) %collective-permute-start.10) | collective-permute-done | bytes 1048608 | tf_op jit(solution)/shard_map/ppermute | solution.py:412
  253.0 3.0 %place_rows.1 = bf16[2048,512]{1,0:T(8,128)(2,1)} custom-call(s32[4]{0:T(128)S(1)} %pad_add_fusion.at, bf16[512,512]{1,0:T(8,128)(2,1)S(1)} %get-tuple-element.135.refs_0_, bf16[2,512,512]{2,1,0:T(8,128)(2,1)} %collective-permute-done.5.refs_1_, bf16[512,512]{1,0:T(8,128)(2,1)S(1)} %copy-done.3, bf16[2,512,512]{2,1,0:T(8,128)(2,1)S(1)} %collective-permute-done.10.refs_3_.near), custom_call_target="tpu_custom_call" | custom-call | flops 1 | bytes 1 | tf_op jit(solution)/shard_map/place_rows/pallas_call | solution.py:33
  256.0 7.3 %spread_back.3 = bf16[2048,512]{1,0:T(8,128)(2,1)} custom-call(s32[4]{0:T(128)S(1)} %pad_add_fusion.at, bf16[2048,2048]{1,0:T(8,128)(2,1)} %get-tuple-element.151.counts, bf16[512,512]{1,0:T(8,128)(2,1)S(1)} %get-tuple-element.152.level, bf16[2,512,512]{2,1,0:T(8,128)(2,1)S(1)} %collective-permute-done.10.refs_3_.near, ...), custom_call_target="tpu_custom_call" | custom-call | flops 1 | bytes 1 | tf_op jit(solution)/shard_map/spread_back/pallas_call | solution.py:33
  (60 shorter events, 26.9 us)
Async XLA Ops:
  1.4 1.6 copy-start
  3.0 3.7 %copy-start.12 = (s32[2048,32]{0,1:T(8,128)S(1)}, s32[2048,32]{0,1:T(8,128)}, u32[]{:S(2)}) copy-start(s32[2048,32]{0,1:T(8,128)} %param.13) | copy-start | bytes 786436
  3.0 6.5 %copy-start.5 = (bf16[2048,512]{1,0:T(8,128)(2,1)S(1)}, bf16[2048,512]{1,0:T(8,128)(2,1)}, u32[]{:S(2)}) copy-start(bf16[2048,512]{1,0:T(8,128)(2,1)} %cot_own.3) | copy-start | bytes 6291460
  3.6 17.5 %collective-permute-start = (bf16[272,512]{1,0:T(8,128)(2,1)S(1)}, bf16[272,512]{1,0:T(8,128)(2,1)}, u32[]{:S(2)}, u32[]{:S(2)}) collective-permute-start(bf16[272,512]{1,0:T(8,128)(2,1)S(1)} %weight_piece.1), channel_id=1, source_target_pairs={{0,1},{1,0},{2,3},{3,2},{4,5},{5,4},{6,7},{7,6},{8,9},{9,8},{10,11... | collective-permute-start | bytes 835592 | tf_op jit(solution)/shard_map/ppermute | solution.py:412
  21.1 51.1 %collective-permute-start.1 = (bf16[2,512,512]{2,1,0:T(8,128)(2,1)}, bf16[2,512,512]{2,1,0:T(8,128)(2,1)}, u32[]{:S(2)}, u32[]{:S(2)}) collective-permute-start(bf16[2,512,512]{2,1,0:T(8,128)(2,1)} %get-tuple-element.130), channel_id=1, source_target_pairs={{0,1},{1,0},{2,3},{3,2},{4,5},{5,4},{6,7},{7,6},{8,9},{9,8},{10,11... | collective-permute-start | bytes 3145736 | tf_op jit(solution)/shard_map/ppermute | solution.py:412
  22.1 42.6 %collective-permute-start.2 = (bf16[512,512]{1,0:T(8,128)(2,1)}, bf16[512,512]{1,0:T(8,128)(2,1)S(1)}, u32[]{:S(2)}, u32[]{:S(2)}) collective-permute-start(bf16[512,512]{1,0:T(8,128)(2,1)} %get-tuple-element.128.part0), channel_id=1, source_target_pairs={{0,2},{1,3},{2,0},{3,1},{4,6},{5,7},{6,4},{7,5},{8,10},{9,11},{10,... | collective-permute-start | bytes 1572872 | tf_op jit(solution)/shard_map/ppermute | solution.py:412
  24.9 47.2 %collective-permute-start.3 = (bf16[512,512]{1,0:T(8,128)(2,1)}, bf16[512,512]{1,0:T(8,128)(2,1)}, u32[]{:S(2)}, u32[]{:S(2)}) collective-permute-start(bf16[512,512]{1,0:T(8,128)(2,1)} %get-tuple-element.132), channel_id=1, source_target_pairs={{0,3},{1,2},{2,1},{3,0},{4,7},{5,6},{6,5},{7,4},{8,11},{9,10},{10,... | collective-permute-start | bytes 1572872 | tf_op jit(solution)/shard_map/ppermute | solution.py:412
  26.2 45.9 %copy-start.1 = (bf16[2048,512]{1,0:T(8,128)(2,1)S(1)}, bf16[2048,512]{1,0:T(8,128)(2,1)}, u32[]{:S(2)}) copy-start(bf16[2048,512]{1,0:T(8,128)(2,1)} %weight_own.3) | copy-start | bytes 6291460
  37.6 16.2 %all-to-all-start.4 = ((bf16[2,512,512]{2,1,0:T(8,128)(2,1)}), bf16[2,512,512]{2,1,0:T(8,128)(2,1)}, u32[]{:S(2)}, u32[]{:S(2)}) async-start(bf16[2,512,512]{2,1,0:T(8,128)(2,1)} %pad_maximum_fusion.1), calls=%async_computation.4 | async-start | bytes 2097152 | tf_op jit(solution)/shard_map/cond/branch_1_fun/all_to_all | solution.py:420
  60.9 11.2 %copy-start.7 = (bf16[2048,512]{1,0:T(8,128)(2,1)}, bf16[2048,512]{1,0:T(8,128)(2,1)S(1)}, u32[]{:S(2)}) copy-start(bf16[2048,512]{1,0:T(8,128)(2,1)S(1)} %get-tuple-element.134.weight_sib) | copy-start | bytes 6291460
  60.9 32.1 %collective-permute-start.4 = (bf16[512,512]{1,0:T(8,128)(2,1)}, bf16[512,512]{1,0:T(8,128)(2,1)S(1)}, u32[]{:S(2)}, u32[]{:S(2)}) collective-permute-start(bf16[512,512]{1,0:T(8,128)(2,1)} %get-tuple-element.137.part0), channel_id=1, source_target_pairs={{0,2},{1,3},{2,0},{3,1},{4,6},{5,7},{6,4},{7,5},{8,10},{9,11},{10,... | collective-permute-start | bytes 1572872 | tf_op jit(solution)/shard_map/ppermute | solution.py:412
  62.6 76.9 %collective-permute-start.6 = (bf16[2,512,512]{2,1,0:T(8,128)(2,1)}, bf16[2,512,512]{2,1,0:T(8,128)(2,1)S(1)}, u32[]{:S(2)}, u32[]{:S(2)}) collective-permute-start(bf16[2,512,512]{2,1,0:T(8,128)(2,1)} %get-tuple-element.139), channel_id=1, source_target_pairs={{0,1},{1,0},{2,3},{3,2},{4,5},{5,4},{6,7},{7,6},{8,9},{9,8},{10,11... | collective-permute-start | bytes 3145736 | tf_op jit(solution)/shard_map/ppermute | solution.py:412
  64.7 7.4 %copy-start.9 = (bf16[512,512]{1,0:T(8,128)(2,1)}, bf16[512,512]{1,0:T(8,128)(2,1)S(1)}, u32[]{:S(2)}) copy-start(bf16[512,512]{1,0:T(8,128)(2,1)S(1)} %collective-permute-done.2.part2) | copy-start | bytes 1572868
  72.2 21.7 %copy-start.11 = (bf16[512,512]{1,0:T(8,128)(2,1)S(1)}, bf16[512,512]{1,0:T(8,128)(2,1)}, u32[]{:S(2)}) copy-start(bf16[512,512]{1,0:T(8,128)(2,1)} %get-tuple-element.140) | copy-start | bytes 1572868
  72.2 67.4 %copy-start.6 = (bf16[2048,512]{1,0:T(8,128)(2,1)S(1)}, bf16[2048,512]{1,0:T(8,128)(2,1)}, u32[]{:S(2)}) copy-start(bf16[2048,512]{1,0:T(8,128)(2,1)} %cot_own.3) | copy-start | bytes 6291460
  72.2 67.4 %copy-start.8 = (bf16[2048,512]{1,0:T(8,128)(2,1)S(1)}, bf16[2048,512]{1,0:T(8,128)(2,1)}, u32[]{:S(2)}) copy-start(bf16[2048,512]{1,0:T(8,128)(2,1)} %copy-done.7) | copy-start | bytes 6291460
  72.2 67.4 %copy-start.10 = (f32[512,1]{1,0:T(8,128)S(1)}, f32[512,1]{1,0:T(8,128)}, u32[]{:S(2)}) copy-start(f32[512,1]{1,0:T(8,128)} %get-tuple-element.125.scale) | copy-start | bytes 6148
  93.1 107.1 %collective-permute-start.5 = (bf16[2,512,512]{2,1,0:T(8,128)(2,1)}, bf16[2,512,512]{2,1,0:T(8,128)(2,1)}, u32[]{:S(2)}, u32[]{:S(2)}) collective-permute-start(bf16[2,512,512]{2,1,0:T(8,128)(2,1)} %get-tuple-element.138), channel_id=1, source_target_pairs={{0,1},{1,0},{2,3},{3,2},{4,5},{5,4},{6,7},{7,6},{8,9},{9,8},{10,11... | collective-permute-start | bytes 3145736 | tf_op jit(solution)/shard_map/ppermute | solution.py:412
  93.8 45.7 %collective-permute-start.7 = (bf16[512,512]{1,0:T(8,128)(2,1)S(1)}, bf16[512,512]{1,0:T(8,128)(2,1)S(1)}, u32[]{:S(2)}, u32[]{:S(2)}) collective-permute-start(bf16[512,512]{1,0:T(8,128)(2,1)S(1)} %copy-done.11), channel_id=1, source_target_pairs={{0,3},{1,2},{2,1},{3,0},{4,7},{5,6},{6,5},{7,4},{8,11},{9,10},{10,... | collective-permute-start | bytes 1572872 | tf_op jit(solution)/shard_map/ppermute | solution.py:412
  97.2 102.9 %collective-permute-start.9 = (bf16[512,512]{1,0:T(8,128)(2,1)}, bf16[512,512]{1,0:T(8,128)(2,1)}, u32[]{:S(2)}, u32[]{:S(2)}) collective-permute-start(bf16[512,512]{1,0:T(8,128)(2,1)} %get-tuple-element.148), channel_id=1, source_target_pairs={{0,3},{1,2},{2,1},{3,0},{4,7},{5,6},{6,5},{7,4},{8,11},{9,10},{10,... | collective-permute-start | bytes 1572872 | tf_op jit(solution)/shard_map/ppermute | solution.py:412
  97.7 102.4 %collective-permute-start.8 = (bf16[512,512]{1,0:T(8,128)(2,1)}, bf16[512,512]{1,0:T(8,128)(2,1)}, u32[]{:S(2)}, u32[]{:S(2)}) collective-permute-start(bf16[512,512]{1,0:T(8,128)(2,1)} %get-tuple-element.146), channel_id=1, source_target_pairs={{0,2},{1,3},{2,0},{3,1},{4,6},{5,7},{6,4},{7,5},{8,10},{9,11},{10,... | collective-permute-start | bytes 1572872 | tf_op jit(solution)/shard_map/ppermute | solution.py:412
  147.4 0.8 copy-start.2
  148.2 0.8 copy-start.4
  209.6 42.3 %collective-permute-start.10 = (bf16[2,512,512]{2,1,0:T(8,128)(2,1)}, bf16[2,512,512]{2,1,0:T(8,128)(2,1)S(1)}, u32[]{:S(2)}, u32[]{:S(2)}) collective-permute-start(bf16[2,512,512]{2,1,0:T(8,128)(2,1)} %get-tuple-element.150), channel_id=1, source_target_pairs={{0,1},{1,0},{2,3},{3,2},{4,5},{5,4},{6,7},{7,6},{8,9},{9,8},{10,11... | collective-permute-start | bytes 3145736 | tf_op jit(solution)/shard_map/ppermute | solution.py:412
  209.9 46.1 %collective-permute-start.12 = (bf16[512,512]{1,0:T(8,128)(2,1)}, bf16[512,512]{1,0:T(8,128)(2,1)S(1)}, u32[]{:S(2)}, u32[]{:S(2)}) collective-permute-start(bf16[512,512]{1,0:T(8,128)(2,1)} %get-tuple-element.156), channel_id=1, source_target_pairs={{0,3},{1,2},{2,1},{3,0},{4,7},{5,6},{6,5},{7,4},{8,11},{9,10},{10,... | collective-permute-start | bytes 1572872 | tf_op jit(solution)/shard_map/ppermute | solution.py:412
  210.6 45.4 %collective-permute-start.11 = (bf16[512,512]{1,0:T(8,128)(2,1)}, bf16[512,512]{1,0:T(8,128)(2,1)S(1)}, u32[]{:S(2)}, u32[]{:S(2)}) collective-permute-start(bf16[512,512]{1,0:T(8,128)(2,1)} %copy-done.4), channel_id=1, source_target_pairs={{0,2},{1,3},{2,0},{3,1},{4,6},{5,7},{6,4},{7,5},{8,10},{9,11},{10,... | collective-permute-start | bytes 1572872 | tf_op jit(solution)/shard_map/ppermute | solution.py:412
  224.3 13.9 %all-to-all-start.7 = ((bf16[2,512,512]{2,1,0:T(8,128)(2,1)}), bf16[2,512,512]{2,1,0:T(8,128)(2,1)}, u32[]{:S(2)}, u32[]{:S(2)}) async-start(bf16[2,512,512]{2,1,0:T(8,128)(2,1)} %pad_maximum_fusion.4), calls=%async_computation.7 | async-start | bytes 2097152 | tf_op jit(solution)/shard_map/cond/branch_1_fun/all_to_all | solution.py:420
  251.9 1.0 copy-start.3

commit v3 on v2

v3 whole, which is shorter than its diff:
```python
import functools

import jax
import jax.numpy as jnp
from jax import lax
from jax.experimental import pallas as pl
from jax.experimental.pallas import tpu as pltpu
from jax.sharding import PartitionSpec as P

BF16 = jnp.bfloat16
F32 = jnp.float32
UNITS = 8
SLABS = ((0, 4), (4, 4))
GROUPS = ((((0, 0), (0, 1)), ((1, 0),)), (((1, 1),),))
PARTS = tuple(tuple(entry for run in group for entry in run) for group in GROUPS)
LANES = 128
PAD = 16
VMEM_LIMIT = 48 << 20
ANY = pl.BlockSpec(memory_space=pl.ANY)


def like(*shape, dtype=BF16):
    return jax.ShapeDtypeStruct(shape, dtype)


def fixed(*shape):
    return pl.BlockSpec(shape, lambda *_: (0,) * len(shape))


def units_of(entry):
    slab, block = entry
    first, length = SLABS[slab]
    return first + block, first + length // 2 + block


def call(
    kernel, name, scalars, operands, out_shape, in_specs=None, out_specs=None, grid=(1,), scratch=(), aliases=None, us=0
):
    if in_specs is None:
        in_specs = [fixed(*o.shape) for o in operands]
    if out_specs is None:
        out_specs = [fixed(*o.shape) for o in out_shape]
    return pl.pallas_call(
        kernel,
        grid_spec=pltpu.PrefetchScalarGridSpec(
            num_scalar_prefetch=len(scalars), grid=grid, in_specs=in_specs, out_specs=out_specs, scratch_shapes=scratch
        ),
        out_shape=out_shape,
        compiler_params=pltpu.CompilerParams(vmem_limit_bytes=VMEM_LIMIT),
        input_output_aliases={len(scalars) + i: o for i, o in (aliases or {}).items()},
        cost_estimate=pl.CostEstimate(flops=1, bytes_accessed=max(1, us * 3000000), transcendentals=0),
        name=name,
    )(*scalars, *operands)


def piece_kernel(at, weight, bias, out):
    rows = out.shape[0] - PAD
    out[:rows, :] = weight[...]
    out[rows:, :] = jnp.broadcast_to(bias[...].astype(F32).reshape(1, -1), (PAD, out.shape[1])).astype(BF16)


def piece_call(at, weight, bias, rows):
    width = weight.shape[1]
    return call(
        piece_kernel,
        "weight_piece",
        (at,),
        (weight, bias),
        [like(rows + PAD, width)],
        in_specs=[pl.BlockSpec((rows, width), lambda i, s: (s[3], 0)), fixed(width)],
    )[0]


def count_kernel(base, slots, at, packed_ref, feat_ref, cot_ref, *refs):
    counts_ref, same_ref, other_ref, pack_ref, scale_ref = refs[-5:]
    rows = counts_ref.shape[0]
    step = pl.program_id(0)
    steps = pl.num_programs(0)
    block = (step + at[1] * (steps // 2)) % steps
    row = lax.broadcasted_iota(jnp.int32, (LANES, 8 * slots), 0)
    owner = lax.broadcasted_iota(jnp.int32, (1, 8 * slots), 1) // slots

    def group(index):
        entry = packed_ref[index : index + 1, :]
        high = (entry >> 7) * 8 + owner
        low = entry & (LANES - 1)
        left = jnp.where(high == row, 1.0, 0.0).astype(BF16)
        right = jnp.where(low == row, 1.0, 0.0).astype(BF16)
        return lax.dot_general(left, right, (((1,), (1,)), ((), ())), preferred_element_type=F32)

    for pair in range(rows // 16):
        first, second = group(2 * pair), group(2 * pair + 1)
        for tile in range(counts_ref.shape[1] // LANES):
            counts_ref[pair * 16 : (pair + 1) * 16, tile * LANES : (tile + 1) * LANES] = jnp.concatenate(
                [first[tile * 8 : (tile + 1) * 8], second[tile * 8 : (tile + 1) * 8]], 0
            ).astype(BF16)
    degree = jnp.sum(counts_ref[...].astype(F32), axis=1, keepdims=True)
    scale = 1.0 / (degree + 1.0)
    down = lax.broadcasted_iota(jnp.int32, (LANES, LANES), 0)
    across = lax.broadcasted_iota(jnp.int32, (LANES, LANES), 1)
    twice = jnp.where(down == across, 2.0, 0.0)
    column = pl.multiple_of(base + block * rows, LANES)
    tile_view = counts_ref[:, pl.ds(column, LANES)].astype(F32)
    counts_ref[:, pl.ds(column, LANES)] = (tile_view + twice).astype(BF16)
    total = jnp.dot(counts_ref[...], feat_ref[...], preferred_element_type=F32)
    result = (total * scale).astype(BF16)

    @pl.when(step < steps // 2)
    def _():
        same_ref[...] = result
        scale_ref[...] = scale

    @pl.when(step >= steps // 2)
    def _():
        other_ref[...] = result
        pack_ref[0] = result
        pack_ref[1] = cot_ref[...]


def count_call(at, packed, features, cotangent, base, size, counts):
    nodes, width = features.shape
    slots = packed.shape[1] // 8
    rows = LANES
    steps = size // rows
    half = steps // 2

    def natural(i, s):
        return base // rows + (i + s[1] * half) % steps

    def early(i, s):
        return jnp.minimum(i, half - 1), 0

    def late(i, s):
        return jnp.maximum(i - half, 0), 0

    operands = [packed, features, cotangent]
    specs = [
        pl.BlockSpec((rows // 8, 8 * slots), lambda i, s: (natural(i, s), 0)),
        fixed(nodes, width),
        pl.BlockSpec((rows, width), lambda i, s: (natural(i, s), 0)),
    ]
    aliases = {}
    if counts is not None:
        aliases = {len(operands): 0}
        operands.append(counts)
        specs.append(ANY)
    return call(
        functools.partial(count_kernel, base, slots),
        "count_and_aggregate",
        (at,),
        operands,
        [
            like(nodes, nodes),
            like(size // 2, width),
            like(size // 2, width),
            like(2, size // 2, width),
            like(size // 2, 1, dtype=F32),
        ],
        in_specs=specs,
        out_specs=[
            pl.BlockSpec((rows, nodes), lambda i, s: (natural(i, s), 0)),
            pl.BlockSpec((rows, width), early),
            pl.BlockSpec((rows, width), late),
            pl.BlockSpec((2, rows, width), lambda i, s: (0, *late(i, s))),
            pl.BlockSpec((rows, 1), early),
        ],
        grid=(steps,),
        aliases=aliases,
    )


def row_kernel(
    units, at, live, part0, near, part2, part3, scale, cot_own, weight_own, weight_sib, bias_own, bias_sib, *refs
):
    out_own, grads, back0, back_near, back2, back3 = refs[-6:]
    rows, width = part0.shape
    place = at[0]
    slot = (units[0] + at[1] * (units[1] - units[0])) * rows + lax.broadcasted_iota(jnp.int32, (rows, width), 0)
    living = slot < live[0]
    starts = [pl.multiple_of((place ^ code) * width, LANES) for code in range(4)]
    values = []
    for half, (weight, bias, cot) in enumerate(
        ((weight_own, bias_own, cot_own[...]), (weight_sib, bias_sib, near[1]))
    ):
        linear = bias[0:1, :].astype(F32)
        for part, start in zip((part0[...], near[0], part2[...], part3[...]), starts):
            linear = linear + jnp.dot(part, weight[pl.ds(start, width), :], preferred_element_type=F32)
        sigma = 1.0 / (1.0 + jnp.exp(-linear))
        result = jnp.where(living, linear * sigma, 0.0).astype(BF16)
        if half == 0:
            out_own[...] = result
        else:
            back_near[0] = result
        slope = sigma * (1.0 + linear * (1.0 - sigma))
        value = jnp.where(living, cot.astype(F32) * slope, 0.0).astype(BF16)
        grads[at[1] if half == 0 else 1 - at[1]] = value
        values.append(value)
    for code, start in enumerate(starts):
        total = jnp.zeros((rows, width), F32)
        for weight, value in zip((weight_own, weight_sib), values):
            total = total + lax.dot_general(
                value, weight[pl.ds(start, width), :], (((1,), (1,)), ((), ())), preferred_element_type=F32
            )
        total = (total * scale[...]).astype(BF16)
        if code == 1:
            back_near[1] = total
        else:
            (back0, None, back2, back3)[code][...] = total


def row_call(at, live, parts, scale, cotangent, weight_own, weight_sib, piece_own, piece_sib, entry, places, buffers):
    width = cotangent.shape[1]
    rows = cotangent.shape[0] // UNITS
    block, (low, high) = entry[1], units_of(entry)
    operands = [*parts, scale, cotangent, weight_own, weight_sib, piece_own, piece_sib]
    chunk = pl.BlockSpec((rows, width), lambda i, s, c: (block, 0))
    bias = pl.BlockSpec((PAD, width), lambda i, s, c: (piece_own.shape[0] // PAD - 1, 0))
    specs = [
        chunk,
        pl.BlockSpec((2, rows, width), lambda i, s, c: (0, block, 0)),
        chunk,
        chunk,
        pl.BlockSpec((rows, 1), lambda i, s, c: (block, 0)),
        pl.BlockSpec((rows, width), lambda i, s, c: (low + s[1] * (high - low), 0)),
        fixed(*weight_own.shape),
        fixed(*weight_sib.shape),
        bias,
        bias,
    ]
    shapes, outs, aliases = [], [], {}
    for number, (double, (index, length)) in enumerate(
        zip((False, True, False, True, False, False), (places[0],) * 4 + (places[1],) * 2)
    ):
        if double:
            shapes.append(like(2, length * rows, width))
            outs.append(pl.BlockSpec((2, rows, width), lambda i, s, c, index=index: (0, index, 0)))
        else:
            shapes.append(like(length * rows, width))
            outs.append(pl.BlockSpec((rows, width), lambda i, s, c, index=index: (index, 0)))
        if index > 0:
            aliases[len(operands)] = number
            operands.append(buffers[number])
            specs.append(ANY)
    return call(
        functools.partial(row_kernel, (low, high)),
        "linear_and_slope",
        (at, live),
        operands,
        shapes,
        in_specs=specs,
        out_specs=outs,
        aliases=aliases,
    )


def put_sums(ref, index, value):
    high = value.astype(BF16)
    low = (value - high.astype(F32)).astype(BF16)
    row = lax.broadcasted_iota(jnp.int32, (PAD, value.shape[1]), 0)
    both = jnp.where(row == 0, high.astype(F32), jnp.where(row == 1, low.astype(F32), 0.0))
    ref[(*index, slice(ref.shape[-2] - PAD, None), slice(None))] = both.astype(BF16)


def get_sums(ref, index):
    rows = ref[(*index, slice(ref.shape[-2] - PAD, None), slice(None))]
    return jnp.sum(rows.astype(F32), axis=0, keepdims=True)


def product_kernel(at, *refs):
    refs, terms = refs[:-1], refs[-1]
    parts, grads = refs[: -len(GROUPS)], refs[-len(GROUPS) :]
    unit = grads[0].shape[1] // len(PARTS[0])
    runs = []
    for group, entries in enumerate(PARTS):
        for index, (slab, block) in enumerate(entries):
            runs.append((slab, slice(block * unit, (block + 1) * unit), group, slice(index * unit, (index + 1) * unit)))
    width = parts[0].shape[-1]
    for half in range(2):
        for code in range(4):
            total = jnp.zeros((width, width), F32)
            for slab, from_rows, group, to_rows in runs:
                part = parts[4 * slab + code]
                part = part[0, from_rows, :] if code == 1 else part[from_rows, :]
                total = total + lax.dot_general(
                    part, grads[group][half, to_rows, :], (((0,), (0,)), ((), ())), preferred_element_type=F32
                )
            block = at[0] ^ code
            rows = pl.ds(pl.multiple_of((block % 2) * width, LANES), width)
            terms[block // 2, half, rows, :] = total.astype(BF16)
        sums = sum(jnp.sum(grad[half].astype(F32), axis=0, keepdims=True) for grad in grads)
        for side in range(2):
            put_sums(terms, (side, half), sums)


def product_call(at, parts, grads):
    width = grads[0].shape[-1]
    operands = [p for quad in parts for p in quad] + list(grads)
    return call(product_kernel, "weight_product", (at,), operands, [like(2, 2, 2 * width + PAD, width)])[0]


def fold_kernel(at, came, out):
    rows = out.shape[2] - PAD
    for half in range(2):
        sums = get_sums(came, (0, half)) + get_sums(came, (1, half))
        for part in range(2):
            low, high = part * rows, (part + 1) * rows
            total = came[0, half, low:high, :].astype(F32) + came[1, half, low:high, :].astype(F32)
            out[part, half, :rows, :] = total.astype(BF16)
            put_sums(out, (part, half), sums)


def fold_call(at, came):
    length, width = came.shape[2:]
    return call(fold_kernel, "fold_terms", (at,), (came,), [like(2, 2, (length - PAD) // 2 + PAD, width)])[0]


def part_kernel(at, came, out):
    rows = out.shape[1] - PAD
    for half in range(2):
        out[half, :rows, :] = (came[0, half, :rows, :].astype(F32) + came[1, half, :rows, :].astype(F32)).astype(BF16)
        put_sums(out, (half,), get_sums(came, (0, half)) + get_sums(came, (1, half)))


def part_call(at, came):
    return call(part_kernel, "part_terms", (at,), (came,), [like(*came.shape[1:])])[0]


def share_kernel(at, came, share, sums):
    rows = share.shape[0]
    share[...] = (came[0, :rows, :].astype(F32) + came[1, :rows, :].astype(F32)).astype(BF16)
    sums[...] = get_sums(came, (0,)) + get_sums(came, (1,))


def share_call(at, came):
    two, length, width = came.shape
    return call(
        share_kernel, "share_terms", (at,), (came,), [like(length - PAD, width), like(1, width, dtype=F32)]
    )


def join_kernel(stage, at, mine, theirs, out):
    rows = mine.shape[0]
    bit = (at[3] >> stage) % 2
    for copy in range(out.shape[0]):
        out[copy, pl.ds(pl.multiple_of(bit * rows, 16), rows), :] = mine[...]
        out[copy, pl.ds(pl.multiple_of((1 - bit) * rows, 16), rows), :] = theirs[...]


def join_call(at, stage, mine, theirs, copies):
    rows, width = mine.shape
    return call(
        functools.partial(join_kernel, stage), "join_halves", (at,), (mine, theirs), [like(copies, 2 * rows, width)]
    )[0]


def place_kernel(entries, at, mine, theirs, out):
    rows = mine.shape[0] // len(entries)
    for index, entry in enumerate(entries):
        low, high = units_of(entry)
        part = slice(index * rows, (index + 1) * rows)
        own = low + at[1] * (high - low)
        out[pl.ds(pl.multiple_of(own * rows, LANES), rows), :] = mine[part, :]
        out[pl.ds(pl.multiple_of((low + high - own) * rows, LANES), rows), :] = theirs[0, part, :]


def place_call(at, entries, mine, theirs):
    rows, width = mine.shape
    return call(
        functools.partial(place_kernel, entries),
        "place_rows",
        (at,),
        (mine, theirs),
        [like(rows // len(entries) * UNITS, width)],
        in_specs=[fixed(rows, width), fixed(1, rows, width)],
        us=3,
    )[0]


def spread_kernel(group, final, at, *refs):
    entries = PARTS[group]
    counts, refs = refs[: 2 * len(entries)], refs[2 * len(entries) :]
    (level, near), refs = refs[:2], refs[2:]
    fars, refs = refs[: 2 * len(GROUPS[group])], refs[2 * len(GROUPS[group]) :]
    scaled = refs[-1]
    rows = level.shape[0] // len(entries)
    step = pl.program_id(0)

    @pl.when(step == 0)
    def _():
        index = 0
        for run, entries in enumerate(GROUPS[group]):
            far, cross = fars[2 * run : 2 * run + 2]
            for number in range(len(entries)):
                part = slice(index * rows, (index + 1) * rows)
                there = slice(number * rows, (number + 1) * rows)
                scaled[2 * index + at[1]] = (level[part, :].astype(F32) + far[there, :].astype(F32)).astype(BF16)
                scaled[2 * index + 1 - at[1]] = (near[1, part, :].astype(F32) + cross[there, :].astype(F32)).astype(BF16)
                index += 1

    total = refs[0][...] if final else None
    for index, block in enumerate(counts):
        term = lax.dot_general(block[...], scaled[index], (((0,), (0,)), ((), ())), preferred_element_type=F32)
        total = term if total is None else total + term
    out = refs[3] if final else refs[0]
    out[...] = total.astype(out.dtype)
    if final:
        mine, output = refs[1], refs[4]
        half = pl.num_programs(0) // 2

        @pl.when(step // half == at[1])
        def _():
            output[...] = mine[...]

        @pl.when(step // half != at[1])
        def _():
            output[...] = near[0]


def spread_call(at, group, counts, level, near, fars, *last):
    nodes = counts.shape[0]
    rows, width = level.shape
    tile = 512
    final = len(last) > 0
    unit_rows = nodes // UNITS
    units = [unit for entry in PARTS[group] for unit in units_of(entry)]
    tiled = pl.BlockSpec((tile, width), lambda i, s: (i, 0))
    operands = [counts] * len(units) + [level, near, *fars, *last]
    specs = [pl.BlockSpec((unit_rows, tile), lambda i, s, unit=unit: (unit, i)) for unit in units]
    specs += [fixed(*o.shape) for o in (level, near, *fars)]
    shapes, outs, aliases = [like(nodes, width, dtype=F32)], [tiled], {}
    if final:
        (low, high), steps = units, nodes // tile
        specs += [tiled, fixed(rows, width), ANY]
        shapes = [like(nodes, width), like(nodes, width)]
        outs.append(pl.BlockSpec((unit_rows, width), lambda i, s: (jnp.where(i < steps // 2, low, high), 0)))
        aliases = {len(operands) - 1: 1}
    return call(
        functools.partial(spread_kernel, group, final),
        "spread_back",
        (at,),
        operands,
        shapes,
        in_specs=specs,
        out_specs=outs,
        grid=(nodes // tile,),
        scratch=[pltpu.VMEM((len(units), unit_rows, width), BF16)],
        aliases=aliases,
        us=8,
    )


def tie(value, *after):
    return lax.optimization_barrier((value, *after))[0]


def local(features, neighbour_lists, node_counts, weight, bias_terms, cotangent):
    dp_count = lax.axis_size("dp")
    mp_count = lax.axis_size("mp")
    bits = dp_count.bit_length() - 1
    place = lax.axis_index("mp")
    line = lax.axis_index("dp")
    core = line % 2
    nodes, width = features.shape
    depth = weight.shape[0]
    slots = neighbour_lists.shape[1]
    live = node_counts.astype(jnp.int32)
    orders = [(low, high) for low, high in zip(range(1, bits), range(bits - 1, 0, -1))] + [(0, 0)]
    piece_rows = depth // dp_count
    piece = jnp.int32(0)
    for stage, (low, high) in enumerate(orders):
        piece = piece + (jnp.where(core == 0, line >> low, line >> high) % 2 << stage)
    at = jnp.stack([place, place % 2, core, piece]).astype(jnp.int32)

    def across(value, code):
        return lax.ppermute(value, "mp", [(i, i ^ code) for i in range(mp_count)])

    def swap(value, stage):
        pairs = []
        for i in range(dp_count):
            bit = 1 << orders[stage][i % 2]
            if not i & bit:
                pairs.append([i, i | bit])
        return lax.all_to_all(value, "dp", 0, 0, axis_index_groups=pairs)

    def along(value, stage):
        return lax.ppermute(value, "dp", [(i, i ^ (1 << orders[stage][i % 2])) for i in range(dp_count)])

    def join_pieces(value):
        for stage in range(bits - 1):
            last = stage == bits - 2
            value = join_call(at, stage, value, along(value, stage), 2 if last else 1)
            value = value if last else value[0]
        return swap(value, bits - 1).reshape(-1, width)

    def gather_pieces(value):
        for stage in range(bits):
            value = swap(value, stage)
            value = value.reshape(-1, width)
            if stage < bits - 1:
                value = jnp.stack([value, value])
        return value

    unit = nodes // UNITS
    packed = neighbour_lists.reshape(nodes // 8, 8 * slots)
    piece_own = piece_call(at, weight, bias_terms, piece_rows)
    piece_sib = across(piece_own, 1)

    def count_slab(slab, counts):
        first, length = slab
        return count_call(tie(at, piece_own), packed, features, cotangent, first * unit, length * unit, counts)

    def zeros_for(function):
        return lambda *operands: jax.tree.map(
            lambda shape: jnp.zeros(shape.shape, shape.dtype), jax.eval_shape(function, *operands)
        )

    def always(function, *operands):
        return lax.cond(live[0] > 0, function, zeros_for(function), *operands)

    def last_rows(piece, counts):
        last = count_slab(SLABS[1], counts)
        return gather_pieces(jnp.stack([piece[:piece_rows]] * 2)), last

    counts, *first = count_slab(SLABS[0], None)
    same, other, pack, scale = (tie(value, piece_sib) for value in first)
    parts, scales = [(same, across(pack, 1), across(same, 2), across(other, 3))], [scale]
    weight_sib, (counts, same, other, pack, scale) = always(last_rows, piece_sib, counts)
    near, far, cross = parts[0][1:]
    parts.append(
        (same, across(tie(pack, cross), 1), across(tie(same, near), 2), across(tie(other, far), 3))
    )
    scales.append(scale)

    sides = []
    for group in GROUPS:
        total, index, buffers, runs = sum(map(len, group)), 0, None, []
        for run in group:
            for number, entry in enumerate(run):
                buffers = row_call(
                    at, live, parts[entry[0]], scales[entry[0]], cotangent, weight, weight_sib, piece_own, piece_sib,
                    entry, ((index, total), (number, len(run))), buffers,
                )
                index += 1
            runs.append(buffers[4:])
        sides.append((*buffers[:4], runs))
    grads = [side[1] for side in sides]

    def fold_terms(parts, grads):
        came = swap(product_call(at, parts, grads), bits - 1)
        for stage in range(bits - 2, -1, -1):
            came = swap(fold_call(at, came), stage)
        return part_call(at, came)

    def share_terms(came, counts, back, out_own):
        share, bias_grad = share_call(at, came)
        partial = spread_call(at, 0, counts, *back)[0]
        output = place_call(at, PARTS[0], out_own, back[1])
        return join_pieces(share).astype(F32), bias_grad, partial, output

    terms = always(fold_terms, parts, grads)
    backs = []
    for index, (_, _, level, near, runs) in enumerate(sides):
        if index == 1:
            mine = lax.dynamic_index_in_dim(terms, place % 2, 0, False)
            theirs = tie(lax.dynamic_index_in_dim(terms, 1 - place % 2, 0, False), backs[0][1], *backs[0][2])
            came = jnp.stack([mine, across(theirs, 1)])
            near = tie(near, came)
        fars = []
        for number, (far, cross) in enumerate(runs):
            if (index, number) == (0, 0):
                far, cross = tie(far, parts[-1][2]), tie(cross, parts[-1][2])
            if index == 1:
                far, cross = tie(far, theirs), tie(cross, theirs)
            fars += [across(far, 2), across(cross, 3)]
        backs.append((level, across(near, 1), fars))
    weight_grad, bias_grad, partial, output = always(share_terms, came, counts, backs[0], sides[0][0])
    features_grad, output = spread_call(at, 1, counts, *backs[1], partial, sides[1][0], output)
    return (output, features_grad, weight_grad, bias_grad.reshape(width))


def solution(mesh):
    in_specs = (P("dp", "mp"), P("dp", None), P("dp"), P(None, "mp"), P("mp"), P("dp", "mp"))
    out_specs = (P("dp", "mp"), P("dp", "mp"), P(None, "mp"), P("mp"))
    return jax.shard_map(local, mesh=mesh, in_specs=in_specs, out_specs=out_specs, check_vma=False)
```

time: 265 us -> 242 us (0.913)
  blocking collectives: 76.9 us -> 58.4 us
  waiting for transfers between devices: 64.9 us -> 56.9 us
  Pallas kernels: 72.7 us -> 78.2 us
  starting transfers between devices: 29 us -> 32.1 us
  other arithmetic: 8.48 us -> 5.7 us
    ppermute x13 -> x16, waiting for transfers between devices: 62.9 us -> 51.5 us  [across(): return lax.ppermute(value, 'mp', [(i, i ^ code) for i in range(mp_count)])]
    all_to_all x1 -> x0, blocking collectives: 9.47 us -> none  [swap_sides(): lax.all_to_all(value, 'mp', 0, 0, axis_index_groups=[[i, i + 1] for i in...]
    all_to_all x7 -> x6, blocking collectives: 67.4 us -> 58.4 us  [swap(): return lax.all_to_all(value, 'dp', 0, 0, axis_index_groups=pairs)]
    pallas_call x13 -> x17, Pallas kernels: 72.7 us -> 78.2 us  [call(): pl.pallas_call(kernel, grid_spec=pltpu.PrefetchScalarGridSpec(num_scalar_...]
    ppermute x0 -> x2, waiting for transfers between devices: none -> 5.31 us  [along(): lax.ppermute(value, 'dp', [(i, i ^ 1 << orders[stage][i % 2]) for i in ra...]
    all_to_all x2 -> x1, starting transfers between devices: 8.9 us -> 4.41 us  [swap(): return lax.all_to_all(value, 'dp', 0, 0, axis_index_groups=pairs)]
    ppermute x0 -> x2, starting transfers between devices: none -> 4.48 us  [along(): lax.ppermute(value, 'dp', [(i, i ^ 1 << orders[stage][i % 2]) for i in ra...]
    ppermute x13 -> x16, starting transfers between devices: 20.1 us -> 23.2 us  [across(): return lax.ppermute(value, 'mp', [(i, i ^ code) for i in range(mp_count)])]
  transfers between devices with their start and end apart: 15 -> 19, of which waited for: 5 -> 7; matrix products, arithmetic and copies ran while one was open for 5% -> 3% of each run, Pallas kernels for 25% -> 28%
where the time goes in v3:
time: 242 us; the launch traced here: 241 us
  Pallas kernels  78.2 us (32%)
  blocking collectives  58.4 us (24%)
  waiting for transfers between devices  56.9 us (24%)
  starting transfers between devices  32.1 us (13%)
  local copies, waits for them, and re-layouts  7.71 us (3%)
  other arithmetic  5.7 us (2%)
    pallas_call x17, Pallas kernels, call(): pl.pallas_call(kernel, grid_spec=pltpu.PrefetchScalarGridSpec(num_scalar_...  78.2 us
    all_to_all x6, blocking collectives, swap(): return lax.all_to_all(value, 'dp', 0, 0, axis_index_groups=pairs)  58.4 us
    ppermute x16, waiting for transfers between devices, across(): return lax.ppermute(value, 'mp', [(i, i ^ code) for i in range(mp_count)])  51.5 us
    ppermute x16, starting transfers between devices, across(): return lax.ppermute(value, 'mp', [(i, i ^ code) for i in range(mp_count)])  23.2 us
    unnamed x49, local copies, waits for them, and re-layouts  6.22 us
    ppermute x2, waiting for transfers between devices, along(): lax.ppermute(value, 'dp', [(i, i ^ 1 << orders[stage][i % 2]) for i in ra...  5.31 us
  transfers between devices with their start and end apart: 19, of which 7 were waited for; matrix products, arithmetic and copies ran while one was open for 3% of the time, Pallas kernels for 28%

profile of v3, /device:TPU:0, one launch (start us, length us, event | category | flops | bytes accessed | tf_op | source)
XLA Modules:
  0.0 240.9 jit_solution(13980316993592296967)
XLA Ops:
  3.6 3.1 %collective-permute-start.2 = (bf16[272,512]{1,0:T(8,128)(2,1)S(1)}, bf16[272,512]{1,0:T(8,128)(2,1)S(1)}, u32[]{:S(2)}, u32[]{:S(2)}) collective-permute-start(bf16[272,512]{1,0:T(8,128)(2,1)S(1)} %weight_piece.1.bias_own), channel_id=1, source_target_pairs={{0,1},{1,0},{2,3},{3,2},{4,5},{5,4},{6,7},{7,6},{8,9},{9,8},{10,11... | collective-permute-start | bytes 835592 | tf_op jit(solution)/shard_map/ppermute | solution.py:475
  7.4 11.6 %count_and_aggregate.3 = (bf16[2048,2048]{1,0:T(8,128)(2,1)}, bf16[512,512]{1,0:T(8,128)(2,1)}, bf16[512,512]{1,0:T(8,128)(2,1)S(1)}, bf16[2,512,512]{2,1,0:T(8,128)(2,1)}, f32[512,1]{1,0:T(8,128)S(1)}) custom-call(s32[4]{0:T(128)S(1)} %pad_add_fusion.at, s32[256,256]{1,0:T(8,128)S(1)} %reshape.36.packed_ref, bf16[2048,512]{1,0:T(8,128)(2,1)} %feat_ref.1, ...), custom_call_target="tpu_custom_call" | custom-call | flops 1 | bytes 1 | tf_op jit(solution)/shard_map/count_and_aggregate/pallas_call | solution.py:43
  19.0 2.5 %collective-permute-start.3 = (bf16[512,512]{1,0:T(8,128)(2,1)S(1)}, bf16[512,512]{1,0:T(8,128)(2,1)}, u32[]{:S(2)}, u32[]{:S(2)}) collective-permute-start(bf16[512,512]{1,0:T(8,128)(2,1)S(1)} %get-tuple-element.158), channel_id=1, source_target_pairs={{0,3},{1,2},{2,1},{3,0},{4,7},{5,6},{6,5},{7,4},{8,11},{9,10},{10,... | collective-permute-start | bytes 1572872 | tf_op jit(solution)/shard_map/ppermute | solution.py:475
  24.1 34.7 %conditional.3 = (bf16[2048,512]{1,0:T(8,128)(2,1)S(1)}, bf16[2048,2048]{1,0:T(8,128)(2,1)}, bf16[512,512]{1,0:T(8,128)(2,1)}, bf16[512,512]{1,0:T(8,128)(2,1)},...) conditional(s32[]{:T(128)} %bitcast.12, () %tuple.47, (bf16[272,512]{1,0:T(8,128)(2,1)}, s32[4]{0:T(128)S(1)}, ...), branch_computations={%region_0.1_spmd, %region_1.2_spmd} | conditional | flops 1835009 | bytes 15466605 | solution.py:518
  25.3 9.1 %all_to_all.28 = bf16[2,256,512]{2,1,0:T(8,128)(2,1)S(1)} all-to-all(bf16[2,256,512]{2,1,0:T(8,128)(2,1)S(1)} %pad_maximum_fusion.2), channel_id=1, replica_groups={{0,8},{4,20},{12,28},{16,24},{1,9},{5,21},{13,29},{17,25},{2,10},{6,22}..., dimensions={0} | all-to-all | bytes 1048576 | tf_op jit(solution)/shard_map/cond/branch_1_fun/all_to_all | solution.py:483
  35.5 4.4 %all-to-all-start.4 = ((bf16[2,512,512]{2,1,0:T(8,128)(2,1)}), bf16[2,512,512]{2,1,0:T(8,128)(2,1)}, u32[]{:S(2)}, u32[]{:S(2)}) async-start(bf16[2,512,512]{2,1,0:T(8,128)(2,1)} %pad_maximum_fusion.1), calls=%async_computation.4 | async-start | bytes 2097152 | tf_op jit(solution)/shard_map/cond/branch_1_fun/all_to_all | solution.py:483
  39.9 11.8 %count_and_aggregate.2 = (bf16[2048,2048]{1,0:T(8,128)(2,1)}, bf16[512,512]{1,0:T(8,128)(2,1)}, bf16[512,512]{1,0:T(8,128)(2,1)}, bf16[2,512,512]{2,1,0:T(8,128)(2,1)}, f32[512,1]{1,0:T(8,128)}) custom-call(s32[4]{0:T(128)S(1)} %get-tuple-element.60.at, s32[256,256]{1,0:T(8,128)S(1)} %copy-done.24, ...), custom_call_target="tpu_custom_call", output_to_operand_aliasing={{0}: (4, {})} | custom-call | flops 1 | bytes 1 | tf_op jit(solution)/shard_map/cond/branch_1_fun/count_and_aggregate/pallas_call | solution.py:43
  53.4 5.4 %all_to_all.29 = bf16[2,1024,512]{2,1,0:T(8,128)(2,1)S(1)} all-to-all(bf16[2,1024,512]{2,1,0:T(8,128)(2,1)S(1)} %pad_maximum_fusion), channel_id=1, replica_groups={{0,4},{8,12},{16,20},{24,28},{1,5},{9,13},{17,21},{25,29},{2,6},{10,14}..., dimensions={0} | all-to-all | bytes 4194304 | tf_op jit(solution)/shard_map/cond/branch_1_fun/all_to_all | solution.py:483
  59.2 8.5 %collective-permute-done.7.part2 = bf16[512,512]{1,0:T(8,128)(2,1)} collective-permute-done((bf16[512,512]{1,0:T(8,128)(2,1)}, bf16[512,512]{1,0:T(8,128)(2,1)}, u32[]{:S(2)}, u32[]{:S(2)}) %collective-permute-start.7) | collective-permute-done | bytes 524320 | tf_op jit(solution)/shard_map/ppermute | solution.py:475
  71.6 6.7 %linear_and_slope.5 = (bf16[768,512]{1,0:T(8,128)(2,1)S(1)}, bf16[2,768,512]{2,1,0:T(8,128)(2,1)}, bf16[768,512]{1,0:T(8,128)(2,1)S(1)}, bf16[2,768,512]{2,1,0:T...) custom-call(s32[4]{0:T(128)S(1)} %pad_add_fusion.at, s32[1]{0:T(128)S(6)} %copy.58.live, ...), custom_call_target="tpu_custom_call" | custom-call | flops 1 | bytes 1 | tf_op jit(solution)/shard_map/linear_and_slope/pallas_call | solution.py:43
  78.3 5.7 %linear_and_slope.6 = (bf16[768,512]{1,0:T(8,128)(2,1)S(1)}, bf16[2,768,512]{2,1,0:T(8,128)(2,1)}, bf16[768,512]{1,0:T(8,128)(2,1)S(1)}, bf16[2,768,512]{2,1,0:T...) custom-call(s32[4]{0:T(128)S(1)} %pad_add_fusion.at, ...), custom_call_target="tpu_custom_call", output_to_operand_aliasing={{0}: (12, {}), {1}: (13, {}), {2}: (14, {}), {3}: (15, {}),... | custom-call | flops 1 | bytes 1 | tf_op jit(solution)/shard_map/linear_and_slope/pallas_call | solution.py:43
  84.0 19.2 %collective-permute-done.8.part3 = bf16[512,512]{1,0:T(8,128)(2,1)S(1)} collective-permute-done((bf16[512,512]{1,0:T(8,128)(2,1)}, bf16[512,512]{1,0:T(8,128)(2,1)S(1)}, u32[]{:S(2)}, u32[]{:S(2)}) %collective-permute-start.8) | collective-permute-done | bytes 524320 | tf_op jit(solution)/shard_map/ppermute | solution.py:475
  103.2 8.1 %collective-permute-done.4.near = bf16[2,512,512]{2,1,0:T(8,128)(2,1)S(1)} collective-permute-done((bf16[2,512,512]{2,1,0:T(8,128)(2,1)}, bf16[2,512,512]{2,1,0:T(8,128)(2,1)S(1)}, u32[]{:S(2)}, u32[]{:S(2)}) %collective-permute-start.4) | collective-permute-done | bytes 1048608 | tf_op jit(solution)/shard_map/ppermute | solution.py:475
  111.3 3.3 %collective-permute-done.6.part2 = bf16[512,512]{1,0:T(8,128)(2,1)S(1)} collective-permute-done((bf16[512,512]{1,0:T(8,128)(2,1)}, bf16[512,512]{1,0:T(8,128)(2,1)S(1)}, u32[]{:S(2)}, u32[]{:S(2)}) %collective-permute-start.6) | collective-permute-done | bytes 524320 | tf_op jit(solution)/shard_map/ppermute | solution.py:475
  114.7 5.5 %linear_and_slope.7 = (bf16[768,512]{1,0:T(8,128)(2,1)S(1)}, bf16[2,768,512]{2,1,0:T(8,128)(2,1)}, bf16[768,512]{1,0:T(8,128)(2,1)S(1)}, bf16[2,768,512]{2,1,0:T...) custom-call(s32[4]{0:T(128)S(1)} %pad_add_fusion.at, ...), custom_call_target="tpu_custom_call", output_to_operand_aliasing={{0}: (12, {}), {1}: (13, {}), {2}: (14, {}), {3}: (15, {})} | custom-call | flops 1 | bytes 1 | tf_op jit(solution)/shard_map/linear_and_slope/pallas_call | solution.py:43
  120.3 2.7 %collective-permute-start.11 = (bf16[512,512]{1,0:T(8,128)(2,1)}, bf16[512,512]{1,0:T(8,128)(2,1)}, u32[]{:S(2)}, u32[]{:S(2)}) collective-permute-start(bf16[512,512]{1,0:T(8,128)(2,1)} %get-tuple-element.189), channel_id=1, source_target_pairs={{0,3},{1,2},{2,1},{3,0},{4,7},{5,6},{6,5},{7,4},{8,11},{9,10},{10,... | collective-permute-start | bytes 1572872 | tf_op jit(solution)/shard_map/ppermute | solution.py:475
  127.1 6.1 %linear_and_slope.4 = (bf16[256,512]{1,0:T(8,128)(2,1)S(1)}, bf16[2,256,512]{2,1,0:T(8,128)(2,1)}, bf16[256,512]{1,0:T(8,128)(2,1)S(1)}, bf16[2,256,512]{2,1,0:T...) custom-call(s32[4]{0:T(128)S(1)} %pad_add_fusion.at, s32[1]{0:T(128)S(6)} %copy.58.live, ...), custom_call_target="tpu_custom_call" | custom-call | flops 1 | bytes 1 | tf_op jit(solution)/shard_map/linear_and_slope/pallas_call | solution.py:43
  135.4 51.5 %conditional.4 = (bf16[2,272,512]{2,1,0:T(8,128)(2,1)S(1)}) conditional(s32[]{:T(128)} %bitcast.12, () %tuple.56, (s32[4]{0:T(128)S(1)}, bf16[512,512]{1,0:T(8,128)(2,1)}, bf16[2,512,512]{2,1,0:T(8,128)(2,1)}, bf16[512,512]{1,0:T(8,128)(2,1)}, bf16[512,512]{1,0:T(8,128)(2,1)}, /*index=5*/bf16[512,512]{1,0:T(8,128)(2,1)}, ...), branch_computations={%region_2.3_spmd, %region_3.4_spmd} | conditional | flops 4 | bytes 15073292 | solution.py:518
  135.4 8.1 %weight_product.1 = bf16[2,2,1040,512]{3,2,1,0:T(8,128)(2,1)S(1)} custom-call(s32[4]{0:T(128)S(1)} %get-tuple-element.70.at, bf16[512,512]{1,0:T(8,128)(2,1)} %get-tuple-element.71.refs_0_, bf16[2,512,512]{2,1,0:T(8,128)(2,1)} %get-tuple-element.72.refs_1_, bf16[512,512]{1,0:T(8,128)(2,1)} %get-tuple-element.73.refs_2_, ...), custom_call_target="tpu_custom_call" | custom-call | flops 1 | bytes 1 | tf_op jit(solution)/shard_map/cond/branch_1_fun/weight_product/pallas_call | solution.py:43
  143.5 8.2 %all_to_all.30.came = bf16[2,2,1040,512]{3,2,1,0:T(8,128)(2,1)} all-to-all(bf16[2,2,1040,512]{3,2,1,0:T(8,128)(2,1)S(1)} %weight_product.1), channel_id=1, replica_groups={{0,4},{8,12},{16,20},{24,28},{1,5},{9,13},{17,21},{25,29},{2,6},{10,14}..., dimensions={0} | all-to-all | bytes 8519680 | tf_op jit(solution)/shard_map/cond/branch_1_fun/all_to_all | solution.py:483
  151.8 3.2 %fold_terms.2 = bf16[2,2,528,512]{3,2,1,0:T(8,128)(2,1)S(1)} custom-call(s32[4]{0:T(128)S(1)} %get-tuple-element.70.at, bf16[2,2,1040,512]{3,2,1,0:T(8,128)(2,1)} %all_to_all.30.came), custom_call_target="tpu_custom_call" | custom-call | flops 1 | bytes 1 | tf_op jit(solution)/shard_map/cond/branch_1_fun/fold_terms/pallas_call | solution.py:43
  155.0 17.9 %all_to_all.31.came = bf16[2,2,528,512]{3,2,1,0:T(8,128)(2,1)S(1)} all-to-all(bf16[2,2,528,512]{3,2,1,0:T(8,128)(2,1)S(1)} %fold_terms.2), channel_id=1, replica_groups={{0,16},{4,12},{8,24},{20,28},{1,17},{5,13},{9,25},{21,29},{2,18},{6,14}..., dimensions={0} | all-to-all | bytes 4325376 | tf_op jit(solution)/shard_map/cond/branch_1_fun/all_to_all | solution.py:483
  173.8 12.3 %all_to_all.32.came = bf16[2,2,272,512]{3,2,1,0:T(8,128)(2,1)S(1)} all-to-all(bf16[2,2,272,512]{3,2,1,0:T(8,128)(2,1)S(1)} %fold_terms.3), channel_id=1, replica_groups={{0,8},{4,20},{12,28},{16,24},{1,9},{5,21},{13,29},{17,25},{2,10},{6,22}..., dimensions={0} | all-to-all | bytes 2228224 | tf_op jit(solution)/shard_map/cond/branch_1_fun/all_to_all | solution.py:483
  189.0 10.5 %collective-permute-done.14 = bf16[272,512]{1,0:T(8,128)(2,1)S(1)} collective-permute-done((bf16[272,512]{1,0:T(8,128)(2,1)S(1)}, bf16[272,512]{1,0:T(8,128)(2,1)S(1)}, u32[]{:S(2)}, u32[]{:S(2)}) %collective-permute-start.14) | collective-permute-done | bytes 278560 | tf_op jit(solution)/shard_map/ppermute | solution.py:475
  199.8 4.3 %collective-permute-start.17 = (bf16[256,512]{1,0:T(8,128)(2,1)S(1)}, bf16[256,512]{1,0:T(8,128)(2,1)S(1)}, u32[]{:S(2)}, u32[]{:S(2)}) collective-permute-start(bf16[256,512]{1,0:T(8,128)(2,1)S(1)} %copy-done.6), channel_id=1, source_target_pairs={{0,3},{1,2},{2,1},{3,0},{4,7},{5,6},{6,5},{7,4},{8,11},{9,10},{10,... | collective-permute-start | bytes 786440 | tf_op jit(solution)/shard_map/ppermute | solution.py:475
  204.1 30.1 %conditional.5 = (f32[2048,512]{1,0:T(8,128)}, f32[2048,512]{1,0:T(8,128)S(1)}, bf16[2048,512]{1,0:T(8,128)(2,1)S(1)}, f32[512]{0:T(512)}) conditional(s32[]{:T(128)} %bitcast.12, () %tuple.65, (s32[4]{0:T(128)S(1)}, bf16[2,272,512]{2,1,0:T(8,128)(2,1)S(1)}, bf16[2048,2048]{1,0:T(8,128)(2,1)}, bf16[768,512]{1,0:T(8,128)(2,1)S(1)}, ...), branch_computations={%region_4.5_spmd, %region_5.6_spmd} | conditional | flops 1048581 | bytes 49777360 | solution.py:518
  205.2 2.8 %collective-permute-start = (bf16[256,512]{1,0:T(8,128)(2,1)S(1)}, bf16[256,512]{1,0:T(8,128)(2,1)S(1)}, u32[]{:S(2)}, u32[]{:S(2)}) collective-permute-start(bf16[256,512]{1,0:T(8,128)(2,1)S(1)} %get-tuple-element.83.mine), channel_id=1, source_target_pairs={{0,8},{4,20},{8,0},{12,28},{16,24},{20,4},{24,16},{28,12},{1,9},{5... | collective-permute-start | bytes 786440 | tf_op jit(solution)/shard_map/cond/branch_1_fun/ppermute | solution.py:486
  208.0 5.3 %collective-permute-done.theirs = bf16[256,512]{1,0:T(8,128)(2,1)S(1)} collective-permute-done((bf16[256,512]{1,0:T(8,128)(2,1)S(1)}, bf16[256,512]{1,0:T(8,128)(2,1)S(1)}, u32[]{:S(2)}, u32[]{:S(2)}) %collective-permute-start) | collective-permute-done | bytes 262176 | tf_op jit(solution)/shard_map/cond/branch_1_fun/ppermute | solution.py:486
  217.4 7.9 %spread_back.2 = f32[2048,512]{1,0:T(8,128)S(1)} custom-call(s32[4]{0:T(128)S(1)} %get-tuple-element.81.at, bf16[2048,2048]{1,0:T(8,128)(2,1)} %get-tuple-element.84.refs_0_.refs_1_.refs_2_.refs_3_.refs_4_.refs_5_, bf16[2048,2048]{1,0:T(8,128)(2,1)} %get-tuple-element.84.refs_0_.refs_1_.refs_2_.refs_3_.refs_4_.refs_5_, ...), custom_call_target="tpu_custom_call" | custom-call | flops 1 | bytes 24000000 | tf_op jit(solution)/shard_map/cond/branch_1_fun/spread_back/pallas_call | solution.py:43
  226.0 5.4 %all_to_all.33 = bf16[2,1024,512]{2,1,0:T(8,128)(2,1)S(1)} all-to-all(bf16[2,1024,512]{2,1,0:T(8,128)(2,1)S(1)} %join_halves.3), channel_id=1, replica_groups={{0,4},{8,12},{16,20},{24,28},{1,5},{9,13},{17,21},{25,29},{2,6},{10,14}..., dimensions={0} | all-to-all | bytes 4194304 | tf_op jit(solution)/shard_map/cond/branch_1_fun/all_to_all | solution.py:483
  231.5 2.7 %bitcast_convert_fusion = f32[2048,512]{1,0:T(8,128)} fusion(bf16[2,1024,512]{2,1,0:T(8,128)(2,1)S(1)} %all_to_all.33), kind=kLoop, calls=%fused_computation.4 | loop fusion | flops 1048576 | bytes 6291456 | tf_op jit(solution)/shard_map/cond/branch_1_fun/convert_element_type | solution.py:558
  234.2 5.3 %spread_back.3 = (bf16[2048,512]{1,0:T(8,128)(2,1)}, bf16[2048,512]{1,0:T(8,128)(2,1)S(1)}) custom-call(s32[4]{0:T(128)S(1)} %pad_add_fusion.at, bf16[2048,2048]{1,0:T(8,128)(2,1)} %get-tuple-element.154.refs_0_.refs_1_, bf16[2048,2048]{1,0:T(8,128)(2,1)} %get-tuple-element.154.refs_0_.refs_1_, ...), custom_call_target="tpu_custom_call", output_to_operand_aliasing={{1}: (9, {})} | custom-call | flops 1 | bytes 24000000 | tf_op jit(solution)/shard_map/spread_back/pallas_call | solution.py:43
  (94 shorter events, 31.1 us)
Async XLA Ops:
  3.6 15.3 %collective-permute-start.2 = (bf16[272,512]{1,0:T(8,128)(2,1)S(1)}, bf16[272,512]{1,0:T(8,128)(2,1)S(1)}, u32[]{:S(2)}, u32[]{:S(2)}) collective-permute-start(bf16[272,512]{1,0:T(8,128)(2,1)S(1)} %weight_piece.1.bias_own), channel_id=1, source_target_pairs={{0,1},{1,0},{2,3},{3,2},{4,5},{5,4},{6,7},{7,6},{8,9},{9,8},{10,11... | collective-permute-start | bytes 835592 | tf_op jit(solution)/shard_map/ppermute | solution.py:475
  7.3 11.6 %copy-start.23 = (s32[256,256]{1,0:T(8,128)}, s32[256,256]{1,0:T(8,128)S(1)}, u32[]{:S(2)}) copy-start(s32[256,256]{1,0:T(8,128)S(1)} %reshape.36.packed_ref) | copy-start | bytes 786436
  19.0 39.9 %collective-permute-start.3 = (bf16[512,512]{1,0:T(8,128)(2,1)S(1)}, bf16[512,512]{1,0:T(8,128)(2,1)}, u32[]{:S(2)}, u32[]{:S(2)}) collective-permute-start(bf16[512,512]{1,0:T(8,128)(2,1)S(1)} %get-tuple-element.158), channel_id=1, source_target_pairs={{0,3},{1,2},{2,1},{3,0},{4,7},{5,6},{6,5},{7,4},{8,11},{9,10},{10,... | collective-permute-start | bytes 1572872 | tf_op jit(solution)/shard_map/ppermute | solution.py:475
  21.5 47.6 %collective-permute-start.5 = (bf16[2,512,512]{2,1,0:T(8,128)(2,1)}, bf16[2,512,512]{2,1,0:T(8,128)(2,1)}, u32[]{:S(2)}, u32[]{:S(2)}) collective-permute-start(bf16[2,512,512]{2,1,0:T(8,128)(2,1)} %get-tuple-element.161), channel_id=1, source_target_pairs={{0,1},{1,0},{2,3},{3,2},{4,5},{5,4},{6,7},{7,6},{8,9},{9,8},{10,11... | collective-permute-start | bytes 3145736 | tf_op jit(solution)/shard_map/ppermute | solution.py:475
  22.8 44.8 %collective-permute-start.7 = (bf16[512,512]{1,0:T(8,128)(2,1)}, bf16[512,512]{1,0:T(8,128)(2,1)}, u32[]{:S(2)}, u32[]{:S(2)}) collective-permute-start(bf16[512,512]{1,0:T(8,128)(2,1)} %get-tuple-element.165.part0), channel_id=1, source_target_pairs={{0,2},{1,3},{2,0},{3,1},{4,6},{5,7},{6,4},{7,5},{8,10},{9,11},{10,... | collective-permute-start | bytes 1572872 | tf_op jit(solution)/shard_map/ppermute | solution.py:475
  24.1 47.4 %copy-start.1 = (bf16[2048,512]{1,0:T(8,128)(2,1)S(1)}, bf16[2048,512]{1,0:T(8,128)(2,1)}, u32[]{:S(2)}) copy-start(bf16[2048,512]{1,0:T(8,128)(2,1)} %weight_own.7) | copy-start | bytes 6291460
  35.5 16.2 %all-to-all-start.4 = ((bf16[2,512,512]{2,1,0:T(8,128)(2,1)}), bf16[2,512,512]{2,1,0:T(8,128)(2,1)}, u32[]{:S(2)}, u32[]{:S(2)}) async-start(bf16[2,512,512]{2,1,0:T(8,128)(2,1)} %pad_maximum_fusion.1), calls=%async_computation.4 | async-start | bytes 2097152 | tf_op jit(solution)/shard_map/cond/branch_1_fun/all_to_all | solution.py:483
  58.8 12.7 %copy-start.10 = (bf16[2048,512]{1,0:T(8,128)(2,1)}, bf16[2048,512]{1,0:T(8,128)(2,1)S(1)}, u32[]{:S(2)}) copy-start(bf16[2048,512]{1,0:T(8,128)(2,1)S(1)} %get-tuple-element.168.weight_sib) | copy-start | bytes 6291460
  58.8 52.5 %collective-permute-start.4 = (bf16[2,512,512]{2,1,0:T(8,128)(2,1)}, bf16[2,512,512]{2,1,0:T(8,128)(2,1)S(1)}, u32[]{:S(2)}, u32[]{:S(2)}) collective-permute-start(bf16[2,512,512]{2,1,0:T(8,128)(2,1)} %get-tuple-element.159), channel_id=1, source_target_pairs={{0,1},{1,0},{2,3},{3,2},{4,5},{5,4},{6,7},{7,6},{8,9},{9,8},{10,11... | collective-permute-start | bytes 3145736 | tf_op jit(solution)/shard_map/ppermute | solution.py:475
  67.7 35.6 %collective-permute-start.8 = (bf16[512,512]{1,0:T(8,128)(2,1)}, bf16[512,512]{1,0:T(8,128)(2,1)S(1)}, u32[]{:S(2)}, u32[]{:S(2)}) collective-permute-start(bf16[512,512]{1,0:T(8,128)(2,1)} %get-tuple-element.166), channel_id=1, source_target_pairs={{0,3},{1,2},{2,1},{3,0},{4,7},{5,6},{6,5},{7,4},{8,11},{9,10},{10,... | collective-permute-start | bytes 1572872 | tf_op jit(solution)/shard_map/ppermute | solution.py:475
  69.1 45.6 %collective-permute-start.6 = (bf16[512,512]{1,0:T(8,128)(2,1)}, bf16[512,512]{1,0:T(8,128)(2,1)S(1)}, u32[]{:S(2)}, u32[]{:S(2)}) collective-permute-start(bf16[512,512]{1,0:T(8,128)(2,1)} %get-tuple-element.162.part0), channel_id=1, source_target_pairs={{0,2},{1,3},{2,0},{3,1},{4,6},{5,7},{6,4},{7,5},{8,10},{9,11},{10,... | collective-permute-start | bytes 1572872 | tf_op jit(solution)/shard_map/ppermute | solution.py:475
  71.6 6.7 %copy-start.9 = (bf16[2048,512]{1,0:T(8,128)(2,1)S(1)}, bf16[2048,512]{1,0:T(8,128)(2,1)}, u32[]{:S(2)}) copy-start(bf16[2048,512]{1,0:T(8,128)(2,1)} %cot_own.7) | copy-start | bytes 6291460
  71.6 6.7 %copy-start.11 = (bf16[2048,512]{1,0:T(8,128)(2,1)S(1)}, bf16[2048,512]{1,0:T(8,128)(2,1)}, u32[]{:S(2)}) copy-start(bf16[2048,512]{1,0:T(8,128)(2,1)} %copy-done.10) | copy-start | bytes 6291460
  78.3 36.4 %copy-start.22 = (f32[512,1]{1,0:T(8,128)S(1)}, f32[512,1]{1,0:T(8,128)}, u32[]{:S(2)}) copy-start(f32[512,1]{1,0:T(8,128)} %get-tuple-element.167.scale) | copy-start | bytes 6148
  103.2 16.9 %copy-start.20 = (bf16[512,512]{1,0:T(8,128)(2,1)}, bf16[512,512]{1,0:T(8,128)(2,1)S(1)}, u32[]{:S(2)}) copy-start(bf16[512,512]{1,0:T(8,128)(2,1)S(1)} %collective-permute-done.8.part3) | copy-start | bytes 1572868
  111.3 8.8 %copy-start.12 = (bf16[2,512,512]{2,1,0:T(8,128)(2,1)}, bf16[2,512,512]{2,1,0:T(8,128)(2,1)S(1)}, u32[]{:S(2)}) copy-start(bf16[2,512,512]{2,1,0:T(8,128)(2,1)S(1)} %collective-permute-done.4.near) | copy-start | bytes 3145732
  120.2 68.7 %collective-permute-start.9 = (bf16[2,768,512]{2,1,0:T(8,128)(2,1)}, bf16[2,768,512]{2,1,0:T(8,128)(2,1)}, u32[]{:S(2)}, u32[]{:S(2)}) collective-permute-start(bf16[2,768,512]{2,1,0:T(8,128)(2,1)} %get-tuple-element.185), channel_id=1, source_target_pairs={{0,1},{1,0},{2,3},{3,2},{4,5},{5,4},{6,7},{7,6},{8,9},{9,8},{10,11... | collective-permute-start | bytes 4718600 | tf_op jit(solution)/shard_map/ppermute | solution.py:475
  120.3 68.6 %collective-permute-start.11 = (bf16[512,512]{1,0:T(8,128)(2,1)}, bf16[512,512]{1,0:T(8,128)(2,1)}, u32[]{:S(2)}, u32[]{:S(2)}) collective-permute-start(bf16[512,512]{1,0:T(8,128)(2,1)} %get-tuple-element.189), channel_id=1, source_target_pairs={{0,3},{1,2},{2,1},{3,0},{4,7},{5,6},{6,5},{7,4},{8,11},{9,10},{10,... | collective-permute-start | bytes 1572872 | tf_op jit(solution)/shard_map/ppermute | solution.py:475
  123.0 65.9 %collective-permute-start.10 = (bf16[512,512]{1,0:T(8,128)(2,1)S(1)}, bf16[512,512]{1,0:T(8,128)(2,1)}, u32[]{:S(2)}, u32[]{:S(2)}) collective-permute-start(bf16[512,512]{1,0:T(8,128)(2,1)S(1)} %get-tuple-element.187), channel_id=1, source_target_pairs={{0,2},{1,3},{2,0},{3,1},{4,6},{5,7},{6,4},{7,5},{8,10},{9,11},{10,... | collective-permute-start | bytes 1572872 | tf_op jit(solution)/shard_map/ppermute | solution.py:475
  123.7 63.3 %collective-permute-start.12 = (bf16[256,512]{1,0:T(8,128)(2,1)}, bf16[256,512]{1,0:T(8,128)(2,1)}, u32[]{:S(2)}, u32[]{:S(2)}) collective-permute-start(bf16[256,512]{1,0:T(8,128)(2,1)} %get-tuple-element.190), channel_id=1, source_target_pairs={{0,2},{1,3},{2,0},{3,1},{4,6},{5,7},{6,4},{7,5},{8,10},{9,11},{10,... | collective-permute-start | bytes 786440 | tf_op jit(solution)/shard_map/ppermute | solution.py:475
  125.9 63.0 %collective-permute-start.13 = (bf16[256,512]{1,0:T(8,128)(2,1)}, bf16[256,512]{1,0:T(8,128)(2,1)}, u32[]{:S(2)}, u32[]{:S(2)}) collective-permute-start(bf16[256,512]{1,0:T(8,128)(2,1)} %get-tuple-element.191), channel_id=1, source_target_pairs={{0,3},{1,2},{2,1},{3,0},{4,7},{5,6},{6,5},{7,4},{8,11},{9,10},{10,... | collective-permute-start | bytes 786440 | tf_op jit(solution)/shard_map/ppermute | solution.py:475
  187.0 12.6 %copy-start.4 = (bf16[2,256,512]{2,1,0:T(8,128)(2,1)S(1)}, bf16[2,256,512]{2,1,0:T(8,128)(2,1)}, u32[]{:S(2)}) copy-start(bf16[2,256,512]{2,1,0:T(8,128)(2,1)} %copy-done.3) | copy-start | bytes 1572868
  187.0 12.7 %copy-start.8 = (bf16[256,512]{1,0:T(8,128)(2,1)S(1)}, bf16[256,512]{1,0:T(8,128)(2,1)}, u32[]{:S(2)}) copy-start(bf16[256,512]{1,0:T(8,128)(2,1)} %copy-done.7) | copy-start | bytes 786436
  187.0 12.8 %copy-start.6 = (bf16[256,512]{1,0:T(8,128)(2,1)S(1)}, bf16[256,512]{1,0:T(8,128)(2,1)}, u32[]{:S(2)}) copy-start(bf16[256,512]{1,0:T(8,128)(2,1)} %copy-done.5) | copy-start | bytes 786436
  187.0 17.1 %copy-start.15 = (bf16[768,512]{1,0:T(8,128)(2,1)S(1)}, bf16[768,512]{1,0:T(8,128)(2,1)}, u32[]{:S(2)}) copy-start(bf16[768,512]{1,0:T(8,128)(2,1)} %copy-done.14) | copy-start | bytes 2359300
  188.9 10.6 %collective-permute-start.14 = (bf16[272,512]{1,0:T(8,128)(2,1)S(1)}, bf16[272,512]{1,0:T(8,128)(2,1)S(1)}, u32[]{:S(2)}, u32[]{:S(2)}) collective-permute-start(bf16[272,512]{1,0:T(8,128)(2,1)S(1)} %get-tuple-element.192), channel_id=1, source_target_pairs={{0,1},{1,0},{2,3},{3,2},{4,5},{5,4},{6,7},{7,6},{8,9},{9,8},{10,11... | collective-permute-start | bytes 835592 | tf_op jit(solution)/shard_map/ppermute | solution.py:475
  199.6 34.6 %collective-permute-start.15 = (bf16[2,256,512]{2,1,0:T(8,128)(2,1)S(1)}, bf16[2,256,512]{2,1,0:T(8,128)(2,1)S(1)}, u32[]{:S(2)}, u32[]{:S(2)}) collective-permute-start(bf16[2,256,512]{2,1,0:T(8,128)(2,1)S(1)} %copy-done.4), channel_id=1, source_target_pairs={{0,1},{1,0},{2,3},{3,2},{4,5},{5,4},{6,7},{7,6},{8,9},{9,8},{10,11... | collective-permute-start | bytes 1572872 | tf_op jit(solution)/shard_map/ppermute | solution.py:475
  199.7 34.5 %collective-permute-start.16 = (bf16[256,512]{1,0:T(8,128)(2,1)S(1)}, bf16[256,512]{1,0:T(8,128)(2,1)S(1)}, u32[]{:S(2)}, u32[]{:S(2)}) collective-permute-start(bf16[256,512]{1,0:T(8,128)(2,1)S(1)} %copy-done.8), channel_id=1, source_target_pairs={{0,2},{1,3},{2,0},{3,1},{4,6},{5,7},{6,4},{7,5},{8,10},{9,11},{10,... | collective-permute-start | bytes 786440 | tf_op jit(solution)/shard_map/ppermute | solution.py:475
  199.8 34.4 %collective-permute-start.17 = (bf16[256,512]{1,0:T(8,128)(2,1)S(1)}, bf16[256,512]{1,0:T(8,128)(2,1)S(1)}, u32[]{:S(2)}, u32[]{:S(2)}) collective-permute-start(bf16[256,512]{1,0:T(8,128)(2,1)S(1)} %copy-done.6), channel_id=1, source_target_pairs={{0,3},{1,2},{2,1},{3,0},{4,7},{5,6},{6,5},{7,4},{8,11},{9,10},{10,... | collective-permute-start | bytes 786440 | tf_op jit(solution)/shard_map/ppermute | solution.py:475
  204.1 11.5 %copy-start.17 = (bf16[768,512]{1,0:T(8,128)(2,1)S(1)}, bf16[768,512]{1,0:T(8,128)(2,1)}, u32[]{:S(2)}) copy-start(bf16[768,512]{1,0:T(8,128)(2,1)} %get-tuple-element.91.mine) | copy-start | bytes 2359300 | tf_op jit(solution)/shard_map/cond
  205.2 8.1 %collective-permute-start = (bf16[256,512]{1,0:T(8,128)(2,1)S(1)}, bf16[256,512]{1,0:T(8,128)(2,1)S(1)}, u32[]{:S(2)}, u32[]{:S(2)}) collective-permute-start(bf16[256,512]{1,0:T(8,128)(2,1)S(1)} %get-tuple-element.83.mine), channel_id=1, source_target_pairs={{0,8},{4,20},{8,0},{12,28},{16,24},{20,4},{24,16},{28,12},{1,9},{5... | collective-permute-start | bytes 786440 | tf_op jit(solution)/shard_map/cond/branch_1_fun/ppermute | solution.py:486
  213.9 11.4 %collective-permute-start.1 = (bf16[512,512]{1,0:T(8,128)(2,1)S(1)}, bf16[512,512]{1,0:T(8,128)(2,1)S(1)}, u32[]{:S(2)}, u32[]{:S(2)}) collective-permute-start(bf16[512,512]{1,0:T(8,128)(2,1)S(1)} %bitcast.18), channel_id=1, source_target_pairs={{0,16},{4,12},{8,24},{12,4},{16,0},{20,28},{24,8},{28,20},{1,17},{... | collective-permute-start | bytes 1572872 | tf_op jit(solution)/shard_map/cond/branch_1_fun/ppermute | solution.py:486
  (13 other events, 39.5 us)

commit v4 on v3

--- a/solution.py
+++ b/solution.py
@@ -11,12 +11,12 @@
 F32 = jnp.float32
 UNITS = 8
 SLABS = ((0, 4), (4, 4))
-GROUPS = ((((0, 0), (0, 1)), ((1, 0),)), (((1, 1),),))
-PARTS = tuple(tuple(entry for run in group for entry in run) for group in GROUPS)
+RUNS = (((0, 0),), ((0, 1), (1, 0)), ((1, 1),))
 LANES = 128
 PAD = 16
-VMEM_LIMIT = 48 << 20
+VMEM_LIMIT = 32 << 20
 ANY = pl.BlockSpec(memory_space=pl.ANY)
+HBM = pl.BlockSpec(memory_space=pltpu.HBM)
 
 
 def like(*shape, dtype=BF16):
@@ -53,10 +53,17 @@
     )(*scalars, *operands)
 
 
-def piece_kernel(at, weight, bias, out):
+def piece_kernel(at, weight, bias, out, row, sems):
     rows = out.shape[0] - PAD
-    out[:rows, :] = weight[...]
-    out[rows:, :] = jnp.broadcast_to(bias[...].astype(F32).reshape(1, -1), (PAD, out.shape[1])).astype(BF16)
+    copies = [
+        pltpu.make_async_copy(weight.at[pl.ds(pl.multiple_of(at[3] * rows, 16), rows), :], out.at[:rows, :], sems.at[0]),
+        pltpu.make_async_copy(bias, row, sems.at[1]),
+    ]
+    for copy in copies:
+        copy.start()
+    for copy in copies:
+        copy.wait()
+    out[rows:, :] = jnp.broadcast_to(row[...].astype(F32).reshape(1, -1), (PAD, out.shape[1])).astype(BF16)
 
 
 def piece_call(at, weight, bias, rows):
@@ -67,7 +74,8 @@
         (at,),
         (weight, bias),
         [like(rows + PAD, width)],
-        in_specs=[pl.BlockSpec((rows, width), lambda i, s: (s[3], 0)), fixed(width)],
+        in_specs=[HBM, HBM],
+        scratch=[pltpu.VMEM((width,), BF16), pltpu.SemaphoreType.DMA((2,))],
     )[0]
 
 
@@ -77,15 +85,19 @@
     step = pl.program_id(0)
     steps = pl.num_programs(0)
     block = (step + at[1] * (steps // 2)) % steps
-    row = lax.broadcasted_iota(jnp.int32, (LANES, 8 * slots), 0)
-    owner = lax.broadcasted_iota(jnp.int32, (1, 8 * slots), 1) // slots
+    lanes = 8 * slots
+    row = lax.broadcasted_iota(jnp.int32, (LANES, lanes), 0).astype(F32).astype(BF16)
+    owner = lax.broadcasted_iota(jnp.int32, (1, lanes), 1) // slots
+    one, zero = jnp.ones((LANES, lanes), BF16), jnp.zeros((LANES, lanes), BF16)
+
+    def one_hot(index):
+        tile = jnp.broadcast_to(index.astype(F32), (16, lanes)).astype(BF16)
+        return jnp.where(jnp.concatenate([tile] * (LANES // 16), 0) == row, one, zero)
 
     def group(index):
         entry = packed_ref[index : index + 1, :]
-        high = (entry >> 7) * 8 + owner
-        low = entry & (LANES - 1)
-        left = jnp.where(high == row, 1.0, 0.0).astype(BF16)
-        right = jnp.where(low == row, 1.0, 0.0).astype(BF16)
+        left = one_hot((entry >> 7) * 8 + owner)
+        right = one_hot(entry & (LANES - 1))
         return lax.dot_general(left, right, (((1,), (1,)), ((), ())), preferred_element_type=F32)
 
     for pair in range(rows // 16):
@@ -99,9 +111,9 @@
     down = lax.broadcasted_iota(jnp.int32, (LANES, LANES), 0)
     across = lax.broadcasted_iota(jnp.int32, (LANES, LANES), 1)
     twice = jnp.where(down == across, 2.0, 0.0)
-    column = pl.multiple_of(base + block * rows, LANES)
-    tile_view = counts_ref[:, pl.ds(column, LANES)].astype(F32)
-    counts_ref[:, pl.ds(column, LANES)] = (tile_view + twice).astype(BF16)
+    for low in range(0, rows, LANES):
+        where = slice(low, low + LANES), pl.ds(pl.multiple_of(base + block * rows + low, LANES), LANES)
+        counts_ref[where] = (counts_ref[where].astype(F32) + twice).astype(BF16)
     total = jnp.dot(counts_ref[...], feat_ref[...], preferred_element_type=F32)
     result = (total * scale).astype(BF16)
 
@@ -120,7 +132,7 @@
 def count_call(at, packed, features, cotangent, base, size, counts):
     nodes, width = features.shape
     slots = packed.shape[1] // 8
-    rows = LANES
+    rows = 2 * LANES
     steps = size // rows
     half = steps // 2
 
@@ -208,7 +220,9 @@
             (back0, None, back2, back3)[code][...] = total
 
 
-def row_call(at, live, parts, scale, cotangent, weight_own, weight_sib, piece_own, piece_sib, entry, places, buffers):
+def row_call(
+    at, live, parts, scale, cotangent, weight_own, weight_sib, piece_own, piece_sib, entry, index, length, buffers
+):
     width = cotangent.shape[1]
     rows = cotangent.shape[0] // UNITS
     block, (low, high) = entry[1], units_of(entry)
@@ -228,15 +242,13 @@
         bias,
     ]
     shapes, outs, aliases = [], [], {}
-    for number, (double, (index, length)) in enumerate(
-        zip((False, True, False, True, False, False), (places[0],) * 4 + (places[1],) * 2)
-    ):
+    for number, double in enumerate((False, True, False, True, False, False)):
         if double:
             shapes.append(like(2, length * rows, width))
-            outs.append(pl.BlockSpec((2, rows, width), lambda i, s, c, index=index: (0, index, 0)))
+            outs.append(pl.BlockSpec((2, rows, width), lambda i, s, c: (0, index, 0)))
         else:
             shapes.append(like(length * rows, width))
-            outs.append(pl.BlockSpec((rows, width), lambda i, s, c, index=index: (index, 0)))
+            outs.append(pl.BlockSpec((rows, width), lambda i, s, c: (index, 0)))
         if index > 0:
             aliases[len(operands)] = number
             operands.append(buffers[number])
@@ -268,10 +280,10 @@
 
 def product_kernel(at, *refs):
     refs, terms = refs[:-1], refs[-1]
-    parts, grads = refs[: -len(GROUPS)], refs[-len(GROUPS) :]
-    unit = grads[0].shape[1] // len(PARTS[0])
+    parts, grads = refs[: -len(RUNS)], refs[-len(RUNS) :]
+    unit = grads[0].shape[1] // len(RUNS[0])
     runs = []
-    for group, entries in enumerate(PARTS):
+    for group, entries in enumerate(RUNS):
         for index, (slab, block) in enumerate(entries):
             runs.append((slab, slice(block * unit, (block + 1) * unit), group, slice(index * unit, (index + 1) * unit)))
     width = parts[0].shape[-1]
@@ -298,31 +310,40 @@
     return call(product_kernel, "weight_product", (at,), operands, [like(2, 2, 2 * width + PAD, width)])[0]
 
 
-def fold_kernel(at, came, out):
-    rows = out.shape[2] - PAD
+def pair_of(refs):
+    return [refs[0].at[0], refs[0].at[1]] if len(refs) == 1 else list(refs)
+
+
+def fold_kernel(stage, at, *refs):
+    first, second = pair_of(refs[:-2])
+    keep, give = refs[-2:]
+    rows = keep.shape[1] - PAD
+    bit = (at[3] >> stage) % 2
     for half in range(2):
-        sums = get_sums(came, (0, half)) + get_sums(came, (1, half))
-        for part in range(2):
-            low, high = part * rows, (part + 1) * rows
-            total = came[0, half, low:high, :].astype(F32) + came[1, half, low:high, :].astype(F32)
-            out[part, half, :rows, :] = total.astype(BF16)
-            put_sums(out, (part, half), sums)
-
-
-def fold_call(at, came):
-    length, width = came.shape[2:]
-    return call(fold_kernel, "fold_terms", (at,), (came,), [like(2, 2, (length - PAD) // 2 + PAD, width)])[0]
-
-
-def part_kernel(at, came, out):
+        sums = get_sums(first, (half,)) + get_sums(second, (half,))
+        for out, part in ((keep, bit), (give, 1 - bit)):
+            where = pl.ds(pl.multiple_of(part * rows, 16), rows)
+            out[half, :rows, :] = (first[half, where, :].astype(F32) + second[half, where, :].astype(F32)).astype(BF16)
+            put_sums(out, (half,), sums)
+
+
+def fold_call(at, stage, operands):
+    length, width = operands[0].shape[-2:]
+    shape = like(2, (length - PAD) // 2 + PAD, width)
+    return call(functools.partial(fold_kernel, stage), "fold_terms", (at,), operands, [shape, shape])
+
+
+def part_kernel(at, *refs):
+    first, second = pair_of(refs[:-1])
+    out = refs[-1]
     rows = out.shape[1] - PAD
     for half in range(2):
-        out[half, :rows, :] = (came[0, half, :rows, :].astype(F32) + came[1, half, :rows, :].astype(F32)).astype(BF16)
-        put_sums(out, (half,), get_sums(came, (0, half)) + get_sums(came, (1, half)))
-
-
-def part_call(at, came):
-    return call(part_kernel, "part_terms", (at,), (came,), [like(*came.shape[1:])])[0]
+        out[half, :rows, :] = (first[half, :rows, :].astype(F32) + second[half, :rows, :].astype(F32)).astype(BF16)
+        put_sums(out, (half,), get_sums(first, (half,)) + get_sums(second, (half,)))
+
+
+def part_call(at, operands):
+    return call(part_kernel, "part_terms", (at,), operands, [like(*operands[0].shape[-3:])])[0]
 
 
 def share_kernel(at, came, share, sums):
@@ -353,49 +374,49 @@
     )[0]
 
 
-def place_kernel(entries, at, mine, theirs, out):
-    rows = mine.shape[0] // len(entries)
-    for index, entry in enumerate(entries):
-        low, high = units_of(entry)
-        part = slice(index * rows, (index + 1) * rows)
-        own = low + at[1] * (high - low)
-        out[pl.ds(pl.multiple_of(own * rows, LANES), rows), :] = mine[part, :]
-        out[pl.ds(pl.multiple_of((low + high - own) * rows, LANES), rows), :] = theirs[0, part, :]
-
-
-def place_call(at, entries, mine, theirs):
-    rows, width = mine.shape
-    return call(
-        functools.partial(place_kernel, entries),
+def place_kernel(runs, at, *refs):
+    out = refs[-1]
+    for run, mine, theirs in zip(runs, refs[0:-1:2], refs[1:-1:2]):
+        rows = mine.shape[0] // len(run)
+        for index, entry in enumerate(run):
+            low, high = units_of(entry)
+            part = slice(index * rows, (index + 1) * rows)
+            own = low + at[1] * (high - low)
+            out[pl.ds(pl.multiple_of(own * rows, LANES), rows), :] = mine[part, :]
+            out[pl.ds(pl.multiple_of((low + high - own) * rows, LANES), rows), :] = theirs[0, part, :]
+
+
+def place_call(at, runs, pairs):
+    rows, width = pairs[0][0].shape
+    specs = [spec for mine, _ in pairs for spec in (fixed(*mine.shape), fixed(1, *mine.shape))]
+    return call(
+        functools.partial(place_kernel, runs),
         "place_rows",
         (at,),
-        (mine, theirs),
-        [like(rows // len(entries) * UNITS, width)],
-        in_specs=[fixed(rows, width), fixed(1, rows, width)],
+        [o for pair in pairs for o in pair],
+        [pltpu.HBM((rows // len(runs[0]) * UNITS, width), BF16)],
+        in_specs=specs,
         us=3,
     )[0]
 
 
-def spread_kernel(group, final, at, *refs):
-    entries = PARTS[group]
-    counts, refs = refs[: 2 * len(entries)], refs[2 * len(entries) :]
-    (level, near), refs = refs[:2], refs[2:]
-    fars, refs = refs[: 2 * len(GROUPS[group])], refs[2 * len(GROUPS[group]) :]
+def spread_kernel(runs, final, at, *refs):
+    units = 2 * sum(map(len, runs))
+    counts, backs, refs = refs[:units], refs[units : units + 4 * len(runs)], refs[units + 4 * len(runs) :]
     scaled = refs[-1]
-    rows = level.shape[0] // len(entries)
     step = pl.program_id(0)
 
     @pl.when(step == 0)
     def _():
-        index = 0
-        for run, entries in enumerate(GROUPS[group]):
-            far, cross = fars[2 * run : 2 * run + 2]
-            for number in range(len(entries)):
+        at_unit = 0
+        for number, run in enumerate(runs):
+            level, near, far, cross = backs[4 * number : 4 * number + 4]
+            rows = level.shape[0] // len(run)
+            for index in range(len(run)):
                 part = slice(index * rows, (index + 1) * rows)
-                there = slice(number * rows, (number + 1) * rows)
-                scaled[2 * index + at[1]] = (level[part, :].astype(F32) + far[there, :].astype(F32)).astype(BF16)
-                scaled[2 * index + 1 - at[1]] = (near[1, part, :].astype(F32) + cross[there, :].astype(F32)).astype(BF16)
-                index += 1
+                scaled[at_unit + at[1]] = (level[part, :].astype(F32) + far[part, :].astype(F32)).astype(BF16)
+                scaled[at_unit + 1 - at[1]] = (near[1, part, :].astype(F32) + cross[part, :].astype(F32)).astype(BF16)
+                at_unit += 2
 
     total = refs[0][...] if final else None
     for index, block in enumerate(counts):
@@ -404,7 +425,7 @@
     out = refs[3] if final else refs[0]
     out[...] = total.astype(out.dtype)
     if final:
-        mine, output = refs[1], refs[4]
+        mine, output, near = refs[1], refs[4], backs[1]
         half = pl.num_programs(0) // 2
 
         @pl.when(step // half == at[1])
@@ -416,26 +437,26 @@
             output[...] = near[0]
 
 
-def spread_call(at, group, counts, level, near, fars, *last):
+def spread_call(at, runs, counts, backs, *last):
     nodes = counts.shape[0]
-    rows, width = level.shape
+    width = backs[0].shape[1]
     tile = 512
     final = len(last) > 0
     unit_rows = nodes // UNITS
-    units = [unit for entry in PARTS[group] for unit in units_of(entry)]
+    units = [unit for run in runs for entry in run for unit in units_of(entry)]
     tiled = pl.BlockSpec((tile, width), lambda i, s: (i, 0))
-    operands = [counts] * len(units) + [level, near, *fars, *last]
+    operands = [counts] * len(units) + [*backs, *last]
     specs = [pl.BlockSpec((unit_rows, tile), lambda i, s, unit=unit: (unit, i)) for unit in units]
-    specs += [fixed(*o.shape) for o in (level, near, *fars)]
+    specs += [fixed(*o.shape) for o in backs]
     shapes, outs, aliases = [like(nodes, width, dtype=F32)], [tiled], {}
     if final:
         (low, high), steps = units, nodes // tile
-        specs += [tiled, fixed(rows, width), ANY]
-        shapes = [like(nodes, width), like(nodes, width)]
+        specs += [tiled, fixed(unit_rows, width), ANY]
+        shapes = [pltpu.HBM((nodes, width), BF16), pltpu.HBM((nodes, width), BF16)]
         outs.append(pl.BlockSpec((unit_rows, width), lambda i, s: (jnp.where(i < steps // 2, low, high), 0)))
         aliases = {len(operands) - 1: 1}
     return call(
-        functools.partial(spread_kernel, group, final),
+        functools.partial(spread_kernel, runs, final),
         "spread_back",
         (at,),
         operands,
@@ -485,20 +506,15 @@
     def along(value, stage):
         return lax.ppermute(value, "dp", [(i, i ^ (1 << orders[stage][i % 2])) for i in range(dp_count)])
 
-    def join_pieces(value):
+    def join_pieces(value, first):
         for stage in range(bits - 1):
             last = stage == bits - 2
-            value = join_call(at, stage, value, along(value, stage), 2 if last else 1)
+            came = along(value, stage)
+            if stage == 0:
+                came = tie(came, first)
+            value = join_call(at, stage, value, came, 2 if last else 1)
             value = value if last else value[0]
         return swap(value, bits - 1).reshape(-1, width)
-
-    def gather_pieces(value):
-        for stage in range(bits):
-            value = swap(value, stage)
-            value = value.reshape(-1, width)
-            if stage < bits - 1:
-                value = jnp.stack([value, value])
-        return value
 
     unit = nodes // UNITS
     packed = neighbour_lists.reshape(nodes // 8, 8 * slots)
@@ -519,7 +535,7 @@
 
     def last_rows(piece, counts):
         last = count_slab(SLABS[1], counts)
-        return gather_pieces(jnp.stack([piece[:piece_rows]] * 2)), last
+        return join_pieces(piece[:piece_rows], last[1]), last
 
     counts, *first = count_slab(SLABS[0], None)
     same, other, pack, scale = (tie(value, piece_sib) for value in first)
@@ -532,49 +548,46 @@
     scales.append(scale)
 
     sides = []
-    for group in GROUPS:
-        total, index, buffers, runs = sum(map(len, group)), 0, None, []
-        for run in group:
-            for number, entry in enumerate(run):
-                buffers = row_call(
-                    at, live, parts[entry[0]], scales[entry[0]], cotangent, weight, weight_sib, piece_own, piece_sib,
-                    entry, ((index, total), (number, len(run))), buffers,
-                )
-                index += 1
-            runs.append(buffers[4:])
-        sides.append((*buffers[:4], runs))
+    for run in RUNS:
+        buffers = None
+        for index, entry in enumerate(run):
+            buffers = row_call(
+                at, live, parts[entry[0]], scales[entry[0]], cotangent, weight, weight_sib, piece_own, piece_sib,
+                entry, index, len(run), buffers,
+            )
+        sides.append(buffers)
     grads = [side[1] for side in sides]
 
     def fold_terms(parts, grads):
-        came = swap(product_call(at, parts, grads), bits - 1)
+        pair = (swap(product_call(at, parts, grads), bits - 1),)
         for stage in range(bits - 2, -1, -1):
-            came = swap(fold_call(at, came), stage)
-        return part_call(at, came)
-
-    def share_terms(came, counts, back, out_own):
+            keep, give = fold_call(at, stage, pair)
+            pair = (keep, along(give, stage))
+        return part_call(at, pair)
+
+    def share_terms(came, counts, backs, outs):
         share, bias_grad = share_call(at, came)
-        partial = spread_call(at, 0, counts, *back)[0]
-        output = place_call(at, PARTS[0], out_own, back[1])
-        return join_pieces(share).astype(F32), bias_grad, partial, output
-
-    terms = always(fold_terms, parts, grads)
+        output = place_call(at, RUNS[:-1], [(out, back[1]) for out, back in zip(outs, backs)])
+        partial = spread_call(at, RUNS[:-1], counts, [o for back in backs for o in back])[0]
+        return join_pieces(share, output).astype(F32), bias_grad, partial, output
+
     backs = []
-    for index, (_, _, level, near, runs) in enumerate(sides):
+    for index, (_, _, level, near, far, cross) in enumerate(sides):
+        if index == 0:
+            far, cross, near = tie(far, parts[-1][2]), tie(cross, parts[-1][2]), tie(near, parts[-1][3])
         if index == 1:
+            terms = always(fold_terms, parts, [tie(grad, *backs[0][1:]) for grad in grads])
+            near = tie(near, *backs[0][1:], grads[-1])
+        if index == 2:
             mine = lax.dynamic_index_in_dim(terms, place % 2, 0, False)
-            theirs = tie(lax.dynamic_index_in_dim(terms, 1 - place % 2, 0, False), backs[0][1], *backs[0][2])
+            theirs = lax.dynamic_index_in_dim(terms, 1 - place % 2, 0, False)
+            theirs = tie(theirs, *backs[0][1:], *backs[1][1:])
             came = jnp.stack([mine, across(theirs, 1)])
-            near = tie(near, came)
-        fars = []
-        for number, (far, cross) in enumerate(runs):
-            if (index, number) == (0, 0):
-                far, cross = tie(far, parts[-1][2]), tie(cross, parts[-1][2])
-            if index == 1:
-                far, cross = tie(far, theirs), tie(cross, theirs)
-            fars += [across(far, 2), across(cross, 3)]
-        backs.append((level, across(near, 1), fars))
-    weight_grad, bias_grad, partial, output = always(share_terms, came, counts, backs[0], sides[0][0])
-    features_grad, output = spread_call(at, 1, counts, *backs[1], partial, sides[1][0], output)
+            near, far, cross = tie(near, came), tie(far, theirs), tie(cross, theirs)
+        backs.append((level, across(near, 1), across(far, 2), across(cross, 3)))
+    outs = [side[0] for side in sides]
+    weight_grad, bias_grad, partial, output = always(share_terms, came, counts, backs[:-1], outs[:-1])
+    features_grad, output = spread_call(at, RUNS[-1:], counts, backs[-1], partial, outs[-1], output)
     return (output, features_grad, weight_grad, bias_grad.reshape(width))
 
 

time: 242 us -> 230 us (0.950)
  blocking collectives: 58.4 us -> 18 us
  waiting for transfers between devices: 56.9 us -> 95.9 us
  Pallas kernels: 78.2 us -> 70.7 us
  other arithmetic: 5.7 us -> 0.85 us
    all_to_all x6 -> x3, blocking collectives: 58.4 us -> 18 us  [swap(): return lax.all_to_all(value, 'dp', 0, 0, axis_index_groups=pairs)]
    ppermute x2 -> x6, waiting for transfers between devices: 5.31 us -> 32 us  [along(): lax.ppermute(value, 'dp', [(i, i ^ 1 << orders[stage][i % 2]) for i in ra...]
    ppermute x16 -> x17, waiting for transfers between devices: 51.5 us -> 63.9 us  [across(): return lax.ppermute(value, 'mp', [(i, i ^ code) for i in range(mp_count)])]
    pallas_call x17 -> x19, Pallas kernels: 78.2 us -> 70.7 us  [call(): pl.pallas_call(kernel, grid_spec=pltpu.PrefetchScalarGridSpec(num_scalar_...]
    ppermute x2 -> x6, starting transfers between devices: 4.48 us -> 9.45 us  [along(): lax.ppermute(value, 'dp', [(i, i ^ 1 << orders[stage][i % 2]) for i in ra...]
    all_to_all x1 -> x0, starting transfers between devices: 4.41 us -> none  [swap(): return lax.all_to_all(value, 'dp', 0, 0, axis_index_groups=pairs)]
    another operation x3 -> x0, other arithmetic: 2.83 us -> none  [the longest x2 2.79 us: gather_pieces(): value = jnp.stack([value, value])]
    unnamed x49 -> x61, local copies, waits for them, and re-layouts: 6.22 us -> 3.7 us
  transfers between devices with their start and end apart: 19 -> 23, of which waited for: 7 -> 11; matrix products, arithmetic and copies ran while one was open for 3% -> 3% of each run, Pallas kernels for 28% -> 28%
where the time goes in v4:
time: 230 us; the launch traced here: 229 us
  waiting for transfers between devices  95.9 us (42%)
  Pallas kernels  70.7 us (31%)
  starting transfers between devices  34 us (15%)
  blocking collectives  18 us (8%)
  local copies, waits for them, and re-layouts  8.14 us (4%)
    pallas_call x19, Pallas kernels, call(): pl.pallas_call(kernel, grid_spec=pltpu.PrefetchScalarGridSpec(num_scalar_...  70.7 us
    ppermute x17, waiting for transfers between devices, across(): return lax.ppermute(value, 'mp', [(i, i ^ code) for i in range(mp_count)])  63.9 us
    ppermute x6, waiting for transfers between devices, along(): lax.ppermute(value, 'dp', [(i, i ^ 1 << orders[stage][i % 2]) for i in ra...  32 us
    ppermute x17, starting transfers between devices, across(): return lax.ppermute(value, 'mp', [(i, i ^ code) for i in range(mp_count)])  24.5 us
    all_to_all x3, blocking collectives, swap(): return lax.all_to_all(value, 'dp', 0, 0, axis_index_groups=pairs)  18 us
    ppermute x6, starting transfers between devices, along(): lax.ppermute(value, 'dp', [(i, i ^ 1 << orders[stage][i % 2]) for i in ra...  9.45 us
  transfers between devices with their start and end apart: 23, of which 11 were waited for; matrix products, arithmetic and copies ran while one was open for 3% of the time, Pallas kernels for 28%

profile of v4, /device:TPU:0, one launch (start us, length us, event | category | flops | bytes accessed | tf_op | source)
XLA Modules:
  0.0 229.3 jit_solution(3460977605807595642)
XLA Ops:
  3.6 3.1 %collective-permute-start.6 = (bf16[272,512]{1,0:T(8,128)(2,1)S(1)}, bf16[272,512]{1,0:T(8,128)(2,1)}, u32[]{:S(2)}, u32[]{:S(2)}) collective-permute-start(bf16[272,512]{1,0:T(8,128)(2,1)S(1)} %weight_piece.1.bias_own), channel_id=1, source_target_pairs={{0,1},{1,0},{2,3},{3,2},{4,5},{5,4},{6,7},{7,6},{8,9},{9,8},{10,11... | collective-permute-start | bytes 835592 | tf_op jit(solution)/shard_map/ppermute | solution.py:496
  9.6 9.5 %count_and_aggregate.3 = (bf16[2048,2048]{1,0:T(8,128)(2,1)S(1)}, bf16[512,512]{1,0:T(8,128)(2,1)}, bf16[512,512]{1,0:T(8,128)(2,1)S(1)}, bf16[2,512,512]{2,1,0:T(8,128)(2,1)}, f32[512,1]{1,0:T(8,128)S(1)}) custom-call(s32[4]{0:T(128)S(1)} %pad_add_fusion.at, s32[256,256]{1,0:T(8,128)S(1)} %reshape.28.packed_ref, bf16[2048,512]{1,0:T(8,128)(2,1)} %feat_ref.1, ...), custom_call_target="tpu_custom_call" | custom-call | flops 1 | bytes 1 | tf_op jit(solution)/shard_map/count_and_aggregate/pallas_call | solution.py:43
  19.4 3.8 %collective-permute-start.7 = (bf16[512,512]{1,0:T(8,128)(2,1)S(1)}, bf16[512,512]{1,0:T(8,128)(2,1)}, u32[]{:S(2)}, u32[]{:S(2)}) collective-permute-start(bf16[512,512]{1,0:T(8,128)(2,1)S(1)} %get-tuple-element.181), channel_id=1, source_target_pairs={{0,3},{1,2},{2,1},{3,0},{4,7},{5,6},{6,5},{7,4},{8,11},{9,10},{10,... | collective-permute-start | bytes 1572872 | tf_op jit(solution)/shard_map/ppermute | solution.py:496
  23.8 27.4 %conditional.3 = (bf16[2048,512]{1,0:T(8,128)(2,1)S(1)}, bf16[2048,2048]{1,0:T(8,128)(2,1)S(1)}, bf16[512,512]{1,0:T(8,128)(2,1)S(1)}, bf16[512,512]{1,0:T(8,128...) conditional(s32[]{:T(128)} %bitcast.10, () %tuple.54, (bf16[272,512]{1,0:T(8,128)(2,1)}, ...), branch_computations={%region_0.1_spmd, %region_1.2_spmd} | conditional | flops 3 | bytes 12585022 | solution.py:534
  27.1 8.1 %count_and_aggregate.2 = (bf16[2048,2048]{1,0:T(8,128)(2,1)S(1)}, bf16[512,512]{1,0:T(8,128)(2,1)S(1)}, bf16[512,512]{1,0:T(8,128)(2,1)S(1)}, bf16[2,512,512]{2,1,0:T(8,128)(2,1)}, f32[512,1]{1,0:T(8,128)S(1)}) custom-call(s32[4]{0:T(128)S(1)} %get-tuple-element.67.at, s32[256,256]{1,0:T(8,128)} %copy-done.22, ...), custom_call_target="tpu_custom_call", output_to_operand_aliasing={{0}: (4, {})} | custom-call | flops 1 | bytes 1 | tf_op jit(solution)/shard_map/cond/branch_1_fun/count_and_aggregate/pallas_call | solution.py:43
  37.4 7.7 %collective-permute-done.1.theirs = bf16[512,512]{1,0:T(8,128)(2,1)S(1)} collective-permute-done((bf16[512,512]{1,0:T(8,128)(2,1)S(1)}, bf16[512,512]{1,0:T(8,128)(2,1)S(1)}, u32[]{:S(2)}, u32[]{:S(2)}) %collective-permute-start.1) | collective-permute-done | bytes 524320 | tf_op jit(solution)/shard_map/cond/branch_1_fun/ppermute | solution.py:507
  45.8 5.4 %all_to_all.12 = bf16[2,1024,512]{2,1,0:T(8,128)(2,1)S(1)} all-to-all(bf16[2,1024,512]{2,1,0:T(8,128)(2,1)S(1)} %join_halves.5), channel_id=1, replica_groups={{0,4},{8,12},{16,20},{24,28},{1,5},{9,13},{17,21},{25,29},{2,6},{10,14}..., dimensions={0} | all-to-all | bytes 4194304 | tf_op jit(solution)/shard_map/cond/branch_1_fun/all_to_all | solution.py:504
  51.2 7.6 %collective-permute-done.7.part3 = bf16[512,512]{1,0:T(8,128)(2,1)} collective-permute-done((bf16[512,512]{1,0:T(8,128)(2,1)S(1)}, bf16[512,512]{1,0:T(8,128)(2,1)}, u32[]{:S(2)}, u32[]{:S(2)}) %collective-permute-start.7) | collective-permute-done | bytes 524320 | tf_op jit(solution)/shard_map/ppermute | solution.py:496
  58.8 7.0 %collective-permute-done.11.part2 = bf16[512,512]{1,0:T(8,128)(2,1)} collective-permute-done((bf16[512,512]{1,0:T(8,128)(2,1)}, bf16[512,512]{1,0:T(8,128)(2,1)}, u32[]{:S(2)}, u32[]{:S(2)}) %collective-permute-start.11) | collective-permute-done | bytes 524320 | tf_op jit(solution)/shard_map/ppermute | solution.py:496
  65.8 4.4 %collective-permute-start.12 = (bf16[512,512]{1,0:T(8,128)(2,1)S(1)}, bf16[512,512]{1,0:T(8,128)(2,1)S(1)}, u32[]{:S(2)}, u32[]{:S(2)}) collective-permute-start(bf16[512,512]{1,0:T(8,128)(2,1)S(1)} %get-tuple-element.189), channel_id=1, source_target_pairs={{0,3},{1,2},{2,1},{3,0},{4,7},{5,6},{6,5},{7,4},{8,11},{9,10},{10,... | collective-permute-start | bytes 1572872 | tf_op jit(solution)/shard_map/ppermute | solution.py:496
  70.2 1.8 collective-permute-start.10
  72.0 5.5 %linear_and_slope.5 = (bf16[256,512]{1,0:T(8,128)(2,1)}, bf16[2,256,512]{2,1,0:T(8,128)(2,1)}, bf16[256,512]{1,0:T(8,128)(2,1)}, bf16[2,256,512]{2,1,0:T(8,128)(...) custom-call(s32[4]{0:T(128)S(1)} %pad_add_fusion.at, s32[1]{0:T(128)S(6)} %copy.50.live, ...), custom_call_target="tpu_custom_call" | custom-call | flops 1 | bytes 1 | tf_op jit(solution)/shard_map/linear_and_slope/pallas_call | solution.py:43
  77.5 26.2 %collective-permute-done.12.part3 = bf16[512,512]{1,0:T(8,128)(2,1)S(1)} collective-permute-done((bf16[512,512]{1,0:T(8,128)(2,1)S(1)}, bf16[512,512]{1,0:T(8,128)(2,1)S(1)}, u32[]{:S(2)}, u32[]{:S(2)}) %collective-permute-start.12) | collective-permute-done | bytes 524320 | tf_op jit(solution)/shard_map/ppermute | solution.py:496
  103.7 11.0 %collective-permute-done.10.part2 = bf16[512,512]{1,0:T(8,128)(2,1)S(1)} collective-permute-done((bf16[512,512]{1,0:T(8,128)(2,1)S(1)}, bf16[512,512]{1,0:T(8,128)(2,1)S(1)}, u32[]{:S(2)}, u32[]{:S(2)}) %collective-permute-start.10) | collective-permute-done | bytes 524320 | tf_op jit(solution)/shard_map/ppermute | solution.py:496
  116.9 5.6 %linear_and_slope.6 = (bf16[512,512]{1,0:T(8,128)(2,1)S(1)}, bf16[2,512,512]{2,1,0:T(8,128)(2,1)S(1)}, bf16[512,512]{1,0:T(8,128)(2,1)S(1)}, bf16[2,512,512]{2,1...) custom-call(s32[4]{0:T(128)S(1)} %pad_add_fusion.at, s32[1]{0:T(128)S(6)} %copy.50.live, ...), custom_call_target="tpu_custom_call" | custom-call | flops 1 | bytes 1 | tf_op jit(solution)/shard_map/linear_and_slope/pallas_call | solution.py:43
  122.5 4.7 %linear_and_slope.4 = (bf16[256,512]{1,0:T(8,128)(2,1)S(1)}, bf16[2,256,512]{2,1,0:T(8,128)(2,1)}, bf16[256,512]{1,0:T(8,128)(2,1)S(1)}, bf16[2,256,512]{2,1,0:T...) custom-call(s32[4]{0:T(128)S(1)} %pad_add_fusion.at, s32[1]{0:T(128)S(6)} %copy.50.live, ...), custom_call_target="tpu_custom_call" | custom-call | flops 1 | bytes 1 | tf_op jit(solution)/shard_map/linear_and_slope/pallas_call | solution.py:43
  127.2 5.0 %linear_and_slope.7 = (bf16[512,512]{1,0:T(8,128)(2,1)S(1)}, bf16[2,512,512]{2,1,0:T(8,128)(2,1)S(1)}, bf16[512,512]{1,0:T(8,128)(2,1)S(1)}, bf16[2,512,512]{2,1...) custom-call(s32[4]{0:T(128)S(1)} %pad_add_fusion.at, ...), custom_call_target="tpu_custom_call", output_to_operand_aliasing={{0}: (12, {}), {1}: (13, {}), {2}: (14, {}), {3}: (15, {}),... | custom-call | flops 1 | bytes 1 | tf_op jit(solution)/shard_map/linear_and_slope/pallas_call | solution.py:43
  132.4 5.0 %collective-permute-done.14 = bf16[256,512]{1,0:T(8,128)(2,1)S(1)} collective-permute-done((bf16[256,512]{1,0:T(8,128)(2,1)S(1)}, bf16[256,512]{1,0:T(8,128)(2,1)S(1)}, u32[]{:S(2)}, u32[]{:S(2)}) %collective-permute-start.14) | collective-permute-done | bytes 262176 | tf_op jit(solution)/shard_map/ppermute | solution.py:496
  139.1 2.8 %collective-permute-start.18 = (bf16[512,512]{1,0:T(8,128)(2,1)}, bf16[512,512]{1,0:T(8,128)(2,1)}, u32[]{:S(2)}, u32[]{:S(2)}) collective-permute-start(bf16[512,512]{1,0:T(8,128)(2,1)} %get-tuple-element.217), channel_id=1, source_target_pairs={{0,3},{1,2},{2,1},{3,0},{4,7},{5,6},{6,5},{7,4},{8,11},{9,10},{10,... | collective-permute-start | bytes 1572872 | tf_op jit(solution)/shard_map/ppermute | solution.py:496
  141.9 43.5 %conditional.4 = (bf16[2,272,512]{2,1,0:T(8,128)(2,1)}) conditional(s32[]{:T(128)} %bitcast.10, () %tuple.63, (s32[4]{0:T(128)S(1)}, bf16[512,512]{1,0:T(8,128)(2,1)}, bf16[2,512,512]{2,1,0:T(8,128)(2,1)}, bf16[512,512]{1,0:T(8,128)(2,1)}, bf16[512,512]{1,0:T(8,128)(2,1)}, /*index=5*/bf16[512,512]{1,0:T(8,128)(2,1)}, bf16[2,512,512]{2,1,0:T(8,128)(2,1)}, ...), branch_computations={%region_2.3_spmd, %region_3.4_spmd} | conditional | flops 4 | bytes 15073372 | solution.py:534
  141.9 8.1 %weight_product.1 = bf16[2,2,1040,512]{3,2,1,0:T(8,128)(2,1)S(1)} custom-call(s32[4]{0:T(128)S(1)} %get-tuple-element.79.at, bf16[512,512]{1,0:T(8,128)(2,1)} %get-tuple-element.80.refs_0_, bf16[2,512,512]{2,1,0:T(8,128)(2,1)} %get-tuple-element.81.refs_1_, bf16[512,512]{1,0:T(8,128)(2,1)} %get-tuple-element.82.refs_2_, ...), custom_call_target="tpu_custom_call" | custom-call | flops 1 | bytes 1 | tf_op jit(solution)/shard_map/cond/branch_1_fun/weight_product/pallas_call | solution.py:43
  150.1 7.2 %all_to_all.13.refs_0_ = bf16[2,2,1040,512]{3,2,1,0:T(8,128)(2,1)S(1)} all-to-all(bf16[2,2,1040,512]{3,2,1,0:T(8,128)(2,1)S(1)} %weight_product.1), channel_id=1, replica_groups={{0,4},{8,12},{16,20},{24,28},{1,5},{9,13},{17,21},{25,29},{2,6},{10,14}..., dimensions={0} | all-to-all | bytes 8519680 | tf_op jit(solution)/shard_map/cond/branch_1_fun/all_to_all | solution.py:504
  159.9 13.6 %collective-permute-done.2.refs_1_ = bf16[2,528,512]{2,1,0:T(8,128)(2,1)S(1)} collective-permute-done((bf16[2,528,512]{2,1,0:T(8,128)(2,1)S(1)}, bf16[2,528,512]{2,1,0:T(8,128)(2,1)S(1)}, u32[]{:S(2)}, u32[]{:S(2)}) %collective-permute-start.2) | collective-permute-done | bytes 1081376 | tf_op jit(solution)/shard_map/cond/branch_1_fun/ppermute | solution.py:507
  175.9 8.0 %collective-permute-done.3.refs_1_ = bf16[2,272,512]{2,1,0:T(8,128)(2,1)S(1)} collective-permute-done((bf16[2,272,512]{2,1,0:T(8,128)(2,1)S(1)}, bf16[2,272,512]{2,1,0:T(8,128)(2,1)S(1)}, u32[]{:S(2)}, u32[]{:S(2)}) %collective-permute-start.3) | collective-permute-done | bytes 557088 | tf_op jit(solution)/shard_map/cond/branch_1_fun/ppermute | solution.py:507
  186.8 7.0 %collective-permute-done.19 = bf16[272,512]{1,0:T(8,128)(2,1)S(1)} collective-permute-done((bf16[272,512]{1,0:T(8,128)(2,1)S(1)}, bf16[272,512]{1,0:T(8,128)(2,1)S(1)}, u32[]{:S(2)}, u32[]{:S(2)}) %collective-permute-start.19) | collective-permute-done | bytes 278560 | tf_op jit(solution)/shard_map/ppermute | solution.py:496
  195.7 2.6 %collective-permute-start.22 = (bf16[256,512]{1,0:T(8,128)(2,1)S(1)}, bf16[256,512]{1,0:T(8,128)(2,1)S(1)}, u32[]{:S(2)}, u32[]{:S(2)}) collective-permute-start(bf16[256,512]{1,0:T(8,128)(2,1)S(1)} %copy-done.6), channel_id=1, source_target_pairs={{0,3},{1,2},{2,1},{3,0},{4,7},{5,6},{6,5},{7,4},{8,11},{9,10},{10,... | collective-permute-start | bytes 786440 | tf_op jit(solution)/shard_map/ppermute | solution.py:496
  198.3 25.1 %conditional.5 = (f32[2048,512]{1,0:T(8,128)S(1)}, f32[2048,512]{1,0:T(8,128)S(1)}, bf16[2048,512]{1,0:T(8,128)(2,1)}, f32[512]{0:T(512)}) conditional(s32[]{:T(128)} %bitcast.10, () %tuple.77, (s32[4]{0:T(128)S(1)}, bf16[2,272,512]{2,1,0:T(8,128)(2,1)S(1)}, bf16[256,512]{1,0:T(8,128)(2,1)}, bf16[2,256,512]{2,1,0:T(8,128)(2,1)S(1)}, ...), branch_computations={%region_4.5_spmd, %region_5.6_spmd} | conditional | flops 1048581 | bytes 52923144 | solution.py:534
  201.0 3.2 %place_rows.1 = bf16[2048,512]{1,0:T(8,128)(2,1)} custom-call(s32[4]{0:T(128)S(1)} %get-tuple-element.95.at, bf16[256,512]{1,0:T(8,128)(2,1)} %get-tuple-element.98.refs_0_, bf16[2,256,512]{2,1,0:T(8,128)(2,1)S(1)} %get-tuple-element.99.refs_1_.refs_7_, bf16[512,512]{1,0:T(8,128)(2,1)} %get-tuple-element.100.refs_2_, ...), custom_call_target="tpu_custom_call" | custom-call | flops 1 | bytes 9000000 | tf_op jit(solution)/shard_map/cond/branch_1_fun/place_rows/pallas_call | solution.py:43
  204.2 2.5 %collective-permute-done.4.theirs = bf16[256,512]{1,0:T(8,128)(2,1)S(1)} collective-permute-done((bf16[256,512]{1,0:T(8,128)(2,1)S(1)}, bf16[256,512]{1,0:T(8,128)(2,1)S(1)}, u32[]{:S(2)}, u32[]{:S(2)}) %collective-permute-start.4) | collective-permute-done | bytes 262176 | tf_op jit(solution)/shard_map/cond/branch_1_fun/ppermute | solution.py:507
  208.9 7.4 %spread_back.2 = f32[2048,512]{1,0:T(8,128)S(1)} custom-call(s32[4]{0:T(128)S(1)} %get-tuple-element.95.at, bf16[2048,2048]{1,0:T(8,128)(2,1)} %get-tuple-element.103.refs_0_.refs_1_.refs_2_.refs_3_.refs_4_.refs_5_, bf16[2048,2048]{1,0:T(8,128)(2,1)} %get-tuple-element.103.refs_0_.refs_1_.refs_2_.refs_3_.refs_4_.refs_5_, ...), custom_call_target="tpu_custom_call" | custom-call | flops 1 | bytes 24000000 | tf_op jit(solution)/shard_map/cond/branch_1_fun/spread_back/pallas_call | solution.py:43
  217.3 5.4 %all_to_all.14 = bf16[2,1024,512]{2,1,0:T(8,128)(2,1)S(1)} all-to-all(bf16[2,1024,512]{2,1,0:T(8,128)(2,1)S(1)} %join_halves.7), channel_id=1, replica_groups={{0,4},{8,12},{16,20},{24,28},{1,5},{9,13},{17,21},{25,29},{2,6},{10,14}..., dimensions={0} | all-to-all | bytes 4194304 | tf_op jit(solution)/shard_map/cond/branch_1_fun/all_to_all | solution.py:504
  223.5 5.9 %spread_back.3 = (bf16[2048,512]{1,0:T(8,128)(2,1)}, bf16[2048,512]{1,0:T(8,128)(2,1)}) custom-call(s32[4]{0:T(128)S(1)} %pad_add_fusion.at, bf16[2048,2048]{1,0:T(8,128)(2,1)} %copy-done.9, bf16[2048,2048]{1,0:T(8,128)(2,1)} %copy-done.9, bf16[256,512]{1,0:T(8,128)(2,1)S(1)} %get-tuple-element.192.refs_2_, ...), custom_call_target="tpu_custom_call", output_to_operand_aliasing={{1}: (9, {})} | custom-call | flops 1 | bytes 24000000 | tf_op jit(solution)/shard_map/spread_back/pallas_call | solution.py:43
  (114 shorter events, 32.5 us)
Async XLA Ops:
  3.6 15.5 %collective-permute-start.6 = (bf16[272,512]{1,0:T(8,128)(2,1)S(1)}, bf16[272,512]{1,0:T(8,128)(2,1)}, u32[]{:S(2)}, u32[]{:S(2)}) collective-permute-start(bf16[272,512]{1,0:T(8,128)(2,1)S(1)} %weight_piece.1.bias_own), channel_id=1, source_target_pairs={{0,1},{1,0},{2,3},{3,2},{4,5},{5,4},{6,7},{7,6},{8,9},{9,8},{10,11... | collective-permute-start | bytes 835592 | tf_op jit(solution)/shard_map/ppermute | solution.py:496
  9.6 14.2 %copy-start.11 = (bf16[2048,512]{1,0:T(8,128)(2,1)S(1)}, bf16[2048,512]{1,0:T(8,128)(2,1)}, u32[]{:S(2)}) copy-start(bf16[2048,512]{1,0:T(8,128)(2,1)} %cot_own.7) | copy-start | bytes 6291460
  9.6 14.2 %copy-start.15 = (bf16[2048,512]{1,0:T(8,128)(2,1)S(1)}, bf16[2048,512]{1,0:T(8,128)(2,1)}, u32[]{:S(2)}) copy-start(bf16[2048,512]{1,0:T(8,128)(2,1)} %feat_ref.1) | copy-start | bytes 6291460
  19.1 51.1 %collective-permute-start.9 = (bf16[2,512,512]{2,1,0:T(8,128)(2,1)}, bf16[2,512,512]{2,1,0:T(8,128)(2,1)}, u32[]{:S(2)}, u32[]{:S(2)}) collective-permute-start(bf16[2,512,512]{2,1,0:T(8,128)(2,1)} %get-tuple-element.184), channel_id=1, source_target_pairs={{0,1},{1,0},{2,3},{3,2},{4,5},{5,4},{6,7},{7,6},{8,9},{9,8},{10,11... | collective-permute-start | bytes 3145736 | tf_op jit(solution)/shard_map/ppermute | solution.py:496
  19.4 39.4 %collective-permute-start.7 = (bf16[512,512]{1,0:T(8,128)(2,1)S(1)}, bf16[512,512]{1,0:T(8,128)(2,1)}, u32[]{:S(2)}, u32[]{:S(2)}) collective-permute-start(bf16[512,512]{1,0:T(8,128)(2,1)S(1)} %get-tuple-element.181), channel_id=1, source_target_pairs={{0,3},{1,2},{2,1},{3,0},{4,7},{5,6},{6,5},{7,4},{8,11},{9,10},{10,... | collective-permute-start | bytes 1572872 | tf_op jit(solution)/shard_map/ppermute | solution.py:496
  23.2 42.6 %collective-permute-start.11 = (bf16[512,512]{1,0:T(8,128)(2,1)}, bf16[512,512]{1,0:T(8,128)(2,1)}, u32[]{:S(2)}, u32[]{:S(2)}) collective-permute-start(bf16[512,512]{1,0:T(8,128)(2,1)} %get-tuple-element.188.part0), channel_id=1, source_target_pairs={{0,2},{1,3},{2,0},{3,1},{4,6},{5,7},{6,4},{7,5},{8,10},{9,11},{10,... | collective-permute-start | bytes 1572872 | tf_op jit(solution)/shard_map/ppermute | solution.py:496
  23.8 48.2 %copy-start.1 = (bf16[2048,512]{1,0:T(8,128)(2,1)S(1)}, bf16[2048,512]{1,0:T(8,128)(2,1)}, u32[]{:S(2)}) copy-start(bf16[2048,512]{1,0:T(8,128)(2,1)} %weight_own.7) | copy-start | bytes 6291460
  25.5 9.7 %collective-permute-start = (bf16[256,512]{1,0:T(8,128)(2,1)S(1)}, bf16[256,512]{1,0:T(8,128)(2,1)S(1)}, u32[]{:S(2)}, u32[]{:S(2)}) collective-permute-start(bf16[256,512]{1,0:T(8,128)(2,1)S(1)} %slice.2.mine), channel_id=1, source_target_pairs={{0,8},{4,20},{8,0},{12,28},{16,24},{20,4},{24,16},{28,12},{1,9},{5... | collective-permute-start | bytes 786440 | tf_op jit(solution)/shard_map/cond/branch_1_fun/ppermute | solution.py:507
  35.8 9.2 %collective-permute-start.1 = (bf16[512,512]{1,0:T(8,128)(2,1)S(1)}, bf16[512,512]{1,0:T(8,128)(2,1)S(1)}, u32[]{:S(2)}, u32[]{:S(2)}) collective-permute-start(bf16[512,512]{1,0:T(8,128)(2,1)S(1)} %bitcast.17), channel_id=1, source_target_pairs={{0,16},{4,12},{8,24},{12,4},{16,0},{20,28},{24,8},{28,20},{1,17},{... | collective-permute-start | bytes 1572872 | tf_op jit(solution)/shard_map/cond/branch_1_fun/ppermute | solution.py:507
  51.2 26.3 %copy-start.9 = (bf16[2048,2048]{1,0:T(8,128)(2,1)}, bf16[2048,2048]{1,0:T(8,128)(2,1)S(1)}, u32[]{:S(2)}) copy-start(bf16[2048,2048]{1,0:T(8,128)(2,1)S(1)} %get-tuple-element.177.refs_0_.refs_1_) | copy-start | bytes 25165828
  51.2 76.0 %copy-start.14 = (bf16[512,512]{1,0:T(8,128)(2,1)}, bf16[512,512]{1,0:T(8,128)(2,1)S(1)}, u32[]{:S(2)}) copy-start(bf16[512,512]{1,0:T(8,128)(2,1)S(1)} %get-tuple-element.185.part0) | copy-start | bytes 1572868
  58.8 63.7 %collective-permute-start.8 = (bf16[2,512,512]{2,1,0:T(8,128)(2,1)}, bf16[2,512,512]{2,1,0:T(8,128)(2,1)S(1)}, u32[]{:S(2)}, u32[]{:S(2)}) collective-permute-start(bf16[2,512,512]{2,1,0:T(8,128)(2,1)} %get-tuple-element.182), channel_id=1, source_target_pairs={{0,1},{1,0},{2,3},{3,2},{4,5},{5,4},{6,7},{7,6},{8,9},{9,8},{10,11... | collective-permute-start | bytes 3145736 | tf_op jit(solution)/shard_map/ppermute | solution.py:496
  65.8 37.9 %collective-permute-start.12 = (bf16[512,512]{1,0:T(8,128)(2,1)S(1)}, bf16[512,512]{1,0:T(8,128)(2,1)S(1)}, u32[]{:S(2)}, u32[]{:S(2)}) collective-permute-start(bf16[512,512]{1,0:T(8,128)(2,1)S(1)} %get-tuple-element.189), channel_id=1, source_target_pairs={{0,3},{1,2},{2,1},{3,0},{4,7},{5,6},{6,5},{7,4},{8,11},{9,10},{10,... | collective-permute-start | bytes 1572872 | tf_op jit(solution)/shard_map/ppermute | solution.py:496
  70.2 44.5 %collective-permute-start.10 = (bf16[512,512]{1,0:T(8,128)(2,1)S(1)}, bf16[512,512]{1,0:T(8,128)(2,1)S(1)}, u32[]{:S(2)}, u32[]{:S(2)}) collective-permute-start(bf16[512,512]{1,0:T(8,128)(2,1)S(1)} %get-tuple-element.185.part0), channel_id=1, source_target_pairs={{0,2},{1,3},{2,0},{3,1},{4,6},{5,7},{6,4},{7,5},{8,10},{9,11},{10,... | collective-permute-start | bytes 1572872 | tf_op jit(solution)/shard_map/ppermute | solution.py:496
  72.0 44.9 %copy-start.12 = (bf16[2048,512]{1,0:T(8,128)(2,1)S(1)}, bf16[2048,512]{1,0:T(8,128)(2,1)}, u32[]{:S(2)}) copy-start(bf16[2048,512]{1,0:T(8,128)(2,1)} %cot_own.7) | copy-start | bytes 6291460
  103.7 23.5 %copy-start.16 = (bf16[512,512]{1,0:T(8,128)(2,1)}, bf16[512,512]{1,0:T(8,128)(2,1)S(1)}, u32[]{:S(2)}) copy-start(bf16[512,512]{1,0:T(8,128)(2,1)S(1)} %collective-permute-done.12.part3) | copy-start | bytes 1572868
  103.7 28.7 %collective-permute-start.13 = (bf16[2,256,512]{2,1,0:T(8,128)(2,1)S(1)}, bf16[2,256,512]{2,1,0:T(8,128)(2,1)S(1)}, u32[]{:S(2)}, u32[]{:S(2)}) collective-permute-start(bf16[2,256,512]{2,1,0:T(8,128)(2,1)S(1)} %get-tuple-element.198), channel_id=1, source_target_pairs={{0,1},{1,0},{2,3},{3,2},{4,5},{5,4},{6,7},{7,6},{8,9},{9,8},{10,11... | collective-permute-start | bytes 1572872 | tf_op jit(solution)/shard_map/ppermute | solution.py:496
  114.7 17.6 %collective-permute-start.15 = (bf16[256,512]{1,0:T(8,128)(2,1)S(1)}, bf16[256,512]{1,0:T(8,128)(2,1)S(1)}, u32[]{:S(2)}, u32[]{:S(2)}) collective-permute-start(bf16[256,512]{1,0:T(8,128)(2,1)S(1)} %get-tuple-element.202), channel_id=1, source_target_pairs={{0,3},{1,2},{2,1},{3,0},{4,7},{5,6},{6,5},{7,4},{8,11},{9,10},{10,... | collective-permute-start | bytes 786440 | tf_op jit(solution)/shard_map/ppermute | solution.py:496
  116.0 21.4 %collective-permute-start.14 = (bf16[256,512]{1,0:T(8,128)(2,1)S(1)}, bf16[256,512]{1,0:T(8,128)(2,1)S(1)}, u32[]{:S(2)}, u32[]{:S(2)}) collective-permute-start(bf16[256,512]{1,0:T(8,128)(2,1)S(1)} %get-tuple-element.200), channel_id=1, source_target_pairs={{0,2},{1,3},{2,0},{3,1},{4,6},{5,7},{6,4},{7,5},{8,10},{9,11},{10,... | collective-permute-start | bytes 786440 | tf_op jit(solution)/shard_map/ppermute | solution.py:496
  137.4 49.3 %collective-permute-start.16 = (bf16[2,512,512]{2,1,0:T(8,128)(2,1)}, bf16[2,512,512]{2,1,0:T(8,128)(2,1)S(1)}, u32[]{:S(2)}, u32[]{:S(2)}) collective-permute-start(bf16[2,512,512]{2,1,0:T(8,128)(2,1)} %get-tuple-element.215), channel_id=1, source_target_pairs={{0,1},{1,0},{2,3},{3,2},{4,5},{5,4},{6,7},{7,6},{8,9},{9,8},{10,11... | collective-permute-start | bytes 3145736 | tf_op jit(solution)/shard_map/ppermute | solution.py:496
  137.4 49.2 %collective-permute-start.17 = (bf16[512,512]{1,0:T(8,128)(2,1)S(1)}, bf16[512,512]{1,0:T(8,128)(2,1)}, u32[]{:S(2)}, u32[]{:S(2)}) collective-permute-start(bf16[512,512]{1,0:T(8,128)(2,1)S(1)} %get-tuple-element.216), channel_id=1, source_target_pairs={{0,2},{1,3},{2,0},{3,1},{4,6},{5,7},{6,4},{7,5},{8,10},{9,11},{10,... | collective-permute-start | bytes 1572872 | tf_op jit(solution)/shard_map/ppermute | solution.py:496
  139.1 47.5 %collective-permute-start.18 = (bf16[512,512]{1,0:T(8,128)(2,1)}, bf16[512,512]{1,0:T(8,128)(2,1)}, u32[]{:S(2)}, u32[]{:S(2)}) collective-permute-start(bf16[512,512]{1,0:T(8,128)(2,1)} %get-tuple-element.217), channel_id=1, source_target_pairs={{0,3},{1,2},{2,1},{3,0},{4,7},{5,6},{6,5},{7,4},{8,11},{9,10},{10,... | collective-permute-start | bytes 1572872 | tf_op jit(solution)/shard_map/ppermute | solution.py:496
  141.9 56.4 %copy-start.28 = (bf16[256,512]{1,0:T(8,128)(2,1)S(1)}, bf16[256,512]{1,0:T(8,128)(2,1)}, u32[]{:S(2)}) copy-start(bf16[256,512]{1,0:T(8,128)(2,1)} %get-tuple-element.226) | copy-start | bytes 786436
  158.3 15.2 %collective-permute-start.2 = (bf16[2,528,512]{2,1,0:T(8,128)(2,1)S(1)}, bf16[2,528,512]{2,1,0:T(8,128)(2,1)S(1)}, u32[]{:S(2)}, u32[]{:S(2)}) collective-permute-start(bf16[2,528,512]{2,1,0:T(8,128)(2,1)S(1)} %get-tuple-element.92), channel_id=1, source_target_pairs={{0,16},{4,12},{8,24},{12,4},{16,0},{20,28},{24,8},{28,20},{1,17},{... | collective-permute-start | bytes 3244040 | tf_op jit(solution)/shard_map/cond/branch_1_fun/ppermute | solution.py:507
  174.3 9.6 %collective-permute-start.3 = (bf16[2,272,512]{2,1,0:T(8,128)(2,1)S(1)}, bf16[2,272,512]{2,1,0:T(8,128)(2,1)S(1)}, u32[]{:S(2)}, u32[]{:S(2)}) collective-permute-start(bf16[2,272,512]{2,1,0:T(8,128)(2,1)S(1)} %get-tuple-element.94), channel_id=1, source_target_pairs={{0,8},{4,20},{8,0},{12,28},{16,24},{20,4},{24,16},{28,12},{1,9},{5... | collective-permute-start | bytes 1671176 | tf_op jit(solution)/shard_map/cond/branch_1_fun/ppermute | solution.py:507
  185.4 12.9 %copy-start.24 = (bf16[2,256,512]{2,1,0:T(8,128)(2,1)S(1)}, bf16[2,256,512]{2,1,0:T(8,128)(2,1)}, u32[]{:S(2)}) copy-start(bf16[2,256,512]{2,1,0:T(8,128)(2,1)} %copy-done.23) | copy-start | bytes 1572868
  186.7 7.1 %collective-permute-start.19 = (bf16[272,512]{1,0:T(8,128)(2,1)S(1)}, bf16[272,512]{1,0:T(8,128)(2,1)S(1)}, u32[]{:S(2)}, u32[]{:S(2)}) collective-permute-start(bf16[272,512]{1,0:T(8,128)(2,1)S(1)} %get-tuple-element.218), channel_id=1, source_target_pairs={{0,1},{1,0},{2,3},{3,2},{4,5},{5,4},{6,7},{7,6},{8,9},{9,8},{10,11... | collective-permute-start | bytes 835592 | tf_op jit(solution)/shard_map/ppermute | solution.py:496
  193.8 29.6 %collective-permute-start.20 = (bf16[2,256,512]{2,1,0:T(8,128)(2,1)S(1)}, bf16[2,256,512]{2,1,0:T(8,128)(2,1)S(1)}, u32[]{:S(2)}, u32[]{:S(2)}) collective-permute-start(bf16[2,256,512]{2,1,0:T(8,128)(2,1)S(1)} %copy-done.4), channel_id=1, source_target_pairs={{0,1},{1,0},{2,3},{3,2},{4,5},{5,4},{6,7},{7,6},{8,9},{9,8},{10,11... | collective-permute-start | bytes 1572872 | tf_op jit(solution)/shard_map/ppermute | solution.py:496
  194.2 29.2 %collective-permute-start.21 = (bf16[256,512]{1,0:T(8,128)(2,1)S(1)}, bf16[256,512]{1,0:T(8,128)(2,1)S(1)}, u32[]{:S(2)}, u32[]{:S(2)}) collective-permute-start(bf16[256,512]{1,0:T(8,128)(2,1)S(1)} %copy-done.8), channel_id=1, source_target_pairs={{0,2},{1,3},{2,0},{3,1},{4,6},{5,7},{6,4},{7,5},{8,10},{9,11},{10,... | collective-permute-start | bytes 786440 | tf_op jit(solution)/shard_map/ppermute | solution.py:496
  195.7 27.8 %collective-permute-start.22 = (bf16[256,512]{1,0:T(8,128)(2,1)S(1)}, bf16[256,512]{1,0:T(8,128)(2,1)S(1)}, u32[]{:S(2)}, u32[]{:S(2)}) collective-permute-start(bf16[256,512]{1,0:T(8,128)(2,1)S(1)} %copy-done.6), channel_id=1, source_target_pairs={{0,3},{1,2},{2,1},{3,0},{4,7},{5,6},{6,5},{7,4},{8,11},{9,10},{10,... | collective-permute-start | bytes 786440 | tf_op jit(solution)/shard_map/ppermute | solution.py:496
  199.5 7.2 %collective-permute-start.4 = (bf16[256,512]{1,0:T(8,128)(2,1)S(1)}, bf16[256,512]{1,0:T(8,128)(2,1)S(1)}, u32[]{:S(2)}, u32[]{:S(2)}) collective-permute-start(bf16[256,512]{1,0:T(8,128)(2,1)S(1)} %get-tuple-element.97.mine), channel_id=1, source_target_pairs={{0,8},{4,20},{8,0},{12,28},{16,24},{20,4},{24,16},{28,12},{1,9},{5... | collective-permute-start | bytes 786440 | tf_op jit(solution)/shard_map/cond/branch_1_fun/ppermute | solution.py:507
  207.3 9.2 %collective-permute-start.5 = (bf16[512,512]{1,0:T(8,128)(2,1)S(1)}, bf16[512,512]{1,0:T(8,128)(2,1)S(1)}, u32[]{:S(2)}, u32[]{:S(2)}) collective-permute-start(bf16[512,512]{1,0:T(8,128)(2,1)S(1)} %bitcast.15), channel_id=1, source_target_pairs={{0,16},{4,12},{8,24},{12,4},{16,0},{20,28},{24,8},{28,20},{1,17},{... | collective-permute-start | bytes 1572872 | tf_op jit(solution)/shard_map/cond/branch_1_fun/ppermute | solution.py:507
  (25 other events, 163.9 us)

commit v5 on v4

--- a/solution.py
+++ b/solution.py
@@ -72,7 +72,7 @@
         piece_kernel,
         "weight_piece",
         (at,),
-        (weight, bias),
+        [pltpu.with_memory_space_constraint(value, pltpu.HBM) for value in (weight, bias)],
         [like(rows + PAD, width)],
         in_specs=[HBM, HBM],
         scratch=[pltpu.VMEM((width,), BF16), pltpu.SemaphoreType.DMA((2,))],
@@ -334,28 +334,28 @@
 
 
 def part_kernel(at, *refs):
-    first, second = pair_of(refs[:-1])
-    out = refs[-1]
-    rows = out.shape[1] - PAD
-    for half in range(2):
-        out[half, :rows, :] = (first[half, :rows, :].astype(F32) + second[half, :rows, :].astype(F32)).astype(BF16)
-        put_sums(out, (half,), get_sums(first, (half,)) + get_sums(second, (half,)))
+    first, second = pair_of(refs[:-2])
+    rows = refs[-1].shape[1] - PAD
+    for out, half in ((refs[-2], at[1]), (refs[-1], 1 - at[1])):
+        out[0, :rows, :] = (first[half, :rows, :].astype(F32) + second[half, :rows, :].astype(F32)).astype(BF16)
+        put_sums(out, (0,), get_sums(first, (half,)) + get_sums(second, (half,)))
 
 
 def part_call(at, operands):
-    return call(part_kernel, "part_terms", (at,), operands, [like(*operands[0].shape[-3:])])[0]
-
-
-def share_kernel(at, came, share, sums):
+    length, width = operands[0].shape[-2:]
+    return call(part_kernel, "part_terms", (at,), operands, [like(1, length, width)] * 2)
+
+
+def share_kernel(at, mine, theirs, share, sums):
     rows = share.shape[0]
-    share[...] = (came[0, :rows, :].astype(F32) + came[1, :rows, :].astype(F32)).astype(BF16)
-    sums[...] = get_sums(came, (0,)) + get_sums(came, (1,))
-
-
-def share_call(at, came):
-    two, length, width = came.shape
-    return call(
-        share_kernel, "share_terms", (at,), (came,), [like(length - PAD, width), like(1, width, dtype=F32)]
+    share[...] = (mine[0, :rows, :].astype(F32) + theirs[0, :rows, :].astype(F32)).astype(BF16)
+    sums[...] = get_sums(mine, (0,)) + get_sums(theirs, (0,))
+
+
+def share_call(at, mine, theirs):
+    one, length, width = mine.shape
+    return call(
+        share_kernel, "share_terms", (at,), (mine, theirs), [like(length - PAD, width), like(1, width, dtype=F32)]
     )
 
 
@@ -440,7 +440,7 @@
 def spread_call(at, runs, counts, backs, *last):
     nodes = counts.shape[0]
     width = backs[0].shape[1]
-    tile = 512
+    tile = 1024
     final = len(last) > 0
     unit_rows = nodes // UNITS
     units = [unit for run in runs for entry in run for unit in units_of(entry)]
@@ -565,8 +565,8 @@
             pair = (keep, along(give, stage))
         return part_call(at, pair)
 
-    def share_terms(came, counts, backs, outs):
-        share, bias_grad = share_call(at, came)
+    def share_terms(mine, theirs, counts, backs, outs):
+        share, bias_grad = share_call(at, mine, theirs)
         output = place_call(at, RUNS[:-1], [(out, back[1]) for out, back in zip(outs, backs)])
         partial = spread_call(at, RUNS[:-1], counts, [o for back in backs for o in back])[0]
         return join_pieces(share, output).astype(F32), bias_grad, partial, output
@@ -574,19 +574,18 @@
     backs = []
     for index, (_, _, level, near, far, cross) in enumerate(sides):
         if index == 0:
-            far, cross, near = tie(far, parts[-1][2]), tie(cross, parts[-1][2]), tie(near, parts[-1][3])
+            far, cross, near = tie(far, parts[-1][2]), tie(cross, parts[-1][3]), tie(near, parts[-1][2])
         if index == 1:
             terms = always(fold_terms, parts, [tie(grad, *backs[0][1:]) for grad in grads])
             near = tie(near, *backs[0][1:], grads[-1])
         if index == 2:
-            mine = lax.dynamic_index_in_dim(terms, place % 2, 0, False)
-            theirs = lax.dynamic_index_in_dim(terms, 1 - place % 2, 0, False)
+            mine, theirs = terms
             theirs = tie(theirs, *backs[0][1:], *backs[1][1:])
-            came = jnp.stack([mine, across(theirs, 1)])
+            came = across(theirs, 1)
             near, far, cross = tie(near, came), tie(far, theirs), tie(cross, theirs)
         backs.append((level, across(near, 1), across(far, 2), across(cross, 3)))
     outs = [side[0] for side in sides]
-    weight_grad, bias_grad, partial, output = always(share_terms, came, counts, backs[:-1], outs[:-1])
+    weight_grad, bias_grad, partial, output = always(share_terms, mine, came, counts, backs[:-1], outs[:-1])
     features_grad, output = spread_call(at, RUNS[-1:], counts, backs[-1], partial, outs[-1], output)
     return (output, features_grad, weight_grad, bias_grad.reshape(width))
 

time: 230 us -> 224 us (0.974)
  waiting for transfers between devices: 95.9 us -> 88.4 us
  starting transfers between devices: 34 us -> 40.9 us
  local copies, waits for them, and re-layouts: 8.14 us -> 2.43 us
    ppermute x17, waiting for transfers between devices: 63.9 us -> 56.7 us  [across(): return lax.ppermute(value, 'mp', [(i, i ^ code) for i in range(mp_count)])]
    ppermute x17, starting transfers between devices: 24.5 us -> 31.5 us  [across(): return lax.ppermute(value, 'mp', [(i, i ^ code) for i in range(mp_count)])]
    unnamed x61 -> x37, local copies, waits for them, and re-layouts: 3.7 us -> 0.41 us
  transfers between devices with their start and end apart: 23 -> 23, of which waited for: 11 -> 11; matrix products, arithmetic and copies ran while one was open for 3% -> 1% of each run, Pallas kernels for 28% -> 29%
where the time goes in v5:
time: 224 us; the launch traced here: 223 us
  waiting for transfers between devices  88.4 us (39%)
  Pallas kernels  71.3 us (32%)
  starting transfers between devices  40.9 us (18%)
  blocking collectives  18 us (8%)
  local copies, waits for them, and re-layouts  2.43 us (1%)
    pallas_call x19, Pallas kernels, call(): pl.pallas_call(kernel, grid_spec=pltpu.PrefetchScalarGridSpec(num_scalar_...  71.3 us
    ppermute x17, waiting for transfers between devices, across(): return lax.ppermute(value, 'mp', [(i, i ^ code) for i in range(mp_count)])  56.7 us
    ppermute x6, waiting for transfers between devices, along(): lax.ppermute(value, 'dp', [(i, i ^ 1 << orders[stage][i % 2]) for i in ra...  31.7 us
    ppermute x17, starting transfers between devices, across(): return lax.ppermute(value, 'mp', [(i, i ^ code) for i in range(mp_count)])  31.5 us
    all_to_all x3, blocking collectives, swap(): return lax.all_to_all(value, 'dp', 0, 0, axis_index_groups=pairs)  18 us
    ppermute x6, starting transfers between devices, along(): lax.ppermute(value, 'dp', [(i, i ^ 1 << orders[stage][i % 2]) for i in ra...  9.35 us
  transfers between devices with their start and end apart: 23, of which 11 were waited for; matrix products, arithmetic and copies ran while one was open for 1% of the time, Pallas kernels for 29%

profile of v5, /device:TPU:0, one launch (start us, length us, event | category | flops | bytes accessed | tf_op | source)
XLA Modules:
  0.0 223.5 jit_solution(11210410057974900189)
XLA Ops:
  2.3 3.1 %collective-permute-start.6 = (bf16[272,512]{1,0:T(8,128)(2,1)S(1)}, bf16[272,512]{1,0:T(8,128)(2,1)}, u32[]{:S(2)}, u32[]{:S(2)}) collective-permute-start(bf16[272,512]{1,0:T(8,128)(2,1)S(1)} %weight_piece.1.bias_own), channel_id=1, source_target_pairs={{0,1},{1,0},{2,3},{3,2},{4,5},{5,4},{6,7},{7,6},{8,9},{9,8},{10,11... | collective-permute-start | bytes 835592 | tf_op jit(solution)/shard_map/ppermute | solution.py:496
  6.1 9.7 %count_and_aggregate.3 = (bf16[2048,2048]{1,0:T(8,128)(2,1)S(1)}, bf16[512,512]{1,0:T(8,128)(2,1)}, bf16[512,512]{1,0:T(8,128)(2,1)S(1)}, bf16[2,512,512]{2,1,0:T(8,128)(2,1)}, f32[512,1]{1,0:T(8,128)S(1)}) custom-call(s32[4]{0:T(128)S(1)} %pad_add_fusion.at, s32[256,256]{1,0:T(8,128)S(1)} %reshape.28.packed_ref, bf16[2048,512]{1,0:T(8,128)(2,1)} %feat_ref.1, ...), custom_call_target="tpu_custom_call" | custom-call | flops 1 | bytes 1 | tf_op jit(solution)/shard_map/count_and_aggregate/pallas_call | solution.py:43
  15.7 4.0 %collective-permute-start.7 = (bf16[512,512]{1,0:T(8,128)(2,1)S(1)}, bf16[512,512]{1,0:T(8,128)(2,1)}, u32[]{:S(2)}, u32[]{:S(2)}) collective-permute-start(bf16[512,512]{1,0:T(8,128)(2,1)S(1)} %get-tuple-element.183), channel_id=1, source_target_pairs={{0,3},{1,2},{2,1},{3,0},{4,7},{5,6},{6,5},{7,4},{8,11},{9,10},{10,... | collective-permute-start | bytes 1572872 | tf_op jit(solution)/shard_map/ppermute | solution.py:496
  20.5 27.4 %conditional.3 = (bf16[2048,512]{1,0:T(8,128)(2,1)S(1)}, bf16[2048,2048]{1,0:T(8,128)(2,1)S(1)}, bf16[512,512]{1,0:T(8,128)(2,1)S(1)}, bf16[512,512]{1,0:T(8,128...) conditional(s32[]{:T(128)} %bitcast.10, () %tuple.55, (bf16[272,512]{1,0:T(8,128)(2,1)}, ...), branch_computations={%region_0.1_spmd, %region_1.2_spmd} | conditional | flops 3 | bytes 12585022 | solution.py:534
  23.7 8.1 %count_and_aggregate.2 = (bf16[2048,2048]{1,0:T(8,128)(2,1)S(1)}, bf16[512,512]{1,0:T(8,128)(2,1)S(1)}, bf16[512,512]{1,0:T(8,128)(2,1)S(1)}, bf16[2,512,512]{2,1,0:T(8,128)(2,1)}, f32[512,1]{1,0:T(8,128)S(1)}) custom-call(s32[4]{0:T(128)S(1)} %get-tuple-element.66.at, s32[256,256]{1,0:T(8,128)} %copy-done.12, ...), custom_call_target="tpu_custom_call", output_to_operand_aliasing={{0}: (4, {})} | custom-call | flops 1 | bytes 1 | tf_op jit(solution)/shard_map/cond/branch_1_fun/count_and_aggregate/pallas_call | solution.py:43
  34.0 7.7 %collective-permute-done.1.theirs = bf16[512,512]{1,0:T(8,128)(2,1)S(1)} collective-permute-done((bf16[512,512]{1,0:T(8,128)(2,1)S(1)}, bf16[512,512]{1,0:T(8,128)(2,1)S(1)}, u32[]{:S(2)}, u32[]{:S(2)}) %collective-permute-start.1) | collective-permute-done | bytes 524320 | tf_op jit(solution)/shard_map/cond/branch_1_fun/ppermute | solution.py:507
  42.4 5.4 %all_to_all.12 = bf16[2,1024,512]{2,1,0:T(8,128)(2,1)S(1)} all-to-all(bf16[2,1024,512]{2,1,0:T(8,128)(2,1)S(1)} %join_halves.5), channel_id=1, replica_groups={{0,4},{8,12},{16,20},{24,28},{1,5},{9,13},{17,21},{25,29},{2,6},{10,14}..., dimensions={0} | all-to-all | bytes 4194304 | tf_op jit(solution)/shard_map/cond/branch_1_fun/all_to_all | solution.py:504
  47.9 7.5 %collective-permute-done.7.part3 = bf16[512,512]{1,0:T(8,128)(2,1)} collective-permute-done((bf16[512,512]{1,0:T(8,128)(2,1)S(1)}, bf16[512,512]{1,0:T(8,128)(2,1)}, u32[]{:S(2)}, u32[]{:S(2)}) %collective-permute-start.7) | collective-permute-done | bytes 524320 | tf_op jit(solution)/shard_map/ppermute | solution.py:496
  55.4 9.2 %collective-permute-done.9.near = bf16[2,512,512]{2,1,0:T(8,128)(2,1)} collective-permute-done((bf16[2,512,512]{2,1,0:T(8,128)(2,1)}, bf16[2,512,512]{2,1,0:T(8,128)(2,1)}, u32[]{:S(2)}, u32[]{:S(2)}) %collective-permute-start.9) | collective-permute-done | bytes 1048608 | tf_op jit(solution)/shard_map/ppermute | solution.py:496
  64.8 7.9 %collective-permute-start.12 = (bf16[512,512]{1,0:T(8,128)(2,1)S(1)}, bf16[512,512]{1,0:T(8,128)(2,1)S(1)}, u32[]{:S(2)}, u32[]{:S(2)}) collective-permute-start(bf16[512,512]{1,0:T(8,128)(2,1)S(1)} %get-tuple-element.191), channel_id=1, source_target_pairs={{0,3},{1,2},{2,1},{3,0},{4,7},{5,6},{6,5},{7,4},{8,11},{9,10},{10,... | collective-permute-start | bytes 1572872 | tf_op jit(solution)/shard_map/ppermute | solution.py:496
  72.7 5.5 %linear_and_slope.5 = (bf16[256,512]{1,0:T(8,128)(2,1)}, bf16[2,256,512]{2,1,0:T(8,128)(2,1)}, bf16[256,512]{1,0:T(8,128)(2,1)}, bf16[2,256,512]{2,1,0:T(8,128)(...) custom-call(s32[4]{0:T(128)S(1)} %pad_add_fusion.at, s32[1]{0:T(128)S(6)} %copy.52.live, ...), custom_call_target="tpu_custom_call" | custom-call | flops 1 | bytes 1 | tf_op jit(solution)/shard_map/linear_and_slope/pallas_call | solution.py:43
  78.2 17.6 %collective-permute-done.10.part2 = bf16[512,512]{1,0:T(8,128)(2,1)S(1)} collective-permute-done((bf16[512,512]{1,0:T(8,128)(2,1)S(1)}, bf16[512,512]{1,0:T(8,128)(2,1)S(1)}, u32[]{:S(2)}, u32[]{:S(2)}) %collective-permute-start.10) | collective-permute-done | bytes 524320 | tf_op jit(solution)/shard_map/ppermute | solution.py:496
  95.8 5.1 %collective-permute-start.13 = (bf16[2,256,512]{2,1,0:T(8,128)(2,1)S(1)}, bf16[2,256,512]{2,1,0:T(8,128)(2,1)S(1)}, u32[]{:S(2)}, u32[]{:S(2)}) collective-permute-start(bf16[2,256,512]{2,1,0:T(8,128)(2,1)S(1)} %get-tuple-element.200), channel_id=1, source_target_pairs={{0,1},{1,0},{2,3},{3,2},{4,5},{5,4},{6,7},{7,6},{8,9},{9,8},{10,11... | collective-permute-start | bytes 1572872 | tf_op jit(solution)/shard_map/ppermute | solution.py:496
  100.9 10.7 %collective-permute-done.12.part3 = bf16[512,512]{1,0:T(8,128)(2,1)S(1)} collective-permute-done((bf16[512,512]{1,0:T(8,128)(2,1)S(1)}, bf16[512,512]{1,0:T(8,128)(2,1)S(1)}, u32[]{:S(2)}, u32[]{:S(2)}) %collective-permute-start.12) | collective-permute-done | bytes 524320 | tf_op jit(solution)/shard_map/ppermute | solution.py:496
  113.6 5.6 %linear_and_slope.6 = (bf16[512,512]{1,0:T(8,128)(2,1)S(1)}, bf16[2,512,512]{2,1,0:T(8,128)(2,1)S(1)}, bf16[512,512]{1,0:T(8,128)(2,1)S(1)}, bf16[2,512,512]{2,1...) custom-call(s32[4]{0:T(128)S(1)} %pad_add_fusion.at, s32[1]{0:T(128)S(6)} %copy.52.live, ...), custom_call_target="tpu_custom_call" | custom-call | flops 1 | bytes 1 | tf_op jit(solution)/shard_map/linear_and_slope/pallas_call | solution.py:43
  119.2 4.7 %linear_and_slope.4 = (bf16[256,512]{1,0:T(8,128)(2,1)S(1)}, bf16[2,256,512]{2,1,0:T(8,128)(2,1)}, bf16[256,512]{1,0:T(8,128)(2,1)S(1)}, bf16[2,256,512]{2,1,0:T...) custom-call(s32[4]{0:T(128)S(1)} %pad_add_fusion.at, s32[1]{0:T(128)S(6)} %copy.52.live, ...), custom_call_target="tpu_custom_call" | custom-call | flops 1 | bytes 1 | tf_op jit(solution)/shard_map/linear_and_slope/pallas_call | solution.py:43
  124.0 5.0 %linear_and_slope.7 = (bf16[512,512]{1,0:T(8,128)(2,1)S(1)}, bf16[2,512,512]{2,1,0:T(8,128)(2,1)S(1)}, bf16[512,512]{1,0:T(8,128)(2,1)S(1)}, bf16[2,512,512]{2,1...) custom-call(s32[4]{0:T(128)S(1)} %pad_add_fusion.at, ...), custom_call_target="tpu_custom_call", output_to_operand_aliasing={{0}: (12, {}), {1}: (13, {}), {2}: (14, {}), {3}: (15, {}),... | custom-call | flops 1 | bytes 1 | tf_op jit(solution)/shard_map/linear_and_slope/pallas_call | solution.py:43
  129.0 4.5 %collective-permute-done.14 = bf16[256,512]{1,0:T(8,128)(2,1)S(1)} collective-permute-done((bf16[256,512]{1,0:T(8,128)(2,1)S(1)}, bf16[256,512]{1,0:T(8,128)(2,1)S(1)}, u32[]{:S(2)}, u32[]{:S(2)}) %collective-permute-start.14) | collective-permute-done | bytes 262176 | tf_op jit(solution)/shard_map/ppermute | solution.py:496
  133.6 2.6 %collective-permute-start.17 = (bf16[512,512]{1,0:T(8,128)(2,1)S(1)}, bf16[512,512]{1,0:T(8,128)(2,1)}, u32[]{:S(2)}, u32[]{:S(2)}) collective-permute-start(bf16[512,512]{1,0:T(8,128)(2,1)S(1)} %get-tuple-element.219), channel_id=1, source_target_pairs={{0,2},{1,3},{2,0},{3,1},{4,6},{5,7},{6,4},{7,5},{8,10},{9,11},{10,... | collective-permute-start | bytes 1572872 | tf_op jit(solution)/shard_map/ppermute | solution.py:496
  138.0 42.4 %conditional.4 = ((bf16[1,272,512]{2,1,0:T(8,128)(2,1)}, bf16[1,272,512]{2,1,0:T(8,128)(2,1)})) conditional(s32[]{:T(128)} %bitcast.10, () %tuple.64, (s32[4]{0:T(128)S(1)}, bf16[512,512]{1,0:T(8,128)(2,1)}, bf16[2,512,512]{2,1,0:T(8,128)(2,1)}, bf16[512,512]{1,0:T(8,128)(2,1)}, bf16[512,512]{1,0:T(8,128)(2,1)}, ...), branch_computations={%region_2.3_spmd, %region_3.4_spmd} | conditional | flops 4 | bytes 15073372 | solution.py:534
  138.0 7.1 %weight_product.1 = bf16[2,2,1040,512]{3,2,1,0:T(8,128)(2,1)S(1)} custom-call(s32[4]{0:T(128)S(1)} %get-tuple-element.78.at, bf16[512,512]{1,0:T(8,128)(2,1)} %get-tuple-element.79.refs_0_, bf16[2,512,512]{2,1,0:T(8,128)(2,1)} %get-tuple-element.80.refs_1_, bf16[512,512]{1,0:T(8,128)(2,1)} %get-tuple-element.81.refs_2_, ...), custom_call_target="tpu_custom_call" | custom-call | flops 1 | bytes 1 | tf_op jit(solution)/shard_map/cond/branch_1_fun/weight_product/pallas_call | solution.py:43
  145.1 7.2 %all_to_all.13.refs_0_ = bf16[2,2,1040,512]{3,2,1,0:T(8,128)(2,1)S(1)} all-to-all(bf16[2,2,1040,512]{3,2,1,0:T(8,128)(2,1)S(1)} %weight_product.1), channel_id=1, replica_groups={{0,4},{8,12},{16,20},{24,28},{1,5},{9,13},{17,21},{25,29},{2,6},{10,14}..., dimensions={0} | all-to-all | bytes 8519680 | tf_op jit(solution)/shard_map/cond/branch_1_fun/all_to_all | solution.py:504
  154.9 13.6 %collective-permute-done.2.refs_1_ = bf16[2,528,512]{2,1,0:T(8,128)(2,1)S(1)} collective-permute-done((bf16[2,528,512]{2,1,0:T(8,128)(2,1)S(1)}, bf16[2,528,512]{2,1,0:T(8,128)(2,1)S(1)}, u32[]{:S(2)}, u32[]{:S(2)}) %collective-permute-start.2) | collective-permute-done | bytes 1081376 | tf_op jit(solution)/shard_map/cond/branch_1_fun/ppermute | solution.py:507
  170.9 8.0 %collective-permute-done.3.refs_1_ = bf16[2,272,512]{2,1,0:T(8,128)(2,1)S(1)} collective-permute-done((bf16[2,272,512]{2,1,0:T(8,128)(2,1)S(1)}, bf16[2,272,512]{2,1,0:T(8,128)(2,1)S(1)}, u32[]{:S(2)}, u32[]{:S(2)}) %collective-permute-start.3) | collective-permute-done | bytes 557088 | tf_op jit(solution)/shard_map/cond/branch_1_fun/ppermute | solution.py:507
  180.7 7.2 %collective-permute-done.19 = bf16[1,272,512]{2,1,0:T(8,128)(2,1)S(1)} collective-permute-done((bf16[1,272,512]{2,1,0:T(8,128)(2,1)}, bf16[1,272,512]{2,1,0:T(8,128)(2,1)S(1)}, u32[]{:S(2)}, u32[]{:S(2)}) %collective-permute-start.19) | collective-permute-done | bytes 278560 | tf_op jit(solution)/shard_map/ppermute | solution.py:496
  188.2 2.3 %collective-permute-start.21 = (bf16[256,512]{1,0:T(8,128)(2,1)S(1)}, bf16[256,512]{1,0:T(8,128)(2,1)S(1)}, u32[]{:S(2)}, u32[]{:S(2)}) collective-permute-start(bf16[256,512]{1,0:T(8,128)(2,1)S(1)} %copy-done.6), channel_id=1, source_target_pairs={{0,2},{1,3},{2,0},{3,1},{4,6},{5,7},{6,4},{7,5},{8,10},{9,11},{10,... | collective-permute-start | bytes 786440 | tf_op jit(solution)/shard_map/ppermute | solution.py:496
  192.3 25.8 %conditional.5 = (f32[2048,512]{1,0:T(8,128)S(1)}, f32[2048,512]{1,0:T(8,128)S(1)}, bf16[2048,512]{1,0:T(8,128)(2,1)}, f32[512]{0:T(512)}) conditional(s32[]{:T(128)} %bitcast.10, () %tuple.78, (s32[4]{0:T(128)S(1)}, bf16[1,272,512]{2,1,0:T(8,128)(2,1)}, bf16[1,272,512]{2,1,0:T(8,128)(2,1)S(1)}, bf16[256,512]{1,0:T(8,128)(2,1)}, ...), branch_computations={%region_4.5_spmd, %region_5.6_spmd} | conditional | flops 1048581 | bytes 53971776 | solution.py:534
  195.9 3.3 %place_rows.1 = bf16[2048,512]{1,0:T(8,128)(2,1)} custom-call(s32[4]{0:T(128)S(1)} %get-tuple-element.94.at, bf16[256,512]{1,0:T(8,128)(2,1)} %get-tuple-element.98.refs_0_, bf16[2,256,512]{2,1,0:T(8,128)(2,1)} %get-tuple-element.99.refs_1_.refs_7_, bf16[512,512]{1,0:T(8,128)(2,1)} %get-tuple-element.100.refs_2_, ...), custom_call_target="tpu_custom_call" | custom-call | flops 1 | bytes 9000000 | tf_op jit(solution)/shard_map/cond/branch_1_fun/place_rows/pallas_call | solution.py:43
  199.2 2.2 collective-permute-done.4.theirs
  203.6 7.4 %spread_back.2 = f32[2048,512]{1,0:T(8,128)S(1)} custom-call(s32[4]{0:T(128)S(1)} %get-tuple-element.94.at, bf16[2048,2048]{1,0:T(8,128)(2,1)} %get-tuple-element.103.refs_0_.refs_1_.refs_2_.refs_3_.refs_4_.refs_5_, bf16[2048,2048]{1,0:T(8,128)(2,1)} %get-tuple-element.103.refs_0_.refs_1_.refs_2_.refs_3_.refs_4_.refs_5_, ...), custom_call_target="tpu_custom_call" | custom-call | flops 1 | bytes 24000000 | tf_op jit(solution)/shard_map/cond/branch_1_fun/spread_back/pallas_call | solution.py:43
  212.0 5.4 %all_to_all.14 = bf16[2,1024,512]{2,1,0:T(8,128)(2,1)S(1)} all-to-all(bf16[2,1024,512]{2,1,0:T(8,128)(2,1)S(1)} %join_halves.7), channel_id=1, replica_groups={{0,4},{8,12},{16,20},{24,28},{1,5},{9,13},{17,21},{25,29},{2,6},{10,14}..., dimensions={0} | all-to-all | bytes 4194304 | tf_op jit(solution)/shard_map/cond/branch_1_fun/all_to_all | solution.py:504
  218.2 5.3 %spread_back.3 = (bf16[2048,512]{1,0:T(8,128)(2,1)}, bf16[2048,512]{1,0:T(8,128)(2,1)}) custom-call(s32[4]{0:T(128)S(1)} %pad_add_fusion.at, bf16[2048,2048]{1,0:T(8,128)(2,1)} %copy-done.7, bf16[2048,2048]{1,0:T(8,128)(2,1)} %copy-done.7, bf16[256,512]{1,0:T(8,128)(2,1)S(1)} %get-tuple-element.194.refs_2_, ...), custom_call_target="tpu_custom_call", output_to_operand_aliasing={{1}: (9, {})} | custom-call | flops 1 | bytes 24000000 | tf_op jit(solution)/shard_map/spread_back/pallas_call | solution.py:43
  (92 shorter events, 28.9 us)
Async XLA Ops:
  2.3 13.4 %collective-permute-start.6 = (bf16[272,512]{1,0:T(8,128)(2,1)S(1)}, bf16[272,512]{1,0:T(8,128)(2,1)}, u32[]{:S(2)}, u32[]{:S(2)}) collective-permute-start(bf16[272,512]{1,0:T(8,128)(2,1)S(1)} %weight_piece.1.bias_own), channel_id=1, source_target_pairs={{0,1},{1,0},{2,3},{3,2},{4,5},{5,4},{6,7},{7,6},{8,9},{9,8},{10,11... | collective-permute-start | bytes 835592 | tf_op jit(solution)/shard_map/ppermute | solution.py:496
  6.0 14.4 %copy-start.8 = (bf16[2048,512]{1,0:T(8,128)(2,1)S(1)}, bf16[2048,512]{1,0:T(8,128)(2,1)}, u32[]{:S(2)}) copy-start(bf16[2048,512]{1,0:T(8,128)(2,1)} %cot_own.7) | copy-start | bytes 6291460
  6.1 14.4 %copy-start.10 = (bf16[2048,512]{1,0:T(8,128)(2,1)S(1)}, bf16[2048,512]{1,0:T(8,128)(2,1)}, u32[]{:S(2)}) copy-start(bf16[2048,512]{1,0:T(8,128)(2,1)} %feat_ref.1) | copy-start | bytes 6291460
  15.7 48.9 %collective-permute-start.9 = (bf16[2,512,512]{2,1,0:T(8,128)(2,1)}, bf16[2,512,512]{2,1,0:T(8,128)(2,1)}, u32[]{:S(2)}, u32[]{:S(2)}) collective-permute-start(bf16[2,512,512]{2,1,0:T(8,128)(2,1)} %get-tuple-element.186), channel_id=1, source_target_pairs={{0,1},{1,0},{2,3},{3,2},{4,5},{5,4},{6,7},{7,6},{8,9},{9,8},{10,11... | collective-permute-start | bytes 3145736 | tf_op jit(solution)/shard_map/ppermute | solution.py:496
  15.7 39.6 %collective-permute-start.7 = (bf16[512,512]{1,0:T(8,128)(2,1)S(1)}, bf16[512,512]{1,0:T(8,128)(2,1)}, u32[]{:S(2)}, u32[]{:S(2)}) collective-permute-start(bf16[512,512]{1,0:T(8,128)(2,1)S(1)} %get-tuple-element.183), channel_id=1, source_target_pairs={{0,3},{1,2},{2,1},{3,0},{4,7},{5,6},{6,5},{7,4},{8,11},{9,10},{10,... | collective-permute-start | bytes 1572872 | tf_op jit(solution)/shard_map/ppermute | solution.py:496
  19.8 45.0 %collective-permute-start.11 = (bf16[512,512]{1,0:T(8,128)(2,1)}, bf16[512,512]{1,0:T(8,128)(2,1)}, u32[]{:S(2)}, u32[]{:S(2)}) collective-permute-start(bf16[512,512]{1,0:T(8,128)(2,1)} %get-tuple-element.190.part0), channel_id=1, source_target_pairs={{0,2},{1,3},{2,0},{3,1},{4,6},{5,7},{6,4},{7,5},{8,10},{9,11},{10,... | collective-permute-start | bytes 1572872 | tf_op jit(solution)/shard_map/ppermute | solution.py:496
  20.5 52.2 %copy-start = (bf16[2048,512]{1,0:T(8,128)(2,1)S(1)}, bf16[2048,512]{1,0:T(8,128)(2,1)}, u32[]{:S(2)}) copy-start(bf16[2048,512]{1,0:T(8,128)(2,1)} %weight_own.7) | copy-start | bytes 6291460
  22.2 9.7 %collective-permute-start = (bf16[256,512]{1,0:T(8,128)(2,1)S(1)}, bf16[256,512]{1,0:T(8,128)(2,1)S(1)}, u32[]{:S(2)}, u32[]{:S(2)}) collective-permute-start(bf16[256,512]{1,0:T(8,128)(2,1)S(1)} %slice.2.mine), channel_id=1, source_target_pairs={{0,8},{4,20},{8,0},{12,28},{16,24},{20,4},{24,16},{28,12},{1,9},{5... | collective-permute-start | bytes 786440 | tf_op jit(solution)/shard_map/cond/branch_1_fun/ppermute | solution.py:507
  32.5 9.2 %collective-permute-start.1 = (bf16[512,512]{1,0:T(8,128)(2,1)S(1)}, bf16[512,512]{1,0:T(8,128)(2,1)S(1)}, u32[]{:S(2)}, u32[]{:S(2)}) collective-permute-start(bf16[512,512]{1,0:T(8,128)(2,1)S(1)} %bitcast.14), channel_id=1, source_target_pairs={{0,16},{4,12},{8,24},{12,4},{16,0},{20,28},{24,8},{28,20},{1,17},{... | collective-permute-start | bytes 1572872 | tf_op jit(solution)/shard_map/cond/branch_1_fun/ppermute | solution.py:507
  47.9 30.4 %copy-start.7 = (bf16[2048,2048]{1,0:T(8,128)(2,1)}, bf16[2048,2048]{1,0:T(8,128)(2,1)S(1)}, u32[]{:S(2)}) copy-start(bf16[2048,2048]{1,0:T(8,128)(2,1)S(1)} %get-tuple-element.179.refs_0_.refs_1_) | copy-start | bytes 25165828
  55.4 63.8 %collective-permute-start.8 = (bf16[2,512,512]{2,1,0:T(8,128)(2,1)}, bf16[2,512,512]{2,1,0:T(8,128)(2,1)S(1)}, u32[]{:S(2)}, u32[]{:S(2)}) collective-permute-start(bf16[2,512,512]{2,1,0:T(8,128)(2,1)} %get-tuple-element.184), channel_id=1, source_target_pairs={{0,1},{1,0},{2,3},{3,2},{4,5},{5,4},{6,7},{7,6},{8,9},{9,8},{10,11... | collective-permute-start | bytes 3145736 | tf_op jit(solution)/shard_map/ppermute | solution.py:496
  64.6 31.2 %collective-permute-start.10 = (bf16[512,512]{1,0:T(8,128)(2,1)S(1)}, bf16[512,512]{1,0:T(8,128)(2,1)S(1)}, u32[]{:S(2)}, u32[]{:S(2)}) collective-permute-start(bf16[512,512]{1,0:T(8,128)(2,1)S(1)} %get-tuple-element.187.part0), channel_id=1, source_target_pairs={{0,2},{1,3},{2,0},{3,1},{4,6},{5,7},{6,4},{7,5},{8,10},{9,11},{10,... | collective-permute-start | bytes 1572872 | tf_op jit(solution)/shard_map/ppermute | solution.py:496
  64.8 46.7 %collective-permute-start.12 = (bf16[512,512]{1,0:T(8,128)(2,1)S(1)}, bf16[512,512]{1,0:T(8,128)(2,1)S(1)}, u32[]{:S(2)}, u32[]{:S(2)}) collective-permute-start(bf16[512,512]{1,0:T(8,128)(2,1)S(1)} %get-tuple-element.191), channel_id=1, source_target_pairs={{0,3},{1,2},{2,1},{3,0},{4,7},{5,6},{6,5},{7,4},{8,11},{9,10},{10,... | collective-permute-start | bytes 1572872 | tf_op jit(solution)/shard_map/ppermute | solution.py:496
  72.7 40.9 %copy-start.9 = (bf16[2048,512]{1,0:T(8,128)(2,1)S(1)}, bf16[2048,512]{1,0:T(8,128)(2,1)}, u32[]{:S(2)}) copy-start(bf16[2048,512]{1,0:T(8,128)(2,1)} %cot_own.7) | copy-start | bytes 6291460
  95.8 37.7 %collective-permute-start.13 = (bf16[2,256,512]{2,1,0:T(8,128)(2,1)S(1)}, bf16[2,256,512]{2,1,0:T(8,128)(2,1)S(1)}, u32[]{:S(2)}, u32[]{:S(2)}) collective-permute-start(bf16[2,256,512]{2,1,0:T(8,128)(2,1)S(1)} %get-tuple-element.200), channel_id=1, source_target_pairs={{0,1},{1,0},{2,3},{3,2},{4,5},{5,4},{6,7},{7,6},{8,9},{9,8},{10,11... | collective-permute-start | bytes 1572872 | tf_op jit(solution)/shard_map/ppermute | solution.py:496
  111.6 17.5 %collective-permute-start.15 = (bf16[256,512]{1,0:T(8,128)(2,1)S(1)}, bf16[256,512]{1,0:T(8,128)(2,1)S(1)}, u32[]{:S(2)}, u32[]{:S(2)}) collective-permute-start(bf16[256,512]{1,0:T(8,128)(2,1)S(1)} %get-tuple-element.204), channel_id=1, source_target_pairs={{0,3},{1,2},{2,1},{3,0},{4,7},{5,6},{6,5},{7,4},{8,11},{9,10},{10,... | collective-permute-start | bytes 786440 | tf_op jit(solution)/shard_map/ppermute | solution.py:496
  111.6 21.9 %collective-permute-start.14 = (bf16[256,512]{1,0:T(8,128)(2,1)S(1)}, bf16[256,512]{1,0:T(8,128)(2,1)S(1)}, u32[]{:S(2)}, u32[]{:S(2)}) collective-permute-start(bf16[256,512]{1,0:T(8,128)(2,1)S(1)} %get-tuple-element.202), channel_id=1, source_target_pairs={{0,2},{1,3},{2,0},{3,1},{4,6},{5,7},{6,4},{7,5},{8,10},{9,11},{10,... | collective-permute-start | bytes 786440 | tf_op jit(solution)/shard_map/ppermute | solution.py:496
  129.0 9.0 %copy-start.15 = (bf16[512,512]{1,0:T(8,128)(2,1)}, bf16[512,512]{1,0:T(8,128)(2,1)S(1)}, u32[]{:S(2)}) copy-start(bf16[512,512]{1,0:T(8,128)(2,1)S(1)} %get-tuple-element.231) | copy-start | bytes 1572868
  133.5 46.9 %collective-permute-start.16 = (bf16[2,512,512]{2,1,0:T(8,128)(2,1)}, bf16[2,512,512]{2,1,0:T(8,128)(2,1)}, u32[]{:S(2)}, u32[]{:S(2)}) collective-permute-start(bf16[2,512,512]{2,1,0:T(8,128)(2,1)} %get-tuple-element.218), channel_id=1, source_target_pairs={{0,1},{1,0},{2,3},{3,2},{4,5},{5,4},{6,7},{7,6},{8,9},{9,8},{10,11... | collective-permute-start | bytes 3145736 | tf_op jit(solution)/shard_map/ppermute | solution.py:496
  133.6 46.8 %collective-permute-start.17 = (bf16[512,512]{1,0:T(8,128)(2,1)S(1)}, bf16[512,512]{1,0:T(8,128)(2,1)}, u32[]{:S(2)}, u32[]{:S(2)}) collective-permute-start(bf16[512,512]{1,0:T(8,128)(2,1)S(1)} %get-tuple-element.219), channel_id=1, source_target_pairs={{0,2},{1,3},{2,0},{3,1},{4,6},{5,7},{6,4},{7,5},{8,10},{9,11},{10,... | collective-permute-start | bytes 1572872 | tf_op jit(solution)/shard_map/ppermute | solution.py:496
  136.2 44.2 %collective-permute-start.18 = (bf16[512,512]{1,0:T(8,128)(2,1)}, bf16[512,512]{1,0:T(8,128)(2,1)}, u32[]{:S(2)}, u32[]{:S(2)}) collective-permute-start(bf16[512,512]{1,0:T(8,128)(2,1)} %get-tuple-element.220), channel_id=1, source_target_pairs={{0,3},{1,2},{2,1},{3,0},{4,7},{5,6},{6,5},{7,4},{8,11},{9,10},{10,... | collective-permute-start | bytes 1572872 | tf_op jit(solution)/shard_map/ppermute | solution.py:496
  138.0 49.9 %copy-start.2 = (bf16[2,256,512]{2,1,0:T(8,128)(2,1)S(1)}, bf16[2,256,512]{2,1,0:T(8,128)(2,1)}, u32[]{:S(2)}) copy-start(bf16[2,256,512]{2,1,0:T(8,128)(2,1)} %copy-done.1) | copy-start | bytes 1572868
  138.0 50.2 %copy-start.6 = (bf16[256,512]{1,0:T(8,128)(2,1)S(1)}, bf16[256,512]{1,0:T(8,128)(2,1)}, u32[]{:S(2)}) copy-start(bf16[256,512]{1,0:T(8,128)(2,1)} %copy-done.5) | copy-start | bytes 786436
  138.0 52.5 %copy-start.4 = (bf16[256,512]{1,0:T(8,128)(2,1)S(1)}, bf16[256,512]{1,0:T(8,128)(2,1)}, u32[]{:S(2)}) copy-start(bf16[256,512]{1,0:T(8,128)(2,1)} %copy-done.3) | copy-start | bytes 786436
  153.4 15.2 %collective-permute-start.2 = (bf16[2,528,512]{2,1,0:T(8,128)(2,1)S(1)}, bf16[2,528,512]{2,1,0:T(8,128)(2,1)S(1)}, u32[]{:S(2)}, u32[]{:S(2)}) collective-permute-start(bf16[2,528,512]{2,1,0:T(8,128)(2,1)S(1)} %get-tuple-element.91), channel_id=1, source_target_pairs={{0,16},{4,12},{8,24},{12,4},{16,0},{20,28},{24,8},{28,20},{1,17},{... | collective-permute-start | bytes 3244040 | tf_op jit(solution)/shard_map/cond/branch_1_fun/ppermute | solution.py:507
  169.4 9.6 %collective-permute-start.3 = (bf16[2,272,512]{2,1,0:T(8,128)(2,1)S(1)}, bf16[2,272,512]{2,1,0:T(8,128)(2,1)S(1)}, u32[]{:S(2)}, u32[]{:S(2)}) collective-permute-start(bf16[2,272,512]{2,1,0:T(8,128)(2,1)S(1)} %get-tuple-element.93), channel_id=1, source_target_pairs={{0,8},{4,20},{8,0},{12,28},{16,24},{20,4},{24,16},{28,12},{1,9},{5... | collective-permute-start | bytes 1671176 | tf_op jit(solution)/shard_map/cond/branch_1_fun/ppermute | solution.py:507
  180.4 7.5 %collective-permute-start.19 = (bf16[1,272,512]{2,1,0:T(8,128)(2,1)}, bf16[1,272,512]{2,1,0:T(8,128)(2,1)S(1)}, u32[]{:S(2)}, u32[]{:S(2)}) collective-permute-start(bf16[1,272,512]{2,1,0:T(8,128)(2,1)} %get-tuple-element.221), channel_id=1, source_target_pairs={{0,1},{1,0},{2,3},{3,2},{4,5},{5,4},{6,7},{7,6},{8,9},{9,8},{10,11... | collective-permute-start | bytes 835592 | tf_op jit(solution)/shard_map/ppermute | solution.py:496
  187.9 30.3 %collective-permute-start.20 = (bf16[2,256,512]{2,1,0:T(8,128)(2,1)S(1)}, bf16[2,256,512]{2,1,0:T(8,128)(2,1)S(1)}, u32[]{:S(2)}, u32[]{:S(2)}) collective-permute-start(bf16[2,256,512]{2,1,0:T(8,128)(2,1)S(1)} %copy-done.2), channel_id=1, source_target_pairs={{0,1},{1,0},{2,3},{3,2},{4,5},{5,4},{6,7},{7,6},{8,9},{9,8},{10,11... | collective-permute-start | bytes 1572872 | tf_op jit(solution)/shard_map/ppermute | solution.py:496
  188.2 30.0 %collective-permute-start.21 = (bf16[256,512]{1,0:T(8,128)(2,1)S(1)}, bf16[256,512]{1,0:T(8,128)(2,1)S(1)}, u32[]{:S(2)}, u32[]{:S(2)}) collective-permute-start(bf16[256,512]{1,0:T(8,128)(2,1)S(1)} %copy-done.6), channel_id=1, source_target_pairs={{0,2},{1,3},{2,0},{3,1},{4,6},{5,7},{6,4},{7,5},{8,10},{9,11},{10,... | collective-permute-start | bytes 786440 | tf_op jit(solution)/shard_map/ppermute | solution.py:496
  190.5 27.7 %collective-permute-start.22 = (bf16[256,512]{1,0:T(8,128)(2,1)S(1)}, bf16[256,512]{1,0:T(8,128)(2,1)S(1)}, u32[]{:S(2)}, u32[]{:S(2)}) collective-permute-start(bf16[256,512]{1,0:T(8,128)(2,1)S(1)} %copy-done.4), channel_id=1, source_target_pairs={{0,3},{1,2},{2,1},{3,0},{4,7},{5,6},{6,5},{7,4},{8,11},{9,10},{10,... | collective-permute-start | bytes 786440 | tf_op jit(solution)/shard_map/ppermute | solution.py:496
  194.4 7.0 %collective-permute-start.4 = (bf16[256,512]{1,0:T(8,128)(2,1)S(1)}, bf16[256,512]{1,0:T(8,128)(2,1)S(1)}, u32[]{:S(2)}, u32[]{:S(2)}) collective-permute-start(bf16[256,512]{1,0:T(8,128)(2,1)S(1)} %get-tuple-element.97.mine), channel_id=1, source_target_pairs={{0,8},{4,20},{8,0},{12,28},{16,24},{20,4},{24,16},{28,12},{1,9},{5... | collective-permute-start | bytes 786440 | tf_op jit(solution)/shard_map/cond/branch_1_fun/ppermute | solution.py:507
  202.0 9.2 %collective-permute-start.5 = (bf16[512,512]{1,0:T(8,128)(2,1)S(1)}, bf16[512,512]{1,0:T(8,128)(2,1)S(1)}, u32[]{:S(2)}, u32[]{:S(2)}) collective-permute-start(bf16[512,512]{1,0:T(8,128)(2,1)S(1)} %bitcast.12), channel_id=1, source_target_pairs={{0,16},{4,12},{8,24},{12,4},{16,0},{20,28},{24,8},{28,20},{1,17},{... | collective-permute-start | bytes 1572872 | tf_op jit(solution)/shard_map/cond/branch_1_fun/ppermute | solution.py:507
  (15 other events, 91.5 us)

commit v6 on v5

--- a/solution.py
+++ b/solution.py
@@ -543,7 +543,7 @@
     weight_sib, (counts, same, other, pack, scale) = always(last_rows, piece_sib, counts)
     near, far, cross = parts[0][1:]
     parts.append(
-        (same, across(tie(pack, cross), 1), across(tie(same, near), 2), across(tie(other, far), 3))
+        (same, across(tie(pack, cross), 1), across(tie(same, far), 2), across(tie(other, near), 3))
     )
     scales.append(scale)
 

time: 224 us -> 223 us (level)
  no operation moved by 1% of the time
where the time goes in v6:
time: 223 us
  waiting for transfers between devices  89.7 us (40%)
  Pallas kernels  71.3 us (32%)
  starting transfers between devices  38.7 us (17%)
  blocking collectives  18 us (8%)
  local copies, waits for them, and re-layouts  2.43 us (1%)
    pallas_call x19, Pallas kernels, call(): pl.pallas_call(kernel, grid_spec=pltpu.PrefetchScalarGridSpec(num_scalar_...  71.3 us
    ppermute x17, waiting for transfers between devices, across(): return lax.ppermute(value, 'mp', [(i, i ^ code) for i in range(mp_count)])  58.1 us
    ppermute x6, waiting for transfers between devices, along(): lax.ppermute(value, 'dp', [(i, i ^ 1 << orders[stage][i % 2]) for i in ra...  31.6 us
    ppermute x17, starting transfers between devices, across(): return lax.ppermute(value, 'mp', [(i, i ^ code) for i in range(mp_count)])  29.3 us
    all_to_all x3, blocking collectives, swap(): return lax.all_to_all(value, 'dp', 0, 0, axis_index_groups=pairs)  18 us
    ppermute x6, starting transfers between devices, along(): lax.ppermute(value, 'dp', [(i, i ^ 1 << orders[stage][i % 2]) for i in ra...  9.37 us
  transfers between devices with their start and end apart: 23, of which 11 were waited for; matrix products, arithmetic and copies ran while one was open for 1% of the time, Pallas kernels for 29%

profile of v6, /device:TPU:0, one launch (start us, length us, event | category | flops | bytes accessed | tf_op | source)
XLA Modules:
  0.0 222.6 jit_solution(17923125237576952335)
XLA Ops:
  2.3 3.1 %collective-permute-start.6 = (bf16[272,512]{1,0:T(8,128)(2,1)S(1)}, bf16[272,512]{1,0:T(8,128)(2,1)}, u32[]{:S(2)}, u32[]{:S(2)}) collective-permute-start(bf16[272,512]{1,0:T(8,128)(2,1)S(1)} %weight_piece.1.bias_own), channel_id=1, source_target_pairs={{0,1},{1,0},{2,3},{3,2},{4,5},{5,4},{6,7},{7,6},{8,9},{9,8},{10,11... | collective-permute-start | bytes 835592 | tf_op jit(solution)/shard_map/ppermute | solution.py:496
  6.1 9.7 %count_and_aggregate.3 = (bf16[2048,2048]{1,0:T(8,128)(2,1)S(1)}, bf16[512,512]{1,0:T(8,128)(2,1)}, bf16[512,512]{1,0:T(8,128)(2,1)S(1)}, bf16[2,512,512]{2,1,0:T(8,128)(2,1)}, f32[512,1]{1,0:T(8,128)S(1)}) custom-call(s32[4]{0:T(128)S(1)} %pad_add_fusion.at, s32[256,256]{1,0:T(8,128)S(1)} %reshape.28.packed_ref, bf16[2048,512]{1,0:T(8,128)(2,1)} %feat_ref.1, ...), custom_call_target="tpu_custom_call" | custom-call | flops 1 | bytes 1 | tf_op jit(solution)/shard_map/count_and_aggregate/pallas_call | solution.py:43
  15.7 4.0 %collective-permute-start.7 = (bf16[512,512]{1,0:T(8,128)(2,1)S(1)}, bf16[512,512]{1,0:T(8,128)(2,1)}, u32[]{:S(2)}, u32[]{:S(2)}) collective-permute-start(bf16[512,512]{1,0:T(8,128)(2,1)S(1)} %get-tuple-element.183), channel_id=1, source_target_pairs={{0,3},{1,2},{2,1},{3,0},{4,7},{5,6},{6,5},{7,4},{8,11},{9,10},{10,... | collective-permute-start | bytes 1572872 | tf_op jit(solution)/shard_map/ppermute | solution.py:496
  20.5 27.4 %conditional.3 = (bf16[2048,512]{1,0:T(8,128)(2,1)S(1)}, bf16[2048,2048]{1,0:T(8,128)(2,1)S(1)}, bf16[512,512]{1,0:T(8,128)(2,1)S(1)}, bf16[512,512]{1,0:T(8,128...) conditional(s32[]{:T(128)} %bitcast.10, () %tuple.55, (bf16[272,512]{1,0:T(8,128)(2,1)}, ...), branch_computations={%region_0.1_spmd, %region_1.2_spmd} | conditional | flops 3 | bytes 12585022 | solution.py:534
  23.7 8.1 %count_and_aggregate.2 = (bf16[2048,2048]{1,0:T(8,128)(2,1)S(1)}, bf16[512,512]{1,0:T(8,128)(2,1)S(1)}, bf16[512,512]{1,0:T(8,128)(2,1)S(1)}, bf16[2,512,512]{2,1,0:T(8,128)(2,1)}, f32[512,1]{1,0:T(8,128)S(1)}) custom-call(s32[4]{0:T(128)S(1)} %get-tuple-element.66.at, s32[256,256]{1,0:T(8,128)} %copy-done.12, ...), custom_call_target="tpu_custom_call", output_to_operand_aliasing={{0}: (4, {})} | custom-call | flops 1 | bytes 1 | tf_op jit(solution)/shard_map/cond/branch_1_fun/count_and_aggregate/pallas_call | solution.py:43
  34.0 7.7 %collective-permute-done.1.theirs = bf16[512,512]{1,0:T(8,128)(2,1)S(1)} collective-permute-done((bf16[512,512]{1,0:T(8,128)(2,1)S(1)}, bf16[512,512]{1,0:T(8,128)(2,1)S(1)}, u32[]{:S(2)}, u32[]{:S(2)}) %collective-permute-start.1) | collective-permute-done | bytes 524320 | tf_op jit(solution)/shard_map/cond/branch_1_fun/ppermute | solution.py:507
  42.4 5.4 %all_to_all.12 = bf16[2,1024,512]{2,1,0:T(8,128)(2,1)S(1)} all-to-all(bf16[2,1024,512]{2,1,0:T(8,128)(2,1)S(1)} %join_halves.5), channel_id=1, replica_groups={{0,4},{8,12},{16,20},{24,28},{1,5},{9,13},{17,21},{25,29},{2,6},{10,14}..., dimensions={0} | all-to-all | bytes 4194304 | tf_op jit(solution)/shard_map/cond/branch_1_fun/all_to_all | solution.py:504
  47.9 7.5 %collective-permute-done.7.part3 = bf16[512,512]{1,0:T(8,128)(2,1)} collective-permute-done((bf16[512,512]{1,0:T(8,128)(2,1)S(1)}, bf16[512,512]{1,0:T(8,128)(2,1)}, u32[]{:S(2)}, u32[]{:S(2)}) %collective-permute-start.7) | collective-permute-done | bytes 524320 | tf_op jit(solution)/shard_map/ppermute | solution.py:496
  55.4 6.7 %collective-permute-done.9.part2 = bf16[512,512]{1,0:T(8,128)(2,1)} collective-permute-done((bf16[512,512]{1,0:T(8,128)(2,1)}, bf16[512,512]{1,0:T(8,128)(2,1)}, u32[]{:S(2)}, u32[]{:S(2)}) %collective-permute-start.9) | collective-permute-done | bytes 524320 | tf_op jit(solution)/shard_map/ppermute | solution.py:496
  62.1 3.4 %collective-permute-start.10 = (bf16[512,512]{1,0:T(8,128)(2,1)S(1)}, bf16[512,512]{1,0:T(8,128)(2,1)S(1)}, u32[]{:S(2)}, u32[]{:S(2)}) collective-permute-start(bf16[512,512]{1,0:T(8,128)(2,1)S(1)} %get-tuple-element.187.part0), channel_id=1, source_target_pairs={{0,2},{1,3},{2,0},{3,1},{4,6},{5,7},{6,4},{7,5},{8,10},{9,11},{10,... | collective-permute-start | bytes 1572872 | tf_op jit(solution)/shard_map/ppermute | solution.py:496
  65.5 4.0 %collective-permute-start.12 = (bf16[512,512]{1,0:T(8,128)(2,1)S(1)}, bf16[512,512]{1,0:T(8,128)(2,1)S(1)}, u32[]{:S(2)}, u32[]{:S(2)}) collective-permute-start(bf16[512,512]{1,0:T(8,128)(2,1)S(1)} %get-tuple-element.191), channel_id=1, source_target_pairs={{0,3},{1,2},{2,1},{3,0},{4,7},{5,6},{6,5},{7,4},{8,11},{9,10},{10,... | collective-permute-start | bytes 1572872 | tf_op jit(solution)/shard_map/ppermute | solution.py:496
  69.6 5.5 %linear_and_slope.5 = (bf16[256,512]{1,0:T(8,128)(2,1)}, bf16[2,256,512]{2,1,0:T(8,128)(2,1)}, bf16[256,512]{1,0:T(8,128)(2,1)}, bf16[2,256,512]{2,1,0:T(8,128)(...) custom-call(s32[4]{0:T(128)S(1)} %pad_add_fusion.at, s32[1]{0:T(128)S(6)} %copy.52.live, ...), custom_call_target="tpu_custom_call" | custom-call | flops 1 | bytes 1 | tf_op jit(solution)/shard_map/linear_and_slope/pallas_call | solution.py:43
  75.1 20.7 %collective-permute-done.10.part2 = bf16[512,512]{1,0:T(8,128)(2,1)S(1)} collective-permute-done((bf16[512,512]{1,0:T(8,128)(2,1)S(1)}, bf16[512,512]{1,0:T(8,128)(2,1)S(1)}, u32[]{:S(2)}, u32[]{:S(2)}) %collective-permute-start.10) | collective-permute-done | bytes 524320 | tf_op jit(solution)/shard_map/ppermute | solution.py:496
  95.8 5.1 %collective-permute-start.13 = (bf16[2,256,512]{2,1,0:T(8,128)(2,1)S(1)}, bf16[2,256,512]{2,1,0:T(8,128)(2,1)S(1)}, u32[]{:S(2)}, u32[]{:S(2)}) collective-permute-start(bf16[2,256,512]{2,1,0:T(8,128)(2,1)S(1)} %get-tuple-element.200), channel_id=1, source_target_pairs={{0,1},{1,0},{2,3},{3,2},{4,5},{5,4},{6,7},{7,6},{8,9},{9,8},{10,11... | collective-permute-start | bytes 1572872 | tf_op jit(solution)/shard_map/ppermute | solution.py:496
  100.9 10.7 %collective-permute-done.12.part3 = bf16[512,512]{1,0:T(8,128)(2,1)S(1)} collective-permute-done((bf16[512,512]{1,0:T(8,128)(2,1)S(1)}, bf16[512,512]{1,0:T(8,128)(2,1)S(1)}, u32[]{:S(2)}, u32[]{:S(2)}) %collective-permute-start.12) | collective-permute-done | bytes 524320 | tf_op jit(solution)/shard_map/ppermute | solution.py:496
  111.6 5.6 %linear_and_slope.6 = (bf16[512,512]{1,0:T(8,128)(2,1)S(1)}, bf16[2,512,512]{2,1,0:T(8,128)(2,1)S(1)}, bf16[512,512]{1,0:T(8,128)(2,1)S(1)}, bf16[2,512,512]{2,1...) custom-call(s32[4]{0:T(128)S(1)} %pad_add_fusion.at, s32[1]{0:T(128)S(6)} %copy.52.live, ...), custom_call_target="tpu_custom_call" | custom-call | flops 1 | bytes 1 | tf_op jit(solution)/shard_map/linear_and_slope/pallas_call | solution.py:43
  117.2 4.7 %linear_and_slope.4 = (bf16[256,512]{1,0:T(8,128)(2,1)S(1)}, bf16[2,256,512]{2,1,0:T(8,128)(2,1)}, bf16[256,512]{1,0:T(8,128)(2,1)S(1)}, bf16[2,256,512]{2,1,0:T...) custom-call(s32[4]{0:T(128)S(1)} %pad_add_fusion.at, s32[1]{0:T(128)S(6)} %copy.52.live, ...), custom_call_target="tpu_custom_call" | custom-call | flops 1 | bytes 1 | tf_op jit(solution)/shard_map/linear_and_slope/pallas_call | solution.py:43
  121.9 5.0 %linear_and_slope.7 = (bf16[512,512]{1,0:T(8,128)(2,1)S(1)}, bf16[2,512,512]{2,1,0:T(8,128)(2,1)S(1)}, bf16[512,512]{1,0:T(8,128)(2,1)S(1)}, bf16[2,512,512]{2,1...) custom-call(s32[4]{0:T(128)S(1)} %pad_add_fusion.at, ...), custom_call_target="tpu_custom_call", output_to_operand_aliasing={{0}: (12, {}), {1}: (13, {}), {2}: (14, {}), {3}: (15, {}),... | custom-call | flops 1 | bytes 1 | tf_op jit(solution)/shard_map/linear_and_slope/pallas_call | solution.py:43
  127.1 5.6 %collective-permute-done.15 = bf16[256,512]{1,0:T(8,128)(2,1)S(1)} collective-permute-done((bf16[256,512]{1,0:T(8,128)(2,1)S(1)}, bf16[256,512]{1,0:T(8,128)(2,1)S(1)}, u32[]{:S(2)}, u32[]{:S(2)}) %collective-permute-start.15) | collective-permute-done | bytes 262176 | tf_op jit(solution)/shard_map/ppermute | solution.py:496
  134.1 2.9 %collective-permute-start.18 = (bf16[512,512]{1,0:T(8,128)(2,1)}, bf16[512,512]{1,0:T(8,128)(2,1)}, u32[]{:S(2)}, u32[]{:S(2)}) collective-permute-start(bf16[512,512]{1,0:T(8,128)(2,1)} %get-tuple-element.220), channel_id=1, source_target_pairs={{0,3},{1,2},{2,1},{3,0},{4,7},{5,6},{6,5},{7,4},{8,11},{9,10},{10,... | collective-permute-start | bytes 1572872 | tf_op jit(solution)/shard_map/ppermute | solution.py:496
  137.1 42.4 %conditional.4 = ((bf16[1,272,512]{2,1,0:T(8,128)(2,1)}, bf16[1,272,512]{2,1,0:T(8,128)(2,1)})) conditional(s32[]{:T(128)} %bitcast.10, () %tuple.64, (s32[4]{0:T(128)S(1)}, bf16[512,512]{1,0:T(8,128)(2,1)}, bf16[2,512,512]{2,1,0:T(8,128)(2,1)}, bf16[512,512]{1,0:T(8,128)(2,1)}, bf16[512,512]{1,0:T(8,128)(2,1)}, ...), branch_computations={%region_2.3_spmd, %region_3.4_spmd} | conditional | flops 4 | bytes 15073372 | solution.py:534
  137.1 7.1 %weight_product.1 = bf16[2,2,1040,512]{3,2,1,0:T(8,128)(2,1)S(1)} custom-call(s32[4]{0:T(128)S(1)} %get-tuple-element.78.at, bf16[512,512]{1,0:T(8,128)(2,1)} %get-tuple-element.79.refs_0_, bf16[2,512,512]{2,1,0:T(8,128)(2,1)} %get-tuple-element.80.refs_1_, bf16[512,512]{1,0:T(8,128)(2,1)} %get-tuple-element.81.refs_2_, ...), custom_call_target="tpu_custom_call" | custom-call | flops 1 | bytes 1 | tf_op jit(solution)/shard_map/cond/branch_1_fun/weight_product/pallas_call | solution.py:43
  144.2 7.2 %all_to_all.13.refs_0_ = bf16[2,2,1040,512]{3,2,1,0:T(8,128)(2,1)S(1)} all-to-all(bf16[2,2,1040,512]{3,2,1,0:T(8,128)(2,1)S(1)} %weight_product.1), channel_id=1, replica_groups={{0,4},{8,12},{16,20},{24,28},{1,5},{9,13},{17,21},{25,29},{2,6},{10,14}..., dimensions={0} | all-to-all | bytes 8519680 | tf_op jit(solution)/shard_map/cond/branch_1_fun/all_to_all | solution.py:504
  154.0 13.6 %collective-permute-done.2.refs_1_ = bf16[2,528,512]{2,1,0:T(8,128)(2,1)S(1)} collective-permute-done((bf16[2,528,512]{2,1,0:T(8,128)(2,1)S(1)}, bf16[2,528,512]{2,1,0:T(8,128)(2,1)S(1)}, u32[]{:S(2)}, u32[]{:S(2)}) %collective-permute-start.2) | collective-permute-done | bytes 1081376 | tf_op jit(solution)/shard_map/cond/branch_1_fun/ppermute | solution.py:507
  170.1 8.0 %collective-permute-done.3.refs_1_ = bf16[2,272,512]{2,1,0:T(8,128)(2,1)S(1)} collective-permute-done((bf16[2,272,512]{2,1,0:T(8,128)(2,1)S(1)}, bf16[2,272,512]{2,1,0:T(8,128)(2,1)S(1)}, u32[]{:S(2)}, u32[]{:S(2)}) %collective-permute-start.3) | collective-permute-done | bytes 557088 | tf_op jit(solution)/shard_map/cond/branch_1_fun/ppermute | solution.py:507
  180.4 6.7 %collective-permute-done.19 = bf16[1,272,512]{2,1,0:T(8,128)(2,1)S(1)} collective-permute-done((bf16[1,272,512]{2,1,0:T(8,128)(2,1)}, bf16[1,272,512]{2,1,0:T(8,128)(2,1)S(1)}, u32[]{:S(2)}, u32[]{:S(2)}) %collective-permute-start.19) | collective-permute-done | bytes 278560 | tf_op jit(solution)/shard_map/ppermute | solution.py:496
  189.3 2.2 %collective-permute-start.22 = (bf16[256,512]{1,0:T(8,128)(2,1)S(1)}, bf16[256,512]{1,0:T(8,128)(2,1)S(1)}, u32[]{:S(2)}, u32[]{:S(2)}) collective-permute-start(bf16[256,512]{1,0:T(8,128)(2,1)S(1)} %copy-done.4), channel_id=1, source_target_pairs={{0,3},{1,2},{2,1},{3,0},{4,7},{5,6},{6,5},{7,4},{8,11},{9,10},{10,... | collective-permute-start | bytes 786440 | tf_op jit(solution)/shard_map/ppermute | solution.py:496
  191.5 25.7 %conditional.5 = (f32[2048,512]{1,0:T(8,128)S(1)}, f32[2048,512]{1,0:T(8,128)S(1)}, bf16[2048,512]{1,0:T(8,128)(2,1)}, f32[512]{0:T(512)}) conditional(s32[]{:T(128)} %bitcast.10, () %tuple.78, (s32[4]{0:T(128)S(1)}, bf16[1,272,512]{2,1,0:T(8,128)(2,1)}, bf16[1,272,512]{2,1,0:T(8,128)(2,1)S(1)}, bf16[256,512]{1,0:T(8,128)(2,1)}, ...), branch_computations={%region_4.5_spmd, %region_5.6_spmd} | conditional | flops 1048581 | bytes 53971776 | solution.py:534
  195.1 3.3 %place_rows.1 = bf16[2048,512]{1,0:T(8,128)(2,1)} custom-call(s32[4]{0:T(128)S(1)} %get-tuple-element.94.at, bf16[256,512]{1,0:T(8,128)(2,1)} %get-tuple-element.98.refs_0_, bf16[2,256,512]{2,1,0:T(8,128)(2,1)} %get-tuple-element.99.refs_1_.refs_7_, bf16[512,512]{1,0:T(8,128)(2,1)} %get-tuple-element.100.refs_2_, ...), custom_call_target="tpu_custom_call" | custom-call | flops 1 | bytes 9000000 | tf_op jit(solution)/shard_map/cond/branch_1_fun/place_rows/pallas_call | solution.py:43
  202.7 7.4 %spread_back.2 = f32[2048,512]{1,0:T(8,128)S(1)} custom-call(s32[4]{0:T(128)S(1)} %get-tuple-element.94.at, bf16[2048,2048]{1,0:T(8,128)(2,1)} %get-tuple-element.103.refs_0_.refs_1_.refs_2_.refs_3_.refs_4_.refs_5_, bf16[2048,2048]{1,0:T(8,128)(2,1)} %get-tuple-element.103.refs_0_.refs_1_.refs_2_.refs_3_.refs_4_.refs_5_, ...), custom_call_target="tpu_custom_call" | custom-call | flops 1 | bytes 24000000 | tf_op jit(solution)/shard_map/cond/branch_1_fun/spread_back/pallas_call | solution.py:43
  211.1 5.4 %all_to_all.14 = bf16[2,1024,512]{2,1,0:T(8,128)(2,1)S(1)} all-to-all(bf16[2,1024,512]{2,1,0:T(8,128)(2,1)S(1)} %join_halves.7), channel_id=1, replica_groups={{0,4},{8,12},{16,20},{24,28},{1,5},{9,13},{17,21},{25,29},{2,6},{10,14}..., dimensions={0} | all-to-all | bytes 4194304 | tf_op jit(solution)/shard_map/cond/branch_1_fun/all_to_all | solution.py:504
  217.3 5.3 %spread_back.3 = (bf16[2048,512]{1,0:T(8,128)(2,1)}, bf16[2048,512]{1,0:T(8,128)(2,1)}) custom-call(s32[4]{0:T(128)S(1)} %pad_add_fusion.at, bf16[2048,2048]{1,0:T(8,128)(2,1)} %copy-done.7, bf16[2048,2048]{1,0:T(8,128)(2,1)} %copy-done.7, bf16[256,512]{1,0:T(8,128)(2,1)S(1)} %get-tuple-element.194.refs_2_, ...), custom_call_target="tpu_custom_call", output_to_operand_aliasing={{1}: (9, {})} | custom-call | flops 1 | bytes 24000000 | tf_op jit(solution)/shard_map/spread_back/pallas_call | solution.py:43
  (92 shorter events, 28.9 us)
Async XLA Ops:
  2.3 13.4 %collective-permute-start.6 = (bf16[272,512]{1,0:T(8,128)(2,1)S(1)}, bf16[272,512]{1,0:T(8,128)(2,1)}, u32[]{:S(2)}, u32[]{:S(2)}) collective-permute-start(bf16[272,512]{1,0:T(8,128)(2,1)S(1)} %weight_piece.1.bias_own), channel_id=1, source_target_pairs={{0,1},{1,0},{2,3},{3,2},{4,5},{5,4},{6,7},{7,6},{8,9},{9,8},{10,11... | collective-permute-start | bytes 835592 | tf_op jit(solution)/shard_map/ppermute | solution.py:496
  6.0 14.4 %copy-start.8 = (bf16[2048,512]{1,0:T(8,128)(2,1)S(1)}, bf16[2048,512]{1,0:T(8,128)(2,1)}, u32[]{:S(2)}) copy-start(bf16[2048,512]{1,0:T(8,128)(2,1)} %cot_own.7) | copy-start | bytes 6291460
  6.1 14.4 %copy-start.10 = (bf16[2048,512]{1,0:T(8,128)(2,1)S(1)}, bf16[2048,512]{1,0:T(8,128)(2,1)}, u32[]{:S(2)}) copy-start(bf16[2048,512]{1,0:T(8,128)(2,1)} %feat_ref.1) | copy-start | bytes 6291460
  15.7 49.8 %collective-permute-start.11 = (bf16[2,512,512]{2,1,0:T(8,128)(2,1)}, bf16[2,512,512]{2,1,0:T(8,128)(2,1)}, u32[]{:S(2)}, u32[]{:S(2)}) collective-permute-start(bf16[2,512,512]{2,1,0:T(8,128)(2,1)} %get-tuple-element.190), channel_id=1, source_target_pairs={{0,1},{1,0},{2,3},{3,2},{4,5},{5,4},{6,7},{7,6},{8,9},{9,8},{10,11... | collective-permute-start | bytes 3145736 | tf_op jit(solution)/shard_map/ppermute | solution.py:496
  15.7 39.6 %collective-permute-start.7 = (bf16[512,512]{1,0:T(8,128)(2,1)S(1)}, bf16[512,512]{1,0:T(8,128)(2,1)}, u32[]{:S(2)}, u32[]{:S(2)}) collective-permute-start(bf16[512,512]{1,0:T(8,128)(2,1)S(1)} %get-tuple-element.183), channel_id=1, source_target_pairs={{0,3},{1,2},{2,1},{3,0},{4,7},{5,6},{6,5},{7,4},{8,11},{9,10},{10,... | collective-permute-start | bytes 1572872 | tf_op jit(solution)/shard_map/ppermute | solution.py:496
  19.8 42.4 %collective-permute-start.9 = (bf16[512,512]{1,0:T(8,128)(2,1)}, bf16[512,512]{1,0:T(8,128)(2,1)}, u32[]{:S(2)}, u32[]{:S(2)}) collective-permute-start(bf16[512,512]{1,0:T(8,128)(2,1)} %get-tuple-element.186.part0), channel_id=1, source_target_pairs={{0,2},{1,3},{2,0},{3,1},{4,6},{5,7},{6,4},{7,5},{8,10},{9,11},{10,... | collective-permute-start | bytes 1572872 | tf_op jit(solution)/shard_map/ppermute | solution.py:496
  20.5 49.1 %copy-start = (bf16[2048,512]{1,0:T(8,128)(2,1)S(1)}, bf16[2048,512]{1,0:T(8,128)(2,1)}, u32[]{:S(2)}) copy-start(bf16[2048,512]{1,0:T(8,128)(2,1)} %weight_own.7) | copy-start | bytes 6291460
  22.2 9.7 %collective-permute-start = (bf16[256,512]{1,0:T(8,128)(2,1)S(1)}, bf16[256,512]{1,0:T(8,128)(2,1)S(1)}, u32[]{:S(2)}, u32[]{:S(2)}) collective-permute-start(bf16[256,512]{1,0:T(8,128)(2,1)S(1)} %slice.2.mine), channel_id=1, source_target_pairs={{0,8},{4,20},{8,0},{12,28},{16,24},{20,4},{24,16},{28,12},{1,9},{5... | collective-permute-start | bytes 786440 | tf_op jit(solution)/shard_map/cond/branch_1_fun/ppermute | solution.py:507
  32.5 9.2 %collective-permute-start.1 = (bf16[512,512]{1,0:T(8,128)(2,1)S(1)}, bf16[512,512]{1,0:T(8,128)(2,1)S(1)}, u32[]{:S(2)}, u32[]{:S(2)}) collective-permute-start(bf16[512,512]{1,0:T(8,128)(2,1)S(1)} %bitcast.14), channel_id=1, source_target_pairs={{0,16},{4,12},{8,24},{12,4},{16,0},{20,28},{24,8},{28,20},{1,17},{... | collective-permute-start | bytes 1572872 | tf_op jit(solution)/shard_map/cond/branch_1_fun/ppermute | solution.py:507
  47.9 27.2 %copy-start.7 = (bf16[2048,2048]{1,0:T(8,128)(2,1)}, bf16[2048,2048]{1,0:T(8,128)(2,1)S(1)}, u32[]{:S(2)}) copy-start(bf16[2048,2048]{1,0:T(8,128)(2,1)S(1)} %get-tuple-element.179.refs_0_.refs_1_) | copy-start | bytes 25165828
  55.4 61.8 %collective-permute-start.8 = (bf16[2,512,512]{2,1,0:T(8,128)(2,1)}, bf16[2,512,512]{2,1,0:T(8,128)(2,1)S(1)}, u32[]{:S(2)}, u32[]{:S(2)}) collective-permute-start(bf16[2,512,512]{2,1,0:T(8,128)(2,1)} %get-tuple-element.184), channel_id=1, source_target_pairs={{0,1},{1,0},{2,3},{3,2},{4,5},{5,4},{6,7},{7,6},{8,9},{9,8},{10,11... | collective-permute-start | bytes 3145736 | tf_op jit(solution)/shard_map/ppermute | solution.py:496
  62.1 33.6 %collective-permute-start.10 = (bf16[512,512]{1,0:T(8,128)(2,1)S(1)}, bf16[512,512]{1,0:T(8,128)(2,1)S(1)}, u32[]{:S(2)}, u32[]{:S(2)}) collective-permute-start(bf16[512,512]{1,0:T(8,128)(2,1)S(1)} %get-tuple-element.187.part0), channel_id=1, source_target_pairs={{0,2},{1,3},{2,0},{3,1},{4,6},{5,7},{6,4},{7,5},{8,10},{9,11},{10,... | collective-permute-start | bytes 1572872 | tf_op jit(solution)/shard_map/ppermute | solution.py:496
  65.5 46.1 %collective-permute-start.12 = (bf16[512,512]{1,0:T(8,128)(2,1)S(1)}, bf16[512,512]{1,0:T(8,128)(2,1)S(1)}, u32[]{:S(2)}, u32[]{:S(2)}) collective-permute-start(bf16[512,512]{1,0:T(8,128)(2,1)S(1)} %get-tuple-element.191), channel_id=1, source_target_pairs={{0,3},{1,2},{2,1},{3,0},{4,7},{5,6},{6,5},{7,4},{8,11},{9,10},{10,... | collective-permute-start | bytes 1572872 | tf_op jit(solution)/shard_map/ppermute | solution.py:496
  69.6 42.1 %copy-start.9 = (bf16[2048,512]{1,0:T(8,128)(2,1)S(1)}, bf16[2048,512]{1,0:T(8,128)(2,1)}, u32[]{:S(2)}) copy-start(bf16[2048,512]{1,0:T(8,128)(2,1)} %cot_own.7) | copy-start | bytes 6291460
  95.8 31.2 %collective-permute-start.13 = (bf16[2,256,512]{2,1,0:T(8,128)(2,1)S(1)}, bf16[2,256,512]{2,1,0:T(8,128)(2,1)S(1)}, u32[]{:S(2)}, u32[]{:S(2)}) collective-permute-start(bf16[2,256,512]{2,1,0:T(8,128)(2,1)S(1)} %get-tuple-element.200), channel_id=1, source_target_pairs={{0,1},{1,0},{2,3},{3,2},{4,5},{5,4},{6,7},{7,6},{8,9},{9,8},{10,11... | collective-permute-start | bytes 1572872 | tf_op jit(solution)/shard_map/ppermute | solution.py:496
  100.9 26.1 %collective-permute-start.14 = (bf16[256,512]{1,0:T(8,128)(2,1)S(1)}, bf16[256,512]{1,0:T(8,128)(2,1)S(1)}, u32[]{:S(2)}, u32[]{:S(2)}) collective-permute-start(bf16[256,512]{1,0:T(8,128)(2,1)S(1)} %get-tuple-element.202), channel_id=1, source_target_pairs={{0,2},{1,3},{2,0},{3,1},{4,6},{5,7},{6,4},{7,5},{8,10},{9,11},{10,... | collective-permute-start | bytes 786440 | tf_op jit(solution)/shard_map/ppermute | solution.py:496
  111.6 21.1 %collective-permute-start.15 = (bf16[256,512]{1,0:T(8,128)(2,1)S(1)}, bf16[256,512]{1,0:T(8,128)(2,1)S(1)}, u32[]{:S(2)}, u32[]{:S(2)}) collective-permute-start(bf16[256,512]{1,0:T(8,128)(2,1)S(1)} %get-tuple-element.204), channel_id=1, source_target_pairs={{0,3},{1,2},{2,1},{3,0},{4,7},{5,6},{6,5},{7,4},{8,11},{9,10},{10,... | collective-permute-start | bytes 786440 | tf_op jit(solution)/shard_map/ppermute | solution.py:496
  127.0 10.1 %copy-start.15 = (bf16[512,512]{1,0:T(8,128)(2,1)}, bf16[512,512]{1,0:T(8,128)(2,1)S(1)}, u32[]{:S(2)}) copy-start(bf16[512,512]{1,0:T(8,128)(2,1)S(1)} %get-tuple-element.231) | copy-start | bytes 1572868
  132.7 46.8 %collective-permute-start.16 = (bf16[2,512,512]{2,1,0:T(8,128)(2,1)}, bf16[2,512,512]{2,1,0:T(8,128)(2,1)}, u32[]{:S(2)}, u32[]{:S(2)}) collective-permute-start(bf16[2,512,512]{2,1,0:T(8,128)(2,1)} %get-tuple-element.218), channel_id=1, source_target_pairs={{0,1},{1,0},{2,3},{3,2},{4,5},{5,4},{6,7},{7,6},{8,9},{9,8},{10,11... | collective-permute-start | bytes 3145736 | tf_op jit(solution)/shard_map/ppermute | solution.py:496
  133.4 46.1 %collective-permute-start.17 = (bf16[512,512]{1,0:T(8,128)(2,1)S(1)}, bf16[512,512]{1,0:T(8,128)(2,1)}, u32[]{:S(2)}, u32[]{:S(2)}) collective-permute-start(bf16[512,512]{1,0:T(8,128)(2,1)S(1)} %get-tuple-element.219), channel_id=1, source_target_pairs={{0,2},{1,3},{2,0},{3,1},{4,6},{5,7},{6,4},{7,5},{8,10},{9,11},{10,... | collective-permute-start | bytes 1572872 | tf_op jit(solution)/shard_map/ppermute | solution.py:496
  134.1 45.4 %collective-permute-start.18 = (bf16[512,512]{1,0:T(8,128)(2,1)}, bf16[512,512]{1,0:T(8,128)(2,1)}, u32[]{:S(2)}, u32[]{:S(2)}) collective-permute-start(bf16[512,512]{1,0:T(8,128)(2,1)} %get-tuple-element.220), channel_id=1, source_target_pairs={{0,3},{1,2},{2,1},{3,0},{4,7},{5,6},{6,5},{7,4},{8,11},{9,10},{10,... | collective-permute-start | bytes 1572872 | tf_op jit(solution)/shard_map/ppermute | solution.py:496
  137.1 50.1 %copy-start.2 = (bf16[2,256,512]{2,1,0:T(8,128)(2,1)S(1)}, bf16[2,256,512]{2,1,0:T(8,128)(2,1)}, u32[]{:S(2)}) copy-start(bf16[2,256,512]{2,1,0:T(8,128)(2,1)} %copy-done.1) | copy-start | bytes 1572868
  137.1 50.4 %copy-start.6 = (bf16[256,512]{1,0:T(8,128)(2,1)S(1)}, bf16[256,512]{1,0:T(8,128)(2,1)}, u32[]{:S(2)}) copy-start(bf16[256,512]{1,0:T(8,128)(2,1)} %copy-done.5) | copy-start | bytes 786436
  137.1 52.2 %copy-start.4 = (bf16[256,512]{1,0:T(8,128)(2,1)S(1)}, bf16[256,512]{1,0:T(8,128)(2,1)}, u32[]{:S(2)}) copy-start(bf16[256,512]{1,0:T(8,128)(2,1)} %copy-done.3) | copy-start | bytes 786436
  152.5 15.2 %collective-permute-start.2 = (bf16[2,528,512]{2,1,0:T(8,128)(2,1)S(1)}, bf16[2,528,512]{2,1,0:T(8,128)(2,1)S(1)}, u32[]{:S(2)}, u32[]{:S(2)}) collective-permute-start(bf16[2,528,512]{2,1,0:T(8,128)(2,1)S(1)} %get-tuple-element.91), channel_id=1, source_target_pairs={{0,16},{4,12},{8,24},{12,4},{16,0},{20,28},{24,8},{28,20},{1,17},{... | collective-permute-start | bytes 3244040 | tf_op jit(solution)/shard_map/cond/branch_1_fun/ppermute | solution.py:507
  168.5 9.6 %collective-permute-start.3 = (bf16[2,272,512]{2,1,0:T(8,128)(2,1)S(1)}, bf16[2,272,512]{2,1,0:T(8,128)(2,1)S(1)}, u32[]{:S(2)}, u32[]{:S(2)}) collective-permute-start(bf16[2,272,512]{2,1,0:T(8,128)(2,1)S(1)} %get-tuple-element.93), channel_id=1, source_target_pairs={{0,8},{4,20},{8,0},{12,28},{16,24},{20,4},{24,16},{28,12},{1,9},{5... | collective-permute-start | bytes 1671176 | tf_op jit(solution)/shard_map/cond/branch_1_fun/ppermute | solution.py:507
  179.5 7.6 %collective-permute-start.19 = (bf16[1,272,512]{2,1,0:T(8,128)(2,1)}, bf16[1,272,512]{2,1,0:T(8,128)(2,1)S(1)}, u32[]{:S(2)}, u32[]{:S(2)}) collective-permute-start(bf16[1,272,512]{2,1,0:T(8,128)(2,1)} %get-tuple-element.221), channel_id=1, source_target_pairs={{0,1},{1,0},{2,3},{3,2},{4,5},{5,4},{6,7},{7,6},{8,9},{9,8},{10,11... | collective-permute-start | bytes 835592 | tf_op jit(solution)/shard_map/ppermute | solution.py:496
  187.1 30.1 %collective-permute-start.20 = (bf16[2,256,512]{2,1,0:T(8,128)(2,1)S(1)}, bf16[2,256,512]{2,1,0:T(8,128)(2,1)S(1)}, u32[]{:S(2)}, u32[]{:S(2)}) collective-permute-start(bf16[2,256,512]{2,1,0:T(8,128)(2,1)S(1)} %copy-done.2), channel_id=1, source_target_pairs={{0,1},{1,0},{2,3},{3,2},{4,5},{5,4},{6,7},{7,6},{8,9},{9,8},{10,11... | collective-permute-start | bytes 1572872 | tf_op jit(solution)/shard_map/ppermute | solution.py:496
  187.4 29.8 %collective-permute-start.21 = (bf16[256,512]{1,0:T(8,128)(2,1)S(1)}, bf16[256,512]{1,0:T(8,128)(2,1)S(1)}, u32[]{:S(2)}, u32[]{:S(2)}) collective-permute-start(bf16[256,512]{1,0:T(8,128)(2,1)S(1)} %copy-done.6), channel_id=1, source_target_pairs={{0,2},{1,3},{2,0},{3,1},{4,6},{5,7},{6,4},{7,5},{8,10},{9,11},{10,... | collective-permute-start | bytes 786440 | tf_op jit(solution)/shard_map/ppermute | solution.py:496
  189.3 28.0 %collective-permute-start.22 = (bf16[256,512]{1,0:T(8,128)(2,1)S(1)}, bf16[256,512]{1,0:T(8,128)(2,1)S(1)}, u32[]{:S(2)}, u32[]{:S(2)}) collective-permute-start(bf16[256,512]{1,0:T(8,128)(2,1)S(1)} %copy-done.4), channel_id=1, source_target_pairs={{0,3},{1,2},{2,1},{3,0},{4,7},{5,6},{6,5},{7,4},{8,11},{9,10},{10,... | collective-permute-start | bytes 786440 | tf_op jit(solution)/shard_map/ppermute | solution.py:496
  193.6 6.9 %collective-permute-start.4 = (bf16[256,512]{1,0:T(8,128)(2,1)S(1)}, bf16[256,512]{1,0:T(8,128)(2,1)S(1)}, u32[]{:S(2)}, u32[]{:S(2)}) collective-permute-start(bf16[256,512]{1,0:T(8,128)(2,1)S(1)} %get-tuple-element.97.mine), channel_id=1, source_target_pairs={{0,8},{4,20},{8,0},{12,28},{16,24},{20,4},{24,16},{28,12},{1,9},{5... | collective-permute-start | bytes 786440 | tf_op jit(solution)/shard_map/cond/branch_1_fun/ppermute | solution.py:507
  201.1 9.2 %collective-permute-start.5 = (bf16[512,512]{1,0:T(8,128)(2,1)S(1)}, bf16[512,512]{1,0:T(8,128)(2,1)S(1)}, u32[]{:S(2)}, u32[]{:S(2)}) collective-permute-start(bf16[512,512]{1,0:T(8,128)(2,1)S(1)} %bitcast.12), channel_id=1, source_target_pairs={{0,16},{4,12},{8,24},{12,4},{16,0},{20,28},{24,8},{28,20},{1,17},{... | collective-permute-start | bytes 1572872 | tf_op jit(solution)/shard_map/cond/branch_1_fun/ppermute | solution.py:507
  (15 other events, 98.5 us)

commit v7 on v6

--- a/solution.py
+++ b/solution.py
@@ -132,7 +132,7 @@
 def count_call(at, packed, features, cotangent, base, size, counts):
     nodes, width = features.shape
     slots = packed.shape[1] // 8
-    rows = 2 * LANES
+    rows = 4 * LANES
     steps = size // rows
     half = steps // 2
 
@@ -574,7 +574,7 @@
     backs = []
     for index, (_, _, level, near, far, cross) in enumerate(sides):
         if index == 0:
-            far, cross, near = tie(far, parts[-1][2]), tie(cross, parts[-1][3]), tie(near, parts[-1][2])
+            far, cross, near = tie(far, parts[-1][2]), tie(cross, parts[-1][3]), tie(near, parts[-1][3])
         if index == 1:
             terms = always(fold_terms, parts, [tie(grad, *backs[0][1:]) for grad in grads])
             near = tie(near, *backs[0][1:], grads[-1])

time: 223 us -> 223 us (level)
  waiting for transfers between devices: 89.7 us -> 93.2 us
  starting transfers between devices: 38.7 us -> 35.6 us
    ppermute x17, waiting for transfers between devices: 58.1 us -> 61.5 us  [across(): return lax.ppermute(value, 'mp', [(i, i ^ code) for i in range(mp_count)])]
    ppermute x17, starting transfers between devices: 29.3 us -> 26.2 us  [across(): return lax.ppermute(value, 'mp', [(i, i ^ code) for i in range(mp_count)])]
where the time goes in v7:
time: 223 us; the launch traced here: 222 us
  waiting for transfers between devices  93.2 us (42%)
  Pallas kernels  70.3 us (32%)
  starting transfers between devices  35.6 us (16%)
  blocking collectives  18 us (8%)
  local copies, waits for them, and re-layouts  2.43 us (1%)
    pallas_call x19, Pallas kernels, call(): pl.pallas_call(kernel, grid_spec=pltpu.PrefetchScalarGridSpec(num_scalar_...  70.3 us
    ppermute x17, waiting for transfers between devices, across(): return lax.ppermute(value, 'mp', [(i, i ^ code) for i in range(mp_count)])  61.5 us
    ppermute x6, waiting for transfers between devices, along(): lax.ppermute(value, 'dp', [(i, i ^ 1 << orders[stage][i % 2]) for i in ra...  31.7 us
    ppermute x17, starting transfers between devices, across(): return lax.ppermute(value, 'mp', [(i, i ^ code) for i in range(mp_count)])  26.2 us
    all_to_all x3, blocking collectives, swap(): return lax.all_to_all(value, 'dp', 0, 0, axis_index_groups=pairs)  18 us
    ppermute x6, starting transfers between devices, along(): lax.ppermute(value, 'dp', [(i, i ^ 1 << orders[stage][i % 2]) for i in ra...  9.38 us
  transfers between devices with their start and end apart: 23, of which 11 were waited for; matrix products, arithmetic and copies ran while one was open for 1% of the time, Pallas kernels for 29%

profile of v7, /device:TPU:0, one launch (start us, length us, event | category | flops | bytes accessed | tf_op | source)
XLA Modules:
  0.0 222.1 jit_solution(5043127540879062180)
XLA Ops:
  2.3 3.1 %collective-permute-start.6 = (bf16[272,512]{1,0:T(8,128)(2,1)S(1)}, bf16[272,512]{1,0:T(8,128)(2,1)}, u32[]{:S(2)}, u32[]{:S(2)}) collective-permute-start(bf16[272,512]{1,0:T(8,128)(2,1)S(1)} %weight_piece.1.bias_own), channel_id=1, source_target_pairs={{0,1},{1,0},{2,3},{3,2},{4,5},{5,4},{6,7},{7,6},{8,9},{9,8},{10,11... | collective-permute-start | bytes 835592 | tf_op jit(solution)/shard_map/ppermute | solution.py:496
  6.1 9.2 %count_and_aggregate.3 = (bf16[2048,2048]{1,0:T(8,128)(2,1)S(1)}, bf16[512,512]{1,0:T(8,128)(2,1)}, bf16[512,512]{1,0:T(8,128)(2,1)S(1)}, bf16[2,512,512]{2,1,0:T(8,128)(2,1)}, f32[512,1]{1,0:T(8,128)S(1)}) custom-call(s32[4]{0:T(128)S(1)} %pad_add_fusion.at, s32[256,256]{1,0:T(8,128)S(1)} %reshape.28.packed_ref, bf16[2048,512]{1,0:T(8,128)(2,1)} %feat_ref.1, ...), custom_call_target="tpu_custom_call" | custom-call | flops 1 | bytes 1 | tf_op jit(solution)/shard_map/count_and_aggregate/pallas_call | solution.py:43
  15.3 4.0 %collective-permute-start.7 = (bf16[512,512]{1,0:T(8,128)(2,1)S(1)}, bf16[512,512]{1,0:T(8,128)(2,1)}, u32[]{:S(2)}, u32[]{:S(2)}) collective-permute-start(bf16[512,512]{1,0:T(8,128)(2,1)S(1)} %get-tuple-element.183), channel_id=1, source_target_pairs={{0,3},{1,2},{2,1},{3,0},{4,7},{5,6},{6,5},{7,4},{8,11},{9,10},{10,... | collective-permute-start | bytes 1572872 | tf_op jit(solution)/shard_map/ppermute | solution.py:496
  20.0 26.9 %conditional.3 = (bf16[2048,512]{1,0:T(8,128)(2,1)S(1)}, bf16[2048,2048]{1,0:T(8,128)(2,1)S(1)}, bf16[512,512]{1,0:T(8,128)(2,1)S(1)}, bf16[512,512]{1,0:T(8,128...) conditional(s32[]{:T(128)} %bitcast.10, () %tuple.55, (bf16[272,512]{1,0:T(8,128)(2,1)}, ...), branch_computations={%region_0.1_spmd, %region_1.2_spmd} | conditional | flops 3 | bytes 12585022 | solution.py:534
  23.3 7.7 %count_and_aggregate.2 = (bf16[2048,2048]{1,0:T(8,128)(2,1)S(1)}, bf16[512,512]{1,0:T(8,128)(2,1)S(1)}, bf16[512,512]{1,0:T(8,128)(2,1)S(1)}, bf16[2,512,512]{2,1,0:T(8,128)(2,1)}, f32[512,1]{1,0:T(8,128)S(1)}) custom-call(s32[4]{0:T(128)S(1)} %get-tuple-element.66.at, s32[256,256]{1,0:T(8,128)} %copy-done.12, ...), custom_call_target="tpu_custom_call", output_to_operand_aliasing={{0}: (4, {})} | custom-call | flops 1 | bytes 1 | tf_op jit(solution)/shard_map/cond/branch_1_fun/count_and_aggregate/pallas_call | solution.py:43
  33.1 7.7 %collective-permute-done.1.theirs = bf16[512,512]{1,0:T(8,128)(2,1)S(1)} collective-permute-done((bf16[512,512]{1,0:T(8,128)(2,1)S(1)}, bf16[512,512]{1,0:T(8,128)(2,1)S(1)}, u32[]{:S(2)}, u32[]{:S(2)}) %collective-permute-start.1) | collective-permute-done | bytes 524320 | tf_op jit(solution)/shard_map/cond/branch_1_fun/ppermute | solution.py:507
  41.5 5.4 %all_to_all.12 = bf16[2,1024,512]{2,1,0:T(8,128)(2,1)S(1)} all-to-all(bf16[2,1024,512]{2,1,0:T(8,128)(2,1)S(1)} %join_halves.5), channel_id=1, replica_groups={{0,4},{8,12},{16,20},{24,28},{1,5},{9,13},{17,21},{25,29},{2,6},{10,14}..., dimensions={0} | all-to-all | bytes 4194304 | tf_op jit(solution)/shard_map/cond/branch_1_fun/all_to_all | solution.py:504
  46.9 8.0 %collective-permute-done.7.part3 = bf16[512,512]{1,0:T(8,128)(2,1)} collective-permute-done((bf16[512,512]{1,0:T(8,128)(2,1)S(1)}, bf16[512,512]{1,0:T(8,128)(2,1)}, u32[]{:S(2)}, u32[]{:S(2)}) %collective-permute-start.7) | collective-permute-done | bytes 524320 | tf_op jit(solution)/shard_map/ppermute | solution.py:496
  54.9 9.2 %collective-permute-done.11.near = bf16[2,512,512]{2,1,0:T(8,128)(2,1)} collective-permute-done((bf16[2,512,512]{2,1,0:T(8,128)(2,1)}, bf16[2,512,512]{2,1,0:T(8,128)(2,1)}, u32[]{:S(2)}, u32[]{:S(2)}) %collective-permute-start.11) | collective-permute-done | bytes 1048608 | tf_op jit(solution)/shard_map/ppermute | solution.py:496
  66.0 5.5 %linear_and_slope.5 = (bf16[256,512]{1,0:T(8,128)(2,1)}, bf16[2,256,512]{2,1,0:T(8,128)(2,1)}, bf16[256,512]{1,0:T(8,128)(2,1)}, bf16[2,256,512]{2,1,0:T(8,128)(...) custom-call(s32[4]{0:T(128)S(1)} %pad_add_fusion.at, s32[1]{0:T(128)S(6)} %copy.52.live, ...), custom_call_target="tpu_custom_call" | custom-call | flops 1 | bytes 1 | tf_op jit(solution)/shard_map/linear_and_slope/pallas_call | solution.py:43
  71.5 28.3 %collective-permute-done.12.part3 = bf16[512,512]{1,0:T(8,128)(2,1)S(1)} collective-permute-done((bf16[512,512]{1,0:T(8,128)(2,1)S(1)}, bf16[512,512]{1,0:T(8,128)(2,1)S(1)}, u32[]{:S(2)}, u32[]{:S(2)}) %collective-permute-start.12) | collective-permute-done | bytes 524320 | tf_op jit(solution)/shard_map/ppermute | solution.py:496
  99.8 6.7 %collective-permute-done.10.part2 = bf16[512,512]{1,0:T(8,128)(2,1)S(1)} collective-permute-done((bf16[512,512]{1,0:T(8,128)(2,1)S(1)}, bf16[512,512]{1,0:T(8,128)(2,1)S(1)}, u32[]{:S(2)}, u32[]{:S(2)}) %collective-permute-start.10) | collective-permute-done | bytes 524320 | tf_op jit(solution)/shard_map/ppermute | solution.py:496
  106.5 3.4 %collective-permute-start.14 = (bf16[256,512]{1,0:T(8,128)(2,1)S(1)}, bf16[256,512]{1,0:T(8,128)(2,1)S(1)}, u32[]{:S(2)}, u32[]{:S(2)}) collective-permute-start(bf16[256,512]{1,0:T(8,128)(2,1)S(1)} %get-tuple-element.202), channel_id=1, source_target_pairs={{0,2},{1,3},{2,0},{3,1},{4,6},{5,7},{6,4},{7,5},{8,10},{9,11},{10,... | collective-permute-start | bytes 786440 | tf_op jit(solution)/shard_map/ppermute | solution.py:496
  109.9 4.0 %collective-permute-start.15 = (bf16[256,512]{1,0:T(8,128)(2,1)S(1)}, bf16[256,512]{1,0:T(8,128)(2,1)S(1)}, u32[]{:S(2)}, u32[]{:S(2)}) collective-permute-start(bf16[256,512]{1,0:T(8,128)(2,1)S(1)} %get-tuple-element.204), channel_id=1, source_target_pairs={{0,3},{1,2},{2,1},{3,0},{4,7},{5,6},{6,5},{7,4},{8,11},{9,10},{10,... | collective-permute-start | bytes 786440 | tf_op jit(solution)/shard_map/ppermute | solution.py:496
  113.9 5.6 %linear_and_slope.6 = (bf16[512,512]{1,0:T(8,128)(2,1)S(1)}, bf16[2,512,512]{2,1,0:T(8,128)(2,1)S(1)}, bf16[512,512]{1,0:T(8,128)(2,1)S(1)}, bf16[2,512,512]{2,1...) custom-call(s32[4]{0:T(128)S(1)} %pad_add_fusion.at, s32[1]{0:T(128)S(6)} %copy.52.live, ...), custom_call_target="tpu_custom_call" | custom-call | flops 1 | bytes 1 | tf_op jit(solution)/shard_map/linear_and_slope/pallas_call | solution.py:43
  119.5 4.7 %linear_and_slope.4 = (bf16[256,512]{1,0:T(8,128)(2,1)S(1)}, bf16[2,256,512]{2,1,0:T(8,128)(2,1)}, bf16[256,512]{1,0:T(8,128)(2,1)S(1)}, bf16[2,256,512]{2,1,0:T...) custom-call(s32[4]{0:T(128)S(1)} %pad_add_fusion.at, s32[1]{0:T(128)S(6)} %copy.52.live, ...), custom_call_target="tpu_custom_call" | custom-call | flops 1 | bytes 1 | tf_op jit(solution)/shard_map/linear_and_slope/pallas_call | solution.py:43
  124.2 5.0 %linear_and_slope.7 = (bf16[512,512]{1,0:T(8,128)(2,1)S(1)}, bf16[2,512,512]{2,1,0:T(8,128)(2,1)S(1)}, bf16[512,512]{1,0:T(8,128)(2,1)S(1)}, bf16[2,512,512]{2,1...) custom-call(s32[4]{0:T(128)S(1)} %pad_add_fusion.at, ...), custom_call_target="tpu_custom_call", output_to_operand_aliasing={{0}: (12, {}), {1}: (13, {}), {2}: (14, {}), {3}: (15, {}),... | custom-call | flops 1 | bytes 1 | tf_op jit(solution)/shard_map/linear_and_slope/pallas_call | solution.py:43
  129.3 2.8 %collective-permute-done.15 = bf16[256,512]{1,0:T(8,128)(2,1)S(1)} collective-permute-done((bf16[256,512]{1,0:T(8,128)(2,1)S(1)}, bf16[256,512]{1,0:T(8,128)(2,1)S(1)}, u32[]{:S(2)}, u32[]{:S(2)}) %collective-permute-start.15) | collective-permute-done | bytes 262176 | tf_op jit(solution)/shard_map/ppermute | solution.py:496
  133.7 2.9 %collective-permute-start.18 = (bf16[512,512]{1,0:T(8,128)(2,1)}, bf16[512,512]{1,0:T(8,128)(2,1)}, u32[]{:S(2)}, u32[]{:S(2)}) collective-permute-start(bf16[512,512]{1,0:T(8,128)(2,1)} %get-tuple-element.220), channel_id=1, source_target_pairs={{0,3},{1,2},{2,1},{3,0},{4,7},{5,6},{6,5},{7,4},{8,11},{9,10},{10,... | collective-permute-start | bytes 1572872 | tf_op jit(solution)/shard_map/ppermute | solution.py:496
  136.6 42.4 %conditional.4 = ((bf16[1,272,512]{2,1,0:T(8,128)(2,1)}, bf16[1,272,512]{2,1,0:T(8,128)(2,1)})) conditional(s32[]{:T(128)} %bitcast.10, () %tuple.64, (s32[4]{0:T(128)S(1)}, bf16[512,512]{1,0:T(8,128)(2,1)}, bf16[2,512,512]{2,1,0:T(8,128)(2,1)}, bf16[512,512]{1,0:T(8,128)(2,1)}, bf16[512,512]{1,0:T(8,128)(2,1)}, ...), branch_computations={%region_2.3_spmd, %region_3.4_spmd} | conditional | flops 4 | bytes 15073372 | solution.py:534
  136.6 7.1 %weight_product.1 = bf16[2,2,1040,512]{3,2,1,0:T(8,128)(2,1)S(1)} custom-call(s32[4]{0:T(128)S(1)} %get-tuple-element.78.at, bf16[512,512]{1,0:T(8,128)(2,1)} %get-tuple-element.79.refs_0_, bf16[2,512,512]{2,1,0:T(8,128)(2,1)} %get-tuple-element.80.refs_1_, bf16[512,512]{1,0:T(8,128)(2,1)} %get-tuple-element.81.refs_2_, ...), custom_call_target="tpu_custom_call" | custom-call | flops 1 | bytes 1 | tf_op jit(solution)/shard_map/cond/branch_1_fun/weight_product/pallas_call | solution.py:43
  143.7 7.2 %all_to_all.13.refs_0_ = bf16[2,2,1040,512]{3,2,1,0:T(8,128)(2,1)S(1)} all-to-all(bf16[2,2,1040,512]{3,2,1,0:T(8,128)(2,1)S(1)} %weight_product.1), channel_id=1, replica_groups={{0,4},{8,12},{16,20},{24,28},{1,5},{9,13},{17,21},{25,29},{2,6},{10,14}..., dimensions={0} | all-to-all | bytes 8519680 | tf_op jit(solution)/shard_map/cond/branch_1_fun/all_to_all | solution.py:504
  153.5 13.6 %collective-permute-done.2.refs_1_ = bf16[2,528,512]{2,1,0:T(8,128)(2,1)S(1)} collective-permute-done((bf16[2,528,512]{2,1,0:T(8,128)(2,1)S(1)}, bf16[2,528,512]{2,1,0:T(8,128)(2,1)S(1)}, u32[]{:S(2)}, u32[]{:S(2)}) %collective-permute-start.2) | collective-permute-done | bytes 1081376 | tf_op jit(solution)/shard_map/cond/branch_1_fun/ppermute | solution.py:507
  169.5 8.0 %collective-permute-done.3.refs_1_ = bf16[2,272,512]{2,1,0:T(8,128)(2,1)S(1)} collective-permute-done((bf16[2,272,512]{2,1,0:T(8,128)(2,1)S(1)}, bf16[2,272,512]{2,1,0:T(8,128)(2,1)S(1)}, u32[]{:S(2)}, u32[]{:S(2)}) %collective-permute-start.3) | collective-permute-done | bytes 557088 | tf_op jit(solution)/shard_map/cond/branch_1_fun/ppermute | solution.py:507
  179.9 6.6 %collective-permute-done.19 = bf16[1,272,512]{2,1,0:T(8,128)(2,1)S(1)} collective-permute-done((bf16[1,272,512]{2,1,0:T(8,128)(2,1)}, bf16[1,272,512]{2,1,0:T(8,128)(2,1)S(1)}, u32[]{:S(2)}, u32[]{:S(2)}) %collective-permute-start.19) | collective-permute-done | bytes 278560 | tf_op jit(solution)/shard_map/ppermute | solution.py:496
  188.7 2.2 %collective-permute-start.22 = (bf16[256,512]{1,0:T(8,128)(2,1)S(1)}, bf16[256,512]{1,0:T(8,128)(2,1)S(1)}, u32[]{:S(2)}, u32[]{:S(2)}) collective-permute-start(bf16[256,512]{1,0:T(8,128)(2,1)S(1)} %copy-done.4), channel_id=1, source_target_pairs={{0,3},{1,2},{2,1},{3,0},{4,7},{5,6},{6,5},{7,4},{8,11},{9,10},{10,... | collective-permute-start | bytes 786440 | tf_op jit(solution)/shard_map/ppermute | solution.py:496
  190.9 25.8 %conditional.5 = (f32[2048,512]{1,0:T(8,128)S(1)}, f32[2048,512]{1,0:T(8,128)S(1)}, bf16[2048,512]{1,0:T(8,128)(2,1)}, f32[512]{0:T(512)}) conditional(s32[]{:T(128)} %bitcast.10, () %tuple.78, (s32[4]{0:T(128)S(1)}, bf16[1,272,512]{2,1,0:T(8,128)(2,1)}, bf16[1,272,512]{2,1,0:T(8,128)(2,1)S(1)}, bf16[256,512]{1,0:T(8,128)(2,1)}, ...), branch_computations={%region_4.5_spmd, %region_5.6_spmd} | conditional | flops 1048581 | bytes 53971776 | solution.py:534
  194.5 3.3 %place_rows.1 = bf16[2048,512]{1,0:T(8,128)(2,1)} custom-call(s32[4]{0:T(128)S(1)} %get-tuple-element.94.at, bf16[256,512]{1,0:T(8,128)(2,1)} %get-tuple-element.98.refs_0_, bf16[2,256,512]{2,1,0:T(8,128)(2,1)} %get-tuple-element.99.refs_1_.refs_7_, bf16[512,512]{1,0:T(8,128)(2,1)} %get-tuple-element.100.refs_2_, ...), custom_call_target="tpu_custom_call" | custom-call | flops 1 | bytes 9000000 | tf_op jit(solution)/shard_map/cond/branch_1_fun/place_rows/pallas_call | solution.py:43
  197.9 2.1 collective-permute-done.4.theirs
  202.2 7.4 %spread_back.2 = f32[2048,512]{1,0:T(8,128)S(1)} custom-call(s32[4]{0:T(128)S(1)} %get-tuple-element.94.at, bf16[2048,2048]{1,0:T(8,128)(2,1)} %get-tuple-element.103.refs_0_.refs_1_.refs_2_.refs_3_.refs_4_.refs_5_, bf16[2048,2048]{1,0:T(8,128)(2,1)} %get-tuple-element.103.refs_0_.refs_1_.refs_2_.refs_3_.refs_4_.refs_5_, ...), custom_call_target="tpu_custom_call" | custom-call | flops 1 | bytes 24000000 | tf_op jit(solution)/shard_map/cond/branch_1_fun/spread_back/pallas_call | solution.py:43
  210.6 5.4 %all_to_all.14 = bf16[2,1024,512]{2,1,0:T(8,128)(2,1)S(1)} all-to-all(bf16[2,1024,512]{2,1,0:T(8,128)(2,1)S(1)} %join_halves.7), channel_id=1, replica_groups={{0,4},{8,12},{16,20},{24,28},{1,5},{9,13},{17,21},{25,29},{2,6},{10,14}..., dimensions={0} | all-to-all | bytes 4194304 | tf_op jit(solution)/shard_map/cond/branch_1_fun/all_to_all | solution.py:504
  216.8 5.3 %spread_back.3 = (bf16[2048,512]{1,0:T(8,128)(2,1)}, bf16[2048,512]{1,0:T(8,128)(2,1)}) custom-call(s32[4]{0:T(128)S(1)} %pad_add_fusion.at, bf16[2048,2048]{1,0:T(8,128)(2,1)} %copy-done.7, bf16[2048,2048]{1,0:T(8,128)(2,1)} %copy-done.7, bf16[256,512]{1,0:T(8,128)(2,1)S(1)} %get-tuple-element.194.refs_2_, ...), custom_call_target="tpu_custom_call", output_to_operand_aliasing={{1}: (9, {})} | custom-call | flops 1 | bytes 24000000 | tf_op jit(solution)/shard_map/spread_back/pallas_call | solution.py:43
  (92 shorter events, 29.0 us)
Async XLA Ops:
  2.3 12.9 %collective-permute-start.6 = (bf16[272,512]{1,0:T(8,128)(2,1)S(1)}, bf16[272,512]{1,0:T(8,128)(2,1)}, u32[]{:S(2)}, u32[]{:S(2)}) collective-permute-start(bf16[272,512]{1,0:T(8,128)(2,1)S(1)} %weight_piece.1.bias_own), channel_id=1, source_target_pairs={{0,1},{1,0},{2,3},{3,2},{4,5},{5,4},{6,7},{7,6},{8,9},{9,8},{10,11... | collective-permute-start | bytes 835592 | tf_op jit(solution)/shard_map/ppermute | solution.py:496
  6.0 13.9 %copy-start.8 = (bf16[2048,512]{1,0:T(8,128)(2,1)S(1)}, bf16[2048,512]{1,0:T(8,128)(2,1)}, u32[]{:S(2)}) copy-start(bf16[2048,512]{1,0:T(8,128)(2,1)} %cot_own.7) | copy-start | bytes 6291460
  6.1 13.9 %copy-start.10 = (bf16[2048,512]{1,0:T(8,128)(2,1)S(1)}, bf16[2048,512]{1,0:T(8,128)(2,1)}, u32[]{:S(2)}) copy-start(bf16[2048,512]{1,0:T(8,128)(2,1)} %feat_ref.1) | copy-start | bytes 6291460
  15.2 48.9 %collective-permute-start.11 = (bf16[2,512,512]{2,1,0:T(8,128)(2,1)}, bf16[2,512,512]{2,1,0:T(8,128)(2,1)}, u32[]{:S(2)}, u32[]{:S(2)}) collective-permute-start(bf16[2,512,512]{2,1,0:T(8,128)(2,1)} %get-tuple-element.190), channel_id=1, source_target_pairs={{0,1},{1,0},{2,3},{3,2},{4,5},{5,4},{6,7},{7,6},{8,9},{9,8},{10,11... | collective-permute-start | bytes 3145736 | tf_op jit(solution)/shard_map/ppermute | solution.py:496
  15.3 39.7 %collective-permute-start.7 = (bf16[512,512]{1,0:T(8,128)(2,1)S(1)}, bf16[512,512]{1,0:T(8,128)(2,1)}, u32[]{:S(2)}, u32[]{:S(2)}) collective-permute-start(bf16[512,512]{1,0:T(8,128)(2,1)S(1)} %get-tuple-element.183), channel_id=1, source_target_pairs={{0,3},{1,2},{2,1},{3,0},{4,7},{5,6},{6,5},{7,4},{8,11},{9,10},{10,... | collective-permute-start | bytes 1572872 | tf_op jit(solution)/shard_map/ppermute | solution.py:496
  19.3 46.7 %collective-permute-start.9 = (bf16[512,512]{1,0:T(8,128)(2,1)}, bf16[512,512]{1,0:T(8,128)(2,1)}, u32[]{:S(2)}, u32[]{:S(2)}) collective-permute-start(bf16[512,512]{1,0:T(8,128)(2,1)} %get-tuple-element.186.part0), channel_id=1, source_target_pairs={{0,2},{1,3},{2,0},{3,1},{4,6},{5,7},{6,4},{7,5},{8,10},{9,11},{10,... | collective-permute-start | bytes 1572872 | tf_op jit(solution)/shard_map/ppermute | solution.py:496
  20.0 46.1 %copy-start = (bf16[2048,512]{1,0:T(8,128)(2,1)S(1)}, bf16[2048,512]{1,0:T(8,128)(2,1)}, u32[]{:S(2)}) copy-start(bf16[2048,512]{1,0:T(8,128)(2,1)} %weight_own.7) | copy-start | bytes 6291460
  21.7 9.2 %collective-permute-start = (bf16[256,512]{1,0:T(8,128)(2,1)S(1)}, bf16[256,512]{1,0:T(8,128)(2,1)S(1)}, u32[]{:S(2)}, u32[]{:S(2)}) collective-permute-start(bf16[256,512]{1,0:T(8,128)(2,1)S(1)} %slice.2.mine), channel_id=1, source_target_pairs={{0,8},{4,20},{8,0},{12,28},{16,24},{20,4},{24,16},{28,12},{1,9},{5... | collective-permute-start | bytes 786440 | tf_op jit(solution)/shard_map/cond/branch_1_fun/ppermute | solution.py:507
  31.5 9.2 %collective-permute-start.1 = (bf16[512,512]{1,0:T(8,128)(2,1)S(1)}, bf16[512,512]{1,0:T(8,128)(2,1)S(1)}, u32[]{:S(2)}, u32[]{:S(2)}) collective-permute-start(bf16[512,512]{1,0:T(8,128)(2,1)S(1)} %bitcast.14), channel_id=1, source_target_pairs={{0,16},{4,12},{8,24},{12,4},{16,0},{20,28},{24,8},{28,20},{1,17},{... | collective-permute-start | bytes 1572872 | tf_op jit(solution)/shard_map/cond/branch_1_fun/ppermute | solution.py:507
  46.9 24.6 %copy-start.7 = (bf16[2048,2048]{1,0:T(8,128)(2,1)}, bf16[2048,2048]{1,0:T(8,128)(2,1)S(1)}, u32[]{:S(2)}) copy-start(bf16[2048,2048]{1,0:T(8,128)(2,1)S(1)} %get-tuple-element.179.refs_0_.refs_1_) | copy-start | bytes 25165828
  54.9 64.6 %collective-permute-start.8 = (bf16[2,512,512]{2,1,0:T(8,128)(2,1)}, bf16[2,512,512]{2,1,0:T(8,128)(2,1)S(1)}, u32[]{:S(2)}, u32[]{:S(2)}) collective-permute-start(bf16[2,512,512]{2,1,0:T(8,128)(2,1)} %get-tuple-element.184), channel_id=1, source_target_pairs={{0,1},{1,0},{2,3},{3,2},{4,5},{5,4},{6,7},{7,6},{8,9},{9,8},{10,11... | collective-permute-start | bytes 3145736 | tf_op jit(solution)/shard_map/ppermute | solution.py:496
  64.1 35.7 %collective-permute-start.12 = (bf16[512,512]{1,0:T(8,128)(2,1)S(1)}, bf16[512,512]{1,0:T(8,128)(2,1)S(1)}, u32[]{:S(2)}, u32[]{:S(2)}) collective-permute-start(bf16[512,512]{1,0:T(8,128)(2,1)S(1)} %get-tuple-element.191), channel_id=1, source_target_pairs={{0,3},{1,2},{2,1},{3,0},{4,7},{5,6},{6,5},{7,4},{8,11},{9,10},{10,... | collective-permute-start | bytes 1572872 | tf_op jit(solution)/shard_map/ppermute | solution.py:496
  66.0 40.5 %collective-permute-start.10 = (bf16[512,512]{1,0:T(8,128)(2,1)S(1)}, bf16[512,512]{1,0:T(8,128)(2,1)S(1)}, u32[]{:S(2)}, u32[]{:S(2)}) collective-permute-start(bf16[512,512]{1,0:T(8,128)(2,1)S(1)} %get-tuple-element.187.part0), channel_id=1, source_target_pairs={{0,2},{1,3},{2,0},{3,1},{4,6},{5,7},{6,4},{7,5},{8,10},{9,11},{10,... | collective-permute-start | bytes 1572872 | tf_op jit(solution)/shard_map/ppermute | solution.py:496
  66.0 47.9 %copy-start.9 = (bf16[2048,512]{1,0:T(8,128)(2,1)S(1)}, bf16[2048,512]{1,0:T(8,128)(2,1)}, u32[]{:S(2)}) copy-start(bf16[2048,512]{1,0:T(8,128)(2,1)} %cot_own.7) | copy-start | bytes 6291460
  99.8 32.3 %collective-permute-start.13 = (bf16[2,256,512]{2,1,0:T(8,128)(2,1)S(1)}, bf16[2,256,512]{2,1,0:T(8,128)(2,1)S(1)}, u32[]{:S(2)}, u32[]{:S(2)}) collective-permute-start(bf16[2,256,512]{2,1,0:T(8,128)(2,1)S(1)} %get-tuple-element.200), channel_id=1, source_target_pairs={{0,1},{1,0},{2,3},{3,2},{4,5},{5,4},{6,7},{7,6},{8,9},{9,8},{10,11... | collective-permute-start | bytes 1572872 | tf_op jit(solution)/shard_map/ppermute | solution.py:496
  106.5 22.8 %collective-permute-start.14 = (bf16[256,512]{1,0:T(8,128)(2,1)S(1)}, bf16[256,512]{1,0:T(8,128)(2,1)S(1)}, u32[]{:S(2)}, u32[]{:S(2)}) collective-permute-start(bf16[256,512]{1,0:T(8,128)(2,1)S(1)} %get-tuple-element.202), channel_id=1, source_target_pairs={{0,2},{1,3},{2,0},{3,1},{4,6},{5,7},{6,4},{7,5},{8,10},{9,11},{10,... | collective-permute-start | bytes 786440 | tf_op jit(solution)/shard_map/ppermute | solution.py:496
  109.9 22.2 %collective-permute-start.15 = (bf16[256,512]{1,0:T(8,128)(2,1)S(1)}, bf16[256,512]{1,0:T(8,128)(2,1)S(1)}, u32[]{:S(2)}, u32[]{:S(2)}) collective-permute-start(bf16[256,512]{1,0:T(8,128)(2,1)S(1)} %get-tuple-element.204), channel_id=1, source_target_pairs={{0,3},{1,2},{2,1},{3,0},{4,7},{5,6},{6,5},{7,4},{8,11},{9,10},{10,... | collective-permute-start | bytes 786440 | tf_op jit(solution)/shard_map/ppermute | solution.py:496
  132.1 46.9 %collective-permute-start.16 = (bf16[2,512,512]{2,1,0:T(8,128)(2,1)}, bf16[2,512,512]{2,1,0:T(8,128)(2,1)}, u32[]{:S(2)}, u32[]{:S(2)}) collective-permute-start(bf16[2,512,512]{2,1,0:T(8,128)(2,1)} %get-tuple-element.218), channel_id=1, source_target_pairs={{0,1},{1,0},{2,3},{3,2},{4,5},{5,4},{6,7},{7,6},{8,9},{9,8},{10,11... | collective-permute-start | bytes 3145736 | tf_op jit(solution)/shard_map/ppermute | solution.py:496
  132.9 46.0 %collective-permute-start.17 = (bf16[512,512]{1,0:T(8,128)(2,1)S(1)}, bf16[512,512]{1,0:T(8,128)(2,1)}, u32[]{:S(2)}, u32[]{:S(2)}) collective-permute-start(bf16[512,512]{1,0:T(8,128)(2,1)S(1)} %get-tuple-element.219), channel_id=1, source_target_pairs={{0,2},{1,3},{2,0},{3,1},{4,6},{5,7},{6,4},{7,5},{8,10},{9,11},{10,... | collective-permute-start | bytes 1572872 | tf_op jit(solution)/shard_map/ppermute | solution.py:496
  133.7 45.3 %collective-permute-start.18 = (bf16[512,512]{1,0:T(8,128)(2,1)}, bf16[512,512]{1,0:T(8,128)(2,1)}, u32[]{:S(2)}, u32[]{:S(2)}) collective-permute-start(bf16[512,512]{1,0:T(8,128)(2,1)} %get-tuple-element.220), channel_id=1, source_target_pairs={{0,3},{1,2},{2,1},{3,0},{4,7},{5,6},{6,5},{7,4},{8,11},{9,10},{10,... | collective-permute-start | bytes 1572872 | tf_op jit(solution)/shard_map/ppermute | solution.py:496
  136.5 50.0 %copy-start.2 = (bf16[2,256,512]{2,1,0:T(8,128)(2,1)S(1)}, bf16[2,256,512]{2,1,0:T(8,128)(2,1)}, u32[]{:S(2)}) copy-start(bf16[2,256,512]{2,1,0:T(8,128)(2,1)} %copy-done.1) | copy-start | bytes 1572868
  136.5 50.3 %copy-start.6 = (bf16[256,512]{1,0:T(8,128)(2,1)S(1)}, bf16[256,512]{1,0:T(8,128)(2,1)}, u32[]{:S(2)}) copy-start(bf16[256,512]{1,0:T(8,128)(2,1)} %copy-done.5) | copy-start | bytes 786436
  136.5 52.1 %copy-start.4 = (bf16[256,512]{1,0:T(8,128)(2,1)S(1)}, bf16[256,512]{1,0:T(8,128)(2,1)}, u32[]{:S(2)}) copy-start(bf16[256,512]{1,0:T(8,128)(2,1)} %copy-done.3) | copy-start | bytes 786436
  151.9 15.2 %collective-permute-start.2 = (bf16[2,528,512]{2,1,0:T(8,128)(2,1)S(1)}, bf16[2,528,512]{2,1,0:T(8,128)(2,1)S(1)}, u32[]{:S(2)}, u32[]{:S(2)}) collective-permute-start(bf16[2,528,512]{2,1,0:T(8,128)(2,1)S(1)} %get-tuple-element.91), channel_id=1, source_target_pairs={{0,16},{4,12},{8,24},{12,4},{16,0},{20,28},{24,8},{28,20},{1,17},{... | collective-permute-start | bytes 3244040 | tf_op jit(solution)/shard_map/cond/branch_1_fun/ppermute | solution.py:507
  168.0 9.6 %collective-permute-start.3 = (bf16[2,272,512]{2,1,0:T(8,128)(2,1)S(1)}, bf16[2,272,512]{2,1,0:T(8,128)(2,1)S(1)}, u32[]{:S(2)}, u32[]{:S(2)}) collective-permute-start(bf16[2,272,512]{2,1,0:T(8,128)(2,1)S(1)} %get-tuple-element.93), channel_id=1, source_target_pairs={{0,8},{4,20},{8,0},{12,28},{16,24},{20,4},{24,16},{28,12},{1,9},{5... | collective-permute-start | bytes 1671176 | tf_op jit(solution)/shard_map/cond/branch_1_fun/ppermute | solution.py:507
  179.0 7.5 %collective-permute-start.19 = (bf16[1,272,512]{2,1,0:T(8,128)(2,1)}, bf16[1,272,512]{2,1,0:T(8,128)(2,1)S(1)}, u32[]{:S(2)}, u32[]{:S(2)}) collective-permute-start(bf16[1,272,512]{2,1,0:T(8,128)(2,1)} %get-tuple-element.221), channel_id=1, source_target_pairs={{0,1},{1,0},{2,3},{3,2},{4,5},{5,4},{6,7},{7,6},{8,9},{9,8},{10,11... | collective-permute-start | bytes 835592 | tf_op jit(solution)/shard_map/ppermute | solution.py:496
  186.5 30.2 %collective-permute-start.20 = (bf16[2,256,512]{2,1,0:T(8,128)(2,1)S(1)}, bf16[2,256,512]{2,1,0:T(8,128)(2,1)S(1)}, u32[]{:S(2)}, u32[]{:S(2)}) collective-permute-start(bf16[2,256,512]{2,1,0:T(8,128)(2,1)S(1)} %copy-done.2), channel_id=1, source_target_pairs={{0,1},{1,0},{2,3},{3,2},{4,5},{5,4},{6,7},{7,6},{8,9},{9,8},{10,11... | collective-permute-start | bytes 1572872 | tf_op jit(solution)/shard_map/ppermute | solution.py:496
  186.8 29.9 %collective-permute-start.21 = (bf16[256,512]{1,0:T(8,128)(2,1)S(1)}, bf16[256,512]{1,0:T(8,128)(2,1)S(1)}, u32[]{:S(2)}, u32[]{:S(2)}) collective-permute-start(bf16[256,512]{1,0:T(8,128)(2,1)S(1)} %copy-done.6), channel_id=1, source_target_pairs={{0,2},{1,3},{2,0},{3,1},{4,6},{5,7},{6,4},{7,5},{8,10},{9,11},{10,... | collective-permute-start | bytes 786440 | tf_op jit(solution)/shard_map/ppermute | solution.py:496
  188.7 28.1 %collective-permute-start.22 = (bf16[256,512]{1,0:T(8,128)(2,1)S(1)}, bf16[256,512]{1,0:T(8,128)(2,1)S(1)}, u32[]{:S(2)}, u32[]{:S(2)}) collective-permute-start(bf16[256,512]{1,0:T(8,128)(2,1)S(1)} %copy-done.4), channel_id=1, source_target_pairs={{0,3},{1,2},{2,1},{3,0},{4,7},{5,6},{6,5},{7,4},{8,11},{9,10},{10,... | collective-permute-start | bytes 786440 | tf_op jit(solution)/shard_map/ppermute | solution.py:496
  193.0 7.0 %collective-permute-start.4 = (bf16[256,512]{1,0:T(8,128)(2,1)S(1)}, bf16[256,512]{1,0:T(8,128)(2,1)S(1)}, u32[]{:S(2)}, u32[]{:S(2)}) collective-permute-start(bf16[256,512]{1,0:T(8,128)(2,1)S(1)} %get-tuple-element.97.mine), channel_id=1, source_target_pairs={{0,8},{4,20},{8,0},{12,28},{16,24},{20,4},{24,16},{28,12},{1,9},{5... | collective-permute-start | bytes 786440 | tf_op jit(solution)/shard_map/cond/branch_1_fun/ppermute | solution.py:507
  194.5 7.6 %copy-start.22 = (bf16[256,512]{1,0:T(8,128)(2,1)S(1)}, bf16[256,512]{1,0:T(8,128)(2,1)}, u32[]{:S(2)}) copy-start(bf16[256,512]{1,0:T(8,128)(2,1)} %get-tuple-element.106.refs_9_) | copy-start | bytes 786436 | tf_op jit(solution)/shard_map/cond
  200.6 9.2 %collective-permute-start.5 = (bf16[512,512]{1,0:T(8,128)(2,1)S(1)}, bf16[512,512]{1,0:T(8,128)(2,1)S(1)}, u32[]{:S(2)}, u32[]{:S(2)}) collective-permute-start(bf16[512,512]{1,0:T(8,128)(2,1)S(1)} %bitcast.12), channel_id=1, source_target_pairs={{0,16},{4,12},{8,24},{12,4},{16,0},{20,28},{24,8},{28,20},{1,17},{... | collective-permute-start | bytes 1572872 | tf_op jit(solution)/shard_map/cond/branch_1_fun/ppermute | solution.py:507
  (15 other events, 87.3 us)

commit v8 on v7

--- a/solution.py
+++ b/solution.py
@@ -565,11 +565,10 @@
             pair = (keep, along(give, stage))
         return part_call(at, pair)
 
-    def share_terms(mine, theirs, counts, backs, outs):
-        share, bias_grad = share_call(at, mine, theirs)
+    def share_terms(share, counts, backs, outs):
         output = place_call(at, RUNS[:-1], [(out, back[1]) for out, back in zip(outs, backs)])
         partial = spread_call(at, RUNS[:-1], counts, [o for back in backs for o in back])[0]
-        return join_pieces(share, output).astype(F32), bias_grad, partial, output
+        return join_pieces(share, output).astype(F32), partial, output
 
     backs = []
     for index, (_, _, level, near, far, cross) in enumerate(sides):
@@ -585,7 +584,8 @@
             near, far, cross = tie(near, came), tie(far, theirs), tie(cross, theirs)
         backs.append((level, across(near, 1), across(far, 2), across(cross, 3)))
     outs = [side[0] for side in sides]
-    weight_grad, bias_grad, partial, output = always(share_terms, mine, came, counts, backs[:-1], outs[:-1])
+    share, bias_grad = share_call(at, mine, came)
+    weight_grad, partial, output = always(share_terms, share, counts, backs[:-1], outs[:-1])
     features_grad, output = spread_call(at, RUNS[-1:], counts, backs[-1], partial, outs[-1], output)
     return (output, features_grad, weight_grad, bias_grad.reshape(width))
 

time: 223 us -> 223 us (level)
  no operation moved by 1% of the time
where the time goes in v8:
time: 223 us; the launch traced here: 222 us
  waiting for transfers between devices  93.2 us (42%)
  Pallas kernels  70.3 us (32%)
  starting transfers between devices  35.6 us (16%)
  blocking collectives  18 us (8%)
  local copies, waits for them, and re-layouts  2.43 us (1%)
    pallas_call x19, Pallas kernels, call(): pl.pallas_call(kernel, grid_spec=pltpu.PrefetchScalarGridSpec(num_scalar_...  70.3 us
    ppermute x17, waiting for transfers between devices, across(): return lax.ppermute(value, 'mp', [(i, i ^ code) for i in range(mp_count)])  61.5 us
    ppermute x6, waiting for transfers between devices, along(): lax.ppermute(value, 'dp', [(i, i ^ 1 << orders[stage][i % 2]) for i in ra...  31.7 us
    ppermute x17, starting transfers between devices, across(): return lax.ppermute(value, 'mp', [(i, i ^ code) for i in range(mp_count)])  26.2 us
    all_to_all x3, blocking collectives, swap(): return lax.all_to_all(value, 'dp', 0, 0, axis_index_groups=pairs)  18 us
    ppermute x6, starting transfers between devices, along(): lax.ppermute(value, 'dp', [(i, i ^ 1 << orders[stage][i % 2]) for i in ra...  9.38 us
  transfers between devices with their start and end apart: 23, of which 11 were waited for; matrix products, arithmetic and copies ran while one was open for 1% of the time, Pallas kernels for 29%

profile of v8, /device:TPU:0, one launch (start us, length us, event | category | flops | bytes accessed | tf_op | source)
XLA Modules:
  0.0 222.1 jit_solution(4777236978804713758)
XLA Ops:
  2.3 3.1 %collective-permute-start.6 = (bf16[272,512]{1,0:T(8,128)(2,1)S(1)}, bf16[272,512]{1,0:T(8,128)(2,1)}, u32[]{:S(2)}, u32[]{:S(2)}) collective-permute-start(bf16[272,512]{1,0:T(8,128)(2,1)S(1)} %weight_piece.1.bias_own), channel_id=1, source_target_pairs={{0,1},{1,0},{2,3},{3,2},{4,5},{5,4},{6,7},{7,6},{8,9},{9,8},{10,11... | collective-permute-start | bytes 835592 | tf_op jit(solution)/shard_map/ppermute | solution.py:496
  6.1 9.2 %count_and_aggregate.3 = (bf16[2048,2048]{1,0:T(8,128)(2,1)S(1)}, bf16[512,512]{1,0:T(8,128)(2,1)}, bf16[512,512]{1,0:T(8,128)(2,1)S(1)}, bf16[2,512,512]{2,1,0:T(8,128)(2,1)}, f32[512,1]{1,0:T(8,128)S(1)}) custom-call(s32[4]{0:T(128)S(1)} %pad_add_fusion.at, s32[256,256]{1,0:T(8,128)S(1)} %reshape.24.packed_ref, bf16[2048,512]{1,0:T(8,128)(2,1)} %feat_ref.1, ...), custom_call_target="tpu_custom_call" | custom-call | flops 1 | bytes 1 | tf_op jit(solution)/shard_map/count_and_aggregate/pallas_call | solution.py:43
  15.3 4.0 %collective-permute-start.7 = (bf16[512,512]{1,0:T(8,128)(2,1)S(1)}, bf16[512,512]{1,0:T(8,128)(2,1)}, u32[]{:S(2)}, u32[]{:S(2)}) collective-permute-start(bf16[512,512]{1,0:T(8,128)(2,1)S(1)} %get-tuple-element.178), channel_id=1, source_target_pairs={{0,3},{1,2},{2,1},{3,0},{4,7},{5,6},{6,5},{7,4},{8,11},{9,10},{10,... | collective-permute-start | bytes 1572872 | tf_op jit(solution)/shard_map/ppermute | solution.py:496
  20.0 26.9 %conditional.3 = (bf16[2048,512]{1,0:T(8,128)(2,1)S(1)}, bf16[2048,2048]{1,0:T(8,128)(2,1)S(1)}, bf16[512,512]{1,0:T(8,128)(2,1)S(1)}, bf16[512,512]{1,0:T(8,128...) conditional(s32[]{:T(128)} %bitcast.9, () %tuple.53, (bf16[272,512]{1,0:T(8,128)(2,1)}, ...), branch_computations={%region_0.1_spmd, %region_1.2_spmd} | conditional | flops 3 | bytes 12585022 | solution.py:534
  23.3 7.7 %count_and_aggregate.2 = (bf16[2048,2048]{1,0:T(8,128)(2,1)S(1)}, bf16[512,512]{1,0:T(8,128)(2,1)S(1)}, bf16[512,512]{1,0:T(8,128)(2,1)S(1)}, bf16[2,512,512]{2,1,0:T(8,128)(2,1)}, f32[512,1]{1,0:T(8,128)S(1)}) custom-call(s32[4]{0:T(128)S(1)} %get-tuple-element.48.at, s32[256,256]{1,0:T(8,128)} %copy-done.12, ...), custom_call_target="tpu_custom_call", output_to_operand_aliasing={{0}: (4, {})} | custom-call | flops 1 | bytes 1 | tf_op jit(solution)/shard_map/cond/branch_1_fun/count_and_aggregate/pallas_call | solution.py:43
  33.1 7.7 %collective-permute-done.1.theirs = bf16[512,512]{1,0:T(8,128)(2,1)S(1)} collective-permute-done((bf16[512,512]{1,0:T(8,128)(2,1)S(1)}, bf16[512,512]{1,0:T(8,128)(2,1)S(1)}, u32[]{:S(2)}, u32[]{:S(2)}) %collective-permute-start.1) | collective-permute-done | bytes 524320 | tf_op jit(solution)/shard_map/cond/branch_1_fun/ppermute | solution.py:507
  41.5 5.4 %all_to_all.12 = bf16[2,1024,512]{2,1,0:T(8,128)(2,1)S(1)} all-to-all(bf16[2,1024,512]{2,1,0:T(8,128)(2,1)S(1)} %join_halves.5), channel_id=1, replica_groups={{0,4},{8,12},{16,20},{24,28},{1,5},{9,13},{17,21},{25,29},{2,6},{10,14}..., dimensions={0} | all-to-all | bytes 4194304 | tf_op jit(solution)/shard_map/cond/branch_1_fun/all_to_all | solution.py:504
  46.9 8.0 %collective-permute-done.7.part3 = bf16[512,512]{1,0:T(8,128)(2,1)} collective-permute-done((bf16[512,512]{1,0:T(8,128)(2,1)S(1)}, bf16[512,512]{1,0:T(8,128)(2,1)}, u32[]{:S(2)}, u32[]{:S(2)}) %collective-permute-start.7) | collective-permute-done | bytes 524320 | tf_op jit(solution)/shard_map/ppermute | solution.py:496
  54.9 9.2 %collective-permute-done.11.near = bf16[2,512,512]{2,1,0:T(8,128)(2,1)} collective-permute-done((bf16[2,512,512]{2,1,0:T(8,128)(2,1)}, bf16[2,512,512]{2,1,0:T(8,128)(2,1)}, u32[]{:S(2)}, u32[]{:S(2)}) %collective-permute-start.11) | collective-permute-done | bytes 1048608 | tf_op jit(solution)/shard_map/ppermute | solution.py:496
  66.0 5.5 %linear_and_slope.5 = (bf16[256,512]{1,0:T(8,128)(2,1)}, bf16[2,256,512]{2,1,0:T(8,128)(2,1)}, bf16[256,512]{1,0:T(8,128)(2,1)}, bf16[2,256,512]{2,1,0:T(8,128)(...) custom-call(s32[4]{0:T(128)S(1)} %pad_add_fusion.at, s32[1]{0:T(128)S(6)} %copy.50.live, ...), custom_call_target="tpu_custom_call" | custom-call | flops 1 | bytes 1 | tf_op jit(solution)/shard_map/linear_and_slope/pallas_call | solution.py:43
  71.5 28.3 %collective-permute-done.12.part3 = bf16[512,512]{1,0:T(8,128)(2,1)S(1)} collective-permute-done((bf16[512,512]{1,0:T(8,128)(2,1)S(1)}, bf16[512,512]{1,0:T(8,128)(2,1)S(1)}, u32[]{:S(2)}, u32[]{:S(2)}) %collective-permute-start.12) | collective-permute-done | bytes 524320 | tf_op jit(solution)/shard_map/ppermute | solution.py:496
  99.8 6.7 %collective-permute-done.10.part2 = bf16[512,512]{1,0:T(8,128)(2,1)S(1)} collective-permute-done((bf16[512,512]{1,0:T(8,128)(2,1)S(1)}, bf16[512,512]{1,0:T(8,128)(2,1)S(1)}, u32[]{:S(2)}, u32[]{:S(2)}) %collective-permute-start.10) | collective-permute-done | bytes 524320 | tf_op jit(solution)/shard_map/ppermute | solution.py:496
  106.5 3.4 %collective-permute-start.14 = (bf16[256,512]{1,0:T(8,128)(2,1)S(1)}, bf16[256,512]{1,0:T(8,128)(2,1)S(1)}, u32[]{:S(2)}, u32[]{:S(2)}) collective-permute-start(bf16[256,512]{1,0:T(8,128)(2,1)S(1)} %get-tuple-element.197), channel_id=1, source_target_pairs={{0,2},{1,3},{2,0},{3,1},{4,6},{5,7},{6,4},{7,5},{8,10},{9,11},{10,... | collective-permute-start | bytes 786440 | tf_op jit(solution)/shard_map/ppermute | solution.py:496
  109.9 4.0 %collective-permute-start.15 = (bf16[256,512]{1,0:T(8,128)(2,1)S(1)}, bf16[256,512]{1,0:T(8,128)(2,1)S(1)}, u32[]{:S(2)}, u32[]{:S(2)}) collective-permute-start(bf16[256,512]{1,0:T(8,128)(2,1)S(1)} %get-tuple-element.199), channel_id=1, source_target_pairs={{0,3},{1,2},{2,1},{3,0},{4,7},{5,6},{6,5},{7,4},{8,11},{9,10},{10,... | collective-permute-start | bytes 786440 | tf_op jit(solution)/shard_map/ppermute | solution.py:496
  113.9 5.6 %linear_and_slope.6 = (bf16[512,512]{1,0:T(8,128)(2,1)S(1)}, bf16[2,512,512]{2,1,0:T(8,128)(2,1)S(1)}, bf16[512,512]{1,0:T(8,128)(2,1)S(1)}, bf16[2,512,512]{2,1...) custom-call(s32[4]{0:T(128)S(1)} %pad_add_fusion.at, s32[1]{0:T(128)S(6)} %copy.50.live, ...), custom_call_target="tpu_custom_call" | custom-call | flops 1 | bytes 1 | tf_op jit(solution)/shard_map/linear_and_slope/pallas_call | solution.py:43
  119.5 4.7 %linear_and_slope.4 = (bf16[256,512]{1,0:T(8,128)(2,1)S(1)}, bf16[2,256,512]{2,1,0:T(8,128)(2,1)}, bf16[256,512]{1,0:T(8,128)(2,1)S(1)}, bf16[2,256,512]{2,1,0:T...) custom-call(s32[4]{0:T(128)S(1)} %pad_add_fusion.at, s32[1]{0:T(128)S(6)} %copy.50.live, ...), custom_call_target="tpu_custom_call" | custom-call | flops 1 | bytes 1 | tf_op jit(solution)/shard_map/linear_and_slope/pallas_call | solution.py:43
  124.2 5.0 %linear_and_slope.7 = (bf16[512,512]{1,0:T(8,128)(2,1)S(1)}, bf16[2,512,512]{2,1,0:T(8,128)(2,1)S(1)}, bf16[512,512]{1,0:T(8,128)(2,1)S(1)}, bf16[2,512,512]{2,1...) custom-call(s32[4]{0:T(128)S(1)} %pad_add_fusion.at, ...), custom_call_target="tpu_custom_call", output_to_operand_aliasing={{0}: (12, {}), {1}: (13, {}), {2}: (14, {}), {3}: (15, {}),... | custom-call | flops 1 | bytes 1 | tf_op jit(solution)/shard_map/linear_and_slope/pallas_call | solution.py:43
  129.3 2.8 %collective-permute-done.15 = bf16[256,512]{1,0:T(8,128)(2,1)S(1)} collective-permute-done((bf16[256,512]{1,0:T(8,128)(2,1)S(1)}, bf16[256,512]{1,0:T(8,128)(2,1)S(1)}, u32[]{:S(2)}, u32[]{:S(2)}) %collective-permute-start.15) | collective-permute-done | bytes 262176 | tf_op jit(solution)/shard_map/ppermute | solution.py:496
  133.7 2.9 %collective-permute-start.18 = (bf16[512,512]{1,0:T(8,128)(2,1)}, bf16[512,512]{1,0:T(8,128)(2,1)}, u32[]{:S(2)}, u32[]{:S(2)}) collective-permute-start(bf16[512,512]{1,0:T(8,128)(2,1)} %get-tuple-element.215), channel_id=1, source_target_pairs={{0,3},{1,2},{2,1},{3,0},{4,7},{5,6},{6,5},{7,4},{8,11},{9,10},{10,... | collective-permute-start | bytes 1572872 | tf_op jit(solution)/shard_map/ppermute | solution.py:496
  136.6 42.4 %conditional.4 = ((bf16[1,272,512]{2,1,0:T(8,128)(2,1)}, bf16[1,272,512]{2,1,0:T(8,128)(2,1)})) conditional(s32[]{:T(128)} %bitcast.9, () %tuple.62, (s32[4]{0:T(128)S(1)}, bf16[512,512]{1,0:T(8,128)(2,1)}, bf16[2,512,512]{2,1,0:T(8,128)(2,1)}, bf16[512,512]{1,0:T(8,128)(2,1)}, bf16[512,512]{1,0:T(8,128)(2,1)}, ...), branch_computations={%region_2.3_spmd, %region_3.4_spmd} | conditional | flops 4 | bytes 15073372 | solution.py:534
  136.6 7.1 %weight_product.1 = bf16[2,2,1040,512]{3,2,1,0:T(8,128)(2,1)S(1)} custom-call(s32[4]{0:T(128)S(1)} %get-tuple-element.75.at, bf16[512,512]{1,0:T(8,128)(2,1)} %get-tuple-element.76.refs_0_, bf16[2,512,512]{2,1,0:T(8,128)(2,1)} %get-tuple-element.77.refs_1_, bf16[512,512]{1,0:T(8,128)(2,1)} %get-tuple-element.78.refs_2_, ...), custom_call_target="tpu_custom_call" | custom-call | flops 1 | bytes 1 | tf_op jit(solution)/shard_map/cond/branch_1_fun/weight_product/pallas_call | solution.py:43
  143.7 7.2 %all_to_all.13.refs_0_ = bf16[2,2,1040,512]{3,2,1,0:T(8,128)(2,1)S(1)} all-to-all(bf16[2,2,1040,512]{3,2,1,0:T(8,128)(2,1)S(1)} %weight_product.1), channel_id=1, replica_groups={{0,4},{8,12},{16,20},{24,28},{1,5},{9,13},{17,21},{25,29},{2,6},{10,14}..., dimensions={0} | all-to-all | bytes 8519680 | tf_op jit(solution)/shard_map/cond/branch_1_fun/all_to_all | solution.py:504
  153.5 13.6 %collective-permute-done.2.refs_1_ = bf16[2,528,512]{2,1,0:T(8,128)(2,1)S(1)} collective-permute-done((bf16[2,528,512]{2,1,0:T(8,128)(2,1)S(1)}, bf16[2,528,512]{2,1,0:T(8,128)(2,1)S(1)}, u32[]{:S(2)}, u32[]{:S(2)}) %collective-permute-start.2) | collective-permute-done | bytes 1081376 | tf_op jit(solution)/shard_map/cond/branch_1_fun/ppermute | solution.py:507
  169.5 8.0 %collective-permute-done.3.refs_1_ = bf16[2,272,512]{2,1,0:T(8,128)(2,1)S(1)} collective-permute-done((bf16[2,272,512]{2,1,0:T(8,128)(2,1)S(1)}, bf16[2,272,512]{2,1,0:T(8,128)(2,1)S(1)}, u32[]{:S(2)}, u32[]{:S(2)}) %collective-permute-start.3) | collective-permute-done | bytes 557088 | tf_op jit(solution)/shard_map/cond/branch_1_fun/ppermute | solution.py:507
  179.9 6.6 %collective-permute-done.19.theirs = bf16[1,272,512]{2,1,0:T(8,128)(2,1)S(1)} collective-permute-done((bf16[1,272,512]{2,1,0:T(8,128)(2,1)}, bf16[1,272,512]{2,1,0:T(8,128)(2,1)S(1)}, u32[]{:S(2)}, u32[]{:S(2)}) %collective-permute-start.19) | collective-permute-done | bytes 278560 | tf_op jit(solution)/shard_map/ppermute | solution.py:496
  188.7 2.2 %collective-permute-start.22 = (bf16[256,512]{1,0:T(8,128)(2,1)S(1)}, bf16[256,512]{1,0:T(8,128)(2,1)S(1)}, u32[]{:S(2)}, u32[]{:S(2)}) collective-permute-start(bf16[256,512]{1,0:T(8,128)(2,1)S(1)} %copy-done.4), channel_id=1, source_target_pairs={{0,3},{1,2},{2,1},{3,0},{4,7},{5,6},{6,5},{7,4},{8,11},{9,10},{10,... | collective-permute-start | bytes 786440 | tf_op jit(solution)/shard_map/ppermute | solution.py:496
  193.0 23.7 %conditional.5 = (f32[2048,512]{1,0:T(8,128)S(1)}, f32[2048,512]{1,0:T(8,128)S(1)}, bf16[2048,512]{1,0:T(8,128)(2,1)}) conditional(s32[]{:T(128)} %bitcast.9, () %tuple.76, (bf16[256,512]{1,0:T(8,128)(2,1)S(1)}, s32[4]{0:T(128)S(1)}, bf16[256,512]{1,0:T(8,128)(2,1)}, bf16[2,256,512]{2,1,0:T(8,128)(2,1)}, bf16[512,512]{1,0:T(8,128)(2,1)}, ...), branch_computations={%region_4.5_spmd, %region_5.6_spmd} | conditional | flops 1048580 | bytes 53971768 | solution.py:534
  194.5 3.3 %place_rows.1 = bf16[2048,512]{1,0:T(8,128)(2,1)} custom-call(s32[4]{0:T(128)S(1)} %get-tuple-element.91.at, bf16[256,512]{1,0:T(8,128)(2,1)} %get-tuple-element.93.refs_0_, bf16[2,256,512]{2,1,0:T(8,128)(2,1)} %get-tuple-element.94.refs_1_.refs_7_, bf16[512,512]{1,0:T(8,128)(2,1)} %get-tuple-element.95.refs_2_, ...), custom_call_target="tpu_custom_call" | custom-call | flops 1 | bytes 9000000 | tf_op jit(solution)/shard_map/cond/branch_1_fun/place_rows/pallas_call | solution.py:43
  197.9 2.1 collective-permute-done.4.theirs
  202.2 7.4 %spread_back.2 = f32[2048,512]{1,0:T(8,128)S(1)} custom-call(s32[4]{0:T(128)S(1)} %get-tuple-element.91.at, bf16[2048,2048]{1,0:T(8,128)(2,1)} %get-tuple-element.98.refs_0_.refs_1_.refs_2_.refs_3_.refs_4_.refs_5_, bf16[2048,2048]{1,0:T(8,128)(2,1)} %get-tuple-element.98.refs_0_.refs_1_.refs_2_.refs_3_.refs_4_.refs_5_, ...), custom_call_target="tpu_custom_call" | custom-call | flops 1 | bytes 24000000 | tf_op jit(solution)/shard_map/cond/branch_1_fun/spread_back/pallas_call | solution.py:43
  210.6 5.4 %all_to_all.14 = bf16[2,1024,512]{2,1,0:T(8,128)(2,1)S(1)} all-to-all(bf16[2,1024,512]{2,1,0:T(8,128)(2,1)S(1)} %join_halves.7), channel_id=1, replica_groups={{0,4},{8,12},{16,20},{24,28},{1,5},{9,13},{17,21},{25,29},{2,6},{10,14}..., dimensions={0} | all-to-all | bytes 4194304 | tf_op jit(solution)/shard_map/cond/branch_1_fun/all_to_all | solution.py:504
  216.8 5.3 %spread_back.3 = (bf16[2048,512]{1,0:T(8,128)(2,1)}, bf16[2048,512]{1,0:T(8,128)(2,1)}) custom-call(s32[4]{0:T(128)S(1)} %pad_add_fusion.at, bf16[2048,2048]{1,0:T(8,128)(2,1)} %copy-done.7, bf16[2048,2048]{1,0:T(8,128)(2,1)} %copy-done.7, bf16[256,512]{1,0:T(8,128)(2,1)S(1)} %get-tuple-element.189.refs_2_, ...), custom_call_target="tpu_custom_call", output_to_operand_aliasing={{1}: (9, {})} | custom-call | flops 1 | bytes 24000000 | tf_op jit(solution)/shard_map/spread_back/pallas_call | solution.py:43
  (92 shorter events, 29.0 us)
Async XLA Ops:
  2.3 12.9 %collective-permute-start.6 = (bf16[272,512]{1,0:T(8,128)(2,1)S(1)}, bf16[272,512]{1,0:T(8,128)(2,1)}, u32[]{:S(2)}, u32[]{:S(2)}) collective-permute-start(bf16[272,512]{1,0:T(8,128)(2,1)S(1)} %weight_piece.1.bias_own), channel_id=1, source_target_pairs={{0,1},{1,0},{2,3},{3,2},{4,5},{5,4},{6,7},{7,6},{8,9},{9,8},{10,11... | collective-permute-start | bytes 835592 | tf_op jit(solution)/shard_map/ppermute | solution.py:496
  6.0 13.9 %copy-start.8 = (bf16[2048,512]{1,0:T(8,128)(2,1)S(1)}, bf16[2048,512]{1,0:T(8,128)(2,1)}, u32[]{:S(2)}) copy-start(bf16[2048,512]{1,0:T(8,128)(2,1)} %cot_own.7) | copy-start | bytes 6291460
  6.1 13.9 %copy-start.10 = (bf16[2048,512]{1,0:T(8,128)(2,1)S(1)}, bf16[2048,512]{1,0:T(8,128)(2,1)}, u32[]{:S(2)}) copy-start(bf16[2048,512]{1,0:T(8,128)(2,1)} %feat_ref.1) | copy-start | bytes 6291460
  15.2 48.9 %collective-permute-start.11 = (bf16[2,512,512]{2,1,0:T(8,128)(2,1)}, bf16[2,512,512]{2,1,0:T(8,128)(2,1)}, u32[]{:S(2)}, u32[]{:S(2)}) collective-permute-start(bf16[2,512,512]{2,1,0:T(8,128)(2,1)} %get-tuple-element.185), channel_id=1, source_target_pairs={{0,1},{1,0},{2,3},{3,2},{4,5},{5,4},{6,7},{7,6},{8,9},{9,8},{10,11... | collective-permute-start | bytes 3145736 | tf_op jit(solution)/shard_map/ppermute | solution.py:496
  15.3 39.7 %collective-permute-start.7 = (bf16[512,512]{1,0:T(8,128)(2,1)S(1)}, bf16[512,512]{1,0:T(8,128)(2,1)}, u32[]{:S(2)}, u32[]{:S(2)}) collective-permute-start(bf16[512,512]{1,0:T(8,128)(2,1)S(1)} %get-tuple-element.178), channel_id=1, source_target_pairs={{0,3},{1,2},{2,1},{3,0},{4,7},{5,6},{6,5},{7,4},{8,11},{9,10},{10,... | collective-permute-start | bytes 1572872 | tf_op jit(solution)/shard_map/ppermute | solution.py:496
  19.3 46.7 %collective-permute-start.9 = (bf16[512,512]{1,0:T(8,128)(2,1)}, bf16[512,512]{1,0:T(8,128)(2,1)}, u32[]{:S(2)}, u32[]{:S(2)}) collective-permute-start(bf16[512,512]{1,0:T(8,128)(2,1)} %get-tuple-element.181.part0), channel_id=1, source_target_pairs={{0,2},{1,3},{2,0},{3,1},{4,6},{5,7},{6,4},{7,5},{8,10},{9,11},{10,... | collective-permute-start | bytes 1572872 | tf_op jit(solution)/shard_map/ppermute | solution.py:496
  20.0 46.1 %copy-start = (bf16[2048,512]{1,0:T(8,128)(2,1)S(1)}, bf16[2048,512]{1,0:T(8,128)(2,1)}, u32[]{:S(2)}) copy-start(bf16[2048,512]{1,0:T(8,128)(2,1)} %weight_own.7) | copy-start | bytes 6291460
  21.7 9.2 %collective-permute-start = (bf16[256,512]{1,0:T(8,128)(2,1)S(1)}, bf16[256,512]{1,0:T(8,128)(2,1)S(1)}, u32[]{:S(2)}, u32[]{:S(2)}) collective-permute-start(bf16[256,512]{1,0:T(8,128)(2,1)S(1)} %slice.2.mine), channel_id=1, source_target_pairs={{0,8},{4,20},{8,0},{12,28},{16,24},{20,4},{24,16},{28,12},{1,9},{5... | collective-permute-start | bytes 786440 | tf_op jit(solution)/shard_map/cond/branch_1_fun/ppermute | solution.py:507
  31.5 9.2 %collective-permute-start.1 = (bf16[512,512]{1,0:T(8,128)(2,1)S(1)}, bf16[512,512]{1,0:T(8,128)(2,1)S(1)}, u32[]{:S(2)}, u32[]{:S(2)}) collective-permute-start(bf16[512,512]{1,0:T(8,128)(2,1)S(1)} %bitcast.12), channel_id=1, source_target_pairs={{0,16},{4,12},{8,24},{12,4},{16,0},{20,28},{24,8},{28,20},{1,17},{... | collective-permute-start | bytes 1572872 | tf_op jit(solution)/shard_map/cond/branch_1_fun/ppermute | solution.py:507
  46.9 24.6 %copy-start.7 = (bf16[2048,2048]{1,0:T(8,128)(2,1)}, bf16[2048,2048]{1,0:T(8,128)(2,1)S(1)}, u32[]{:S(2)}) copy-start(bf16[2048,2048]{1,0:T(8,128)(2,1)S(1)} %get-tuple-element.174.refs_0_.refs_1_) | copy-start | bytes 25165828
  54.9 64.6 %collective-permute-start.8 = (bf16[2,512,512]{2,1,0:T(8,128)(2,1)}, bf16[2,512,512]{2,1,0:T(8,128)(2,1)S(1)}, u32[]{:S(2)}, u32[]{:S(2)}) collective-permute-start(bf16[2,512,512]{2,1,0:T(8,128)(2,1)} %get-tuple-element.179), channel_id=1, source_target_pairs={{0,1},{1,0},{2,3},{3,2},{4,5},{5,4},{6,7},{7,6},{8,9},{9,8},{10,11... | collective-permute-start | bytes 3145736 | tf_op jit(solution)/shard_map/ppermute | solution.py:496
  64.1 35.7 %collective-permute-start.12 = (bf16[512,512]{1,0:T(8,128)(2,1)S(1)}, bf16[512,512]{1,0:T(8,128)(2,1)S(1)}, u32[]{:S(2)}, u32[]{:S(2)}) collective-permute-start(bf16[512,512]{1,0:T(8,128)(2,1)S(1)} %get-tuple-element.186), channel_id=1, source_target_pairs={{0,3},{1,2},{2,1},{3,0},{4,7},{5,6},{6,5},{7,4},{8,11},{9,10},{10,... | collective-permute-start | bytes 1572872 | tf_op jit(solution)/shard_map/ppermute | solution.py:496
  66.0 40.5 %collective-permute-start.10 = (bf16[512,512]{1,0:T(8,128)(2,1)S(1)}, bf16[512,512]{1,0:T(8,128)(2,1)S(1)}, u32[]{:S(2)}, u32[]{:S(2)}) collective-permute-start(bf16[512,512]{1,0:T(8,128)(2,1)S(1)} %get-tuple-element.182.part0), channel_id=1, source_target_pairs={{0,2},{1,3},{2,0},{3,1},{4,6},{5,7},{6,4},{7,5},{8,10},{9,11},{10,... | collective-permute-start | bytes 1572872 | tf_op jit(solution)/shard_map/ppermute | solution.py:496
  66.0 47.9 %copy-start.9 = (bf16[2048,512]{1,0:T(8,128)(2,1)S(1)}, bf16[2048,512]{1,0:T(8,128)(2,1)}, u32[]{:S(2)}) copy-start(bf16[2048,512]{1,0:T(8,128)(2,1)} %cot_own.7) | copy-start | bytes 6291460
  99.8 32.3 %collective-permute-start.13 = (bf16[2,256,512]{2,1,0:T(8,128)(2,1)S(1)}, bf16[2,256,512]{2,1,0:T(8,128)(2,1)S(1)}, u32[]{:S(2)}, u32[]{:S(2)}) collective-permute-start(bf16[2,256,512]{2,1,0:T(8,128)(2,1)S(1)} %get-tuple-element.195), channel_id=1, source_target_pairs={{0,1},{1,0},{2,3},{3,2},{4,5},{5,4},{6,7},{7,6},{8,9},{9,8},{10,11... | collective-permute-start | bytes 1572872 | tf_op jit(solution)/shard_map/ppermute | solution.py:496
  106.5 22.8 %collective-permute-start.14 = (bf16[256,512]{1,0:T(8,128)(2,1)S(1)}, bf16[256,512]{1,0:T(8,128)(2,1)S(1)}, u32[]{:S(2)}, u32[]{:S(2)}) collective-permute-start(bf16[256,512]{1,0:T(8,128)(2,1)S(1)} %get-tuple-element.197), channel_id=1, source_target_pairs={{0,2},{1,3},{2,0},{3,1},{4,6},{5,7},{6,4},{7,5},{8,10},{9,11},{10,... | collective-permute-start | bytes 786440 | tf_op jit(solution)/shard_map/ppermute | solution.py:496
  109.9 22.2 %collective-permute-start.15 = (bf16[256,512]{1,0:T(8,128)(2,1)S(1)}, bf16[256,512]{1,0:T(8,128)(2,1)S(1)}, u32[]{:S(2)}, u32[]{:S(2)}) collective-permute-start(bf16[256,512]{1,0:T(8,128)(2,1)S(1)} %get-tuple-element.199), channel_id=1, source_target_pairs={{0,3},{1,2},{2,1},{3,0},{4,7},{5,6},{6,5},{7,4},{8,11},{9,10},{10,... | collective-permute-start | bytes 786440 | tf_op jit(solution)/shard_map/ppermute | solution.py:496
  132.1 46.9 %collective-permute-start.16 = (bf16[2,512,512]{2,1,0:T(8,128)(2,1)}, bf16[2,512,512]{2,1,0:T(8,128)(2,1)}, u32[]{:S(2)}, u32[]{:S(2)}) collective-permute-start(bf16[2,512,512]{2,1,0:T(8,128)(2,1)} %get-tuple-element.213), channel_id=1, source_target_pairs={{0,1},{1,0},{2,3},{3,2},{4,5},{5,4},{6,7},{7,6},{8,9},{9,8},{10,11... | collective-permute-start | bytes 3145736 | tf_op jit(solution)/shard_map/ppermute | solution.py:496
  132.9 46.0 %collective-permute-start.17 = (bf16[512,512]{1,0:T(8,128)(2,1)S(1)}, bf16[512,512]{1,0:T(8,128)(2,1)}, u32[]{:S(2)}, u32[]{:S(2)}) collective-permute-start(bf16[512,512]{1,0:T(8,128)(2,1)S(1)} %get-tuple-element.214), channel_id=1, source_target_pairs={{0,2},{1,3},{2,0},{3,1},{4,6},{5,7},{6,4},{7,5},{8,10},{9,11},{10,... | collective-permute-start | bytes 1572872 | tf_op jit(solution)/shard_map/ppermute | solution.py:496
  133.7 45.3 %collective-permute-start.18 = (bf16[512,512]{1,0:T(8,128)(2,1)}, bf16[512,512]{1,0:T(8,128)(2,1)}, u32[]{:S(2)}, u32[]{:S(2)}) collective-permute-start(bf16[512,512]{1,0:T(8,128)(2,1)} %get-tuple-element.215), channel_id=1, source_target_pairs={{0,3},{1,2},{2,1},{3,0},{4,7},{5,6},{6,5},{7,4},{8,11},{9,10},{10,... | collective-permute-start | bytes 1572872 | tf_op jit(solution)/shard_map/ppermute | solution.py:496
  136.5 50.0 %copy-start.2 = (bf16[2,256,512]{2,1,0:T(8,128)(2,1)S(1)}, bf16[2,256,512]{2,1,0:T(8,128)(2,1)}, u32[]{:S(2)}) copy-start(bf16[2,256,512]{2,1,0:T(8,128)(2,1)} %copy-done.1) | copy-start | bytes 1572868
  136.5 50.3 %copy-start.6 = (bf16[256,512]{1,0:T(8,128)(2,1)S(1)}, bf16[256,512]{1,0:T(8,128)(2,1)}, u32[]{:S(2)}) copy-start(bf16[256,512]{1,0:T(8,128)(2,1)} %copy-done.5) | copy-start | bytes 786436
  136.5 52.1 %copy-start.4 = (bf16[256,512]{1,0:T(8,128)(2,1)S(1)}, bf16[256,512]{1,0:T(8,128)(2,1)}, u32[]{:S(2)}) copy-start(bf16[256,512]{1,0:T(8,128)(2,1)} %copy-done.3) | copy-start | bytes 786436
  151.9 15.2 %collective-permute-start.2 = (bf16[2,528,512]{2,1,0:T(8,128)(2,1)S(1)}, bf16[2,528,512]{2,1,0:T(8,128)(2,1)S(1)}, u32[]{:S(2)}, u32[]{:S(2)}) collective-permute-start(bf16[2,528,512]{2,1,0:T(8,128)(2,1)S(1)} %get-tuple-element.88), channel_id=1, source_target_pairs={{0,16},{4,12},{8,24},{12,4},{16,0},{20,28},{24,8},{28,20},{1,17},{... | collective-permute-start | bytes 3244040 | tf_op jit(solution)/shard_map/cond/branch_1_fun/ppermute | solution.py:507
  168.0 9.6 %collective-permute-start.3 = (bf16[2,272,512]{2,1,0:T(8,128)(2,1)S(1)}, bf16[2,272,512]{2,1,0:T(8,128)(2,1)S(1)}, u32[]{:S(2)}, u32[]{:S(2)}) collective-permute-start(bf16[2,272,512]{2,1,0:T(8,128)(2,1)S(1)} %get-tuple-element.90), channel_id=1, source_target_pairs={{0,8},{4,20},{8,0},{12,28},{16,24},{20,4},{24,16},{28,12},{1,9},{5... | collective-permute-start | bytes 1671176 | tf_op jit(solution)/shard_map/cond/branch_1_fun/ppermute | solution.py:507
  179.0 7.5 %collective-permute-start.19 = (bf16[1,272,512]{2,1,0:T(8,128)(2,1)}, bf16[1,272,512]{2,1,0:T(8,128)(2,1)S(1)}, u32[]{:S(2)}, u32[]{:S(2)}) collective-permute-start(bf16[1,272,512]{2,1,0:T(8,128)(2,1)} %get-tuple-element.216), channel_id=1, source_target_pairs={{0,1},{1,0},{2,3},{3,2},{4,5},{5,4},{6,7},{7,6},{8,9},{9,8},{10,11... | collective-permute-start | bytes 835592 | tf_op jit(solution)/shard_map/ppermute | solution.py:496
  186.5 30.2 %collective-permute-start.20 = (bf16[2,256,512]{2,1,0:T(8,128)(2,1)S(1)}, bf16[2,256,512]{2,1,0:T(8,128)(2,1)S(1)}, u32[]{:S(2)}, u32[]{:S(2)}) collective-permute-start(bf16[2,256,512]{2,1,0:T(8,128)(2,1)S(1)} %copy-done.2), channel_id=1, source_target_pairs={{0,1},{1,0},{2,3},{3,2},{4,5},{5,4},{6,7},{7,6},{8,9},{9,8},{10,11... | collective-permute-start | bytes 1572872 | tf_op jit(solution)/shard_map/ppermute | solution.py:496
  186.8 29.9 %collective-permute-start.21 = (bf16[256,512]{1,0:T(8,128)(2,1)S(1)}, bf16[256,512]{1,0:T(8,128)(2,1)S(1)}, u32[]{:S(2)}, u32[]{:S(2)}) collective-permute-start(bf16[256,512]{1,0:T(8,128)(2,1)S(1)} %copy-done.6), channel_id=1, source_target_pairs={{0,2},{1,3},{2,0},{3,1},{4,6},{5,7},{6,4},{7,5},{8,10},{9,11},{10,... | collective-permute-start | bytes 786440 | tf_op jit(solution)/shard_map/ppermute | solution.py:496
  188.7 28.1 %collective-permute-start.22 = (bf16[256,512]{1,0:T(8,128)(2,1)S(1)}, bf16[256,512]{1,0:T(8,128)(2,1)S(1)}, u32[]{:S(2)}, u32[]{:S(2)}) collective-permute-start(bf16[256,512]{1,0:T(8,128)(2,1)S(1)} %copy-done.4), channel_id=1, source_target_pairs={{0,3},{1,2},{2,1},{3,0},{4,7},{5,6},{6,5},{7,4},{8,11},{9,10},{10,... | collective-permute-start | bytes 786440 | tf_op jit(solution)/shard_map/ppermute | solution.py:496
  193.0 7.0 %collective-permute-start.4 = (bf16[256,512]{1,0:T(8,128)(2,1)S(1)}, bf16[256,512]{1,0:T(8,128)(2,1)S(1)}, u32[]{:S(2)}, u32[]{:S(2)}) collective-permute-start(bf16[256,512]{1,0:T(8,128)(2,1)S(1)} %get-tuple-element.92.mine), channel_id=1, source_target_pairs={{0,8},{4,20},{8,0},{12,28},{16,24},{20,4},{24,16},{28,12},{1,9},{5... | collective-permute-start | bytes 786440 | tf_op jit(solution)/shard_map/cond/branch_1_fun/ppermute | solution.py:507
  194.5 7.6 %copy-start.22 = (bf16[256,512]{1,0:T(8,128)(2,1)S(1)}, bf16[256,512]{1,0:T(8,128)(2,1)}, u32[]{:S(2)}) copy-start(bf16[256,512]{1,0:T(8,128)(2,1)} %get-tuple-element.101.refs_9_) | copy-start | bytes 786436 | tf_op jit(solution)/shard_map/cond
  200.6 9.2 %collective-permute-start.5 = (bf16[512,512]{1,0:T(8,128)(2,1)S(1)}, bf16[512,512]{1,0:T(8,128)(2,1)S(1)}, u32[]{:S(2)}, u32[]{:S(2)}) collective-permute-start(bf16[512,512]{1,0:T(8,128)(2,1)S(1)} %bitcast.14), channel_id=1, source_target_pairs={{0,16},{4,12},{8,24},{12,4},{16,0},{20,28},{24,8},{28,20},{1,17},{... | collective-permute-start | bytes 1572872 | tf_op jit(solution)/shard_map/cond/branch_1_fun/ppermute | solution.py:507
  (15 other events, 87.3 us)
